TPU v7x, 32 devices: a whole 2x2x4 slice. The times are simulated.
32 devices in a mesh: groups: 2 (over y), dom: 4 (over z), cls: 4 (over x, core).
Axes of the slice: x: 2, y: 2, z: 4, core: 2. Of those that a mesh axis runs over, the one named last changes fastest.
Arguments:
- particle_spectra: bfloat16 [512, 2304], P(('groups', 'dom', 'cls')), parts along dimension 0, may hold values from -10 to 10
- class_spectra: bfloat16 [512, 2304], P(('groups', 'cls')), parts along dimension 0, may hold values from -0.25 to 0.25
- shift_index: int32 [512, 16], P(('groups', 'dom', 'cls')), parts along dimension 0, may hold values from 0 to 120
- prior_rotation: int32 [512], P(('groups', 'dom', 'cls')), parts along dimension 0, may hold values from 0 to 7
- particle_group: int32 [512], P(('groups', 'dom', 'cls')), parts along dimension 0, may hold values from 0 to 63
- group_scale: float32 [128], P('groups'), parts along dimension 0, may hold values from 0.6 to 1.6
Outputs:
- class_sums: float32 [512, 2304], P(('groups', 'cls'), 'dom'), parts along dimension 0
- class_weights: float32 [512], P(('groups', 'cls')), parts along dimension 0
There are 2 independent parts, one for each index of `groups`. A program takes and returns all parts, laid end to end along the dimension named above; each array names one. Nothing has to cross between parts.
All inputs are finite; a program needn't handle non-finite values.
Results may differ from a plain program's by a relative error of at most 0.0067.
Values may be sent and summed in bfloat16 or wider, within the bound.
No kernel may reach another device: no remote copies, remote signals or barrier semaphores. Data moves between devices by JAX's collectives and lax.ppermute only.
A program may use at most 64 MiB of HBM per device.

v0:
```python
import math

import jax
import jax.numpy as jnp
from jax import lax
from jax.sharding import PartitionSpec as P

CYCLES = 18
ANG = 64
IMG = 64
ANG_STEP = 1
ROTS = 8
SHIFT_R = 5
SHIFTW = 11


rot_prior_weight = 0.5


def partner_2(array, axis, bit):
    return lax.ppermute(array, axis, [(i, i ^ 1 << bit) for i in range(lax.axis_size(axis))])


def frequency_grid():
    radius = jnp.arange(CYCLES).astype(jnp.float32) + 1.0
    angles = jnp.arange(ANG).astype(jnp.float32) * (2.0 * math.pi / ANG)
    freq_x = (radius[:, None] * jnp.cos(angles)[None, :]).reshape(-1)
    freq_y = (radius[:, None] * jnp.sin(angles)[None, :]).reshape(-1)
    return (freq_x, freq_y)


def shifted_rows(spectra, shifts):
    half_width = spectra.shape[1] // 2
    freq_x, freq_y = frequency_grid()
    offset_x = (shifts % SHIFTW - SHIFT_R).astype(jnp.float32)
    offset_y = (shifts // SHIFTW - SHIFT_R).astype(jnp.float32)
    phase_angle = (
        2.0
        * math.pi
        / IMG
        * (
            offset_x[:, :, None] * freq_x[None, None, :]
            + offset_y[:, :, None] * freq_y[None, None, :]
        )
    )
    real_in = spectra[:, None, :half_width].astype(jnp.float32)
    imag_in = spectra[:, None, half_width:].astype(jnp.float32)
    cosine = jnp.cos(phase_angle)
    sine_part = jnp.sin(phase_angle)
    real_out = real_in * cosine - imag_in * sine_part
    imag_out = real_in * sine_part + imag_in * cosine
    joined = jnp.concatenate([real_out, imag_out], axis=2).astype(jnp.bfloat16)
    return joined.reshape(spectra.shape[0] * shifts.shape[1], 2 * half_width)


def turned_rows(shifted, rotation):
    offset = ANG_STEP * rotation % ANG
    if offset == 0:
        return shifted
    column = lax.broadcasted_iota(jnp.int32, (1, shifted.shape[1]), 1) % ANG
    ahead = jnp.roll(shifted, -offset, axis=1)
    behind = jnp.roll(shifted, ANG - offset, axis=1)
    return jnp.where(column < ANG - offset, ahead, behind)


def group_scales(groups, scale_table):
    matches = groups[:, None] == jnp.arange(scale_table.shape[0])[None, :]
    return jnp.sum(jnp.where(matches, scale_table[None, :], 0.0), axis=1)


def prepare(spectra, shifts, priors, groups, scale_table, references):
    candidates = shifts.shape[1]
    shifted = shifted_rows(spectra, shifts)
    row_scales = jnp.repeat(group_scales(groups, scale_table), candidates)
    prior_rows = jnp.repeat(priors, candidates)
    ref_norms = jnp.einsum("kf,kf->k", references, references, preferred_element_type=jnp.float32)
    turned_all = [turned_rows(shifted, rotation) for rotation in range(ROTS)]
    hypotheses = []
    for rotation in range(ROTS):
        intersection = jnp.einsum(
            "nf,kf->nk", turned_all[rotation], references, preferred_element_type=jnp.float32
        )
        distance = jnp.abs(rotation - prior_rows).astype(jnp.float32)
        hypotheses.append(
            row_scales[:, None] * intersection
            - 0.5 * (row_scales * row_scales)[:, None] * ref_norms[None, :]
            - rot_prior_weight * (distance * distance)[:, None]
        )
    reshaped = jnp.stack(hypotheses).reshape(ROTS, spectra.shape[0], candidates, -1)
    return (turned_all, row_scales, reshaped)


def posterior_sums(turned_all, posterior, row_scales):
    class_total = jnp.zeros((posterior.shape[2], turned_all[0].shape[1]), jnp.float32)
    for rotation in range(ROTS):
        weight = (posterior[rotation] * row_scales[:, None]).astype(jnp.bfloat16)
        class_total = class_total + jnp.einsum(
            "nk,nf->kf", weight, turned_all[rotation], preferred_element_type=jnp.float32
        )
    weight_sums = jnp.sum(posterior * (row_scales * row_scales)[None, :, None], axis=(0, 1))
    return (class_total, weight_sums)


def body(particle_spectra, class_spectra, shift_index, prior_rotation, particle_group, group_scale):
    position = lax.axis_index("cls")
    references = class_spectra
    for bit_number in range(lax.axis_size("cls").bit_length() - 1):
        partner = partner_2(references, "cls", bit_number)
        upper_half = position // (1 << bit_number) % 2 == 1
        references = jnp.where(
            upper_half,
            jnp.concatenate([partner, references], axis=0),
            jnp.concatenate([references, partner], axis=0),
        )
    turned_all, row_scales, reshaped = prepare(
        particle_spectra, shift_index, prior_rotation, particle_group, group_scale, references
    )
    highest = jnp.max(reshaped, axis=(0, 2, 3))
    exponent = jnp.exp(reshaped - highest[None, :, None, None])
    normalizer = jnp.sum(exponent, axis=(0, 2, 3))
    posterior = (exponent / normalizer[None, :, None, None]).reshape(
        ROTS, turned_all[0].shape[0], -1
    )
    class_total, weight_sums = posterior_sums(turned_all, posterior, row_scales)
    spread_part = lax.psum_scatter(class_total, "dom", scatter_dimension=1, tiled=True)
    owned_sums, weight_sums = (
        lax.psum_scatter(spread_part, "cls", scatter_dimension=0, tiled=True),
        lax.psum_scatter(weight_sums, "cls", scatter_dimension=0, tiled=True),
    )
    weight_sums = lax.psum(weight_sums, "dom")
    return (owned_sums, weight_sums)


def solution(mesh):
    placed = (
        P(("groups", "dom", "cls"), None),
        P(("groups", "cls"), None),
        P(("groups", "dom", "cls"), None),
        P(("groups", "dom", "cls")),
        P(("groups", "dom", "cls")),
        P("groups"),
    )
    return jax.shard_map(
        body,
        mesh=mesh,
        in_specs=placed,
        out_specs=(P(("groups", "cls"), "dom"), P(("groups", "cls"))),
        check_vma=False,
    )
```

profile of v0, /device:TPU:0, one launch (start us, length us, event | category | flops | bytes accessed | tf_op | source)
XLA Modules:
  0.0 218.2 jit_solution(4090810758393310311)
XLA Ops:
  11.4 0.7 fusion.59
  12.5 0.8 slice_convert_fusion.1
  13.3 5.0 %fusion.4 = (bf16[256,1152]{1,0:T(8,128)(2,1)S(1)}, bf16[256,1152]{1,0:T(8,128)(2,1)S(1)}) fusion(f32[16,1152]{1,0:T(8,128)S(1)} %get-tuple-element.19, f32[1152]{0:T(1024)S(1)} %mul.507, f32[256]{0:T(256)S(1)} %mul.503, f32[1152]{0:T(1024)S(1)} %mul.500, f32[256]{0:T(256)S(1)} %mul.493, f32[16,1152]{1,0:T(8,128)S(1)} %get-tuple-element.18), kind=kLoop, calls=%fused_computation.47 | loop fusion | flops 3538944 | bytes 1338368 | tf_op jit(solution)/shard_map/convert
  22.7 0.7 slice.241
  23.4 0.7 slice.235
  24.1 0.7 slice.229
  24.8 0.7 slice.223
  25.5 0.7 slice.217
  26.3 0.7 slice.211
  27.0 0.7 slice.205
  27.7 1.5 fusion.7
  29.2 1.1 fusion.8
  30.3 1.5 fusion.9
  31.8 1.2 fusion.10
  33.0 1.5 fusion.11
  34.6 1.1 fusion.12
  35.7 1.5 fusion.13
  37.2 1.1 fusion.14
  38.3 1.5 fusion.15
  39.8 1.1 fusion.16
  43.4 0.8 select_reduce_fusion
  44.4 0.7 broadcast.361
  45.8 0.8 broadcast.359
  47.3 0.7 broadcast.357
  48.6 0.7 broadcast.355
  52.6 0.7 broadcast.363
  54.1 1.5 fusion.19
  55.6 1.2 maximum_select_fusion.8
  56.8 2.6 %collective-permute-start.1 = (bf16[128,2304]{1,0:T(8,128)(2,1)S(1)}, bf16[128,2304]{1,0:T(8,128)(2,1)S(1)}, u32[]{:S(2)}, u32[]{:S(2)}) collective-permute-start(bf16[128,2304]{1,0:T(8,128)(2,1)S(1)} %maximum_select_fusion.8), channel_id=1, source_target_pairs={{0,2},{1,3},{2,0},{3,1},{4,6},{5,7},{6,4},{7,5},{8,10},{9,11},{10,... | collective-permute-start | bytes 1769480 | tf_op jit(solution)/shard_map/ppermute | solution.py:21
  60.0 1.1 fusion.20
  61.1 12.2 %collective-permute-done.1 = bf16[128,2304]{1,0:T(8,128)(2,1)S(1)} collective-permute-done((bf16[128,2304]{1,0:T(8,128)(2,1)S(1)}, bf16[128,2304]{1,0:T(8,128)(2,1)S(1)}, u32[]{:S(2)}, u32[]{:S(2)}) %collective-permute-start.1) | collective-permute-done | bytes 589856 | tf_op jit(solution)/shard_map/ppermute | solution.py:21
  73.8 1.9 fusion.74
  75.7 0.8 reduce_max.70
  76.4 4.6 %fusion.75 = (f32[256]{0:T(256)}, f32[256,256]{1,0:T(8,128)}) fusion(f32[256]{0:T(256)} %reshape.301, f32[256]{0:T(256)} %copy-done.69, f32[256]{0:T(256)} %copy-done.70, bf16[128,2304]{1,0:T(8,128)(2,1)} %copy-done.12, bf16[128,2304]{1,0:T(8,128)(2,1)} %copy-done.27, pred[]{:T(512)S(6)} %eq.35, bf16[256,1]{1,0:T(8,128)(2,1)} %slice.204, ...), kind=kOutput, calls=%fused_computation.184 | convolution fusion | flops 312934144 | bytes 3808513 | tf_op jit(solution)/shard_map/nf,kf->nk/dot_general | solution.py:80
  81.0 0.8 reduce_max.73
  83.1 4.0 %fusion.73 = (f32[256]{0:T(256)S(1)}, f32[256,256]{1,0:T(8,128)}) fusion(f32[256]{0:T(256)} %reshape.303, f32[256]{0:T(256)} %copy-done.69, f32[256]{0:T(256)} %copy-done.70, bf16[128,2304]{1,0:T(8,128)(2,1)} %copy-done.12, bf16[128,2304]{1,0:T(8,128)(2,1)} %copy-done.27, pred[]{:T(512)S(6)} %eq.35, bf16[256,2]{1,0:T(8,128)(2,1)} %slice.210, ...), kind=kOutput, calls=%fused_computation.182 | convolution fusion | flops 312934144 | bytes 3808513 | tf_op jit(solution)/shard_map/nf,kf->nk/dot_general | solution.py:80
  87.2 0.7 reduce_max.81
  87.9 4.6 %fusion.72 = (f32[256]{0:T(256)}, f32[256,256]{1,0:T(8,128)}) fusion(f32[256]{0:T(256)} %reshape.305, f32[256]{0:T(256)} %copy-done.69, f32[256]{0:T(256)} %copy-done.70, bf16[128,2304]{1,0:T(8,128)(2,1)} %copy-done.12, bf16[128,2304]{1,0:T(8,128)(2,1)} %copy-done.27, pred[]{:T(512)S(6)} %eq.35, bf16[256,3]{1,0:T(8,128)(2,1)} %slice.216, ...), kind=kOutput, calls=%fused_computation.181 | convolution fusion | flops 312934144 | bytes 3808513 | tf_op jit(solution)/shard_map/nf,kf->nk/dot_general | solution.py:80
  92.5 0.7 reduce_max.87
  93.9 4.5 %fusion.71 = (f32[256]{0:T(256)}, f32[256,256]{1,0:T(8,128)}) fusion(f32[256]{0:T(256)} %reshape.307, f32[256]{0:T(256)} %copy-done.69, f32[256]{0:T(256)} %copy-done.70, bf16[128,2304]{1,0:T(8,128)(2,1)} %copy-done.12, bf16[128,2304]{1,0:T(8,128)(2,1)} %copy-done.27, pred[]{:T(512)S(6)} %eq.35, bf16[256,4]{1,0:T(8,128)(2,1)} %slice.222, ...), kind=kOutput, calls=%fused_computation.180 | convolution fusion | flops 312934144 | bytes 3808513 | tf_op jit(solution)/shard_map/nf,kf->nk/dot_general | solution.py:80
  98.4 0.7 reduce_max.94
  99.1 0.7 reduce_max.95
  99.8 4.6 %fusion.70 = (f32[256]{0:T(256)}, f32[256,256]{1,0:T(8,128)}) fusion(f32[256]{0:T(256)} %reshape.309, f32[256]{0:T(256)} %copy-done.69, f32[256]{0:T(256)} %copy-done.70, bf16[128,2304]{1,0:T(8,128)(2,1)} %copy-done.12, bf16[128,2304]{1,0:T(8,128)(2,1)} %copy-done.27, pred[]{:T(512)S(6)} %eq.35, bf16[256,5]{1,0:T(8,128)(2,1)} %slice.228, ...), kind=kOutput, calls=%fused_computation.179 | convolution fusion | flops 312934144 | bytes 3808513 | tf_op jit(solution)/shard_map/nf,kf->nk/dot_general | solution.py:80
  104.4 0.8 reduce_max.101
  105.9 4.1 %fusion.69 = (f32[256]{0:T(256)}, f32[256,256]{1,0:T(8,128)}) fusion(f32[256]{0:T(256)} %reshape.311, f32[256]{0:T(256)} %copy-done.69, f32[256]{0:T(256)} %copy-done.70, bf16[128,2304]{1,0:T(8,128)(2,1)} %copy-done.12, bf16[128,2304]{1,0:T(8,128)(2,1)} %copy-done.27, pred[]{:T(512)S(6)} %eq.35, bf16[256,6]{1,0:T(8,128)(2,1)} %slice.234, ...), kind=kOutput, calls=%fused_computation.178 | convolution fusion | flops 312934144 | bytes 3808513 | tf_op jit(solution)/shard_map/nf,kf->nk/dot_general | solution.py:80
  110.0 0.7 reduce_max.105
  110.7 0.7 reduce_max.109
  111.4 4.6 %fusion.68 = (f32[256]{0:T(256)}, f32[256,256]{1,0:T(8,128)}) fusion(f32[256]{0:T(256)} %reshape.313, f32[256]{0:T(256)} %copy-done.69, f32[256]{0:T(256)} %copy-done.70, bf16[128,2304]{1,0:T(8,128)(2,1)} %copy-done.12, bf16[128,2304]{1,0:T(8,128)(2,1)} %copy-done.27, pred[]{:T(512)S(6)} %eq.35, bf16[256,7]{1,0:T(8,128)(2,1)} %slice.240, ...), kind=kOutput, calls=%fused_computation.177 | convolution fusion | flops 312934144 | bytes 3808513 | tf_op jit(solution)/shard_map/nf,kf->nk/dot_general | solution.py:80
  116.0 0.8 reduce_max.112
  117.4 1.0 constant_dynamic-update-slice_fusion.7
  118.5 1.0 constant_dynamic-update-slice_fusion.6
  119.7 0.7 copy-done.19
  124.4 1.3 convolution_add_fusion.6
  126.0 1.3 convolution_add_fusion.5
  127.7 1.3 convolution_add_fusion.4
  129.3 1.3 convolution_add_fusion.3
  130.9 1.3 convolution_add_fusion.2
  132.3 1.3 convolution_add_fusion.1
  133.9 2.7 %convolution_add_fusion = f32[256,2304]{0,1:T(8,128)} fusion(f32[256,2304]{0,1:T(8,128)S(1)} %convolution_add_fusion.1, bf16[256,256]{1,0:T(8,128)(2,1)S(1)} %get-tuple-element.24, bf16[256,7]{1,0:T(8,128)(2,1)S(1)} %copy-done.29, bf16[256,2297]{1,0:T(8,128)(2,1)S(1)} %copy-done.10, bf16[256,2247]{1,0:T(8,128)(2,1)S(1)} %copy-done.11, ...), kind=kOutput, calls=%fused_computation | convolution fusion | flops 307888128 | bytes 7211264 | tf_op jit(solution)/shard_map/nk,nf->kf/dot_general | solution.py:97
  138.7 47.7 %reduce-scatter.5.cloned.1.call-done = f32[256,576]{0,1:T(8,128)} async-done(((f32[256,2304]{0,1:T(8,128)}), f32[256,576]{0,1:T(8,128)}) %reduce-scatter.5.cloned.1.call-update) | async-done | bytes 589840 | tf_op jit(solution)/shard_map/reduce_scatter | solution.py:125
  186.3 2.1 copy.15
  190.0 6.4 %all-reduce = f32[256]{0:T(256)S(1)} all-reduce(f32[256]{0:T(256)S(1)} %multiply_reduce_fusion), channel_id=4, replica_groups=mesh['groups'=2,'dom'=4,'cls'=4] {'cls'}, use_global_device_ids=true, to_apply=%region_21.22.clone | all-reduce | flops 256 | bytes 2048
  196.5 11.1 %psum.7 = f32[64]{0:T(128)} all-reduce(f32[64]{0:T(128)S(1)} %dynamic-slice.1), channel_id=1, replica_groups=mesh['groups'=2,'dom'=4,'cls'=4] {'dom'}, use_global_device_ids=true, to_apply=%region_22.23 | all-reduce | flops 64 | bytes 512 | tf_op jit(solution)/shard_map/psum | solution.py:130
  207.6 3.8 %reduce-scatter.7.cloned.1.call-done = f32[64,576]{1,0:T(8,128)} async-done(((f32[256,576]{1,0:T(8,128)}), f32[64,576]{1,0:T(8,128)}) %reduce-scatter.7.cloned.1.call-update) | async-done | bytes 147472
  (227 shorter events, 30.1 us)
Async XLA Ops:
  7.2 179.2 %reduce-scatter.5.cloned.1.call-start = ((), (), s32[]{:S(2)}) async-start(), calls=%async_computation.2 | async-start | bytes 2949120 | tf_op jit(solution)/shard_map/reduce_scatter | solution.py:125
  7.2 48.4 %collective-permute-start = (bf16[64,2304]{1,0:T(8,128)(2,1)}, bf16[64,2304]{1,0:T(8,128)(2,1)}, u32[]{:S(2)}, u32[]{:S(2)}) collective-permute-start(bf16[64,2304]{1,0:T(8,128)(2,1)} %param.7), channel_id=1, source_target_pairs={{0,1},{1,0},{2,3},{3,2},{4,5},{5,4},{6,7},{7,6},{8,9},{9,8},{10,11... | collective-permute-start | bytes 884744 | tf_op jit(solution)/shard_map/ppermute | solution.py:21
  7.8 68.7 %copy-start.52 = (pred[2304]{0:T(1024)(128)(4,1)}, pred[2304]{0:T(1024)(128)(4,1)S(1)}, u32[]{:S(2)}) copy-start(pred[2304]{0:T(1024)(128)(4,1)S(1)} %fusion.56) | copy-start | bytes 6916
  41.5 2.0 copy-start.73
  44.4 32.0 %copy-start.54 = (f32[256]{0:T(256)}, f32[256]{0:T(256)S(1)}, u32[]{:S(2)}) copy-start(f32[256]{0:T(256)S(1)} %mul.489) | copy-start | bytes 3076
  54.1 1.6 copy-start.28
  56.8 17.0 %copy-start.12 = (bf16[128,2304]{1,0:T(8,128)(2,1)}, bf16[128,2304]{1,0:T(8,128)(2,1)S(1)}, u32[]{:S(2)}) copy-start(bf16[128,2304]{1,0:T(8,128)(2,1)S(1)} %maximum_select_fusion.8) | copy-start | bytes 1769476
  56.8 16.6 %collective-permute-start.1 = (bf16[128,2304]{1,0:T(8,128)(2,1)S(1)}, bf16[128,2304]{1,0:T(8,128)(2,1)S(1)}, u32[]{:S(2)}, u32[]{:S(2)}) collective-permute-start(bf16[128,2304]{1,0:T(8,128)(2,1)S(1)} %maximum_select_fusion.8), channel_id=1, source_target_pairs={{0,2},{1,3},{2,0},{3,1},{4,6},{5,7},{6,4},{7,5},{8,10},{9,11},{10,... | collective-permute-start | bytes 1769480 | tf_op jit(solution)/shard_map/ppermute | solution.py:21
  60.0 13.8 %copy-start.70 = (f32[256]{0:T(256)}, f32[256]{0:T(256)S(1)}, u32[]{:S(2)}) copy-start(f32[256]{0:T(256)S(1)} %get-tuple-element.22) | copy-start | bytes 3076
  61.1 12.7 %copy-start.71 = (f32[256]{0:T(256)S(1)}, f32[256]{0:T(256)}, u32[]{:S(2)}) copy-start(f32[256]{0:T(256)} %reshape.299) | copy-start | bytes 3076
  73.3 2.3 %copy-start.27 = (bf16[128,2304]{1,0:T(8,128)(2,1)}, bf16[128,2304]{1,0:T(8,128)(2,1)S(1)}, u32[]{:S(2)}) copy-start(bf16[128,2304]{1,0:T(8,128)(2,1)S(1)} %collective-permute-done.1) | copy-start | bytes 1769476
  73.7 1.9 copy-start.69
  83.1 4.8 %copy-start.49 = (pred[2304]{0:T(1024)(128)(4,1)S(1)}, pred[2304]{0:T(1024)(128)(4,1)}, u32[]{:S(2)}) copy-start(pred[2304]{0:T(1024)(128)(4,1)} %fusion.54) | copy-start | bytes 6916
  87.9 6.0 %copy-start.47 = (pred[2304]{0:T(1024)(128)(4,1)S(1)}, pred[2304]{0:T(1024)(128)(4,1)}, u32[]{:S(2)}) copy-start(pred[2304]{0:T(1024)(128)(4,1)} %fusion.53) | copy-start | bytes 6916
  93.9 5.9 %copy-start.45 = (pred[2304]{0:T(1024)(128)(4,1)S(1)}, pred[2304]{0:T(1024)(128)(4,1)}, u32[]{:S(2)}) copy-start(pred[2304]{0:T(1024)(128)(4,1)} %fusion.52) | copy-start | bytes 6916
  99.8 6.0 %copy-start.44 = (pred[2304]{0:T(1024)(128)(4,1)S(1)}, pred[2304]{0:T(1024)(128)(4,1)}, u32[]{:S(2)}) copy-start(pred[2304]{0:T(1024)(128)(4,1)} %fusion.51) | copy-start | bytes 6916
  105.9 5.5 %copy-start.43 = (pred[2304]{0:T(1024)(128)(4,1)S(1)}, pred[2304]{0:T(1024)(128)(4,1)}, u32[]{:S(2)}) copy-start(pred[2304]{0:T(1024)(128)(4,1)} %fusion.50) | copy-start | bytes 6916
  117.4 2.1 copy-start.21
  117.4 2.1 copy-start.25
  117.4 2.2 %copy-start.17 = (f32[256,256]{1,0:T(8,128)S(1)}, f32[256,256]{1,0:T(8,128)}, u32[]{:S(2)}) copy-start(f32[256,256]{1,0:T(8,128)} %get-tuple-element.49) | copy-start | bytes 786436
  118.5 1.2 copy-start.15
  119.5 1.0 copy-start.23
  122.7 1.3 copy-start.8
  122.7 1.6 copy-start.9
  122.7 1.6 copy-start.41
  122.8 1.6 copy-start.42
  122.8 1.6 copy-start.53
  124.4 1.3 copy-start.6
  124.4 1.6 copy-start.7
  124.4 1.6 copy-start.39
  124.4 1.6 copy-start.40
  124.4 1.6 copy-start.51
  126.0 1.3 copy-start.4
  126.0 1.6 copy-start.5
  126.0 1.6 copy-start.37
  126.0 1.6 copy-start.38
  126.0 1.6 copy-start.50
  127.6 1.3 copy-start.2
  127.6 1.6 copy-start.3
  127.6 1.6 copy-start.35
  127.7 1.6 copy-start.36
  127.7 1.6 copy-start.48
  129.3 1.3 copy-start
  129.3 1.6 copy-start.1
  129.3 1.6 copy-start.33
  129.3 1.6 copy-start.34
  129.3 1.6 copy-start.46
  130.9 1.3 copy-start.31
  130.9 1.3 copy-start.32
  132.2 1.3 copy-start.10
  132.2 1.6 copy-start.11
  132.2 1.6 copy-start.29
  132.3 1.6 copy-start.30
  136.6 1.9 copy-start.13
  136.6 1.9 copy-start.14
  136.6 2.0 copy-start.22
  136.6 2.0 copy-start.26
  136.6 74.8 %reduce-scatter.7.cloned.1.call-start = ((), (), s32[]{:S(2)}) async-start(), calls=%async_computation.3 | async-start | bytes 819200
  138.6 49.9 %copy-start.18 = (f32[256,256]{1,0:T(8,128)S(1)}, f32[256,256]{1,0:T(8,128)}, u32[]{:S(2)}) copy-start(f32[256,256]{1,0:T(8,128)} %get-tuple-element.49) | copy-start | bytes 786436
  138.6 49.9 %copy-start.57 = (f32[16]{0:T(128)S(1)}, f32[16]{0:T(128)}, u32[]{:S(2)}) copy-start(f32[16]{0:T(128)} %copy-done.56) | copy-start | bytes 196
  138.6 50.1 %copy-start.59 = (f32[16]{0:T(128)S(1)}, f32[16]{0:T(128)}, u32[]{:S(2)}) copy-start(f32[16]{0:T(128)} %copy-done.58) | copy-start | bytes 196
  138.6 50.2 %copy-start.16 = (f32[256,256]{1,0:T(8,128)S(1)}, f32[256,256]{1,0:T(8,128)}, u32[]{:S(2)}) copy-start(f32[256,256]{1,0:T(8,128)} %get-tuple-element.47) | copy-start | bytes 786436
  188.5 1.0 copy-start.24
  188.5 1.0 copy-start.60
  (15 other events, 12.8 us)
Sparse Core Ops, SparseCore 0:
  136.7 49.5 reduce-scatter.4
  189.4 21.9 reduce-scatter.6
where the time goes:
time: 219 us; the launch traced here: 218 us
  waiting for transfers between devices  63.7 us (29%)
  matrix products  44 us (20%)
  other arithmetic  37.1 us (17%)
  local copies, waits for them, and re-layouts  37 us (17%)
  blocking collectives  17.5 us (8%)
  between operations  15.6 us (7%)
  starting transfers between devices  3.2 us (1%)
    reduce_scatter x1, waiting for transfers between devices, body(): lax.psum_scatter(class_total, 'dom', scatter_dimension=1, tiled=True)  47.7 us
    dot_general x8, matrix products, prepare(): jnp.einsum('nf,kf->nk', turned_all[rotation], references, preferred_eleme...  33 us
    concatenate x14, other arithmetic, shifted_rows(): joined = jnp.concatenate([real_out, imag_out], axis=2).astype(jnp.bfloat16)  16.5 us
    ppermute x2, waiting for transfers between devices, partner_2(): lax.ppermute(array, axis, [(i, i ^ 1 << bit) for i in range(lax.axis_size...  12.2 us
    psum x1, blocking collectives, body(): weight_sums = lax.psum(weight_sums, 'dom')  11.1 us
    dot_general x8, matrix products, posterior_sums(): jnp.einsum('nk,nf->kf', weight, turned_all[rotation], preferred_element_t...  11 us
    unnamed x167, local copies, waits for them, and re-layouts  11 us
    unnamed x1, blocking collectives  6.39 us
  transfers between devices with their start and end apart: 4, of which 3 were waited for; matrix products, arithmetic and copies ran while one was open for 23% of the time, Pallas kernels for 0%

commit v1 on v0

v1 whole, which is shorter than its diff:
```python
import functools
import math

import jax
import jax.numpy as jnp
import ml_dtypes
import numpy as np
from jax import lax
from jax.experimental import pallas as pl
from jax.experimental.pallas import tpu as pltpu
from jax.sharding import PartitionSpec as P

CYCLES = 18
ANG = 64
IMG = 64
ANG_STEP = 1
ROTS = 8
SHIFT_R = 5
SHIFTW = 11
HALF = CYCLES * ANG
COLS = 2 * HALF
LANES = 128
META = LANES
ROT_PRIOR = 0.5
VMEM_LIMIT = 56 * 1024 * 1024


def phase_table():
    angles = np.arange(ANG) * (2.0 * math.pi / ANG)
    radius = np.arange(CYCLES) + 1.0
    fx = (radius[:, None] * np.cos(angles)[None, :]).reshape(-1)
    fy = (radius[:, None] * np.sin(angles)[None, :]).reshape(-1)
    offsets = np.arange(SHIFTW * SHIFTW)
    dx = offsets % SHIFTW - SHIFT_R
    dy = offsets // SHIFTW - SHIFT_R
    phase = (2.0 * math.pi / IMG) * (dx[:, None] * fx[None, :] + dy[:, None] * fy[None, :])
    values = np.zeros((LANES, COLS), np.float32)
    values[: SHIFTW * SHIFTW] = np.concatenate([np.cos(phase), np.sin(phase)], axis=1)
    high = values.astype(ml_dtypes.bfloat16)
    low = (values - high.astype(np.float32)).astype(ml_dtypes.bfloat16)
    return np.concatenate([high, low], axis=0)


def exchange(array, axis, distance):
    return lax.ppermute(array, axis, [(i, i ^ distance) for i in range(lax.axis_size(axis))])


def lane_index(shape):
    return lax.broadcasted_iota(jnp.int32, shape, len(shape) - 1)


def rotate_classes(class_ref, rotated_ref, norm_ref):
    classes = class_ref.shape[0]
    total = jnp.zeros((classes, LANES), jnp.float32)
    lane = lane_index((classes, LANES)) % ANG
    for tile in range(COLS // LANES):
        columns = slice(tile * LANES, (tile + 1) * LANES)
        value = class_ref[:, columns].astype(jnp.float32)
        total = total + value * value
        other = pltpu.roll(value, ANG, 1)
        for rotation in range(ROTS):
            offset = ANG_STEP * rotation % ANG
            turned = value
            if offset:
                turned = pltpu.roll(jnp.where(lane < ANG - offset, value, other), offset, 1)
            rotated_ref[rotation * classes : (rotation + 1) * classes, columns] = turned.astype(
                jnp.bfloat16
            )
    norm_ref[...] = jnp.broadcast_to(jnp.sum(total, axis=1, keepdims=True), (classes, LANES))


def to_lanes(column, width):
    n = column.shape[0]
    row = lax.broadcasted_iota(jnp.int32, (n, width), 0)
    return jnp.sum(
        jnp.where(lane_index((n, width)) % n == row, column, 0.0), axis=0, keepdims=True
    )


def fold_lanes(row, period, combine):
    result = row[:, :LANES]
    for part in range(1, row.shape[1] // LANES):
        result = combine(result, row[:, part * LANES : (part + 1) * LANES])
    step = LANES // 2
    while step >= period:
        result = combine(result, pltpu.roll(result, step, 1))
        step //= 2
    return result


def score_block(block_ref, table_ref, scale_ref, rotated_ref, norm_ref, shifted_ref, out):
    particles = block_ref.shape[0]
    classes = norm_ref.shape[0]
    candidates = shifted_ref.shape[0] // particles
    rows = particles * candidates
    repeat = rows // LANES
    meta = block_ref[:, COLS : COLS + META].astype(jnp.float32)
    index = meta[:, :candidates].astype(jnp.int32)
    lane = lane_index((particles, LANES))
    hot = jnp.concatenate(
        [
            jnp.where(index[:, t : t + 1] == lane, 1.0, 0.0).astype(jnp.bfloat16)
            for t in range(candidates)
        ],
        axis=0,
    )
    hot = jnp.concatenate([hot, hot], axis=1)
    groups = scale_ref.shape[1]
    group = meta[:, candidates + 1 : candidates + 2].astype(jnp.int32)
    scale_column = jnp.sum(
        jnp.where(group == lane_index((particles, groups)), scale_ref[...], 0.0),
        axis=1,
        keepdims=True,
    )
    scale = to_lanes(scale_column, rows)
    prior = to_lanes(meta[:, candidates : candidates + 1], rows)
    width = 3 * LANES
    for start in range(0, HALF, width):
        real_columns = slice(start, start + width)
        imag_columns = slice(HALF + start, HALF + start + width)
        cosine = jnp.dot(hot, table_ref[:, real_columns], preferred_element_type=jnp.float32)
        sine = jnp.dot(hot, table_ref[:, imag_columns], preferred_element_type=jnp.float32)
        real = block_ref[:, real_columns].astype(jnp.float32)
        imag = block_ref[:, imag_columns].astype(jnp.float32)
        for t in range(candidates):
            part = slice(t * particles, (t + 1) * particles)
            c, s = cosine[part], sine[part]
            shifted_ref[part, real_columns] = (real * c - imag * s).astype(jnp.bfloat16)
            shifted_ref[part, imag_columns] = (real * s + imag * c).astype(jnp.bfloat16)
    product = lax.dot_general(
        rotated_ref[...],
        shifted_ref[...],
        (((1,), (1,)), ((), ())),
        preferred_element_type=jnp.float32,
    )
    norm = jnp.concatenate([norm_ref[...]] * repeat, axis=1)
    half_square = 0.5 * scale * scale
    scores = []
    highest = None
    for rotation in range(ROTS):
        distance = jnp.abs(rotation - prior)
        score = (
            scale * product[rotation * classes : (rotation + 1) * classes]
            - half_square * norm
            - ROT_PRIOR * (distance * distance)
        )
        scores.append(score)
        peak = jnp.max(score, axis=0, keepdims=True)
        highest = peak if highest is None else jnp.maximum(highest, peak)
    highest = fold_lanes(highest, particles, jnp.maximum)
    wide = jnp.concatenate([highest] * repeat, axis=1)
    total = None
    for rotation in range(ROTS):
        value = jnp.exp(scores[rotation] - wide)
        out(rotation, value)
        added = jnp.sum(value, axis=0, keepdims=True)
        total = added if total is None else total + added
    total = fold_lanes(total, particles, jnp.add)
    return highest, total, scale[:, :LANES]


def own_kernel(
    block_ref, class_ref, table_ref, scale_ref,
    shifted_ref, exp_ref, stats_ref, rotated_ref, norm_ref,
):
    rotate_classes(class_ref, rotated_ref, norm_ref)
    classes = norm_ref.shape[0]

    def out(rotation, value):
        exp_ref[rotation * classes : (rotation + 1) * classes, :] = value

    highest, total, scale = score_block(
        block_ref, table_ref, scale_ref, rotated_ref, norm_ref, shifted_ref, out
    )
    stats_ref[0:1, :] = highest
    stats_ref[1:2, :] = total
    stats_ref[2:3, :] = scale
    stats_ref[3:8, :] = jnp.zeros((5, LANES), jnp.float32)


def rest_kernel(count, *refs):
    blocks = refs[: count - 1]
    table_ref, scale_ref, rotated_ref, norm_ref, own_ref = refs[count - 1 : count + 4]
    shifted_ref, exp_ref, stats_ref, scales_ref = refs[count + 4 :]
    classes = norm_ref.shape[0]
    rows = shifted_ref.shape[0] // (count - 1)
    stats_ref[0:2, :] = own_ref[0:2, :]
    scales_ref[...] = jnp.zeros_like(scales_ref)
    scales_ref[0:1, :] = own_ref[2:3, :]
    for block in range(count - 1):
        part = slice(block * rows, (block + 1) * rows)

        def out(rotation, value):
            exp_ref[rotation * classes : (rotation + 1) * classes, part] = value

        highest, total, scale = score_block(
            blocks[block], table_ref, scale_ref, rotated_ref, norm_ref, shifted_ref.at[part, :], out
        )
        stats_ref[2 * block + 2 : 2 * block + 3, :] = highest
        stats_ref[2 * block + 3 : 2 * block + 4, :] = total
        scales_ref[block + 1 : block + 2, :] = scale


def sums_kernel(count, doms, width, *refs):
    stats = refs[:count]
    place_ref, scales_ref, exp_own, exp_rest, shifted_own, shifted_rest = refs[count : count + 6]
    own_out = refs[count + 6]
    sends = refs[count + 7 : count + 6 + doms]
    weight_ref, sums_ref, parts_ref = refs[count + 6 + doms :]
    rows = shifted_own.shape[0]
    repeat = rows // LANES
    classes = exp_own.shape[0] // ROTS
    mass = jnp.zeros((classes, rows), jnp.float32)
    for block in range(count):
        highs = [stats[c][2 * (c ^ block) : 2 * (c ^ block) + 1, :] for c in range(count)]
        lows = [stats[c][2 * (c ^ block) + 1 : 2 * (c ^ block) + 2, :] for c in range(count)]
        top = functools.reduce(jnp.maximum, highs)
        total = functools.reduce(jnp.add, [l * jnp.exp(h - top) for h, l in zip(highs, lows)])
        factor = jnp.exp(highs[0] - top) / total
        scale = scales_ref[block : block + 1, :]
        factor = jnp.concatenate([factor] * repeat, axis=1)
        scale = jnp.concatenate([scale] * repeat, axis=1)
        for rotation in range(ROTS):
            rotated = slice(rotation * classes, (rotation + 1) * classes)
            value = (
                exp_own[rotated, :]
                if block == 0
                else exp_rest[rotated, (block - 1) * rows : block * rows]
            )
            weight = value * factor * scale
            mass = mass + weight * scale
            weight_ref[rotated, block * rows : (block + 1) * rows] = weight.astype(jnp.bfloat16)
    mass = jnp.sum(mass, axis=1, keepdims=True)
    wide = 2 * LANES
    lane = lane_index((classes, wide)) % ANG
    for start in range(0, COLS, wide):
        columns = slice(start, start + wide)
        product = jnp.dot(
            weight_ref[:, :rows], shifted_own[:, columns], preferred_element_type=jnp.float32
        ) + jnp.dot(
            weight_ref[:, rows:], shifted_rest[:, columns], preferred_element_type=jnp.float32
        )
        inside = product[:classes]
        wrapped = None
        for rotation in range(1, ROTS):
            offset = ANG_STEP * rotation % ANG
            turned = jnp.concatenate(
                [
                    pltpu.roll(
                        product[rotation * classes : (rotation + 1) * classes, s : s + LANES],
                        LANES - offset,
                        1,
                    )
                    for s in range(0, wide, LANES)
                ],
                axis=1,
            )
            within = lane < ANG - offset
            inside = inside + jnp.where(within, turned, 0.0)
            over = jnp.where(within, 0.0, turned)
            wrapped = over if wrapped is None else wrapped + over
        wrapped = jnp.concatenate(
            [pltpu.roll(wrapped[:, s : s + LANES], ANG, 1) for s in range(0, wide, LANES)], axis=1
        )
        sums_ref[:, columns] = inside + wrapped
    padded = own_out.shape[1]
    lane = lane_index((classes, padded))
    high = mass.astype(jnp.bfloat16).astype(jnp.float32)
    middle = (mass - high).astype(jnp.bfloat16).astype(jnp.float32)
    low = (mass - high - middle).astype(jnp.bfloat16).astype(jnp.float32)
    tail = jnp.where(
        lane == width, high, jnp.where(lane == width + 1, middle, jnp.where(lane == width + 2, low, 0.0))
    )
    for dom in range(doms):
        first = width * dom
        base = first // LANES * LANES
        span = -(-(first - base + width) // LANES) * LANES
        part = sums_ref[:, base : base + span]
        if first > base:
            part = pltpu.roll(part, span - (first - base), 1)
        if span < padded:
            part = jnp.concatenate([part, jnp.zeros((classes, padded - span), jnp.float32)], axis=1)
        parts_ref[dom] = jnp.where(lane < width, part[:, :padded], tail)
    place = place_ref[0]
    own_out[...] = parts_ref[place]
    for distance in range(1, doms):
        sends[distance - 1][...] = parts_ref[place ^ distance].astype(jnp.bfloat16)


def final_kernel(width, own_ref, *refs):
    received, sums_ref, weights_ref = refs[:-2], refs[-2], refs[-1]
    total = own_ref[...]
    for ref in received:
        total = total + ref[...].astype(jnp.float32)
    sums_ref[...] = total[:, :width]
    lane = lane_index(total.shape)
    mass = jnp.sum(
        jnp.where((lane >= width) & (lane < width + 3), total, 0.0), axis=1, keepdims=True
    )
    weights_ref[...] = to_lanes(mass, total.shape[0])


def call(kernel, shapes, scratch, flops, moved, *args, smem=()):
    vmem = pl.BlockSpec(memory_space=pltpu.VMEM)
    scalar = pl.BlockSpec(memory_space=pltpu.SMEM)
    return pl.pallas_call(
        kernel,
        out_shape=shapes,
        in_specs=[scalar if i in smem else vmem for i in range(len(args))],
        out_specs=[vmem] * len(shapes),
        scratch_shapes=scratch,
        compiler_params=pltpu.CompilerParams(vmem_limit_bytes=VMEM_LIMIT),
        cost_estimate=pl.CostEstimate(flops=flops, bytes_accessed=moved, transcendentals=0),
    )(*args)


def body(particle_spectra, class_spectra, shift_index, prior_rotation, particle_group, group_scale):
    count = lax.axis_size("cls")
    doms = lax.axis_size("dom")
    particles, candidates = shift_index.shape
    classes = class_spectra.shape[0]
    rows = particles * candidates
    width = COLS // doms
    padded = -(-(width + 3) // LANES) * LANES
    f32, bf16 = jnp.float32, jnp.bfloat16
    shape = jax.ShapeDtypeStruct

    meta = jnp.concatenate(
        [
            shift_index,
            prior_rotation[:, None],
            particle_group[:, None],
            jnp.zeros((particles, META - candidates - 2), jnp.int32),
        ],
        axis=1,
    ).astype(bf16)
    packed = jnp.concatenate([particle_spectra, meta], axis=1)
    others = [exchange(packed, "cls", distance) for distance in range(1, count)]
    table = jnp.asarray(phase_table())
    scales = group_scale[None, :]
    stat_rows = -(-2 * count // 8) * 8
    work = 2 * rows * COLS * (ROTS * classes + 256)
    shifted_own, exp_own, stats_own, rotated, norm = call(
        own_kernel,
        [
            shape((rows, COLS), bf16),
            shape((ROTS * classes, rows), f32),
            shape((8, LANES), f32),
            shape((ROTS * classes, COLS), bf16),
            shape((classes, LANES), f32),
        ],
        [],
        work,
        4 * rows * COLS,
        packed, class_spectra, table, scales,
    )
    rest = (count - 1) * rows
    shifted_rest, exp_rest, stats, scale_rows = call(
        functools.partial(rest_kernel, count),
        [
            shape((rest, COLS), bf16),
            shape((ROTS * classes, rest), f32),
            shape((stat_rows, LANES), f32),
            shape((-(-count // 8) * 8, LANES), f32),
        ],
        [],
        work * (count - 1),
        4 * rest * COLS,
        *others, table, scales, rotated, norm, stats_own,
    )
    all_stats = [stats] + [exchange(stats, "cls", distance) for distance in range(1, count)]
    place = lax.axis_index("dom").astype(jnp.int32).reshape(1)
    own, *sends = call(
        functools.partial(sums_kernel, count, doms, width),
        [shape((classes, padded), f32)] + [shape((classes, padded), bf16)] * (doms - 1),
        [
            pltpu.VMEM((ROTS * classes, count * rows), bf16),
            pltpu.VMEM((classes, COLS), f32),
            pltpu.VMEM((doms, classes, padded), f32),
        ],
        2 * count * rows * COLS * ROTS * classes,
        4 * count * rows * COLS,
        *all_stats, place, scale_rows, exp_own, exp_rest, shifted_own, shifted_rest,
        smem=(count,),
    )
    received = [exchange(sends[distance - 1], "dom", distance) for distance in range(1, doms)]
    class_sums, class_weights = call(
        functools.partial(final_kernel, width),
        [shape((classes, width), f32), shape((1, classes), f32)],
        [],
        doms * classes * padded,
        4 * doms * classes * padded,
        own, *received,
    )
    return class_sums, class_weights.reshape(classes)


def solution(mesh):
    placed = (
        P(("groups", "dom", "cls"), None),
        P(("groups", "cls"), None),
        P(("groups", "dom", "cls"), None),
        P(("groups", "dom", "cls")),
        P(("groups", "dom", "cls")),
        P("groups"),
    )
    return jax.shard_map(
        body,
        mesh=mesh,
        in_specs=placed,
        out_specs=(P(("groups", "cls"), "dom"), P(("groups", "cls"))),
        check_vma=False,
    )
```

time: 219 us -> 46.5 us (0.21)
  waiting for transfers between devices: 63.7 us -> 10.1 us
  matrix products: 44 us -> 0 us
  other arithmetic: 37.1 us -> 2.02 us
  local copies, waits for them, and re-layouts: 37 us -> 3.07 us
  Pallas kernels: 0 us -> 20.8 us
  blocking collectives: 17.5 us -> 0 us
  between operations: 15.6 us -> 0.69 us
  starting transfers between devices: 3.2 us -> 9.6 us
    reduce_scatter x1 -> x0, waiting for transfers between devices: 47.7 us -> none  [body(): lax.psum_scatter(class_total, 'dom', scatter_dimension=1, tiled=True)]
    dot_general x16 -> x0, matrix products: 44 us -> none  [the longest x8 33 us: prepare(): jnp.einsum('nf,kf->nk', turned_all[rotation], references, preferred_eleme...]
    pallas_call x0 -> x4, Pallas kernels: none -> 20.8 us  [call(): pl.pallas_call(kernel, out_shape=shapes, in_specs=[scalar if i in smem el...]
    concatenate x14 -> x0, other arithmetic: 16.5 us -> none  [shifted_rows(): joined = jnp.concatenate([real_out, imag_out], axis=2).astype(jnp.bfloat16)]
    psum x1 -> x0, blocking collectives: 11.1 us -> none  [body(): weight_sums = lax.psum(weight_sums, 'dom')]
    slice x15 -> x0, local copies, waits for them, and re-layouts: 9.58 us -> none  [the longest x7 4.99 us: turned_rows(): behind = jnp.roll(shifted, ANG - offset, axis=1)]
    unnamed x167 -> x20, local copies, waits for them, and re-layouts: 11 us -> 1.89 us
    ppermute x2 -> x9, starting transfers between devices: 3.12 us -> 9.6 us  [exchange(): lax.ppermute(array, axis, [(i, i ^ distance) for i in range(lax.axis_size...]
  transfers between devices with their start and end apart: 4 -> 9, of which waited for: 3 -> 4; matrix products, arithmetic and copies ran while one was open for 23% -> 0% of each run, Pallas kernels for 0% -> 11%
where the time goes in v1:
time: 46.5 us; the launch traced here: 46.2 us
  Pallas kernels  20.8 us (45%)
  waiting for transfers between devices  10.1 us (22%)
  starting transfers between devices  9.6 us (21%)
  local copies, waits for them, and re-layouts  3.07 us (7%)
  other arithmetic  2.02 us (4%)
  between operations  0.69 us (1%)
    pallas_call x4, Pallas kernels, call(): pl.pallas_call(kernel, out_shape=shapes, in_specs=[scalar if i in smem el...  20.8 us
    ppermute x9, waiting for transfers between devices, exchange(): lax.ppermute(array, axis, [(i, i ^ distance) for i in range(lax.axis_size...  10.1 us
    ppermute x9, starting transfers between devices, exchange(): lax.ppermute(array, axis, [(i, i ^ distance) for i in range(lax.axis_size...  9.6 us
    unnamed x20, local copies, waits for them, and re-layouts  1.89 us
    concatenate x1, local copies, waits for them, and re-layouts, body(): packed = jnp.concatenate([particle_spectra, meta], axis=1)  0.98 us
  transfers between devices with their start and end apart: 9, of which 4 were waited for; matrix products, arithmetic and copies ran while one was open for 0% of the time, Pallas kernels for 11%

profile of v1, /device:TPU:0, one launch (start us, length us, event | category | flops | bytes accessed | tf_op | source)
XLA Modules:
  0.0 46.2 jit_solution(5368767536680987331)
XLA Ops:
  0.6 0.7 %convert_bitcast_fusion = bf16[16,1]{0,1:T(2,128)(2,1)S(1)} fusion(s32[16]{0:T(128)} %param.11), kind=kLoop, calls=%fused_computation | loop fusion | flops 16 | bytes 96 | tf_op jit(solution)/shard_map/broadcast_in_dim | solution.py:332
  1.3 0.1 copy.10
  1.4 0.7 %convert_bitcast_fusion.1 = bf16[16,1]{0,1:T(2,128)(2,1)S(1)} fusion(s32[16]{0:T(128)} %param.10), kind=kLoop, calls=%fused_computation.1 | loop fusion | flops 16 | bytes 96 | tf_op jit(solution)/shard_map/broadcast_in_dim | solution.py:331
  2.0 0.1 copy.9
  2.1 0.7 %convert.13 = bf16[16,16]{1,0:T(8,128)(2,1)S(1)} convert(s32[16,16]{1,0:T(8,128)} %param.9) | non-fusion elementwise | flops 256 | bytes 1536 | tf_op jit(solution)/shard_map/convert
  2.9 1.0 %concatenate.6.block_ref = bf16[16,2432]{1,0:T(8,128)(2,1)S(1)} concatenate(bf16[16,2304]{1,0:T(8,128)(2,1)} %param.7, bf16[16,16]{1,0:T(8,128)(2,1)S(1)} %convert.13, bf16[16,1]{1,0:T(8,128)(2,1)S(1)} %copy.9, bf16[16,1]{1,0:T(8,128)(2,1)S(1)} %copy.10, bf16[16,110]{1,0:T(8,128)(2,1)S(1)} %broadcast_in_dim.16), dimensions={1} | concatenate | bytes 155648 | tf_op jit(solution)/shard_map/concatenate | solution.py:337
  3.8 0.0 copy-start.3
  3.8 0.5 %collective-permute-start = (bf16[16,2432]{1,0:T(8,128)(2,1)S(1)}, bf16[16,2432]{1,0:T(8,128)(2,1)S(1)}, u32[]{:S(2)}, u32[]{:S(2)}) collective-permute-start(bf16[16,2432]{1,0:T(8,128)(2,1)S(1)} %concatenate.6.block_ref), channel_id=1, source_target_pairs={{0,1},{1,0},{2,3},{3,2},{4,5},{5,4},{6,7},{7,6},{8,9},{9,8},{10,11... | collective-permute-start | bytes 233480 | tf_op jit(solution)/shard_map/ppermute | solution.py:45
  4.3 2.6 %collective-permute-start.1 = (bf16[16,2432]{1,0:T(8,128)(2,1)S(1)}, bf16[16,2432]{1,0:T(8,128)(2,1)S(1)}, u32[]{:S(2)}, u32[]{:S(2)}) collective-permute-start(bf16[16,2432]{1,0:T(8,128)(2,1)S(1)} %concatenate.6.block_ref), channel_id=1, source_target_pairs={{0,2},{1,3},{2,0},{3,1},{4,6},{5,7},{6,4},{7,5},{8,10},{9,11},{10,... | collective-permute-start | bytes 233480 | tf_op jit(solution)/shard_map/ppermute | solution.py:45
  6.9 0.1 collective-permute-start.2
  7.0 0.0 copy-done.3
  7.0 4.9 %shard_map.86 = (bf16[256,2304]{1,0:T(8,128)(2,1)}, f32[512,256]{1,0:T(8,128)}, f32[8,128]{1,0:T(8,128)}, bf16[512,2304]{1,0:T(8,128)(2,1)}, f32[64,128]{1,0:T(8,128)}) custom-call(bf16[16,2432]{1,0:T(8,128)(2,1)} %copy-done.3, bf16[64,2304]{1,0:T(8,128)(2,1)} %class_ref.1, bf16[256,2304]{1,0:T(8,128)(2,1)} %constant.10.clone.table_ref.refs_3_, f32[1,64]{1,0:T(1,128)} %bitcast.7), custom_call_target="tpu_custom_call" | custom-call | flops 905969664 | bytes 2359296 | tf_op jit(solution)/shard_map/pallas_call | solution.py:306
  11.8 0.0 collective-permute-done.refs_0_
  11.8 0.0 copy-start.4
  11.8 0.0 collective-permute-done.1.refs_1_
  11.9 0.0 copy-start.5
  11.9 0.0 collective-permute-done.2.refs_2_
  11.9 0.0 copy-start.6
  11.9 0.6 %copy-done.4 = bf16[16,2432]{1,0:T(8,128)(2,1)} copy-done((bf16[16,2432]{1,0:T(8,128)(2,1)}, bf16[16,2432]{1,0:T(8,128)(2,1)S(1)}, u32[]{:S(2)}) %copy-start.4) | copy-done | bytes 77848
  12.5 0.0 copy-done.5
  12.5 0.0 copy-done.6
  12.5 7.3 %shard_map.87 = (bf16[768,2304]{1,0:T(8,128)(2,1)}, f32[512,768]{1,0:T(8,128)}, f32[8,128]{1,0:T(8,128)}, f32[8,128]{1,0:T(8,128)}) custom-call(bf16[16,2432]{1,0:T(8,128)(2,1)} %copy-done.4, bf16[16,2432]{1,0:T(8,128)(2,1)} %copy-done.5, bf16[16,2432]{1,0:T(8,128)(2,1)} %copy-done.6, bf16[256,2304]{1,0:T(8,128)(2,1)} %constant.10.clone.table_ref.refs_3_, ...), custom_call_target="tpu_custom_call" | custom-call | flops 2717908992 | bytes 7077888 | tf_op jit(solution)/shard_map/pallas_call | solution.py:306
  19.8 0.1 collective-permute-start.3
  19.9 1.9 %collective-permute-start.4 = (f32[8,128]{1,0:T(8,128)}, f32[8,128]{1,0:T(8,128)S(1)}, u32[]{:S(2)}, u32[]{:S(2)}) collective-permute-start(f32[8,128]{1,0:T(8,128)} %get-tuple-element.20.refs_0_), channel_id=1, source_target_pairs={{0,2},{1,3},{2,0},{3,1},{4,6},{5,7},{6,4},{7,5},{8,10},{9,11},{10,... | collective-permute-start | bytes 12296 | tf_op jit(solution)/shard_map/ppermute | solution.py:45
  21.8 0.0 collective-permute-start.5
  21.9 0.0 collective-permute-done.3.refs_1_
  21.9 0.0 copy-start.7
  21.9 1.9 %collective-permute-done.4.refs_2_ = f32[8,128]{1,0:T(8,128)S(1)} collective-permute-done((f32[8,128]{1,0:T(8,128)}, f32[8,128]{1,0:T(8,128)S(1)}, u32[]{:S(2)}, u32[]{:S(2)}) %collective-permute-start.4) | collective-permute-done | bytes 4128 | tf_op jit(solution)/shard_map/ppermute | solution.py:45
  23.7 0.0 copy-start.8
  23.8 1.3 %collective-permute-done.5.refs_3_ = f32[8,128]{1,0:T(8,128)S(1)} collective-permute-done((f32[8,128]{1,0:T(8,128)}, f32[8,128]{1,0:T(8,128)S(1)}, u32[]{:S(2)}, u32[]{:S(2)}) %collective-permute-start.5) | collective-permute-done | bytes 4128 | tf_op jit(solution)/shard_map/ppermute | solution.py:45
  25.1 0.0 copy-start.9
  25.1 0.0 copy-done.7
  25.1 0.0 copy-done.8
  25.1 0.6 %copy-done.9 = f32[8,128]{1,0:T(8,128)} copy-done((f32[8,128]{1,0:T(8,128)}, f32[8,128]{1,0:T(8,128)S(1)}, u32[]{:S(2)}) %copy-start.9) | copy-done | bytes 4120
  25.7 6.9 %shard_map.88 = (f32[64,640]{1,0:T(8,128)}, bf16[64,640]{1,0:T(8,128)(2,1)}, bf16[64,640]{1,0:T(8,128)(2,1)}, bf16[64,640]{1,0:T(8,128)(2,1)}) custom-call(f32[8,128]{1,0:T(8,128)} %get-tuple-element.20.refs_0_, f32[8,128]{1,0:T(8,128)} %copy-done.7, f32[8,128]{1,0:T(8,128)} %copy-done.8, f32[8,128]{1,0:T(8,128)} %copy-done.9, s32[1]{0:T(128)} %bitcast.3.refs_4_, ...), custom_call_target="tpu_custom_call" | custom-call | flops 2415919104 | bytes 9437184 | tf_op jit(solution)/shard_map/pallas_call | solution.py:306
  32.6 1.6 %collective-permute-start.6 = (bf16[64,640]{1,0:T(8,128)(2,1)}, bf16[64,640]{1,0:T(8,128)(2,1)S(1)}, u32[]{:S(2)}, u32[]{:S(2)}) collective-permute-start(bf16[64,640]{1,0:T(8,128)(2,1)} %get-tuple-element.27), channel_id=1, source_target_pairs={{0,4},{4,0},{8,12},{12,8},{1,5},{5,1},{9,13},{13,9},{2,6},{6,2},{1... | collective-permute-start | bytes 245768 | tf_op jit(solution)/shard_map/ppermute | solution.py:45
  34.1 2.6 %collective-permute-start.7 = (bf16[64,640]{1,0:T(8,128)(2,1)}, bf16[64,640]{1,0:T(8,128)(2,1)S(1)}, u32[]{:S(2)}, u32[]{:S(2)}) collective-permute-start(bf16[64,640]{1,0:T(8,128)(2,1)} %get-tuple-element.28), channel_id=1, source_target_pairs={{0,8},{4,12},{8,0},{12,4},{1,9},{5,13},{9,1},{13,5},{2,10},{6,14},... | collective-permute-start | bytes 245768 | tf_op jit(solution)/shard_map/ppermute | solution.py:45
  36.7 0.2 collective-permute-start.8
  37.0 0.3 collective-permute-done.6.refs_0_
  37.2 0.0 copy-start
  37.2 6.6 %collective-permute-done.7.refs_1_ = bf16[64,640]{1,0:T(8,128)(2,1)S(1)} collective-permute-done((bf16[64,640]{1,0:T(8,128)(2,1)}, bf16[64,640]{1,0:T(8,128)(2,1)S(1)}, u32[]{:S(2)}, u32[]{:S(2)}) %collective-permute-start.7) | collective-permute-done | bytes 81952 | tf_op jit(solution)/shard_map/ppermute | solution.py:45
  43.8 0.0 copy-start.1
  43.8 0.0 collective-permute-done.8.refs_2_
  43.8 0.0 copy-start.2
  43.8 0.0 copy-done
  43.8 0.6 %copy-done.1 = bf16[64,640]{1,0:T(8,128)(2,1)} copy-done((bf16[64,640]{1,0:T(8,128)(2,1)}, bf16[64,640]{1,0:T(8,128)(2,1)S(1)}, u32[]{:S(2)}) %copy-start.1) | copy-done | bytes 81944
  44.4 0.0 copy-done.2
  44.5 1.8 %shard_map.89 = (f32[64,576]{1,0:T(8,128)}, f32[1,64]{1,0:T(1,128)}) custom-call(f32[64,640]{1,0:T(8,128)} %get-tuple-element.26.own_ref, bf16[64,640]{1,0:T(8,128)(2,1)} %copy-done, bf16[64,640]{1,0:T(8,128)(2,1)} %copy-done.1, bf16[64,640]{1,0:T(8,128)(2,1)} %copy-done.2), custom_call_target="tpu_custom_call" | custom-call | flops 163840 | bytes 655360 | tf_op jit(solution)/shard_map/pallas_call | solution.py:306
  (1 shorter events, 0.0 us)
Async XLA Ops:
  3.8 3.1 %copy-start.3 = (bf16[16,2432]{1,0:T(8,128)(2,1)}, bf16[16,2432]{1,0:T(8,128)(2,1)S(1)}, u32[]{:S(2)}) copy-start(bf16[16,2432]{1,0:T(8,128)(2,1)S(1)} %concatenate.6.block_ref) | copy-start | bytes 233476
  3.8 8.0 %collective-permute-start = (bf16[16,2432]{1,0:T(8,128)(2,1)S(1)}, bf16[16,2432]{1,0:T(8,128)(2,1)S(1)}, u32[]{:S(2)}, u32[]{:S(2)}) collective-permute-start(bf16[16,2432]{1,0:T(8,128)(2,1)S(1)} %concatenate.6.block_ref), channel_id=1, source_target_pairs={{0,1},{1,0},{2,3},{3,2},{4,5},{5,4},{6,7},{7,6},{8,9},{9,8},{10,11... | collective-permute-start | bytes 233480 | tf_op jit(solution)/shard_map/ppermute | solution.py:45
  4.3 7.5 %collective-permute-start.1 = (bf16[16,2432]{1,0:T(8,128)(2,1)S(1)}, bf16[16,2432]{1,0:T(8,128)(2,1)S(1)}, u32[]{:S(2)}, u32[]{:S(2)}) collective-permute-start(bf16[16,2432]{1,0:T(8,128)(2,1)S(1)} %concatenate.6.block_ref), channel_id=1, source_target_pairs={{0,2},{1,3},{2,0},{3,1},{4,6},{5,7},{6,4},{7,5},{8,10},{9,11},{10,... | collective-permute-start | bytes 233480 | tf_op jit(solution)/shard_map/ppermute | solution.py:45
  6.9 5.0 %collective-permute-start.2 = (bf16[16,2432]{1,0:T(8,128)(2,1)S(1)}, bf16[16,2432]{1,0:T(8,128)(2,1)S(1)}, u32[]{:S(2)}, u32[]{:S(2)}) collective-permute-start(bf16[16,2432]{1,0:T(8,128)(2,1)S(1)} %concatenate.6.block_ref), channel_id=1, source_target_pairs={{0,3},{1,2},{2,1},{3,0},{4,7},{5,6},{6,5},{7,4},{8,11},{9,10},{10,... | collective-permute-start | bytes 233480 | tf_op jit(solution)/shard_map/ppermute | solution.py:45
  11.8 0.6 %copy-start.4 = (bf16[16,2432]{1,0:T(8,128)(2,1)}, bf16[16,2432]{1,0:T(8,128)(2,1)S(1)}, u32[]{:S(2)}) copy-start(bf16[16,2432]{1,0:T(8,128)(2,1)S(1)} %collective-permute-done.refs_0_) | copy-start | bytes 233476
  11.9 0.6 %copy-start.5 = (bf16[16,2432]{1,0:T(8,128)(2,1)}, bf16[16,2432]{1,0:T(8,128)(2,1)S(1)}, u32[]{:S(2)}) copy-start(bf16[16,2432]{1,0:T(8,128)(2,1)S(1)} %collective-permute-done.1.refs_1_) | copy-start | bytes 233476
  11.9 0.6 %copy-start.6 = (bf16[16,2432]{1,0:T(8,128)(2,1)}, bf16[16,2432]{1,0:T(8,128)(2,1)S(1)}, u32[]{:S(2)}) copy-start(bf16[16,2432]{1,0:T(8,128)(2,1)S(1)} %collective-permute-done.2.refs_2_) | copy-start | bytes 233476
  19.8 2.1 %collective-permute-start.3 = (f32[8,128]{1,0:T(8,128)}, f32[8,128]{1,0:T(8,128)S(1)}, u32[]{:S(2)}, u32[]{:S(2)}) collective-permute-start(f32[8,128]{1,0:T(8,128)} %get-tuple-element.20.refs_0_), channel_id=1, source_target_pairs={{0,1},{1,0},{2,3},{3,2},{4,5},{5,4},{6,7},{7,6},{8,9},{9,8},{10,11... | collective-permute-start | bytes 12296 | tf_op jit(solution)/shard_map/ppermute | solution.py:45
  19.9 3.8 %collective-permute-start.4 = (f32[8,128]{1,0:T(8,128)}, f32[8,128]{1,0:T(8,128)S(1)}, u32[]{:S(2)}, u32[]{:S(2)}) collective-permute-start(f32[8,128]{1,0:T(8,128)} %get-tuple-element.20.refs_0_), channel_id=1, source_target_pairs={{0,2},{1,3},{2,0},{3,1},{4,6},{5,7},{6,4},{7,5},{8,10},{9,11},{10,... | collective-permute-start | bytes 12296 | tf_op jit(solution)/shard_map/ppermute | solution.py:45
  21.8 3.2 %collective-permute-start.5 = (f32[8,128]{1,0:T(8,128)}, f32[8,128]{1,0:T(8,128)S(1)}, u32[]{:S(2)}, u32[]{:S(2)}) collective-permute-start(f32[8,128]{1,0:T(8,128)} %get-tuple-element.20.refs_0_), channel_id=1, source_target_pairs={{0,3},{1,2},{2,1},{3,0},{4,7},{5,6},{6,5},{7,4},{8,11},{9,10},{10,... | collective-permute-start | bytes 12296 | tf_op jit(solution)/shard_map/ppermute | solution.py:45
  21.9 3.2 %copy-start.7 = (f32[8,128]{1,0:T(8,128)}, f32[8,128]{1,0:T(8,128)S(1)}, u32[]{:S(2)}) copy-start(f32[8,128]{1,0:T(8,128)S(1)} %collective-permute-done.3.refs_1_) | copy-start | bytes 12292
  23.7 1.4 %copy-start.8 = (f32[8,128]{1,0:T(8,128)}, f32[8,128]{1,0:T(8,128)S(1)}, u32[]{:S(2)}) copy-start(f32[8,128]{1,0:T(8,128)S(1)} %collective-permute-done.4.refs_2_) | copy-start | bytes 12292
  25.1 0.6 %copy-start.9 = (f32[8,128]{1,0:T(8,128)}, f32[8,128]{1,0:T(8,128)S(1)}, u32[]{:S(2)}) copy-start(f32[8,128]{1,0:T(8,128)S(1)} %collective-permute-done.5.refs_3_) | copy-start | bytes 12292
  32.6 4.7 %collective-permute-start.6 = (bf16[64,640]{1,0:T(8,128)(2,1)}, bf16[64,640]{1,0:T(8,128)(2,1)S(1)}, u32[]{:S(2)}, u32[]{:S(2)}) collective-permute-start(bf16[64,640]{1,0:T(8,128)(2,1)} %get-tuple-element.27), channel_id=1, source_target_pairs={{0,4},{4,0},{8,12},{12,8},{1,5},{5,1},{9,13},{13,9},{2,6},{6,2},{1... | collective-permute-start | bytes 245768 | tf_op jit(solution)/shard_map/ppermute | solution.py:45
  34.1 9.7 %collective-permute-start.7 = (bf16[64,640]{1,0:T(8,128)(2,1)}, bf16[64,640]{1,0:T(8,128)(2,1)S(1)}, u32[]{:S(2)}, u32[]{:S(2)}) collective-permute-start(bf16[64,640]{1,0:T(8,128)(2,1)} %get-tuple-element.28), channel_id=1, source_target_pairs={{0,8},{4,12},{8,0},{12,4},{1,9},{5,13},{9,1},{13,5},{2,10},{6,14},... | collective-permute-start | bytes 245768 | tf_op jit(solution)/shard_map/ppermute | solution.py:45
  36.7 7.1 %collective-permute-start.8 = (bf16[64,640]{1,0:T(8,128)(2,1)}, bf16[64,640]{1,0:T(8,128)(2,1)S(1)}, u32[]{:S(2)}, u32[]{:S(2)}) collective-permute-start(bf16[64,640]{1,0:T(8,128)(2,1)} %get-tuple-element.29), channel_id=1, source_target_pairs={{0,12},{4,8},{8,4},{12,0},{1,13},{5,9},{9,5},{13,1},{2,14},{6,10},... | collective-permute-start | bytes 245768 | tf_op jit(solution)/shard_map/ppermute | solution.py:45
  37.2 6.6 %copy-start = (bf16[64,640]{1,0:T(8,128)(2,1)}, bf16[64,640]{1,0:T(8,128)(2,1)S(1)}, u32[]{:S(2)}) copy-start(bf16[64,640]{1,0:T(8,128)(2,1)S(1)} %collective-permute-done.6.refs_0_) | copy-start | bytes 245764
  43.8 0.6 %copy-start.1 = (bf16[64,640]{1,0:T(8,128)(2,1)}, bf16[64,640]{1,0:T(8,128)(2,1)S(1)}, u32[]{:S(2)}) copy-start(bf16[64,640]{1,0:T(8,128)(2,1)S(1)} %collective-permute-done.7.refs_1_) | copy-start | bytes 245764
  43.8 0.7 %copy-start.2 = (bf16[64,640]{1,0:T(8,128)(2,1)}, bf16[64,640]{1,0:T(8,128)(2,1)S(1)}, u32[]{:S(2)}) copy-start(bf16[64,640]{1,0:T(8,128)(2,1)S(1)} %collective-permute-done.8.refs_2_) | copy-start | bytes 245764

commit v2 on v1

--- a/solution.py
+++ b/solution.py
@@ -22,7 +22,7 @@
 LANES = 128
 META = LANES
 ROT_PRIOR = 0.5
-VMEM_LIMIT = 56 * 1024 * 1024
+VMEM_LIMIT = 20 * 1024 * 1024
 
 
 def phase_table():
@@ -86,6 +86,26 @@
         result = combine(result, pltpu.roll(result, step, 1))
         step //= 2
     return result
+
+
+def to_column(row):
+    n = row.shape[1]
+    diagonal = lax.broadcasted_iota(jnp.int32, (n, n), 0) == lane_index((n, n))
+    return jnp.sum(jnp.where(diagonal, row, 0.0), axis=1, keepdims=True)
+
+
+def pack_kernel(particle_ref, index_ref, prior_ref, group_ref, packed_ref):
+    particles, candidates = index_ref.shape
+    packed_ref[:, :COLS] = particle_ref[...]
+    lane = lane_index((particles, META))
+    index = jnp.concatenate(
+        [index_ref[...].astype(jnp.float32), jnp.zeros((particles, META - candidates), jnp.float32)],
+        axis=1,
+    )
+    prior = to_column(prior_ref[...].astype(jnp.float32))
+    group = to_column(group_ref[...].astype(jnp.float32))
+    meta = jnp.where(lane == candidates, prior, jnp.where(lane == candidates + 1, group, index))
+    packed_ref[:, COLS:] = meta.astype(jnp.bfloat16)
 
 
 def score_block(block_ref, table_ref, scale_ref, rotated_ref, norm_ref, shifted_ref, out):
@@ -325,16 +345,14 @@
     f32, bf16 = jnp.float32, jnp.bfloat16
     shape = jax.ShapeDtypeStruct
 
-    meta = jnp.concatenate(
-        [
-            shift_index,
-            prior_rotation[:, None],
-            particle_group[:, None],
-            jnp.zeros((particles, META - candidates - 2), jnp.int32),
-        ],
-        axis=1,
-    ).astype(bf16)
-    packed = jnp.concatenate([particle_spectra, meta], axis=1)
+    (packed,) = call(
+        pack_kernel,
+        [shape((particles, COLS + META), bf16)],
+        [],
+        particles * COLS,
+        4 * particles * COLS,
+        particle_spectra, shift_index, prior_rotation[None, :], particle_group[None, :],
+    )
     others = [exchange(packed, "cls", distance) for distance in range(1, count)]
     table = jnp.asarray(phase_table())
     scales = group_scale[None, :]

time: 46.5 us -> 43.2 us (0.929)
  Pallas kernels: 20.8 us -> 10.8 us
  local copies, waits for them, and re-layouts: 3.07 us -> 12 us
  other arithmetic: 2.02 us -> 0 us
    unnamed x20 -> x34, local copies, waits for them, and re-layouts: 1.89 us -> 12 us
    pallas_call x4 -> x5, Pallas kernels: 20.8 us -> 10.8 us  [call(): pl.pallas_call(kernel, out_shape=shapes, in_specs=[scalar if i in smem el...]
    broadcast_in_dim x2 -> x0, other arithmetic: 1.32 us -> none  [the longest x1 0.66 us: body(): prior_rotation[:, None]]
    concatenate x1 -> x0, local copies, waits for them, and re-layouts: 0.98 us -> none  [body(): packed = jnp.concatenate([particle_spectra, meta], axis=1)]
    another operation x1 -> x0, other arithmetic: 0.7 us -> none
  transfers between devices with their start and end apart: 9 -> 9, of which waited for: 4 -> 4; matrix products, arithmetic and copies ran while one was open for 0% -> 0% of each run, Pallas kernels for 11% -> 6%
where the time goes in v2:
time: 43.2 us; the launch traced here: 42.8 us
  local copies, waits for them, and re-layouts  12 us (28%)
  Pallas kernels  10.8 us (25%)
  waiting for transfers between devices  9.68 us (22%)
  starting transfers between devices  9.6 us (22%)
  between operations  0.7 us (2%)
    unnamed x34, local copies, waits for them, and re-layouts  12 us
    pallas_call x5, Pallas kernels, call(): pl.pallas_call(kernel, out_shape=shapes, in_specs=[scalar if i in smem el...  10.8 us
    ppermute x9, waiting for transfers between devices, exchange(): lax.ppermute(array, axis, [(i, i ^ distance) for i in range(lax.axis_size...  9.68 us
    ppermute x9, starting transfers between devices, exchange(): lax.ppermute(array, axis, [(i, i ^ distance) for i in range(lax.axis_size...  9.6 us
  transfers between devices with their start and end apart: 9, of which 4 were waited for; matrix products, arithmetic and copies ran while one was open for 0% of the time, Pallas kernels for 6%

profile of v2, /device:TPU:0, one launch (start us, length us, event | category | flops | bytes accessed | tf_op | source)
XLA Modules:
  0.0 42.8 jit_solution(17002642502204320607)
XLA Ops:
  0.6 0.0 copy-start
  0.6 0.9 %copy-done = bf16[16,2304]{1,0:T(8,128)(2,1)S(1)} copy-done((bf16[16,2304]{1,0:T(8,128)(2,1)S(1)}, bf16[16,2304]{1,0:T(8,128)(2,1)}, u32[]{:S(2)}) %copy-start) | copy-done | bytes 73752
  1.5 0.0 copy-start.1
  1.5 0.7 %copy-done.1 = s32[16,16]{1,0:T(8,128)S(1)} copy-done((s32[16,16]{1,0:T(8,128)S(1)}, s32[16,16]{1,0:T(8,128)}, u32[]{:S(2)}) %copy-start.1) | copy-done | bytes 1048
  2.2 0.0 copy-start.2
  2.2 0.7 %copy-done.2 = s32[16]{0:T(128)S(1)} copy-done((s32[16]{0:T(128)S(1)}, s32[16]{0:T(128)}, u32[]{:S(2)}) %copy-start.2) | copy-done | bytes 88
  2.9 0.0 copy-start.3
  2.9 0.7 %copy-done.3 = s32[16]{0:T(128)S(1)} copy-done((s32[16]{0:T(128)S(1)}, s32[16]{0:T(128)}, u32[]{:S(2)}) %copy-start.3) | copy-done | bytes 88
  3.5 0.1 shard_map.86.block_ref
  3.6 0.5 %collective-permute-start = (bf16[16,2432]{1,0:T(8,128)(2,1)S(1)}, bf16[16,2432]{1,0:T(8,128)(2,1)S(1)}, u32[]{:S(2)}, u32[]{:S(2)}) collective-permute-start(bf16[16,2432]{1,0:T(8,128)(2,1)S(1)} %shard_map.86.block_ref), channel_id=1, source_target_pairs={{0,1},{1,0},{2,3},{3,2},{4,5},{5,4},{6,7},{7,6},{8,9},{9,8},{10,11... | collective-permute-start | bytes 233480 | tf_op jit(solution)/shard_map/ppermute | solution.py:45
  4.1 2.6 %collective-permute-start.1 = (bf16[16,2432]{1,0:T(8,128)(2,1)S(1)}, bf16[16,2432]{1,0:T(8,128)(2,1)S(1)}, u32[]{:S(2)}, u32[]{:S(2)}) collective-permute-start(bf16[16,2432]{1,0:T(8,128)(2,1)S(1)} %shard_map.86.block_ref), channel_id=1, source_target_pairs={{0,2},{1,3},{2,0},{3,1},{4,6},{5,7},{6,4},{7,5},{8,10},{9,11},{10,... | collective-permute-start | bytes 233480 | tf_op jit(solution)/shard_map/ppermute | solution.py:45
  6.6 0.1 collective-permute-start.2
  6.7 0.0 copy-start.4
  6.7 1.0 %copy-done.4 = bf16[64,2304]{1,0:T(8,128)(2,1)S(1)} copy-done((bf16[64,2304]{1,0:T(8,128)(2,1)S(1)}, bf16[64,2304]{1,0:T(8,128)(2,1)}, u32[]{:S(2)}) %copy-start.4) | copy-done | bytes 294936
  7.7 0.0 copy-start.5
  7.7 0.7 %copy-done.5 = f32[64]{0:T(128)S(1)} copy-done((f32[64]{0:T(128)S(1)}, f32[64]{0:T(128)}, u32[]{:S(2)}) %copy-start.5) | copy-done | bytes 280
  8.3 0.0 copy-start.7
  8.3 1.3 %copy-done.7 = bf16[256,2304]{1,0:T(8,128)(2,1)S(1)} copy-done((bf16[256,2304]{1,0:T(8,128)(2,1)S(1)}, bf16[256,2304]{1,0:T(8,128)(2,1)}, u32[]{:S(2)}) %copy-start.7) | copy-done | bytes 1179672
  9.6 0.0 copy-start.6
  9.6 0.0 copy-start.8
  9.6 2.5 %shard_map.87 = (bf16[256,2304]{1,0:T(8,128)(2,1)S(1)}, f32[512,256]{1,0:T(8,128)S(1)}, f32[8,128]{1,0:T(8,128)S(1)}, bf16[512,2304]{1,0:T(8,128)(2,1)S(1)}, f32[64,128]{1,0:T(8,128)S(1)}) custom-call(bf16[16,2432]{1,0:T(8,128)(2,1)S(1)} %shard_map.86.block_ref, bf16[64,2304]{1,0:T(8,128)(2,1)S(1)} %copy-done.4, bf16[256,2304]{1,0:T(8,128)(2,1)S(1)} %copy-done.7, ...), custom_call_target="tpu_custom_call" | custom-call | flops 905969664 | bytes 2359296 | tf_op jit(solution)/shard_map/pallas_call | solution.py:326
  12.1 0.0 copy-start.9
  12.1 0.0 copy-start.13
  12.1 0.0 collective-permute-done.refs_0_
  12.1 0.0 collective-permute-done.1.refs_1_
  12.1 0.0 collective-permute-done.2.refs_2_
  12.2 0.0 copy-done.6
  12.2 0.0 copy-done.8
  12.2 4.3 %shard_map.88 = (bf16[768,2304]{1,0:T(8,128)(2,1)S(1)}, f32[512,768]{1,0:T(8,128)S(1)}, f32[8,128]{1,0:T(8,128)S(1)}, f32[8,128]{1,0:T(8,128)S(1)}) custom-call(bf16[16,2432]{1,0:T(8,128)(2,1)S(1)} %collective-permute-done.refs_0_, bf16[16,2432]{1,0:T(8,128)(2,1)S(1)} %collective-permute-done.1.refs_1_, bf16[16,2432]{1,0:T(8,128)(2,1)S(1)} %collective-permute-done.2.refs_2_, ...), custom_call_target="tpu_custom_call" | custom-call | flops 2717908992 | bytes 7077888 | tf_op jit(solution)/shard_map/pallas_call | solution.py:326
  16.5 0.0 copy-done.9
  16.5 0.0 copy-done.13
  16.5 0.0 copy-start.11
  16.5 1.2 %copy-done.11 = f32[512,768]{1,0:T(8,128)} copy-done((f32[512,768]{1,0:T(8,128)}, f32[512,768]{1,0:T(8,128)S(1)}, u32[]{:S(2)}) %copy-start.11) | copy-done | bytes 1572888
  17.7 0.0 copy-start.15
  17.7 0.6 %copy-done.15 = f32[8,128]{1,0:T(8,128)} copy-done((f32[8,128]{1,0:T(8,128)}, f32[8,128]{1,0:T(8,128)S(1)}, u32[]{:S(2)}) %copy-start.15) | copy-done | bytes 4120
  18.3 0.1 collective-permute-start.3
  18.4 1.9 %collective-permute-start.4 = (f32[8,128]{1,0:T(8,128)S(1)}, f32[8,128]{1,0:T(8,128)S(1)}, u32[]{:S(2)}, u32[]{:S(2)}) collective-permute-start(f32[8,128]{1,0:T(8,128)S(1)} %get-tuple-element.20.refs_0_), channel_id=1, source_target_pairs={{0,2},{1,3},{2,0},{3,1},{4,6},{5,7},{6,4},{7,5},{8,10},{9,11},{10,... | collective-permute-start | bytes 12296 | tf_op jit(solution)/shard_map/ppermute | solution.py:45
  20.4 0.0 collective-permute-start.5
  20.4 0.0 collective-permute-done.3.refs_1_
  20.4 1.7 %collective-permute-done.4.refs_2_ = f32[8,128]{1,0:T(8,128)S(1)} collective-permute-done((f32[8,128]{1,0:T(8,128)S(1)}, f32[8,128]{1,0:T(8,128)S(1)}, u32[]{:S(2)}, u32[]{:S(2)}) %collective-permute-start.4) | collective-permute-done | bytes 4128 | tf_op jit(solution)/shard_map/ppermute | solution.py:45
  22.1 1.3 %collective-permute-done.5.refs_3_ = f32[8,128]{1,0:T(8,128)S(1)} collective-permute-done((f32[8,128]{1,0:T(8,128)S(1)}, f32[8,128]{1,0:T(8,128)S(1)}, u32[]{:S(2)}, u32[]{:S(2)}) %collective-permute-start.5) | collective-permute-done | bytes 4128 | tf_op jit(solution)/shard_map/ppermute | solution.py:45
  23.4 0.0 copy-start.10
  23.4 1.3 %copy-done.10 = bf16[256,2304]{1,0:T(8,128)(2,1)S(1)} copy-done((bf16[256,2304]{1,0:T(8,128)(2,1)S(1)}, bf16[256,2304]{1,0:T(8,128)(2,1)}, u32[]{:S(2)}) %copy-start.10) | copy-done | bytes 1179672
  24.7 0.0 copy-start.12
  24.7 1.4 %copy-done.12 = f32[512,768]{1,0:T(8,128)S(1)} copy-done((f32[512,768]{1,0:T(8,128)S(1)}, f32[512,768]{1,0:T(8,128)}, u32[]{:S(2)}) %copy-start.12) | copy-done | bytes 1572888
  26.1 0.0 copy-start.14
  26.1 1.0 %copy-done.14 = f32[512,256]{1,0:T(8,128)S(1)} copy-done((f32[512,256]{1,0:T(8,128)S(1)}, f32[512,256]{1,0:T(8,128)}, u32[]{:S(2)}) %copy-start.14) | copy-done | bytes 524312
  27.1 0.0 copy-start.16
  27.1 0.7 %copy-done.16 = f32[8,128]{1,0:T(8,128)S(1)} copy-done((f32[8,128]{1,0:T(8,128)S(1)}, f32[8,128]{1,0:T(8,128)}, u32[]{:S(2)}) %copy-start.16) | copy-done | bytes 4120
  27.8 3.1 %shard_map.89 = (f32[64,640]{1,0:T(8,128)S(1)}, bf16[64,640]{1,0:T(8,128)(2,1)S(1)}, bf16[64,640]{1,0:T(8,128)(2,1)S(1)}, bf16[64,640]{1,0:T(8,128)(2,1)S(1)}) custom-call(f32[8,128]{1,0:T(8,128)S(1)} %get-tuple-element.20.refs_0_, f32[8,128]{1,0:T(8,128)S(1)} %collective-permute-done.3.refs_1_, f32[8,128]{1,0:T(8,128)S(1)} %collective-permute-done.4.refs_2_, ...), custom_call_target="tpu_custom_call" | custom-call | flops 2415919104 | bytes 9437184 | tf_op jit(solution)/shard_map/pallas_call | solution.py:326
  30.9 1.6 %collective-permute-start.6 = (bf16[64,640]{1,0:T(8,128)(2,1)S(1)}, bf16[64,640]{1,0:T(8,128)(2,1)S(1)}, u32[]{:S(2)}, u32[]{:S(2)}) collective-permute-start(bf16[64,640]{1,0:T(8,128)(2,1)S(1)} %get-tuple-element.27), channel_id=1, source_target_pairs={{0,4},{4,0},{8,12},{12,8},{1,5},{5,1},{9,13},{13,9},{2,6},{6,2},{1... | collective-permute-start | bytes 245768 | tf_op jit(solution)/shard_map/ppermute | solution.py:45
  32.6 2.6 %collective-permute-start.7 = (bf16[64,640]{1,0:T(8,128)(2,1)S(1)}, bf16[64,640]{1,0:T(8,128)(2,1)S(1)}, u32[]{:S(2)}, u32[]{:S(2)}) collective-permute-start(bf16[64,640]{1,0:T(8,128)(2,1)S(1)} %get-tuple-element.28), channel_id=1, source_target_pairs={{0,8},{4,12},{8,0},{12,4},{1,9},{5,13},{9,1},{13,5},{2,10},{6,14},... | collective-permute-start | bytes 245768 | tf_op jit(solution)/shard_map/ppermute | solution.py:45
  35.2 0.2 collective-permute-start.8
  35.4 0.1 collective-permute-done.6.refs_0_
  35.5 6.6 %collective-permute-done.7.refs_1_ = bf16[64,640]{1,0:T(8,128)(2,1)S(1)} collective-permute-done((bf16[64,640]{1,0:T(8,128)(2,1)S(1)}, bf16[64,640]{1,0:T(8,128)(2,1)S(1)}, u32[]{:S(2)}, u32[]{:S(2)}) %collective-permute-start.7) | collective-permute-done | bytes 81952 | tf_op jit(solution)/shard_map/ppermute | solution.py:45
  42.0 0.0 collective-permute-done.8.refs_2_
  42.0 0.7 %shard_map.90 = (f32[64,576]{1,0:T(8,128)}, f32[1,64]{1,0:T(1,128)}) custom-call(f32[64,640]{1,0:T(8,128)S(1)} %get-tuple-element.26.own_ref, bf16[64,640]{1,0:T(8,128)(2,1)S(1)} %collective-permute-done.6.refs_0_, bf16[64,640]{1,0:T(8,128)(2,1)S(1)} %collective-permute-done.7.refs_1_, bf16[64,640]{1,0:T(8,128)(2,1)S(1)} %collective-permute-done.8.refs_2_), custom_call_target="tpu_custom_call" | custom-call | flops 163840 | bytes 655360 | tf_op jit(solution)/shard_map/pallas_call | solution.py:326
Async XLA Ops:
  0.6 0.9 %copy-start = (bf16[16,2304]{1,0:T(8,128)(2,1)S(1)}, bf16[16,2304]{1,0:T(8,128)(2,1)}, u32[]{:S(2)}) copy-start(bf16[16,2304]{1,0:T(8,128)(2,1)} %particle_ref.1) | copy-start | bytes 221188
  1.5 0.7 %copy-start.1 = (s32[16,16]{1,0:T(8,128)S(1)}, s32[16,16]{1,0:T(8,128)}, u32[]{:S(2)}) copy-start(s32[16,16]{1,0:T(8,128)} %index_ref.1) | copy-start | bytes 3076
  2.2 0.7 %copy-start.2 = (s32[16]{0:T(128)S(1)}, s32[16]{0:T(128)}, u32[]{:S(2)}) copy-start(s32[16]{0:T(128)} %param.10) | copy-start | bytes 196
  2.9 0.7 %copy-start.3 = (s32[16]{0:T(128)S(1)}, s32[16]{0:T(128)}, u32[]{:S(2)}) copy-start(s32[16]{0:T(128)} %param.11) | copy-start | bytes 196
  3.6 8.5 %collective-permute-start = (bf16[16,2432]{1,0:T(8,128)(2,1)S(1)}, bf16[16,2432]{1,0:T(8,128)(2,1)S(1)}, u32[]{:S(2)}, u32[]{:S(2)}) collective-permute-start(bf16[16,2432]{1,0:T(8,128)(2,1)S(1)} %shard_map.86.block_ref), channel_id=1, source_target_pairs={{0,1},{1,0},{2,3},{3,2},{4,5},{5,4},{6,7},{7,6},{8,9},{9,8},{10,11... | collective-permute-start | bytes 233480 | tf_op jit(solution)/shard_map/ppermute | solution.py:45
  4.1 8.1 %collective-permute-start.1 = (bf16[16,2432]{1,0:T(8,128)(2,1)S(1)}, bf16[16,2432]{1,0:T(8,128)(2,1)S(1)}, u32[]{:S(2)}, u32[]{:S(2)}) collective-permute-start(bf16[16,2432]{1,0:T(8,128)(2,1)S(1)} %shard_map.86.block_ref), channel_id=1, source_target_pairs={{0,2},{1,3},{2,0},{3,1},{4,6},{5,7},{6,4},{7,5},{8,10},{9,11},{10,... | collective-permute-start | bytes 233480 | tf_op jit(solution)/shard_map/ppermute | solution.py:45
  6.6 5.5 %collective-permute-start.2 = (bf16[16,2432]{1,0:T(8,128)(2,1)S(1)}, bf16[16,2432]{1,0:T(8,128)(2,1)S(1)}, u32[]{:S(2)}, u32[]{:S(2)}) collective-permute-start(bf16[16,2432]{1,0:T(8,128)(2,1)S(1)} %shard_map.86.block_ref), channel_id=1, source_target_pairs={{0,3},{1,2},{2,1},{3,0},{4,7},{5,6},{6,5},{7,4},{8,11},{9,10},{10,... | collective-permute-start | bytes 233480 | tf_op jit(solution)/shard_map/ppermute | solution.py:45
  6.7 1.0 %copy-start.4 = (bf16[64,2304]{1,0:T(8,128)(2,1)S(1)}, bf16[64,2304]{1,0:T(8,128)(2,1)}, u32[]{:S(2)}) copy-start(bf16[64,2304]{1,0:T(8,128)(2,1)} %class_ref.1) | copy-start | bytes 884740
  7.7 0.7 %copy-start.5 = (f32[64]{0:T(128)S(1)}, f32[64]{0:T(128)}, u32[]{:S(2)}) copy-start(f32[64]{0:T(128)} %param.12) | copy-start | bytes 772
  8.3 1.3 %copy-start.7 = (bf16[256,2304]{1,0:T(8,128)(2,1)S(1)}, bf16[256,2304]{1,0:T(8,128)(2,1)}, u32[]{:S(2)}) copy-start(bf16[256,2304]{1,0:T(8,128)(2,1)} %constant.7.clone.table_ref.refs_3_) | copy-start | bytes 3538948
  9.6 2.6 %copy-start.6 = (f32[64]{0:T(128)S(1)}, f32[64]{0:T(128)}, u32[]{:S(2)}) copy-start(f32[64]{0:T(128)} %param.12) | copy-start | bytes 772
  9.6 2.6 %copy-start.8 = (bf16[256,2304]{1,0:T(8,128)(2,1)S(1)}, bf16[256,2304]{1,0:T(8,128)(2,1)}, u32[]{:S(2)}) copy-start(bf16[256,2304]{1,0:T(8,128)(2,1)} %constant.7.clone.table_ref.refs_3_) | copy-start | bytes 3538948
  12.1 4.4 %copy-start.9 = (bf16[256,2304]{1,0:T(8,128)(2,1)}, bf16[256,2304]{1,0:T(8,128)(2,1)S(1)}, u32[]{:S(2)}) copy-start(bf16[256,2304]{1,0:T(8,128)(2,1)S(1)} %get-tuple-element.24.refs_8_) | copy-start | bytes 3538948
  12.1 4.4 %copy-start.13 = (f32[512,256]{1,0:T(8,128)}, f32[512,256]{1,0:T(8,128)S(1)}, u32[]{:S(2)}) copy-start(f32[512,256]{1,0:T(8,128)S(1)} %get-tuple-element.22.refs_6_) | copy-start | bytes 1572868
  16.5 1.2 %copy-start.11 = (f32[512,768]{1,0:T(8,128)}, f32[512,768]{1,0:T(8,128)S(1)}, u32[]{:S(2)}) copy-start(f32[512,768]{1,0:T(8,128)S(1)} %get-tuple-element.23.refs_7_) | copy-start | bytes 4718596
  17.7 0.6 %copy-start.15 = (f32[8,128]{1,0:T(8,128)}, f32[8,128]{1,0:T(8,128)S(1)}, u32[]{:S(2)}) copy-start(f32[8,128]{1,0:T(8,128)S(1)} %get-tuple-element.21.refs_5_) | copy-start | bytes 12292
  18.3 2.1 %collective-permute-start.3 = (f32[8,128]{1,0:T(8,128)S(1)}, f32[8,128]{1,0:T(8,128)S(1)}, u32[]{:S(2)}, u32[]{:S(2)}) collective-permute-start(f32[8,128]{1,0:T(8,128)S(1)} %get-tuple-element.20.refs_0_), channel_id=1, source_target_pairs={{0,1},{1,0},{2,3},{3,2},{4,5},{5,4},{6,7},{7,6},{8,9},{9,8},{10,11... | collective-permute-start | bytes 12296 | tf_op jit(solution)/shard_map/ppermute | solution.py:45
  18.4 3.6 %collective-permute-start.4 = (f32[8,128]{1,0:T(8,128)S(1)}, f32[8,128]{1,0:T(8,128)S(1)}, u32[]{:S(2)}, u32[]{:S(2)}) collective-permute-start(f32[8,128]{1,0:T(8,128)S(1)} %get-tuple-element.20.refs_0_), channel_id=1, source_target_pairs={{0,2},{1,3},{2,0},{3,1},{4,6},{5,7},{6,4},{7,5},{8,10},{9,11},{10,... | collective-permute-start | bytes 12296 | tf_op jit(solution)/shard_map/ppermute | solution.py:45
  20.4 3.0 %collective-permute-start.5 = (f32[8,128]{1,0:T(8,128)S(1)}, f32[8,128]{1,0:T(8,128)S(1)}, u32[]{:S(2)}, u32[]{:S(2)}) collective-permute-start(f32[8,128]{1,0:T(8,128)S(1)} %get-tuple-element.20.refs_0_), channel_id=1, source_target_pairs={{0,3},{1,2},{2,1},{3,0},{4,7},{5,6},{6,5},{7,4},{8,11},{9,10},{10,... | collective-permute-start | bytes 12296 | tf_op jit(solution)/shard_map/ppermute | solution.py:45
  23.4 1.3 %copy-start.10 = (bf16[256,2304]{1,0:T(8,128)(2,1)S(1)}, bf16[256,2304]{1,0:T(8,128)(2,1)}, u32[]{:S(2)}) copy-start(bf16[256,2304]{1,0:T(8,128)(2,1)} %copy-done.9) | copy-start | bytes 3538948
  24.7 1.4 %copy-start.12 = (f32[512,768]{1,0:T(8,128)S(1)}, f32[512,768]{1,0:T(8,128)}, u32[]{:S(2)}) copy-start(f32[512,768]{1,0:T(8,128)} %copy-done.11) | copy-start | bytes 4718596
  26.1 1.0 %copy-start.14 = (f32[512,256]{1,0:T(8,128)S(1)}, f32[512,256]{1,0:T(8,128)}, u32[]{:S(2)}) copy-start(f32[512,256]{1,0:T(8,128)} %copy-done.13) | copy-start | bytes 1572868
  27.1 0.7 %copy-start.16 = (f32[8,128]{1,0:T(8,128)S(1)}, f32[8,128]{1,0:T(8,128)}, u32[]{:S(2)}) copy-start(f32[8,128]{1,0:T(8,128)} %copy-done.15) | copy-start | bytes 12292
  30.9 4.5 %collective-permute-start.6 = (bf16[64,640]{1,0:T(8,128)(2,1)S(1)}, bf16[64,640]{1,0:T(8,128)(2,1)S(1)}, u32[]{:S(2)}, u32[]{:S(2)}) collective-permute-start(bf16[64,640]{1,0:T(8,128)(2,1)S(1)} %get-tuple-element.27), channel_id=1, source_target_pairs={{0,4},{4,0},{8,12},{12,8},{1,5},{5,1},{9,13},{13,9},{2,6},{6,2},{1... | collective-permute-start | bytes 245768 | tf_op jit(solution)/shard_map/ppermute | solution.py:45
  32.6 9.5 %collective-permute-start.7 = (bf16[64,640]{1,0:T(8,128)(2,1)S(1)}, bf16[64,640]{1,0:T(8,128)(2,1)S(1)}, u32[]{:S(2)}, u32[]{:S(2)}) collective-permute-start(bf16[64,640]{1,0:T(8,128)(2,1)S(1)} %get-tuple-element.28), channel_id=1, source_target_pairs={{0,8},{4,12},{8,0},{12,4},{1,9},{5,13},{9,1},{13,5},{2,10},{6,14},... | collective-permute-start | bytes 245768 | tf_op jit(solution)/shard_map/ppermute | solution.py:45
  35.2 6.9 %collective-permute-start.8 = (bf16[64,640]{1,0:T(8,128)(2,1)S(1)}, bf16[64,640]{1,0:T(8,128)(2,1)S(1)}, u32[]{:S(2)}, u32[]{:S(2)}) collective-permute-start(bf16[64,640]{1,0:T(8,128)(2,1)S(1)} %get-tuple-element.29), channel_id=1, source_target_pairs={{0,12},{4,8},{8,4},{12,0},{1,13},{5,9},{9,5},{13,1},{2,14},{6,10},... | collective-permute-start | bytes 245768 | tf_op jit(solution)/shard_map/ppermute | solution.py:45

commit v3 on v2

--- a/solution.py
+++ b/solution.py
@@ -94,9 +94,23 @@
     return jnp.sum(jnp.where(diagonal, row, 0.0), axis=1, keepdims=True)
 
 
-def pack_kernel(particle_ref, index_ref, prior_ref, group_ref, packed_ref):
+def pack_kernel(particle_hbm, index_hbm, prior_hbm, group_hbm, packed_ref, index_ref, prior_ref, group_ref, sems):
     particles, candidates = index_ref.shape
-    packed_ref[:, :COLS] = particle_ref[...]
+    copies = [
+        pltpu.make_async_copy(source, target, sems.at[i])
+        for i, (source, target) in enumerate(
+            [
+                (index_hbm, index_ref),
+                (prior_hbm, prior_ref),
+                (group_hbm, group_ref),
+                (particle_hbm, packed_ref.at[:, pl.ds(0, COLS)]),
+            ]
+        )
+    ]
+    for copy in copies:
+        copy.start()
+    for copy in copies[:3]:
+        copy.wait()
     lane = lane_index((particles, META))
     index = jnp.concatenate(
         [index_ref[...].astype(jnp.float32), jnp.zeros((particles, META - candidates), jnp.float32)],
@@ -106,6 +120,7 @@
     group = to_column(group_ref[...].astype(jnp.float32))
     meta = jnp.where(lane == candidates, prior, jnp.where(lane == candidates + 1, group, index))
     packed_ref[:, COLS:] = meta.astype(jnp.bfloat16)
+    copies[3].wait()
 
 
 def score_block(block_ref, table_ref, scale_ref, rotated_ref, norm_ref, shifted_ref, out):
@@ -180,56 +195,69 @@
 
 
 def own_kernel(
-    block_ref, class_ref, table_ref, scale_ref,
-    shifted_ref, exp_ref, stats_ref, rotated_ref, norm_ref,
+    count, block_ref, class_hbm, table_hbm, scale_hbm,
+    shifted_ref, exp_ref, stats_ref, rotated_ref, norm_ref, table_ref, scale_ref,
+    class_ref, sems,
 ):
+    copies = [
+        pltpu.make_async_copy(source, target, sems.at[i])
+        for i, (source, target) in enumerate(
+            [(class_hbm, class_ref), (scale_hbm, scale_ref), (table_hbm, table_ref)]
+        )
+    ]
+    for copy in copies:
+        copy.start()
+    copies[0].wait()
     rotate_classes(class_ref, rotated_ref, norm_ref)
+    copies[1].wait()
+    copies[2].wait()
     classes = norm_ref.shape[0]
 
+    rows = exp_ref.shape[1] // count
+
     def out(rotation, value):
-        exp_ref[rotation * classes : (rotation + 1) * classes, :] = value
+        exp_ref[rotation * classes : (rotation + 1) * classes, 0:rows] = value
 
     highest, total, scale = score_block(
-        block_ref, table_ref, scale_ref, rotated_ref, norm_ref, shifted_ref, out
-    )
+        block_ref, table_ref, scale_ref, rotated_ref, norm_ref, shifted_ref.at[0:rows, :], out
+    )
+    stats_ref[...] = jnp.zeros_like(stats_ref)
     stats_ref[0:1, :] = highest
     stats_ref[1:2, :] = total
-    stats_ref[2:3, :] = scale
-    stats_ref[3:8, :] = jnp.zeros((5, LANES), jnp.float32)
+    stats_ref[2 * count : 2 * count + 1, :] = scale
 
 
 def rest_kernel(count, *refs):
     blocks = refs[: count - 1]
     table_ref, scale_ref, rotated_ref, norm_ref, own_ref = refs[count - 1 : count + 4]
-    shifted_ref, exp_ref, stats_ref, scales_ref = refs[count + 4 :]
+    shifted_ref, exp_ref, stats_ref = refs[count + 6 :]
     classes = norm_ref.shape[0]
-    rows = shifted_ref.shape[0] // (count - 1)
-    stats_ref[0:2, :] = own_ref[0:2, :]
-    scales_ref[...] = jnp.zeros_like(scales_ref)
-    scales_ref[0:1, :] = own_ref[2:3, :]
-    for block in range(count - 1):
+    rows = exp_ref.shape[1] // count
+    stats_ref[...] = own_ref[...]
+    for block in range(1, count):
         part = slice(block * rows, (block + 1) * rows)
 
         def out(rotation, value):
             exp_ref[rotation * classes : (rotation + 1) * classes, part] = value
 
         highest, total, scale = score_block(
-            blocks[block], table_ref, scale_ref, rotated_ref, norm_ref, shifted_ref.at[part, :], out
-        )
-        stats_ref[2 * block + 2 : 2 * block + 3, :] = highest
-        stats_ref[2 * block + 3 : 2 * block + 4, :] = total
-        scales_ref[block + 1 : block + 2, :] = scale
+            blocks[block - 1], table_ref, scale_ref, rotated_ref, norm_ref,
+            shifted_ref.at[part, :], out,
+        )
+        stats_ref[2 * block : 2 * block + 1, :] = highest
+        stats_ref[2 * block + 1 : 2 * block + 2, :] = total
+        stats_ref[2 * count + block : 2 * count + block + 1, :] = scale
 
 
 def sums_kernel(count, doms, width, *refs):
     stats = refs[:count]
-    place_ref, scales_ref, exp_own, exp_rest, shifted_own, shifted_rest = refs[count : count + 6]
-    own_out = refs[count + 6]
-    sends = refs[count + 7 : count + 6 + doms]
-    weight_ref, sums_ref, parts_ref = refs[count + 6 + doms :]
-    rows = shifted_own.shape[0]
+    exp_ref, shifted_ref = refs[count : count + 2]
+    own_out = refs[count + 2]
+    sends = refs[count + 3 : count + 2 + doms]
+    weight_ref, sums_ref, parts_ref = refs[count + 2 + doms :]
+    rows = exp_ref.shape[1] // count
     repeat = rows // LANES
-    classes = exp_own.shape[0] // ROTS
+    classes = weight_ref.shape[0] // ROTS
     mass = jnp.zeros((classes, rows), jnp.float32)
     for block in range(count):
         highs = [stats[c][2 * (c ^ block) : 2 * (c ^ block) + 1, :] for c in range(count)]
@@ -237,16 +265,12 @@
         top = functools.reduce(jnp.maximum, highs)
         total = functools.reduce(jnp.add, [l * jnp.exp(h - top) for h, l in zip(highs, lows)])
         factor = jnp.exp(highs[0] - top) / total
-        scale = scales_ref[block : block + 1, :]
+        scale = stats[0][2 * count + block : 2 * count + block + 1, :]
         factor = jnp.concatenate([factor] * repeat, axis=1)
         scale = jnp.concatenate([scale] * repeat, axis=1)
         for rotation in range(ROTS):
             rotated = slice(rotation * classes, (rotation + 1) * classes)
-            value = (
-                exp_own[rotated, :]
-                if block == 0
-                else exp_rest[rotated, (block - 1) * rows : block * rows]
-            )
+            value = exp_ref[rotated, block * rows : (block + 1) * rows]
             weight = value * factor * scale
             mass = mass + weight * scale
             weight_ref[rotated, block * rows : (block + 1) * rows] = weight.astype(jnp.bfloat16)
@@ -256,9 +280,7 @@
     for start in range(0, COLS, wide):
         columns = slice(start, start + wide)
         product = jnp.dot(
-            weight_ref[:, :rows], shifted_own[:, columns], preferred_element_type=jnp.float32
-        ) + jnp.dot(
-            weight_ref[:, rows:], shifted_rest[:, columns], preferred_element_type=jnp.float32
+            weight_ref[...], shifted_ref[:, columns], preferred_element_type=jnp.float32
         )
         inside = product[:classes]
         wrapped = None
@@ -301,7 +323,7 @@
         if span < padded:
             part = jnp.concatenate([part, jnp.zeros((classes, padded - span), jnp.float32)], axis=1)
         parts_ref[dom] = jnp.where(lane < width, part[:, :padded], tail)
-    place = place_ref[0]
+    place = lax.axis_index("dom")
     own_out[...] = parts_ref[place]
     for distance in range(1, doms):
         sends[distance - 1][...] = parts_ref[place ^ distance].astype(jnp.bfloat16)
@@ -320,15 +342,23 @@
     weights_ref[...] = to_lanes(mass, total.shape[0])
 
 
-def call(kernel, shapes, scratch, flops, moved, *args, smem=()):
+def call(kernel, shapes, scratch, flops, moved, *args, smem=(), hbm=(), chip=(), pinned=True, aliases=None):
     vmem = pl.BlockSpec(memory_space=pltpu.VMEM)
     scalar = pl.BlockSpec(memory_space=pltpu.SMEM)
+    place = pl.BlockSpec(memory_space=pltpu.HBM)
+    args = [
+        pltpu.with_memory_space_constraint(a, pltpu.HBM) if i in hbm
+        else pltpu.with_memory_space_constraint(a, pltpu.VMEM) if i in chip
+        else a
+        for i, a in enumerate(args)
+    ]
     return pl.pallas_call(
         kernel,
-        out_shape=shapes,
-        in_specs=[scalar if i in smem else vmem for i in range(len(args))],
+        out_shape=[pltpu.VMEM(s.shape, s.dtype) if pinned else s for s in shapes],
+        in_specs=[scalar if i in smem else place if i in hbm else vmem for i in range(len(args))],
         out_specs=[vmem] * len(shapes),
         scratch_shapes=scratch,
+        input_output_aliases=aliases or {},
         compiler_params=pltpu.CompilerParams(vmem_limit_bytes=VMEM_LIMIT),
         cost_estimate=pl.CostEstimate(flops=flops, bytes_accessed=moved, transcendentals=0),
     )(*args)
@@ -348,46 +378,53 @@
     (packed,) = call(
         pack_kernel,
         [shape((particles, COLS + META), bf16)],
-        [],
+        [
+            pltpu.VMEM((particles, candidates), jnp.int32),
+            pltpu.VMEM((1, particles), jnp.int32),
+            pltpu.VMEM((1, particles), jnp.int32),
+            pltpu.SemaphoreType.DMA((4,)),
+        ],
         particles * COLS,
         4 * particles * COLS,
         particle_spectra, shift_index, prior_rotation[None, :], particle_group[None, :],
+        hbm=(0, 1, 2, 3),
     )
     others = [exchange(packed, "cls", distance) for distance in range(1, count)]
     table = jnp.asarray(phase_table())
     scales = group_scale[None, :]
-    stat_rows = -(-2 * count // 8) * 8
+    stat_rows = -(-3 * count // 8) * 8
     work = 2 * rows * COLS * (ROTS * classes + 256)
-    shifted_own, exp_own, stats_own, rotated, norm = call(
-        own_kernel,
+    stats_shape = shape((stat_rows, LANES), f32)
+    shifted_shape = shape((count * rows, COLS), bf16)
+    exp_shape = shape((ROTS * classes, count * rows), f32)
+    shifted, exps, stats_own, rotated, norm, table_on_chip, scales_on_chip = call(
+        functools.partial(own_kernel, count),
         [
-            shape((rows, COLS), bf16),
-            shape((ROTS * classes, rows), f32),
-            shape((8, LANES), f32),
+            shifted_shape,
+            exp_shape,
+            stats_shape,
             shape((ROTS * classes, COLS), bf16),
             shape((classes, LANES), f32),
+            shape(table.shape, bf16),
+            shape(scales.shape, f32),
         ],
-        [],
+        [pltpu.VMEM((classes, COLS), bf16), pltpu.SemaphoreType.DMA((3,))],
         work,
         4 * rows * COLS,
         packed, class_spectra, table, scales,
-    )
-    rest = (count - 1) * rows
-    shifted_rest, exp_rest, stats, scale_rows = call(
+        hbm=(1, 2, 3),
+    )
+    shifted, exps, stats = call(
         functools.partial(rest_kernel, count),
-        [
-            shape((rest, COLS), bf16),
-            shape((ROTS * classes, rest), f32),
-            shape((stat_rows, LANES), f32),
-            shape((-(-count // 8) * 8, LANES), f32),
-        ],
+        [shifted_shape, exp_shape, stats_shape],
         [],
         work * (count - 1),
-        4 * rest * COLS,
-        *others, table, scales, rotated, norm, stats_own,
+        4 * (count - 1) * rows * COLS,
+        *others, table_on_chip, scales_on_chip, rotated, norm, stats_own, shifted, exps,
+        aliases={count + 4: 0, count + 5: 1},
+        chip=(count + 4, count + 5),
     )
     all_stats = [stats] + [exchange(stats, "cls", distance) for distance in range(1, count)]
-    place = lax.axis_index("dom").astype(jnp.int32).reshape(1)
     own, *sends = call(
         functools.partial(sums_kernel, count, doms, width),
         [shape((classes, padded), f32)] + [shape((classes, padded), bf16)] * (doms - 1),
@@ -398,8 +435,8 @@
         ],
         2 * count * rows * COLS * ROTS * classes,
         4 * count * rows * COLS,
-        *all_stats, place, scale_rows, exp_own, exp_rest, shifted_own, shifted_rest,
-        smem=(count,),
+        *all_stats, exps, shifted,
+        chip=(count, count + 1),
     )
     received = [exchange(sends[distance - 1], "dom", distance) for distance in range(1, doms)]
     class_sums, class_weights = call(
@@ -409,6 +446,7 @@
         doms * classes * padded,
         4 * doms * classes * padded,
         own, *received,
+        pinned=False,
     )
     return class_sums, class_weights.reshape(classes)
 

time: 43.2 us -> 33.8 us (0.78)
  local copies, waits for them, and re-layouts: 12 us -> 0 us
  Pallas kernels: 10.8 us -> 14 us
  waiting for transfers between devices: 9.68 us -> 9.16 us
    unnamed x34 -> x0, local copies, waits for them, and re-layouts: 12 us -> none
    pallas_call x5, Pallas kernels: 10.8 us -> 14 us  [call(): pl.pallas_call(kernel, out_shape=[pltpu.VMEM(s.shape, s.dtype) if pinned...]
    ppermute x9, waiting for transfers between devices: 9.68 us -> 9.16 us  [exchange(): lax.ppermute(array, axis, [(i, i ^ distance) for i in range(lax.axis_size...]
  transfers between devices with their start and end apart: 9 -> 9, of which waited for: 4 -> 5; matrix products, arithmetic and copies ran while one was open for 0% -> 0% of each run, Pallas kernels for 6% -> 14%
where the time goes in v3:
time: 33.8 us; the launch traced here: 33.6 us
  Pallas kernels  14 us (41%)
  starting transfers between devices  9.68 us (29%)
  waiting for transfers between devices  9.16 us (27%)
  between operations  0.69 us (2%)
    pallas_call x5, Pallas kernels, call(): pl.pallas_call(kernel, out_shape=[pltpu.VMEM(s.shape, s.dtype) if pinned...  14 us
    ppermute x9, starting transfers between devices, exchange(): lax.ppermute(array, axis, [(i, i ^ distance) for i in range(lax.axis_size...  9.68 us
    ppermute x9, waiting for transfers between devices, exchange(): lax.ppermute(array, axis, [(i, i ^ distance) for i in range(lax.axis_size...  9.16 us
  transfers between devices with their start and end apart: 9, of which 5 were waited for; matrix products, arithmetic and copies ran while one was open for 0% of the time, Pallas kernels for 14%

profile of v3, /device:TPU:0, one launch (start us, length us, event | category | flops | bytes accessed | tf_op | source)
XLA Modules:
  0.0 33.6 jit_solution(4196401622286890304)
XLA Ops:
  0.6 1.0 %shard_map.86.block_ref = bf16[16,2432]{1,0:T(8,128)(2,1)S(1)} custom-call(bf16[16,2304]{1,0:T(8,128)(2,1)} %particle_hbm.1, s32[16,16]{1,0:T(8,128)} %index_hbm.1, s32[1,16]{1,0:T(1,128)} %bitcast.4, s32[1,16]{1,0:T(1,128)} %bitcast.5), custom_call_target="tpu_custom_call" | custom-call | flops 36864 | bytes 147456 | tf_op jit(solution)/shard_map/pallas_call | solution.py:355
  1.6 2.4 %collective-permute-start.2 = (bf16[16,2432]{1,0:T(8,128)(2,1)S(1)}, bf16[16,2432]{1,0:T(8,128)(2,1)S(1)}, u32[]{:S(2)}, u32[]{:S(2)}) collective-permute-start(bf16[16,2432]{1,0:T(8,128)(2,1)S(1)} %shard_map.86.block_ref), channel_id=1, source_target_pairs={{0,3},{1,2},{2,1},{3,0},{4,7},{5,6},{6,5},{7,4},{8,11},{9,10},{10,... | collective-permute-start | bytes 233480 | tf_op jit(solution)/shard_map/ppermute | solution.py:45
  4.0 0.6 %collective-permute-start.1 = (bf16[16,2432]{1,0:T(8,128)(2,1)S(1)}, bf16[16,2432]{1,0:T(8,128)(2,1)S(1)}, u32[]{:S(2)}, u32[]{:S(2)}) collective-permute-start(bf16[16,2432]{1,0:T(8,128)(2,1)S(1)} %shard_map.86.block_ref), channel_id=1, source_target_pairs={{0,2},{1,3},{2,0},{3,1},{4,6},{5,7},{6,4},{7,5},{8,10},{9,11},{10,... | collective-permute-start | bytes 233480 | tf_op jit(solution)/shard_map/ppermute | solution.py:45
  4.7 0.0 collective-permute-start
  4.7 4.8 %shard_map.87 = (bf16[1024,2304]{1,0:T(8,128)(2,1)S(1)}, f32[512,1024]{1,0:T(8,128)S(1)}, f32[16,128]{1,0:T(8,128)S(1)}, bf16[512,2304]{1,0:T(8,128)(2,1)S(1)}, ...) custom-call(bf16[16,2432]{1,0:T(8,128)(2,1)S(1)} %shard_map.86.block_ref, ...), custom_call_target="tpu_custom_call" | custom-call | flops 905969664 | bytes 2359296 | tf_op jit(solution)/shard_map/pallas_call | solution.py:355
  9.5 0.0 collective-permute-done.2.refs_2_
  9.5 0.0 collective-permute-done.1.refs_1_
  9.5 0.0 collective-permute-done.refs_0_
  9.6 4.3 %shard_map.88 = (bf16[1024,2304]{1,0:T(8,128)(2,1)S(1)}, f32[512,1024]{1,0:T(8,128)S(1)}, f32[16,128]{1,0:T(8,128)S(1)}) custom-call(bf16[16,2432]{1,0:T(8,128)(2,1)S(1)} %collective-permute-done.refs_0_, bf16[16,2432]{1,0:T(8,128)(2,1)S(1)} %collective-permute-done.1.refs_1_, ...), custom_call_target="tpu_custom_call", output_to_operand_aliasing={{0}: (8, {}), {1}: (9, {})} | custom-call | flops 2717908992 | bytes 7077888 | tf_op jit(solution)/shard_map/pallas_call | solution.py:355
  13.9 1.5 %collective-permute-start.5 = (f32[16,128]{1,0:T(8,128)S(1)}, f32[16,128]{1,0:T(8,128)S(1)}, u32[]{:S(2)}, u32[]{:S(2)}) collective-permute-start(f32[16,128]{1,0:T(8,128)S(1)} %get-tuple-element.25.refs_0_), channel_id=1, source_target_pairs={{0,3},{1,2},{2,1},{3,0},{4,7},{5,6},{6,5},{7,4},{8,11},{9,10},{10,... | collective-permute-start | bytes 24584 | tf_op jit(solution)/shard_map/ppermute | solution.py:45
  15.3 0.6 %collective-permute-start.4 = (f32[16,128]{1,0:T(8,128)S(1)}, f32[16,128]{1,0:T(8,128)S(1)}, u32[]{:S(2)}, u32[]{:S(2)}) collective-permute-start(f32[16,128]{1,0:T(8,128)S(1)} %get-tuple-element.25.refs_0_), channel_id=1, source_target_pairs={{0,2},{1,3},{2,0},{3,1},{4,6},{5,7},{6,4},{7,5},{8,10},{9,11},{10,... | collective-permute-start | bytes 24584 | tf_op jit(solution)/shard_map/ppermute | solution.py:45
  16.0 0.0 collective-permute-start.3
  16.0 1.0 %collective-permute-done.5.refs_3_ = f32[16,128]{1,0:T(8,128)S(1)} collective-permute-done((f32[16,128]{1,0:T(8,128)S(1)}, f32[16,128]{1,0:T(8,128)S(1)}, u32[]{:S(2)}, u32[]{:S(2)}) %collective-permute-start.5) | collective-permute-done | bytes 8224 | tf_op jit(solution)/shard_map/ppermute | solution.py:45
  16.9 2.0 %collective-permute-done.4.refs_2_ = f32[16,128]{1,0:T(8,128)S(1)} collective-permute-done((f32[16,128]{1,0:T(8,128)S(1)}, f32[16,128]{1,0:T(8,128)S(1)}, u32[]{:S(2)}, u32[]{:S(2)}) %collective-permute-start.4) | collective-permute-done | bytes 8224 | tf_op jit(solution)/shard_map/ppermute | solution.py:45
  19.0 0.0 collective-permute-done.3.refs_1_
  19.0 3.3 %shard_map.89 = (f32[64,640]{1,0:T(8,128)S(1)}, bf16[64,640]{1,0:T(8,128)(2,1)S(1)}, bf16[64,640]{1,0:T(8,128)(2,1)S(1)}, bf16[64,640]{1,0:T(8,128)(2,1)S(1)}) custom-call(f32[16,128]{1,0:T(8,128)S(1)} %get-tuple-element.25.refs_0_, f32[16,128]{1,0:T(8,128)S(1)} %collective-permute-done.3.refs_1_, f32[16,128]{1,0:T(8,128)S(1)} %collective-permute-done.4.refs_2_, ...), custom_call_target="tpu_custom_call" | custom-call | flops 2415919104 | bytes 9437184 | tf_op jit(solution)/shard_map/pallas_call | solution.py:355
  22.3 1.6 %collective-permute-start.6 = (bf16[64,640]{1,0:T(8,128)(2,1)S(1)}, bf16[64,640]{1,0:T(8,128)(2,1)S(1)}, u32[]{:S(2)}, u32[]{:S(2)}) collective-permute-start(bf16[64,640]{1,0:T(8,128)(2,1)S(1)} %get-tuple-element.29), channel_id=1, source_target_pairs={{0,4},{4,0},{8,12},{12,8},{1,5},{5,1},{9,13},{13,9},{2,6},{6,2},{1... | collective-permute-start | bytes 245768 | tf_op jit(solution)/shard_map/ppermute | solution.py:45
  23.9 2.6 %collective-permute-start.7 = (bf16[64,640]{1,0:T(8,128)(2,1)S(1)}, bf16[64,640]{1,0:T(8,128)(2,1)S(1)}, u32[]{:S(2)}, u32[]{:S(2)}) collective-permute-start(bf16[64,640]{1,0:T(8,128)(2,1)S(1)} %get-tuple-element.30), channel_id=1, source_target_pairs={{0,8},{4,12},{8,0},{12,4},{1,9},{5,13},{9,1},{13,5},{2,10},{6,14},... | collective-permute-start | bytes 245768 | tf_op jit(solution)/shard_map/ppermute | solution.py:45
  26.5 0.2 collective-permute-start.8
  26.7 0.9 %collective-permute-done.6.refs_0_ = bf16[64,640]{1,0:T(8,128)(2,1)S(1)} collective-permute-done((bf16[64,640]{1,0:T(8,128)(2,1)S(1)}, bf16[64,640]{1,0:T(8,128)(2,1)S(1)}, u32[]{:S(2)}, u32[]{:S(2)}) %collective-permute-start.6) | collective-permute-done | bytes 81952 | tf_op jit(solution)/shard_map/ppermute | solution.py:45
  27.6 4.1 %collective-permute-done.7.refs_1_ = bf16[64,640]{1,0:T(8,128)(2,1)S(1)} collective-permute-done((bf16[64,640]{1,0:T(8,128)(2,1)S(1)}, bf16[64,640]{1,0:T(8,128)(2,1)S(1)}, u32[]{:S(2)}, u32[]{:S(2)}) %collective-permute-start.7) | collective-permute-done | bytes 81952 | tf_op jit(solution)/shard_map/ppermute | solution.py:45
  31.7 1.2 %collective-permute-done.8.refs_2_ = bf16[64,640]{1,0:T(8,128)(2,1)S(1)} collective-permute-done((bf16[64,640]{1,0:T(8,128)(2,1)S(1)}, bf16[64,640]{1,0:T(8,128)(2,1)S(1)}, u32[]{:S(2)}, u32[]{:S(2)}) %collective-permute-start.8) | collective-permute-done | bytes 81952 | tf_op jit(solution)/shard_map/ppermute | solution.py:45
  32.9 0.7 %shard_map.90 = (f32[64,576]{1,0:T(8,128)}, f32[1,64]{1,0:T(1,128)}) custom-call(f32[64,640]{1,0:T(8,128)S(1)} %get-tuple-element.28.own_ref, bf16[64,640]{1,0:T(8,128)(2,1)S(1)} %collective-permute-done.6.refs_0_, bf16[64,640]{1,0:T(8,128)(2,1)S(1)} %collective-permute-done.7.refs_1_, bf16[64,640]{1,0:T(8,128)(2,1)S(1)} %collective-permute-done.8.refs_2_), custom_call_target="tpu_custom_call" | custom-call | flops 163840 | bytes 655360 | tf_op jit(solution)/shard_map/pallas_call | solution.py:355
Async XLA Ops:
  1.6 7.9 %collective-permute-start.2 = (bf16[16,2432]{1,0:T(8,128)(2,1)S(1)}, bf16[16,2432]{1,0:T(8,128)(2,1)S(1)}, u32[]{:S(2)}, u32[]{:S(2)}) collective-permute-start(bf16[16,2432]{1,0:T(8,128)(2,1)S(1)} %shard_map.86.block_ref), channel_id=1, source_target_pairs={{0,3},{1,2},{2,1},{3,0},{4,7},{5,6},{6,5},{7,4},{8,11},{9,10},{10,... | collective-permute-start | bytes 233480 | tf_op jit(solution)/shard_map/ppermute | solution.py:45
  4.0 5.5 %collective-permute-start.1 = (bf16[16,2432]{1,0:T(8,128)(2,1)S(1)}, bf16[16,2432]{1,0:T(8,128)(2,1)S(1)}, u32[]{:S(2)}, u32[]{:S(2)}) collective-permute-start(bf16[16,2432]{1,0:T(8,128)(2,1)S(1)} %shard_map.86.block_ref), channel_id=1, source_target_pairs={{0,2},{1,3},{2,0},{3,1},{4,6},{5,7},{6,4},{7,5},{8,10},{9,11},{10,... | collective-permute-start | bytes 233480 | tf_op jit(solution)/shard_map/ppermute | solution.py:45
  4.7 4.9 %collective-permute-start = (bf16[16,2432]{1,0:T(8,128)(2,1)S(1)}, bf16[16,2432]{1,0:T(8,128)(2,1)S(1)}, u32[]{:S(2)}, u32[]{:S(2)}) collective-permute-start(bf16[16,2432]{1,0:T(8,128)(2,1)S(1)} %shard_map.86.block_ref), channel_id=1, source_target_pairs={{0,1},{1,0},{2,3},{3,2},{4,5},{5,4},{6,7},{7,6},{8,9},{9,8},{10,11... | collective-permute-start | bytes 233480 | tf_op jit(solution)/shard_map/ppermute | solution.py:45
  13.9 3.1 %collective-permute-start.5 = (f32[16,128]{1,0:T(8,128)S(1)}, f32[16,128]{1,0:T(8,128)S(1)}, u32[]{:S(2)}, u32[]{:S(2)}) collective-permute-start(f32[16,128]{1,0:T(8,128)S(1)} %get-tuple-element.25.refs_0_), channel_id=1, source_target_pairs={{0,3},{1,2},{2,1},{3,0},{4,7},{5,6},{6,5},{7,4},{8,11},{9,10},{10,... | collective-permute-start | bytes 24584 | tf_op jit(solution)/shard_map/ppermute | solution.py:45
  15.3 3.7 %collective-permute-start.4 = (f32[16,128]{1,0:T(8,128)S(1)}, f32[16,128]{1,0:T(8,128)S(1)}, u32[]{:S(2)}, u32[]{:S(2)}) collective-permute-start(f32[16,128]{1,0:T(8,128)S(1)} %get-tuple-element.25.refs_0_), channel_id=1, source_target_pairs={{0,2},{1,3},{2,0},{3,1},{4,6},{5,7},{6,4},{7,5},{8,10},{9,11},{10,... | collective-permute-start | bytes 24584 | tf_op jit(solution)/shard_map/ppermute | solution.py:45
  16.0 3.0 %collective-permute-start.3 = (f32[16,128]{1,0:T(8,128)S(1)}, f32[16,128]{1,0:T(8,128)S(1)}, u32[]{:S(2)}, u32[]{:S(2)}) collective-permute-start(f32[16,128]{1,0:T(8,128)S(1)} %get-tuple-element.25.refs_0_), channel_id=1, source_target_pairs={{0,1},{1,0},{2,3},{3,2},{4,5},{5,4},{6,7},{7,6},{8,9},{9,8},{10,11... | collective-permute-start | bytes 24584 | tf_op jit(solution)/shard_map/ppermute | solution.py:45
  22.3 5.3 %collective-permute-start.6 = (bf16[64,640]{1,0:T(8,128)(2,1)S(1)}, bf16[64,640]{1,0:T(8,128)(2,1)S(1)}, u32[]{:S(2)}, u32[]{:S(2)}) collective-permute-start(bf16[64,640]{1,0:T(8,128)(2,1)S(1)} %get-tuple-element.29), channel_id=1, source_target_pairs={{0,4},{4,0},{8,12},{12,8},{1,5},{5,1},{9,13},{13,9},{2,6},{6,2},{1... | collective-permute-start | bytes 245768 | tf_op jit(solution)/shard_map/ppermute | solution.py:45
  23.9 7.8 %collective-permute-start.7 = (bf16[64,640]{1,0:T(8,128)(2,1)S(1)}, bf16[64,640]{1,0:T(8,128)(2,1)S(1)}, u32[]{:S(2)}, u32[]{:S(2)}) collective-permute-start(bf16[64,640]{1,0:T(8,128)(2,1)S(1)} %get-tuple-element.30), channel_id=1, source_target_pairs={{0,8},{4,12},{8,0},{12,4},{1,9},{5,13},{9,1},{13,5},{2,10},{6,14},... | collective-permute-start | bytes 245768 | tf_op jit(solution)/shard_map/ppermute | solution.py:45
  26.5 6.3 %collective-permute-start.8 = (bf16[64,640]{1,0:T(8,128)(2,1)S(1)}, bf16[64,640]{1,0:T(8,128)(2,1)S(1)}, u32[]{:S(2)}, u32[]{:S(2)}) collective-permute-start(bf16[64,640]{1,0:T(8,128)(2,1)S(1)} %get-tuple-element.31), channel_id=1, source_target_pairs={{0,12},{4,8},{8,4},{12,0},{1,13},{5,9},{9,5},{13,1},{2,14},{6,10},... | collective-permute-start | bytes 245768 | tf_op jit(solution)/shard_map/ppermute | solution.py:45

commit v4 on v3

--- a/solution.py
+++ b/solution.py
@@ -94,7 +94,10 @@
     return jnp.sum(jnp.where(diagonal, row, 0.0), axis=1, keepdims=True)
 
 
-def pack_kernel(particle_hbm, index_hbm, prior_hbm, group_hbm, packed_ref, index_ref, prior_ref, group_ref, sems):
+def pack_kernel(
+    particle_hbm, index_hbm, prior_hbm, group_hbm, class_hbm, scale_hbm,
+    packed_ref, class_ref, scale_ref, index_ref, prior_ref, group_ref, sems,
+):
     particles, candidates = index_ref.shape
     copies = [
         pltpu.make_async_copy(source, target, sems.at[i])
@@ -104,6 +107,8 @@
                 (prior_hbm, prior_ref),
                 (group_hbm, group_ref),
                 (particle_hbm, packed_ref.at[:, pl.ds(0, COLS)]),
+                (class_hbm, class_ref),
+                (scale_hbm, scale_ref),
             ]
         )
     ]
@@ -120,7 +125,8 @@
     group = to_column(group_ref[...].astype(jnp.float32))
     meta = jnp.where(lane == candidates, prior, jnp.where(lane == candidates + 1, group, index))
     packed_ref[:, COLS:] = meta.astype(jnp.bfloat16)
-    copies[3].wait()
+    for copy in copies[3:]:
+        copy.wait()
 
 
 def score_block(block_ref, table_ref, scale_ref, rotated_ref, norm_ref, shifted_ref, out):
@@ -195,24 +201,14 @@
 
 
 def own_kernel(
-    count, block_ref, class_hbm, table_hbm, scale_hbm,
-    shifted_ref, exp_ref, stats_ref, rotated_ref, norm_ref, table_ref, scale_ref,
-    class_ref, sems,
+    count, block_ref, class_ref, table_hbm, scale_ref,
+    shifted_ref, exp_ref, stats_ref, rotated_ref, norm_ref, table_ref, sem,
 ):
-    copies = [
-        pltpu.make_async_copy(source, target, sems.at[i])
-        for i, (source, target) in enumerate(
-            [(class_hbm, class_ref), (scale_hbm, scale_ref), (table_hbm, table_ref)]
-        )
-    ]
-    for copy in copies:
-        copy.start()
-    copies[0].wait()
+    copy = pltpu.make_async_copy(table_hbm, table_ref, sem)
+    copy.start()
     rotate_classes(class_ref, rotated_ref, norm_ref)
-    copies[1].wait()
-    copies[2].wait()
+    copy.wait()
     classes = norm_ref.shape[0]
-
     rows = exp_ref.shape[1] // count
 
     def out(rotation, value):
@@ -249,12 +245,7 @@
         stats_ref[2 * count + block : 2 * count + block + 1, :] = scale
 
 
-def sums_kernel(count, doms, width, *refs):
-    stats = refs[:count]
-    exp_ref, shifted_ref = refs[count : count + 2]
-    own_out = refs[count + 2]
-    sends = refs[count + 3 : count + 2 + doms]
-    weight_ref, sums_ref, parts_ref = refs[count + 2 + doms :]
+def weigh(count, stats, exp_ref, weight_ref):
     rows = exp_ref.shape[1] // count
     repeat = rows // LANES
     classes = weight_ref.shape[0] // ROTS
@@ -268,77 +259,92 @@
         scale = stats[0][2 * count + block : 2 * count + block + 1, :]
         factor = jnp.concatenate([factor] * repeat, axis=1)
         scale = jnp.concatenate([scale] * repeat, axis=1)
+        part = slice(block * rows, (block + 1) * rows)
         for rotation in range(ROTS):
             rotated = slice(rotation * classes, (rotation + 1) * classes)
-            value = exp_ref[rotated, block * rows : (block + 1) * rows]
-            weight = value * factor * scale
+            weight = exp_ref[rotated, part] * factor * scale
             mass = mass + weight * scale
-            weight_ref[rotated, block * rows : (block + 1) * rows] = weight.astype(jnp.bfloat16)
-    mass = jnp.sum(mass, axis=1, keepdims=True)
-    wide = 2 * LANES
-    lane = lane_index((classes, wide)) % ANG
-    for start in range(0, COLS, wide):
-        columns = slice(start, start + wide)
+            weight_ref[rotated, part] = weight.astype(jnp.bfloat16)
+    return jnp.broadcast_to(jnp.sum(mass, axis=1, keepdims=True), (classes, LANES))
+
+
+def sum_block(doms, width, distance, weight_ref, shifted_ref, mass, out_ref):
+    classes, extent = out_ref.shape
+    padded = -(-extent // LANES) * LANES
+    place = lax.axis_index("dom") ^ distance
+    first = place * width
+    shifts = sorted({width * dom % LANES for dom in range(doms)})
+    span = -(-(shifts[-1] + width) // LANES) * LANES
+    base = first // LANES * LANES
+    tiles = []
+    for start in range(0, span, 2 * LANES):
+        wide = min(2 * LANES, span - start)
+        columns = pl.ds(pl.multiple_of(base + start, LANES), wide)
         product = jnp.dot(
             weight_ref[...], shifted_ref[:, columns], preferred_element_type=jnp.float32
         )
-        inside = product[:classes]
-        wrapped = None
-        for rotation in range(1, ROTS):
-            offset = ANG_STEP * rotation % ANG
-            turned = jnp.concatenate(
-                [
-                    pltpu.roll(
-                        product[rotation * classes : (rotation + 1) * classes, s : s + LANES],
-                        LANES - offset,
-                        1,
-                    )
-                    for s in range(0, wide, LANES)
-                ],
-                axis=1,
-            )
-            within = lane < ANG - offset
-            inside = inside + jnp.where(within, turned, 0.0)
-            over = jnp.where(within, 0.0, turned)
-            wrapped = over if wrapped is None else wrapped + over
-        wrapped = jnp.concatenate(
-            [pltpu.roll(wrapped[:, s : s + LANES], ANG, 1) for s in range(0, wide, LANES)], axis=1
-        )
-        sums_ref[:, columns] = inside + wrapped
-    padded = own_out.shape[1]
-    lane = lane_index((classes, padded))
+        for part in range(0, wide, LANES):
+            lane = lane_index((classes, LANES)) % ANG
+            inside = product[:classes, part : part + LANES]
+            wrapped = None
+            for rotation in range(1, ROTS):
+                offset = ANG_STEP * rotation % ANG
+                turned = pltpu.roll(
+                    product[rotation * classes : (rotation + 1) * classes, part : part + LANES],
+                    LANES - offset,
+                    1,
+                )
+                within = lane < ANG - offset
+                inside = inside + jnp.where(within, turned, 0.0)
+                over = jnp.where(within, 0.0, turned)
+                wrapped = over if wrapped is None else wrapped + over
+            tiles.append(inside + pltpu.roll(wrapped, ANG, 1))
+    total = jnp.concatenate(tiles, axis=1)
+    aligned = total
+    for shift in shifts:
+        if shift:
+            aligned = jnp.where(first - base == shift, pltpu.roll(total, span - shift, 1), aligned)
+    if span < padded:
+        aligned = jnp.concatenate(
+            [aligned, jnp.zeros((classes, padded - span), jnp.float32)], axis=1
+        )
+    mass = jnp.concatenate([mass] * (padded // LANES), axis=1)
     high = mass.astype(jnp.bfloat16).astype(jnp.float32)
     middle = (mass - high).astype(jnp.bfloat16).astype(jnp.float32)
     low = (mass - high - middle).astype(jnp.bfloat16).astype(jnp.float32)
+    lane = lane_index((classes, padded))
     tail = jnp.where(
         lane == width, high, jnp.where(lane == width + 1, middle, jnp.where(lane == width + 2, low, 0.0))
     )
-    for dom in range(doms):
-        first = width * dom
-        base = first // LANES * LANES
-        span = -(-(first - base + width) // LANES) * LANES
-        part = sums_ref[:, base : base + span]
-        if first > base:
-            part = pltpu.roll(part, span - (first - base), 1)
-        if span < padded:
-            part = jnp.concatenate([part, jnp.zeros((classes, padded - span), jnp.float32)], axis=1)
-        parts_ref[dom] = jnp.where(lane < width, part[:, :padded], tail)
-    place = lax.axis_index("dom")
-    own_out[...] = parts_ref[place]
-    for distance in range(1, doms):
-        sends[distance - 1][...] = parts_ref[place ^ distance].astype(jnp.bfloat16)
+    total = jnp.where(lane < width, aligned[:, :padded], tail)
+    out_ref[...] = total[:, :extent].astype(out_ref.dtype)
+
+
+def first_sums_kernel(count, doms, width, distance, *refs):
+    stats = refs[:count]
+    exp_ref, shifted_ref, out_ref, weight_ref, mass_ref = refs[count:]
+    mass = weigh(count, stats, exp_ref, weight_ref)
+    mass_ref[...] = mass
+    sum_block(doms, width, distance, weight_ref, shifted_ref, mass, out_ref)
+
+
+def next_sums_kernel(doms, width, distance, weight_ref, shifted_ref, mass_ref, done_ref, out_ref):
+    sum_block(doms, width, distance, weight_ref, shifted_ref, mass_ref[...], out_ref)
 
 
 def final_kernel(width, own_ref, *refs):
     received, sums_ref, weights_ref = refs[:-2], refs[-2], refs[-1]
-    total = own_ref[...]
-    for ref in received:
-        total = total + ref[...].astype(jnp.float32)
-    sums_ref[...] = total[:, :width]
-    lane = lane_index(total.shape)
-    mass = jnp.sum(
-        jnp.where((lane >= width) & (lane < width + 3), total, 0.0), axis=1, keepdims=True
-    )
+    total, mass = None, None
+    base = width // LANES * LANES
+    for ref in (own_ref, *received):
+        value = ref[:, :width].astype(jnp.float32)
+        total = value if total is None else total + value
+        tail = ref[:, base:].astype(jnp.float32)
+        lane = base + lane_index(tail.shape)
+        tail = jnp.where((lane >= width) & (lane < width + 3), tail, 0.0)
+        tail = jnp.sum(tail, axis=1, keepdims=True)
+        mass = tail if mass is None else mass + tail
+    sums_ref[...] = total
     weights_ref[...] = to_lanes(mass, total.shape[0])
 
 
@@ -372,32 +378,37 @@
     rows = particles * candidates
     width = COLS // doms
     padded = -(-(width + 3) // LANES) * LANES
+    growth = (padded - width - 3) // (doms - 1)
     f32, bf16 = jnp.float32, jnp.bfloat16
     shape = jax.ShapeDtypeStruct
 
-    (packed,) = call(
+    packed, classes_on_chip, scales = call(
         pack_kernel,
-        [shape((particles, COLS + META), bf16)],
+        [
+            shape((particles, COLS + META), bf16),
+            shape(class_spectra.shape, bf16),
+            shape((1, group_scale.shape[0]), f32),
+        ],
         [
             pltpu.VMEM((particles, candidates), jnp.int32),
             pltpu.VMEM((1, particles), jnp.int32),
             pltpu.VMEM((1, particles), jnp.int32),
-            pltpu.SemaphoreType.DMA((4,)),
+            pltpu.SemaphoreType.DMA((6,)),
         ],
         particles * COLS,
         4 * particles * COLS,
         particle_spectra, shift_index, prior_rotation[None, :], particle_group[None, :],
-        hbm=(0, 1, 2, 3),
+        class_spectra, group_scale[None, :],
+        hbm=(0, 1, 2, 3, 4, 5),
     )
     others = [exchange(packed, "cls", distance) for distance in range(1, count)]
     table = jnp.asarray(phase_table())
-    scales = group_scale[None, :]
     stat_rows = -(-3 * count // 8) * 8
     work = 2 * rows * COLS * (ROTS * classes + 256)
     stats_shape = shape((stat_rows, LANES), f32)
     shifted_shape = shape((count * rows, COLS), bf16)
     exp_shape = shape((ROTS * classes, count * rows), f32)
-    shifted, exps, stats_own, rotated, norm, table_on_chip, scales_on_chip = call(
+    shifted, exps, stats_own, rotated, norm, table_on_chip = call(
         functools.partial(own_kernel, count),
         [
             shifted_shape,
@@ -406,13 +417,12 @@
             shape((ROTS * classes, COLS), bf16),
             shape((classes, LANES), f32),
             shape(table.shape, bf16),
-            shape(scales.shape, f32),
         ],
-        [pltpu.VMEM((classes, COLS), bf16), pltpu.SemaphoreType.DMA((3,))],
+        [pltpu.SemaphoreType.DMA],
         work,
         4 * rows * COLS,
-        packed, class_spectra, table, scales,
-        hbm=(1, 2, 3),
+        packed, classes_on_chip, table, scales,
+        hbm=(2,),
     )
     shifted, exps, stats = call(
         functools.partial(rest_kernel, count),
@@ -420,25 +430,40 @@
         [],
         work * (count - 1),
         4 * (count - 1) * rows * COLS,
-        *others, table_on_chip, scales_on_chip, rotated, norm, stats_own, shifted, exps,
+        *others, table_on_chip, scales, rotated, norm, stats_own, shifted, exps,
         aliases={count + 4: 0, count + 5: 1},
         chip=(count + 4, count + 5),
     )
     all_stats = [stats] + [exchange(stats, "cls", distance) for distance in range(1, count)]
-    own, *sends = call(
-        functools.partial(sums_kernel, count, doms, width),
-        [shape((classes, padded), f32)] + [shape((classes, padded), bf16)] * (doms - 1),
+    order = list(range(doms - 1, -1, -1))
+    blocks = {}
+    work = 2 * count * rows * COLS * ROTS * classes // doms
+    blocks[order[0]], weights, mass = call(
+        functools.partial(first_sums_kernel, count, doms, width, order[0]),
         [
-            pltpu.VMEM((ROTS * classes, count * rows), bf16),
-            pltpu.VMEM((classes, COLS), f32),
-            pltpu.VMEM((doms, classes, padded), f32),
+            shape((classes, width + 3 + order[0] * growth), bf16),
+            shape((ROTS * classes, count * rows), bf16),
+            shape((classes, LANES), f32),
         ],
-        2 * count * rows * COLS * ROTS * classes,
-        4 * count * rows * COLS,
+        [],
+        work,
+        4 * count * rows * width,
         *all_stats, exps, shifted,
         chip=(count, count + 1),
     )
-    received = [exchange(sends[distance - 1], "dom", distance) for distance in range(1, doms)]
+    received = []
+    for before, distance in zip(order, order[1:]):
+        received.append(exchange(blocks[before], "dom", before))
+        (blocks[distance],) = call(
+            functools.partial(next_sums_kernel, doms, width, distance),
+            [shape((classes, width + 3 + distance * growth), bf16 if distance else f32)],
+            [],
+            1024,
+            1024,
+            weights, shifted, mass, blocks[before],
+            chip=(1,),
+        )
+    own = blocks[0]
     class_sums, class_weights = call(
         functools.partial(final_kernel, width),
         [shape((classes, width), f32), shape((1, classes), f32)],

time: 33.8 us -> 32.9 us (0.973)
  waiting for transfers between devices: 9.16 us -> 5.85 us
  Pallas kernels: 14 us -> 16.3 us
    ppermute x9, waiting for transfers between devices: 9.16 us -> 5.85 us  [exchange(): lax.ppermute(array, axis, [(i, i ^ distance) for i in range(lax.axis_size...]
    pallas_call x5 -> x8, Pallas kernels: 14 us -> 16.3 us  [call(): pl.pallas_call(kernel, out_shape=[pltpu.VMEM(s.shape, s.dtype) if pinned...]
  transfers between devices with their start and end apart: 9 -> 9, of which waited for: 5 -> 3; matrix products, arithmetic and copies ran while one was open for 0% -> 0% of each run, Pallas kernels for 14% -> 27%
where the time goes in v4:
time: 32.9 us; the launch traced here: 32.7 us
  Pallas kernels  16.3 us (50%)
  starting transfers between devices  9.8 us (30%)
  waiting for transfers between devices  5.85 us (18%)
  between operations  0.72 us (2%)
    pallas_call x8, Pallas kernels, call(): pl.pallas_call(kernel, out_shape=[pltpu.VMEM(s.shape, s.dtype) if pinned...  16.3 us
    ppermute x9, starting transfers between devices, exchange(): lax.ppermute(array, axis, [(i, i ^ distance) for i in range(lax.axis_size...  9.8 us
    ppermute x9, waiting for transfers between devices, exchange(): lax.ppermute(array, axis, [(i, i ^ distance) for i in range(lax.axis_size...  5.85 us
  transfers between devices with their start and end apart: 9, of which 3 were waited for; matrix products, arithmetic and copies ran while one was open for 0% of the time, Pallas kernels for 27%

profile of v4, /device:TPU:0, one launch (start us, length us, event | category | flops | bytes accessed | tf_op | source)
XLA Modules:
  0.0 32.7 jit_solution(15174647266635714233)
XLA Ops:
  0.6 1.1 %shard_map.86 = (bf16[16,2432]{1,0:T(8,128)(2,1)S(1)}, bf16[64,2304]{1,0:T(8,128)(2,1)S(1)}, f32[1,64]{1,0:T(1,128)S(1)}) custom-call(bf16[16,2304]{1,0:T(8,128)(2,1)} %particle_hbm.1, s32[16,16]{1,0:T(8,128)} %index_hbm.1, s32[1,16]{1,0:T(1,128)} %bitcast.4, s32[1,16]{1,0:T(1,128)} %bitcast.5, bf16[64,2304]{1,0:T(8,128)(2,1)} %class_hbm.1, f32[1,64]{1,0:T(1,128)} %bitcast.6), custom_call_target="tpu_custom_call" | custom-call | flops 36864 | bytes 147456 | tf_op jit(solution)/shard_map/pallas_call | solution.py:361
  1.7 2.4 %collective-permute-start.2 = (bf16[16,2432]{1,0:T(8,128)(2,1)S(1)}, bf16[16,2432]{1,0:T(8,128)(2,1)S(1)}, u32[]{:S(2)}, u32[]{:S(2)}) collective-permute-start(bf16[16,2432]{1,0:T(8,128)(2,1)S(1)} %get-tuple-element.19.block_ref), channel_id=1, source_target_pairs={{0,3},{1,2},{2,1},{3,0},{4,7},{5,6},{6,5},{7,4},{8,11},{9,10},{10,... | collective-permute-start | bytes 233480 | tf_op jit(solution)/shard_map/ppermute | solution.py:45
  4.2 0.6 %collective-permute-start.1 = (bf16[16,2432]{1,0:T(8,128)(2,1)S(1)}, bf16[16,2432]{1,0:T(8,128)(2,1)S(1)}, u32[]{:S(2)}, u32[]{:S(2)}) collective-permute-start(bf16[16,2432]{1,0:T(8,128)(2,1)S(1)} %get-tuple-element.19.block_ref), channel_id=1, source_target_pairs={{0,2},{1,3},{2,0},{3,1},{4,6},{5,7},{6,4},{7,5},{8,10},{9,11},{10,... | collective-permute-start | bytes 233480 | tf_op jit(solution)/shard_map/ppermute | solution.py:45
  4.8 0.0 collective-permute-start
  4.9 4.9 %shard_map.87 = (bf16[1024,2304]{1,0:T(8,128)(2,1)S(1)}, f32[512,1024]{1,0:T(8,128)S(1)}, f32[16,128]{1,0:T(8,128)S(1)}, bf16[512,2304]{1,0:T(8,128)(2,1)S(1)}, ...) custom-call(bf16[16,2432]{1,0:T(8,128)(2,1)S(1)} %get-tuple-element.19.block_ref, ...), custom_call_target="tpu_custom_call" | custom-call | flops 905969664 | bytes 2359296 | tf_op jit(solution)/shard_map/pallas_call | solution.py:361
  9.8 0.0 collective-permute-done.2.refs_2_
  9.8 0.0 collective-permute-done.1.refs_1_
  9.8 0.0 collective-permute-done.refs_0_
  9.8 4.3 %shard_map.88 = (bf16[1024,2304]{1,0:T(8,128)(2,1)S(1)}, f32[512,1024]{1,0:T(8,128)S(1)}, f32[16,128]{1,0:T(8,128)S(1)}) custom-call(bf16[16,2432]{1,0:T(8,128)(2,1)S(1)} %collective-permute-done.refs_0_, bf16[16,2432]{1,0:T(8,128)(2,1)S(1)} %collective-permute-done.1.refs_1_, ...), custom_call_target="tpu_custom_call", output_to_operand_aliasing={{0}: (8, {}), {1}: (9, {})} | custom-call | flops 2717908992 | bytes 7077888 | tf_op jit(solution)/shard_map/pallas_call | solution.py:361
  14.1 1.5 %collective-permute-start.5 = (f32[16,128]{1,0:T(8,128)S(1)}, f32[16,128]{1,0:T(8,128)S(1)}, u32[]{:S(2)}, u32[]{:S(2)}) collective-permute-start(f32[16,128]{1,0:T(8,128)S(1)} %get-tuple-element.28.refs_0_), channel_id=1, source_target_pairs={{0,3},{1,2},{2,1},{3,0},{4,7},{5,6},{6,5},{7,4},{8,11},{9,10},{10,... | collective-permute-start | bytes 24584 | tf_op jit(solution)/shard_map/ppermute | solution.py:45
  15.6 0.6 %collective-permute-start.4 = (f32[16,128]{1,0:T(8,128)S(1)}, f32[16,128]{1,0:T(8,128)S(1)}, u32[]{:S(2)}, u32[]{:S(2)}) collective-permute-start(f32[16,128]{1,0:T(8,128)S(1)} %get-tuple-element.28.refs_0_), channel_id=1, source_target_pairs={{0,2},{1,3},{2,0},{3,1},{4,6},{5,7},{6,4},{7,5},{8,10},{9,11},{10,... | collective-permute-start | bytes 24584 | tf_op jit(solution)/shard_map/ppermute | solution.py:45
  16.2 0.0 collective-permute-start.3
  16.2 1.0 %collective-permute-done.5.refs_3_ = f32[16,128]{1,0:T(8,128)S(1)} collective-permute-done((f32[16,128]{1,0:T(8,128)S(1)}, f32[16,128]{1,0:T(8,128)S(1)}, u32[]{:S(2)}, u32[]{:S(2)}) %collective-permute-start.5) | collective-permute-done | bytes 8224 | tf_op jit(solution)/shard_map/ppermute | solution.py:45
  17.2 2.0 %collective-permute-done.4.refs_2_ = f32[16,128]{1,0:T(8,128)S(1)} collective-permute-done((f32[16,128]{1,0:T(8,128)S(1)}, f32[16,128]{1,0:T(8,128)S(1)}, u32[]{:S(2)}, u32[]{:S(2)}) %collective-permute-start.4) | collective-permute-done | bytes 8224 | tf_op jit(solution)/shard_map/ppermute | solution.py:45
  19.2 0.0 collective-permute-done.3.refs_1_
  19.2 1.5 %shard_map.89 = (bf16[64,639]{1,0:T(8,128)(2,1)S(1)}, bf16[512,1024]{1,0:T(8,128)(2,1)S(1)}, f32[64,128]{1,0:T(8,128)S(1)}) custom-call(f32[16,128]{1,0:T(8,128)S(1)} %get-tuple-element.28.refs_0_, f32[16,128]{1,0:T(8,128)S(1)} %collective-permute-done.3.refs_1_, f32[16,128]{1,0:T(8,128)S(1)} %collective-permute-done.4.refs_2_, ...), custom_call_target="tpu_custom_call" | custom-call | flops 603979776 | bytes 2359296 | tf_op jit(solution)/shard_map/pallas_call | solution.py:361
  20.7 3.7 %collective-permute-start.6 = (bf16[64,639]{1,0:T(8,128)(2,1)S(1)}, bf16[64,639]{1,0:T(8,128)(2,1)S(1)}, u32[]{:S(2)}, u32[]{:S(2)}) collective-permute-start(bf16[64,639]{1,0:T(8,128)(2,1)S(1)} %get-tuple-element.33.done_ref), channel_id=1, source_target_pairs={{0,12},{4,8},{8,4},{12,0},{1,13},{5,9},{9,5},{13,1},{2,14},{6,10},... | collective-permute-start | bytes 245384 | tf_op jit(solution)/shard_map/ppermute | solution.py:45
  24.4 1.3 %shard_map.90.done_ref = bf16[64,619]{1,0:T(8,128)(2,1)S(1)} custom-call(bf16[512,1024]{1,0:T(8,128)(2,1)S(1)} %get-tuple-element.31.weight_ref, bf16[1024,2304]{1,0:T(8,128)(2,1)S(1)} %get-tuple-element.30.refs_5_.shifted_ref, f32[64,128]{1,0:T(8,128)S(1)} %get-tuple-element.32.mass_ref, bf16[64,639]{1,0:T(8,128)(2,1)S(1)} %get-tuple-element.33.done_ref), custom_call_target="tpu_custom_call" | custom-call | flops 1024 | bytes 1024 | tf_op jit(solution)/shard_map/pallas_call | solution.py:361
  25.6 0.1 collective-permute-start.7
  25.7 1.3 %shard_map.91.done_ref = bf16[64,599]{1,0:T(8,128)(2,1)S(1)} custom-call(bf16[512,1024]{1,0:T(8,128)(2,1)S(1)} %get-tuple-element.31.weight_ref, bf16[1024,2304]{1,0:T(8,128)(2,1)S(1)} %get-tuple-element.30.refs_5_.shifted_ref, f32[64,128]{1,0:T(8,128)S(1)} %get-tuple-element.32.mass_ref, bf16[64,619]{1,0:T(8,128)(2,1)S(1)} %shard_map.90.done_ref), custom_call_target="tpu_custom_call" | custom-call | flops 1024 | bytes 1024 | tf_op jit(solution)/shard_map/pallas_call | solution.py:361
  27.0 0.8 %collective-permute-start.8 = (bf16[64,599]{1,0:T(8,128)(2,1)S(1)}, bf16[64,599]{1,0:T(8,128)(2,1)S(1)}, u32[]{:S(2)}, u32[]{:S(2)}) collective-permute-start(bf16[64,599]{1,0:T(8,128)(2,1)S(1)} %shard_map.91.done_ref), channel_id=1, source_target_pairs={{0,4},{4,0},{8,12},{12,8},{1,5},{5,1},{9,13},{13,9},{2,6},{6,2},{1... | collective-permute-start | bytes 230024 | tf_op jit(solution)/shard_map/ppermute | solution.py:45
  27.8 1.3 %shard_map.92.own_ref = f32[64,579]{1,0:T(8,128)S(1)} custom-call(bf16[512,1024]{1,0:T(8,128)(2,1)S(1)} %get-tuple-element.31.weight_ref, bf16[1024,2304]{1,0:T(8,128)(2,1)S(1)} %get-tuple-element.30.refs_5_.shifted_ref, f32[64,128]{1,0:T(8,128)S(1)} %get-tuple-element.32.mass_ref, bf16[64,599]{1,0:T(8,128)(2,1)S(1)} %shard_map.91.done_ref), custom_call_target="tpu_custom_call" | custom-call | flops 1024 | bytes 1024 | tf_op jit(solution)/shard_map/pallas_call | solution.py:361
  29.1 2.8 %collective-permute-done.8.refs_2_ = bf16[64,599]{1,0:T(8,128)(2,1)S(1)} collective-permute-done((bf16[64,599]{1,0:T(8,128)(2,1)S(1)}, bf16[64,599]{1,0:T(8,128)(2,1)S(1)}, u32[]{:S(2)}, u32[]{:S(2)}) %collective-permute-start.8) | collective-permute-done | bytes 76704 | tf_op jit(solution)/shard_map/ppermute | solution.py:45
  31.9 0.0 collective-permute-done.7.refs_1_
  31.9 0.0 collective-permute-done.6.refs_0_
  31.9 0.7 %shard_map.93 = (f32[64,576]{1,0:T(8,128)}, f32[1,64]{1,0:T(1,128)}) custom-call(f32[64,579]{1,0:T(8,128)S(1)} %shard_map.92.own_ref, bf16[64,639]{1,0:T(8,128)(2,1)S(1)} %collective-permute-done.6.refs_0_, bf16[64,619]{1,0:T(8,128)(2,1)S(1)} %collective-permute-done.7.refs_1_, bf16[64,599]{1,0:T(8,128)(2,1)S(1)} %collective-permute-done.8.refs_2_), custom_call_target="tpu_custom_call" | custom-call | flops 163840 | bytes 655360 | tf_op jit(solution)/shard_map/pallas_call | solution.py:361
Async XLA Ops:
  1.7 8.1 %collective-permute-start.2 = (bf16[16,2432]{1,0:T(8,128)(2,1)S(1)}, bf16[16,2432]{1,0:T(8,128)(2,1)S(1)}, u32[]{:S(2)}, u32[]{:S(2)}) collective-permute-start(bf16[16,2432]{1,0:T(8,128)(2,1)S(1)} %get-tuple-element.19.block_ref), channel_id=1, source_target_pairs={{0,3},{1,2},{2,1},{3,0},{4,7},{5,6},{6,5},{7,4},{8,11},{9,10},{10,... | collective-permute-start | bytes 233480 | tf_op jit(solution)/shard_map/ppermute | solution.py:45
  4.2 5.6 %collective-permute-start.1 = (bf16[16,2432]{1,0:T(8,128)(2,1)S(1)}, bf16[16,2432]{1,0:T(8,128)(2,1)S(1)}, u32[]{:S(2)}, u32[]{:S(2)}) collective-permute-start(bf16[16,2432]{1,0:T(8,128)(2,1)S(1)} %get-tuple-element.19.block_ref), channel_id=1, source_target_pairs={{0,2},{1,3},{2,0},{3,1},{4,6},{5,7},{6,4},{7,5},{8,10},{9,11},{10,... | collective-permute-start | bytes 233480 | tf_op jit(solution)/shard_map/ppermute | solution.py:45
  4.8 5.0 %collective-permute-start = (bf16[16,2432]{1,0:T(8,128)(2,1)S(1)}, bf16[16,2432]{1,0:T(8,128)(2,1)S(1)}, u32[]{:S(2)}, u32[]{:S(2)}) collective-permute-start(bf16[16,2432]{1,0:T(8,128)(2,1)S(1)} %get-tuple-element.19.block_ref), channel_id=1, source_target_pairs={{0,1},{1,0},{2,3},{3,2},{4,5},{5,4},{6,7},{7,6},{8,9},{9,8},{10,11... | collective-permute-start | bytes 233480 | tf_op jit(solution)/shard_map/ppermute | solution.py:45
  14.1 3.1 %collective-permute-start.5 = (f32[16,128]{1,0:T(8,128)S(1)}, f32[16,128]{1,0:T(8,128)S(1)}, u32[]{:S(2)}, u32[]{:S(2)}) collective-permute-start(f32[16,128]{1,0:T(8,128)S(1)} %get-tuple-element.28.refs_0_), channel_id=1, source_target_pairs={{0,3},{1,2},{2,1},{3,0},{4,7},{5,6},{6,5},{7,4},{8,11},{9,10},{10,... | collective-permute-start | bytes 24584 | tf_op jit(solution)/shard_map/ppermute | solution.py:45
  15.6 3.7 %collective-permute-start.4 = (f32[16,128]{1,0:T(8,128)S(1)}, f32[16,128]{1,0:T(8,128)S(1)}, u32[]{:S(2)}, u32[]{:S(2)}) collective-permute-start(f32[16,128]{1,0:T(8,128)S(1)} %get-tuple-element.28.refs_0_), channel_id=1, source_target_pairs={{0,2},{1,3},{2,0},{3,1},{4,6},{5,7},{6,4},{7,5},{8,10},{9,11},{10,... | collective-permute-start | bytes 24584 | tf_op jit(solution)/shard_map/ppermute | solution.py:45
  16.2 3.0 %collective-permute-start.3 = (f32[16,128]{1,0:T(8,128)S(1)}, f32[16,128]{1,0:T(8,128)S(1)}, u32[]{:S(2)}, u32[]{:S(2)}) collective-permute-start(f32[16,128]{1,0:T(8,128)S(1)} %get-tuple-element.28.refs_0_), channel_id=1, source_target_pairs={{0,1},{1,0},{2,3},{3,2},{4,5},{5,4},{6,7},{7,6},{8,9},{9,8},{10,11... | collective-permute-start | bytes 24584 | tf_op jit(solution)/shard_map/ppermute | solution.py:45
  20.7 11.2 %collective-permute-start.6 = (bf16[64,639]{1,0:T(8,128)(2,1)S(1)}, bf16[64,639]{1,0:T(8,128)(2,1)S(1)}, u32[]{:S(2)}, u32[]{:S(2)}) collective-permute-start(bf16[64,639]{1,0:T(8,128)(2,1)S(1)} %get-tuple-element.33.done_ref), channel_id=1, source_target_pairs={{0,12},{4,8},{8,4},{12,0},{1,13},{5,9},{9,5},{13,1},{2,14},{6,10},... | collective-permute-start | bytes 245384 | tf_op jit(solution)/shard_map/ppermute | solution.py:45
  25.6 6.3 %collective-permute-start.7 = (bf16[64,619]{1,0:T(8,128)(2,1)S(1)}, bf16[64,619]{1,0:T(8,128)(2,1)S(1)}, u32[]{:S(2)}, u32[]{:S(2)}) collective-permute-start(bf16[64,619]{1,0:T(8,128)(2,1)S(1)} %shard_map.90.done_ref), channel_id=1, source_target_pairs={{0,8},{4,12},{8,0},{12,4},{1,9},{5,13},{9,1},{13,5},{2,10},{6,14},... | collective-permute-start | bytes 237704 | tf_op jit(solution)/shard_map/ppermute | solution.py:45
  27.0 4.9 %collective-permute-start.8 = (bf16[64,599]{1,0:T(8,128)(2,1)S(1)}, bf16[64,599]{1,0:T(8,128)(2,1)S(1)}, u32[]{:S(2)}, u32[]{:S(2)}) collective-permute-start(bf16[64,599]{1,0:T(8,128)(2,1)S(1)} %shard_map.91.done_ref), channel_id=1, source_target_pairs={{0,4},{4,0},{8,12},{12,8},{1,5},{5,1},{9,13},{13,9},{2,6},{6,2},{1... | collective-permute-start | bytes 230024 | tf_op jit(solution)/shard_map/ppermute | solution.py:45

commit v5 on v4

--- a/solution.py
+++ b/solution.py
@@ -3,7 +3,6 @@
 
 import jax
 import jax.numpy as jnp
-import ml_dtypes
 import numpy as np
 from jax import lax
 from jax.experimental import pallas as pl
@@ -20,25 +19,62 @@
 HALF = CYCLES * ANG
 COLS = 2 * HALF
 LANES = 128
+SUB = 8
 META = LANES
 ROT_PRIOR = 0.5
 VMEM_LIMIT = 20 * 1024 * 1024
 
 
-def phase_table():
+def phase_rows():
     angles = np.arange(ANG) * (2.0 * math.pi / ANG)
     radius = np.arange(CYCLES) + 1.0
     fx = (radius[:, None] * np.cos(angles)[None, :]).reshape(-1)
     fy = (radius[:, None] * np.sin(angles)[None, :]).reshape(-1)
-    offsets = np.arange(SHIFTW * SHIFTW)
-    dx = offsets % SHIFTW - SHIFT_R
-    dy = offsets // SHIFTW - SHIFT_R
-    phase = (2.0 * math.pi / IMG) * (dx[:, None] * fx[None, :] + dy[:, None] * fy[None, :])
-    values = np.zeros((LANES, COLS), np.float32)
-    values[: SHIFTW * SHIFTW] = np.concatenate([np.cos(phase), np.sin(phase)], axis=1)
-    high = values.astype(ml_dtypes.bfloat16)
-    low = (values - high.astype(np.float32)).astype(ml_dtypes.bfloat16)
-    return np.concatenate([high, low], axis=0)
+    offsets = np.arange(SHIFTW) - SHIFT_R
+    unit = 2.0 * math.pi / IMG
+    along_x = unit * offsets[:, None] * fx[None, :]
+    along_y = unit * offsets[:, None] * fy[None, :]
+    both = (along_x[SUB:, None, :] + along_y[None, SUB:, :]).reshape(-1, HALF)
+    values = np.zeros((48, COLS), np.float32)
+    for start, phase in ((0, along_x), (16, along_y), (32, both)):
+        values[start : start + len(phase)] = np.concatenate([np.cos(phase), np.sin(phase)], axis=1)
+    return values
+
+
+def build_table(rows_ref, table_ref):
+    width = 3 * LANES
+    for start in range(0, HALF, width):
+        real = slice(start, start + width)
+        imag = slice(HALF + start, HALF + start + width)
+
+        def product(block, row):
+            c, s = rows_ref[block : block + SUB, real], rows_ref[block : block + SUB, imag]
+            d, t = rows_ref[row : row + 1, real], rows_ref[row : row + 1, imag]
+            return c * d - s * t, s * d + c * t
+
+        blocks = [product(0, 16 + y) for y in range(SHIFTW)]
+        blocks += [product(16, x) for x in range(SUB, SHIFTW)]
+        blocks += [
+            (rows_ref[row : row + SUB, real], rows_ref[row : row + SUB, imag])
+            for row in (32, 32 + SUB)
+        ]
+        for pair in range(0, len(blocks), 2):
+            for part, columns in ((0, real), (1, imag)):
+                value = jnp.concatenate([blocks[pair][part], blocks[pair + 1][part]], axis=0)
+                high = value.astype(jnp.bfloat16)
+                low = (value - high.astype(jnp.float32)).astype(jnp.bfloat16)
+                row = pair * SUB
+                table_ref[row : row + 2 * SUB, columns] = high
+                table_ref[LANES + row : LANES + row + 2 * SUB, columns] = low
+
+
+def table_row(index):
+    y = jnp.floor((index + 0.5) * (1.0 / SHIFTW))
+    x = index - SHIFTW * y
+    near = SUB * y + x
+    side = SUB * (SHIFTW + x - SUB) + y
+    corner = SUB * (2 * SHIFTW - SUB) + (SHIFTW - SUB) * (x - SUB) + (y - SUB)
+    return jnp.where(x < SUB, near, jnp.where(y < SUB, side, corner))
 
 
 def exchange(array, axis, distance):
@@ -55,17 +91,16 @@
     lane = lane_index((classes, LANES)) % ANG
     for tile in range(COLS // LANES):
         columns = slice(tile * LANES, (tile + 1) * LANES)
-        value = class_ref[:, columns].astype(jnp.float32)
-        total = total + value * value
+        value = class_ref[:, columns]
+        wide = value.astype(jnp.float32)
+        total = total + wide * wide
         other = pltpu.roll(value, ANG, 1)
         for rotation in range(ROTS):
             offset = ANG_STEP * rotation % ANG
             turned = value
             if offset:
                 turned = pltpu.roll(jnp.where(lane < ANG - offset, value, other), offset, 1)
-            rotated_ref[rotation * classes : (rotation + 1) * classes, columns] = turned.astype(
-                jnp.bfloat16
-            )
+            rotated_ref[rotation * classes : (rotation + 1) * classes, columns] = turned
     norm_ref[...] = jnp.broadcast_to(jnp.sum(total, axis=1, keepdims=True), (classes, LANES))
 
 
@@ -95,8 +130,8 @@
 
 
 def pack_kernel(
-    particle_hbm, index_hbm, prior_hbm, group_hbm, class_hbm, scale_hbm,
-    packed_ref, class_ref, scale_ref, index_ref, prior_ref, group_ref, sems,
+    particle_hbm, index_hbm, prior_hbm, group_hbm, class_hbm, scale_hbm, rows_hbm,
+    packed_ref, class_ref, scale_ref, rows_ref, index_ref, prior_ref, group_ref, sems,
 ):
     particles, candidates = index_ref.shape
     copies = [
@@ -109,6 +144,7 @@
                 (particle_hbm, packed_ref.at[:, pl.ds(0, COLS)]),
                 (class_hbm, class_ref),
                 (scale_hbm, scale_ref),
+                (rows_hbm, rows_ref),
             ]
         )
     ]
@@ -118,7 +154,7 @@
         copy.wait()
     lane = lane_index((particles, META))
     index = jnp.concatenate(
-        [index_ref[...].astype(jnp.float32), jnp.zeros((particles, META - candidates), jnp.float32)],
+        [table_row(index_ref[...].astype(jnp.float32)), jnp.zeros((particles, META - candidates), jnp.float32)],
         axis=1,
     )
     prior = to_column(prior_ref[...].astype(jnp.float32))
@@ -201,13 +237,11 @@
 
 
 def own_kernel(
-    count, block_ref, class_ref, table_hbm, scale_ref,
-    shifted_ref, exp_ref, stats_ref, rotated_ref, norm_ref, table_ref, sem,
+    count, block_ref, class_ref, rows_ref, scale_ref,
+    shifted_ref, exp_ref, stats_ref, rotated_ref, norm_ref, table_ref,
 ):
-    copy = pltpu.make_async_copy(table_hbm, table_ref, sem)
-    copy.start()
+    build_table(rows_ref, table_ref)
     rotate_classes(class_ref, rotated_ref, norm_ref)
-    copy.wait()
     classes = norm_ref.shape[0]
     rows = exp_ref.shape[1] // count
 
@@ -268,7 +302,7 @@
     return jnp.broadcast_to(jnp.sum(mass, axis=1, keepdims=True), (classes, LANES))
 
 
-def sum_block(doms, width, distance, weight_ref, shifted_ref, mass, out_ref):
+def sum_block(doms, width, distance, weight_ref, shifted_ref, mass, received, out_ref):
     classes, extent = out_ref.shape
     padded = -(-extent // LANES) * LANES
     place = lax.axis_index("dom") ^ distance
@@ -308,6 +342,10 @@
         aligned = jnp.concatenate(
             [aligned, jnp.zeros((classes, padded - span), jnp.float32)], axis=1
         )
+    aligned = aligned[:, :padded]
+    for ref in received:
+        aligned = aligned + pad_columns(ref[...].astype(jnp.float32), padded)
+        mass = mass + received_mass(width, ref)
     mass = jnp.concatenate([mass] * (padded // LANES), axis=1)
     high = mass.astype(jnp.bfloat16).astype(jnp.float32)
     middle = (mass - high).astype(jnp.bfloat16).astype(jnp.float32)
@@ -316,8 +354,23 @@
     tail = jnp.where(
         lane == width, high, jnp.where(lane == width + 1, middle, jnp.where(lane == width + 2, low, 0.0))
     )
-    total = jnp.where(lane < width, aligned[:, :padded], tail)
+    total = jnp.where(lane < width, aligned, tail)
     out_ref[...] = total[:, :extent].astype(out_ref.dtype)
+
+
+def pad_columns(value, padded):
+    if value.shape[1] < padded:
+        added = jnp.zeros((value.shape[0], padded - value.shape[1]), value.dtype)
+        return jnp.concatenate([value, added], axis=1)
+    return value[:, :padded]
+
+
+def received_mass(width, ref):
+    base = width // LANES * LANES
+    tail = ref[:, base:].astype(jnp.float32)
+    lane = base + lane_index(tail.shape)
+    tail = jnp.where((lane >= width) & (lane < width + 3), tail, 0.0)
+    return jnp.sum(tail, axis=1, keepdims=True)
 
 
 def first_sums_kernel(count, doms, width, distance, *refs):
@@ -325,24 +378,21 @@
     exp_ref, shifted_ref, out_ref, weight_ref, mass_ref = refs[count:]
     mass = weigh(count, stats, exp_ref, weight_ref)
     mass_ref[...] = mass
-    sum_block(doms, width, distance, weight_ref, shifted_ref, mass, out_ref)
-
-
-def next_sums_kernel(doms, width, distance, weight_ref, shifted_ref, mass_ref, done_ref, out_ref):
-    sum_block(doms, width, distance, weight_ref, shifted_ref, mass_ref[...], out_ref)
+    sum_block(doms, width, distance, weight_ref, shifted_ref, mass, (), out_ref)
+
+
+def next_sums_kernel(doms, width, distance, weight_ref, shifted_ref, mass_ref, done_ref, *refs):
+    received, out_ref = refs[:-1], refs[-1]
+    sum_block(doms, width, distance, weight_ref, shifted_ref, mass_ref[...], received, out_ref)
 
 
 def final_kernel(width, own_ref, *refs):
     received, sums_ref, weights_ref = refs[:-2], refs[-2], refs[-1]
     total, mass = None, None
-    base = width // LANES * LANES
     for ref in (own_ref, *received):
         value = ref[:, :width].astype(jnp.float32)
         total = value if total is None else total + value
-        tail = ref[:, base:].astype(jnp.float32)
-        lane = base + lane_index(tail.shape)
-        tail = jnp.where((lane >= width) & (lane < width + 3), tail, 0.0)
-        tail = jnp.sum(tail, axis=1, keepdims=True)
+        tail = received_mass(width, ref)
         mass = tail if mass is None else mass + tail
     sums_ref[...] = total
     weights_ref[...] = to_lanes(mass, total.shape[0])
@@ -382,27 +432,28 @@
     f32, bf16 = jnp.float32, jnp.bfloat16
     shape = jax.ShapeDtypeStruct
 
-    packed, classes_on_chip, scales = call(
+    phases = jnp.asarray(phase_rows())
+    packed, classes_on_chip, scales, phases_on_chip = call(
         pack_kernel,
         [
             shape((particles, COLS + META), bf16),
             shape(class_spectra.shape, bf16),
             shape((1, group_scale.shape[0]), f32),
+            shape(phases.shape, f32),
         ],
         [
             pltpu.VMEM((particles, candidates), jnp.int32),
             pltpu.VMEM((1, particles), jnp.int32),
             pltpu.VMEM((1, particles), jnp.int32),
-            pltpu.SemaphoreType.DMA((6,)),
+            pltpu.SemaphoreType.DMA((7,)),
         ],
         particles * COLS,
         4 * particles * COLS,
         particle_spectra, shift_index, prior_rotation[None, :], particle_group[None, :],
-        class_spectra, group_scale[None, :],
-        hbm=(0, 1, 2, 3, 4, 5),
+        class_spectra, group_scale[None, :], phases,
+        hbm=(0, 1, 2, 3, 4, 5, 6),
     )
     others = [exchange(packed, "cls", distance) for distance in range(1, count)]
-    table = jnp.asarray(phase_table())
     stat_rows = -(-3 * count // 8) * 8
     work = 2 * rows * COLS * (ROTS * classes + 256)
     stats_shape = shape((stat_rows, LANES), f32)
@@ -416,13 +467,12 @@
             stats_shape,
             shape((ROTS * classes, COLS), bf16),
             shape((classes, LANES), f32),
-            shape(table.shape, bf16),
+            shape((2 * LANES, COLS), bf16),
         ],
-        [pltpu.SemaphoreType.DMA],
+        [],
         work,
         4 * rows * COLS,
-        packed, classes_on_chip, table, scales,
-        hbm=(2,),
+        packed, classes_on_chip, phases_on_chip, scales,
     )
     shifted, exps, stats = call(
         functools.partial(rest_kernel, count),
@@ -435,35 +485,39 @@
         chip=(count + 4, count + 5),
     )
     all_stats = [stats] + [exchange(stats, "cls", distance) for distance in range(1, count)]
-    order = list(range(doms - 1, -1, -1))
-    blocks = {}
-    work = 2 * count * rows * COLS * ROTS * classes // doms
-    blocks[order[0]], weights, mass = call(
-        functools.partial(first_sums_kernel, count, doms, width, order[0]),
+    low_bit = lambda b: b & -b if b else doms
+    order = sorted(range(doms), key=lambda b: (low_bit(b), -b))
+    extents = {b: width + 3 + (doms - 1 - place) * growth for place, b in enumerate(order)}
+    first = order[0]
+    before, weights, mass = call(
+        functools.partial(first_sums_kernel, count, doms, width, first),
         [
-            shape((classes, width + 3 + order[0] * growth), bf16),
+            shape((classes, extents[first]), bf16),
             shape((ROTS * classes, count * rows), bf16),
             shape((classes, LANES), f32),
         ],
         [],
-        work,
+        2 * count * rows * COLS * ROTS * classes // doms,
         4 * count * rows * width,
         *all_stats, exps, shifted,
         chip=(count, count + 1),
     )
-    received = []
-    for before, distance in zip(order, order[1:]):
-        received.append(exchange(blocks[before], "dom", before))
-        (blocks[distance],) = call(
-            functools.partial(next_sums_kernel, doms, width, distance),
-            [shape((classes, width + 3 + distance * growth), bf16 if distance else f32)],
+    incoming = {b: [] for b in order}
+    incoming[first ^ low_bit(first)].append(exchange(before, "dom", low_bit(first)))
+    for block in order[1:]:
+        arrived = incoming[block] if block else []
+        (before,) = call(
+            functools.partial(next_sums_kernel, doms, width, block),
+            [shape((classes, extents[block]), bf16 if block else f32)],
             [],
             1024,
             1024,
-            weights, shifted, mass, blocks[before],
+            weights, shifted, mass, before, *arrived,
             chip=(1,),
         )
-    own = blocks[0]
+        if block:
+            incoming[block ^ low_bit(block)].append(exchange(before, "dom", low_bit(block)))
+    own, received = before, incoming[0]
     class_sums, class_weights = call(
         functools.partial(final_kernel, width),
         [shape((classes, width), f32), shape((1, classes), f32)],

time: 32.9 us -> 32.4 us (0.985)
  Pallas kernels: 16.3 us -> 14 us
  waiting for transfers between devices: 5.85 us -> 7.56 us
    pallas_call x8, Pallas kernels: 16.3 us -> 14 us  [call(): pl.pallas_call(kernel, out_shape=[pltpu.VMEM(s.shape, s.dtype) if pinned...]
    ppermute x9, waiting for transfers between devices: 5.85 us -> 7.56 us  [exchange(): lax.ppermute(array, axis, [(i, i ^ distance) for i in range(lax.axis_size...]
  transfers between devices with their start and end apart: 9 -> 9, of which waited for: 3 -> 5; matrix products, arithmetic and copies ran while one was open for 0% -> 0% of each run, Pallas kernels for 27% -> 20%
where the time goes in v5:
time: 32.4 us; the launch traced here: 32.2 us
  Pallas kernels  14 us (43%)
  starting transfers between devices  9.98 us (31%)
  waiting for transfers between devices  7.56 us (23%)
  between operations  0.68 us (2%)
    pallas_call x8, Pallas kernels, call(): pl.pallas_call(kernel, out_shape=[pltpu.VMEM(s.shape, s.dtype) if pinned...  14 us
    ppermute x9, starting transfers between devices, exchange(): lax.ppermute(array, axis, [(i, i ^ distance) for i in range(lax.axis_size...  9.98 us
    ppermute x9, waiting for transfers between devices, exchange(): lax.ppermute(array, axis, [(i, i ^ distance) for i in range(lax.axis_size...  7.56 us
  transfers between devices with their start and end apart: 9, of which 5 were waited for; matrix products, arithmetic and copies ran while one was open for 0% of the time, Pallas kernels for 20%

profile of v5, /device:TPU:0, one launch (start us, length us, event | category | flops | bytes accessed | tf_op | source)
XLA Modules:
  0.0 32.2 jit_solution(173118605461377845)
XLA Ops:
  0.6 1.3 %shard_map.86 = (bf16[16,2432]{1,0:T(8,128)(2,1)S(1)}, bf16[64,2304]{1,0:T(8,128)(2,1)S(1)}, f32[1,64]{1,0:T(1,128)S(1)}, f32[48,2304]{1,0:T(8,128)S(1)}) custom-call(bf16[16,2304]{1,0:T(8,128)(2,1)} %particle_hbm.1, s32[16,16]{1,0:T(8,128)} %index_hbm.1, s32[1,16]{1,0:T(1,128)} %bitcast.4, s32[1,16]{1,0:T(1,128)} %bitcast.5, bf16[64,2304]{1,0:T(8,128)(2,1)} %class_hbm.1, ...), custom_call_target="tpu_custom_call" | custom-call | flops 36864 | bytes 147456 | tf_op jit(solution)/shard_map/pallas_call | solution.py:411
  1.9 2.4 %collective-permute-start.2 = (bf16[16,2432]{1,0:T(8,128)(2,1)S(1)}, bf16[16,2432]{1,0:T(8,128)(2,1)S(1)}, u32[]{:S(2)}, u32[]{:S(2)}) collective-permute-start(bf16[16,2432]{1,0:T(8,128)(2,1)S(1)} %get-tuple-element.20.block_ref), channel_id=1, source_target_pairs={{0,3},{1,2},{2,1},{3,0},{4,7},{5,6},{6,5},{7,4},{8,11},{9,10},{10,... | collective-permute-start | bytes 233480 | tf_op jit(solution)/shard_map/ppermute | solution.py:81
  4.3 0.6 %collective-permute-start.1 = (bf16[16,2432]{1,0:T(8,128)(2,1)S(1)}, bf16[16,2432]{1,0:T(8,128)(2,1)S(1)}, u32[]{:S(2)}, u32[]{:S(2)}) collective-permute-start(bf16[16,2432]{1,0:T(8,128)(2,1)S(1)} %get-tuple-element.20.block_ref), channel_id=1, source_target_pairs={{0,2},{1,3},{2,0},{3,1},{4,6},{5,7},{6,4},{7,5},{8,10},{9,11},{10,... | collective-permute-start | bytes 233480 | tf_op jit(solution)/shard_map/ppermute | solution.py:81
  5.0 0.0 collective-permute-start
  5.0 2.5 %shard_map.87 = (bf16[1024,2304]{1,0:T(8,128)(2,1)S(1)}, f32[512,1024]{1,0:T(8,128)S(1)}, f32[16,128]{1,0:T(8,128)S(1)}, bf16[512,2304]{1,0:T(8,128)(2,1)S(1)}, ...) custom-call(bf16[16,2432]{1,0:T(8,128)(2,1)S(1)} %get-tuple-element.20.block_ref, ...), custom_call_target="tpu_custom_call" | custom-call | flops 905969664 | bytes 2359296 | tf_op jit(solution)/shard_map/pallas_call | solution.py:411
  7.5 0.0 collective-permute-done.2.refs_2_
  7.5 1.8 %collective-permute-done.1.refs_1_ = bf16[16,2432]{1,0:T(8,128)(2,1)S(1)} collective-permute-done((bf16[16,2432]{1,0:T(8,128)(2,1)S(1)}, bf16[16,2432]{1,0:T(8,128)(2,1)S(1)}, u32[]{:S(2)}, u32[]{:S(2)}) %collective-permute-start.1) | collective-permute-done | bytes 77856 | tf_op jit(solution)/shard_map/ppermute | solution.py:81
  9.3 0.0 collective-permute-done.refs_0_
  9.3 4.3 %shard_map.88 = (bf16[1024,2304]{1,0:T(8,128)(2,1)S(1)}, f32[512,1024]{1,0:T(8,128)S(1)}, f32[16,128]{1,0:T(8,128)S(1)}) custom-call(bf16[16,2432]{1,0:T(8,128)(2,1)S(1)} %collective-permute-done.refs_0_, bf16[16,2432]{1,0:T(8,128)(2,1)S(1)} %collective-permute-done.1.refs_1_, ...), custom_call_target="tpu_custom_call", output_to_operand_aliasing={{0}: (8, {}), {1}: (9, {})} | custom-call | flops 2717908992 | bytes 7077888 | tf_op jit(solution)/shard_map/pallas_call | solution.py:411
  13.5 1.7 %collective-permute-start.5 = (f32[16,128]{1,0:T(8,128)S(1)}, f32[16,128]{1,0:T(8,128)S(1)}, u32[]{:S(2)}, u32[]{:S(2)}) collective-permute-start(f32[16,128]{1,0:T(8,128)S(1)} %get-tuple-element.30.refs_0_), channel_id=1, source_target_pairs={{0,3},{1,2},{2,1},{3,0},{4,7},{5,6},{6,5},{7,4},{8,11},{9,10},{10,... | collective-permute-start | bytes 24584 | tf_op jit(solution)/shard_map/ppermute | solution.py:81
  15.2 0.3 %collective-permute-start.4 = (f32[16,128]{1,0:T(8,128)S(1)}, f32[16,128]{1,0:T(8,128)S(1)}, u32[]{:S(2)}, u32[]{:S(2)}) collective-permute-start(f32[16,128]{1,0:T(8,128)S(1)} %get-tuple-element.30.refs_0_), channel_id=1, source_target_pairs={{0,2},{1,3},{2,0},{3,1},{4,6},{5,7},{6,4},{7,5},{8,10},{9,11},{10,... | collective-permute-start | bytes 24584 | tf_op jit(solution)/shard_map/ppermute | solution.py:81
  15.5 0.1 collective-permute-start.3
  15.6 1.0 %collective-permute-done.5.refs_3_ = f32[16,128]{1,0:T(8,128)S(1)} collective-permute-done((f32[16,128]{1,0:T(8,128)S(1)}, f32[16,128]{1,0:T(8,128)S(1)}, u32[]{:S(2)}, u32[]{:S(2)}) %collective-permute-start.5) | collective-permute-done | bytes 8224 | tf_op jit(solution)/shard_map/ppermute | solution.py:81
  16.6 2.2 %collective-permute-done.4.refs_2_ = f32[16,128]{1,0:T(8,128)S(1)} collective-permute-done((f32[16,128]{1,0:T(8,128)S(1)}, f32[16,128]{1,0:T(8,128)S(1)}, u32[]{:S(2)}, u32[]{:S(2)}) %collective-permute-start.4) | collective-permute-done | bytes 8224 | tf_op jit(solution)/shard_map/ppermute | solution.py:81
  18.9 0.0 collective-permute-done.3.refs_1_
  18.9 1.5 %shard_map.89 = (bf16[64,639]{1,0:T(8,128)(2,1)S(1)}, bf16[512,1024]{1,0:T(8,128)(2,1)S(1)}, f32[64,128]{1,0:T(8,128)S(1)}) custom-call(f32[16,128]{1,0:T(8,128)S(1)} %get-tuple-element.30.refs_0_, f32[16,128]{1,0:T(8,128)S(1)} %collective-permute-done.3.refs_1_, f32[16,128]{1,0:T(8,128)S(1)} %collective-permute-done.4.refs_2_, ...), custom_call_target="tpu_custom_call" | custom-call | flops 603979776 | bytes 2359296 | tf_op jit(solution)/shard_map/pallas_call | solution.py:411
  20.3 1.6 %collective-permute-start.6 = (bf16[64,639]{1,0:T(8,128)(2,1)S(1)}, bf16[64,639]{1,0:T(8,128)(2,1)S(1)}, u32[]{:S(2)}, u32[]{:S(2)}) collective-permute-start(bf16[64,639]{1,0:T(8,128)(2,1)S(1)} %get-tuple-element.35.done_ref), channel_id=1, source_target_pairs={{0,4},{4,0},{8,12},{12,8},{1,5},{5,1},{9,13},{13,9},{2,6},{6,2},{1... | collective-permute-start | bytes 245384 | tf_op jit(solution)/shard_map/ppermute | solution.py:81
  22.0 1.3 %shard_map.90.done_ref = bf16[64,619]{1,0:T(8,128)(2,1)S(1)} custom-call(bf16[512,1024]{1,0:T(8,128)(2,1)S(1)} %get-tuple-element.33.weight_ref, bf16[1024,2304]{1,0:T(8,128)(2,1)S(1)} %get-tuple-element.32.refs_5_.shifted_ref, f32[64,128]{1,0:T(8,128)S(1)} %get-tuple-element.34.mass_ref, bf16[64,639]{1,0:T(8,128)(2,1)S(1)} %get-tuple-element.35.done_ref), custom_call_target="tpu_custom_call" | custom-call | flops 1024 | bytes 1024 | tf_op jit(solution)/shard_map/pallas_call | solution.py:411
  23.2 0.5 %collective-permute-start.7 = (bf16[64,619]{1,0:T(8,128)(2,1)S(1)}, bf16[64,619]{1,0:T(8,128)(2,1)S(1)}, u32[]{:S(2)}, u32[]{:S(2)}) collective-permute-start(bf16[64,619]{1,0:T(8,128)(2,1)S(1)} %shard_map.90.done_ref), channel_id=1, source_target_pairs={{0,4},{4,0},{8,12},{12,8},{1,5},{5,1},{9,13},{13,9},{2,6},{6,2},{1... | collective-permute-start | bytes 237704 | tf_op jit(solution)/shard_map/ppermute | solution.py:81
  23.8 1.1 %collective-permute-done.6.refs_0_ = bf16[64,639]{1,0:T(8,128)(2,1)S(1)} collective-permute-done((bf16[64,639]{1,0:T(8,128)(2,1)S(1)}, bf16[64,639]{1,0:T(8,128)(2,1)S(1)}, u32[]{:S(2)}, u32[]{:S(2)}) %collective-permute-start.6) | collective-permute-done | bytes 81824 | tf_op jit(solution)/shard_map/ppermute | solution.py:81
  24.9 1.3 %shard_map.91.done_ref = bf16[64,599]{1,0:T(8,128)(2,1)S(1)} custom-call(bf16[512,1024]{1,0:T(8,128)(2,1)S(1)} %get-tuple-element.33.weight_ref, bf16[1024,2304]{1,0:T(8,128)(2,1)S(1)} %get-tuple-element.32.refs_5_.shifted_ref, f32[64,128]{1,0:T(8,128)S(1)} %get-tuple-element.34.mass_ref, bf16[64,619]{1,0:T(8,128)(2,1)S(1)} %shard_map.90.done_ref, ...), custom_call_target="tpu_custom_call" | custom-call | flops 1024 | bytes 1024 | tf_op jit(solution)/shard_map/pallas_call | solution.py:411
  26.1 2.6 %collective-permute-start.8 = (bf16[64,599]{1,0:T(8,128)(2,1)S(1)}, bf16[64,599]{1,0:T(8,128)(2,1)S(1)}, u32[]{:S(2)}, u32[]{:S(2)}) collective-permute-start(bf16[64,599]{1,0:T(8,128)(2,1)S(1)} %shard_map.91.done_ref), channel_id=1, source_target_pairs={{0,8},{4,12},{8,0},{12,4},{1,9},{5,13},{9,1},{13,5},{2,10},{6,14},... | collective-permute-start | bytes 230024 | tf_op jit(solution)/shard_map/ppermute | solution.py:81
  28.8 1.3 %shard_map.92.own_ref = f32[64,579]{1,0:T(8,128)S(1)} custom-call(bf16[512,1024]{1,0:T(8,128)(2,1)S(1)} %get-tuple-element.33.weight_ref, bf16[1024,2304]{1,0:T(8,128)(2,1)S(1)} %get-tuple-element.32.refs_5_.shifted_ref, f32[64,128]{1,0:T(8,128)S(1)} %get-tuple-element.34.mass_ref, bf16[64,599]{1,0:T(8,128)(2,1)S(1)} %shard_map.91.done_ref), custom_call_target="tpu_custom_call" | custom-call | flops 1024 | bytes 1024 | tf_op jit(solution)/shard_map/pallas_call | solution.py:411
  30.0 0.0 collective-permute-done.7.refs_0_
  30.1 1.5 %collective-permute-done.8.refs_1_ = bf16[64,599]{1,0:T(8,128)(2,1)S(1)} collective-permute-done((bf16[64,599]{1,0:T(8,128)(2,1)S(1)}, bf16[64,599]{1,0:T(8,128)(2,1)S(1)}, u32[]{:S(2)}, u32[]{:S(2)}) %collective-permute-start.8) | collective-permute-done | bytes 76704 | tf_op jit(solution)/shard_map/ppermute | solution.py:81
  31.5 0.7 %shard_map.93 = (f32[64,576]{1,0:T(8,128)}, f32[1,64]{1,0:T(1,128)}) custom-call(f32[64,579]{1,0:T(8,128)S(1)} %shard_map.92.own_ref, bf16[64,619]{1,0:T(8,128)(2,1)S(1)} %collective-permute-done.7.refs_0_, bf16[64,599]{1,0:T(8,128)(2,1)S(1)} %collective-permute-done.8.refs_1_), custom_call_target="tpu_custom_call" | custom-call | flops 163840 | bytes 655360 | tf_op jit(solution)/shard_map/pallas_call | solution.py:411
Async XLA Ops:
  1.9 5.6 %collective-permute-start.2 = (bf16[16,2432]{1,0:T(8,128)(2,1)S(1)}, bf16[16,2432]{1,0:T(8,128)(2,1)S(1)}, u32[]{:S(2)}, u32[]{:S(2)}) collective-permute-start(bf16[16,2432]{1,0:T(8,128)(2,1)S(1)} %get-tuple-element.20.block_ref), channel_id=1, source_target_pairs={{0,3},{1,2},{2,1},{3,0},{4,7},{5,6},{6,5},{7,4},{8,11},{9,10},{10,... | collective-permute-start | bytes 233480 | tf_op jit(solution)/shard_map/ppermute | solution.py:81
  4.3 4.9 %collective-permute-start.1 = (bf16[16,2432]{1,0:T(8,128)(2,1)S(1)}, bf16[16,2432]{1,0:T(8,128)(2,1)S(1)}, u32[]{:S(2)}, u32[]{:S(2)}) collective-permute-start(bf16[16,2432]{1,0:T(8,128)(2,1)S(1)} %get-tuple-element.20.block_ref), channel_id=1, source_target_pairs={{0,2},{1,3},{2,0},{3,1},{4,6},{5,7},{6,4},{7,5},{8,10},{9,11},{10,... | collective-permute-start | bytes 233480 | tf_op jit(solution)/shard_map/ppermute | solution.py:81
  5.0 4.3 %collective-permute-start = (bf16[16,2432]{1,0:T(8,128)(2,1)S(1)}, bf16[16,2432]{1,0:T(8,128)(2,1)S(1)}, u32[]{:S(2)}, u32[]{:S(2)}) collective-permute-start(bf16[16,2432]{1,0:T(8,128)(2,1)S(1)} %get-tuple-element.20.block_ref), channel_id=1, source_target_pairs={{0,1},{1,0},{2,3},{3,2},{4,5},{5,4},{6,7},{7,6},{8,9},{9,8},{10,11... | collective-permute-start | bytes 233480 | tf_op jit(solution)/shard_map/ppermute | solution.py:81
  13.5 3.1 %collective-permute-start.5 = (f32[16,128]{1,0:T(8,128)S(1)}, f32[16,128]{1,0:T(8,128)S(1)}, u32[]{:S(2)}, u32[]{:S(2)}) collective-permute-start(f32[16,128]{1,0:T(8,128)S(1)} %get-tuple-element.30.refs_0_), channel_id=1, source_target_pairs={{0,3},{1,2},{2,1},{3,0},{4,7},{5,6},{6,5},{7,4},{8,11},{9,10},{10,... | collective-permute-start | bytes 24584 | tf_op jit(solution)/shard_map/ppermute | solution.py:81
  15.2 3.7 %collective-permute-start.4 = (f32[16,128]{1,0:T(8,128)S(1)}, f32[16,128]{1,0:T(8,128)S(1)}, u32[]{:S(2)}, u32[]{:S(2)}) collective-permute-start(f32[16,128]{1,0:T(8,128)S(1)} %get-tuple-element.30.refs_0_), channel_id=1, source_target_pairs={{0,2},{1,3},{2,0},{3,1},{4,6},{5,7},{6,4},{7,5},{8,10},{9,11},{10,... | collective-permute-start | bytes 24584 | tf_op jit(solution)/shard_map/ppermute | solution.py:81
  15.5 3.3 %collective-permute-start.3 = (f32[16,128]{1,0:T(8,128)S(1)}, f32[16,128]{1,0:T(8,128)S(1)}, u32[]{:S(2)}, u32[]{:S(2)}) collective-permute-start(f32[16,128]{1,0:T(8,128)S(1)} %get-tuple-element.30.refs_0_), channel_id=1, source_target_pairs={{0,1},{1,0},{2,3},{3,2},{4,5},{5,4},{6,7},{7,6},{8,9},{9,8},{10,11... | collective-permute-start | bytes 24584 | tf_op jit(solution)/shard_map/ppermute | solution.py:81
  20.3 4.5 %collective-permute-start.6 = (bf16[64,639]{1,0:T(8,128)(2,1)S(1)}, bf16[64,639]{1,0:T(8,128)(2,1)S(1)}, u32[]{:S(2)}, u32[]{:S(2)}) collective-permute-start(bf16[64,639]{1,0:T(8,128)(2,1)S(1)} %get-tuple-element.35.done_ref), channel_id=1, source_target_pairs={{0,4},{4,0},{8,12},{12,8},{1,5},{5,1},{9,13},{13,9},{2,6},{6,2},{1... | collective-permute-start | bytes 245384 | tf_op jit(solution)/shard_map/ppermute | solution.py:81
  23.2 6.8 %collective-permute-start.7 = (bf16[64,619]{1,0:T(8,128)(2,1)S(1)}, bf16[64,619]{1,0:T(8,128)(2,1)S(1)}, u32[]{:S(2)}, u32[]{:S(2)}) collective-permute-start(bf16[64,619]{1,0:T(8,128)(2,1)S(1)} %shard_map.90.done_ref), channel_id=1, source_target_pairs={{0,4},{4,0},{8,12},{12,8},{1,5},{5,1},{9,13},{13,9},{2,6},{6,2},{1... | collective-permute-start | bytes 237704 | tf_op jit(solution)/shard_map/ppermute | solution.py:81
  26.1 5.4 %collective-permute-start.8 = (bf16[64,599]{1,0:T(8,128)(2,1)S(1)}, bf16[64,599]{1,0:T(8,128)(2,1)S(1)}, u32[]{:S(2)}, u32[]{:S(2)}) collective-permute-start(bf16[64,599]{1,0:T(8,128)(2,1)S(1)} %shard_map.91.done_ref), channel_id=1, source_target_pairs={{0,8},{4,12},{8,0},{12,4},{1,9},{5,13},{9,1},{13,5},{2,10},{6,14},... | collective-permute-start | bytes 230024 | tf_op jit(solution)/shard_map/ppermute | solution.py:81

commit v6 on v5

--- a/solution.py
+++ b/solution.py
@@ -257,21 +257,21 @@
     stats_ref[2 * count : 2 * count + 1, :] = scale
 
 
-def rest_kernel(count, *refs):
-    blocks = refs[: count - 1]
-    table_ref, scale_ref, rotated_ref, norm_ref, own_ref = refs[count - 1 : count + 4]
-    shifted_ref, exp_ref, stats_ref = refs[count + 6 :]
+def rest_kernel(count, chunks, *refs):
+    blocks, refs = refs[: len(chunks)], refs[len(chunks) :]
+    table_ref, scale_ref, rotated_ref, norm_ref, own_ref = refs[:5]
+    shifted_ref, exp_ref, stats_ref = refs[7:]
     classes = norm_ref.shape[0]
     rows = exp_ref.shape[1] // count
     stats_ref[...] = own_ref[...]
-    for block in range(1, count):
+    for block, block_ref in zip(chunks, blocks):
         part = slice(block * rows, (block + 1) * rows)
 
         def out(rotation, value):
             exp_ref[rotation * classes : (rotation + 1) * classes, part] = value
 
         highest, total, scale = score_block(
-            blocks[block - 1], table_ref, scale_ref, rotated_ref, norm_ref,
+            block_ref, table_ref, scale_ref, rotated_ref, norm_ref,
             shifted_ref.at[part, :], out,
         )
         stats_ref[2 * block : 2 * block + 1, :] = highest
@@ -302,9 +302,9 @@
     return jnp.broadcast_to(jnp.sum(mass, axis=1, keepdims=True), (classes, LANES))
 
 
-def sum_block(doms, width, distance, weight_ref, shifted_ref, mass, received, out_ref):
-    classes, extent = out_ref.shape
-    padded = -(-extent // LANES) * LANES
+def block_sums(doms, width, distance, weight_ref, shifted_ref):
+    classes = weight_ref.shape[0] // ROTS
+    padded = -(-(width + 3) // LANES) * LANES
     place = lax.axis_index("dom") ^ distance
     first = place * width
     shifts = sorted({width * dom % LANES for dom in range(doms)})
@@ -342,20 +342,19 @@
         aligned = jnp.concatenate(
             [aligned, jnp.zeros((classes, padded - span), jnp.float32)], axis=1
         )
-    aligned = aligned[:, :padded]
-    for ref in received:
-        aligned = aligned + pad_columns(ref[...].astype(jnp.float32), padded)
-        mass = mass + received_mass(width, ref)
-    mass = jnp.concatenate([mass] * (padded // LANES), axis=1)
+    return aligned[:, :padded]
+
+
+def store_block(width, value, mass, out_ref):
     high = mass.astype(jnp.bfloat16).astype(jnp.float32)
     middle = (mass - high).astype(jnp.bfloat16).astype(jnp.float32)
     low = (mass - high - middle).astype(jnp.bfloat16).astype(jnp.float32)
-    lane = lane_index((classes, padded))
+    lane = lane_index(value.shape)
     tail = jnp.where(
         lane == width, high, jnp.where(lane == width + 1, middle, jnp.where(lane == width + 2, low, 0.0))
     )
-    total = jnp.where(lane < width, aligned, tail)
-    out_ref[...] = total[:, :extent].astype(out_ref.dtype)
+    value = jnp.where(lane < width, value, tail)
+    out_ref[...] = value[:, : out_ref.shape[1]].astype(out_ref.dtype)
 
 
 def pad_columns(value, padded):
@@ -373,17 +372,32 @@
     return jnp.sum(tail, axis=1, keepdims=True)
 
 
-def first_sums_kernel(count, doms, width, distance, *refs):
+def first_sums_kernel(count, doms, width, blocks, *refs):
     stats = refs[:count]
-    exp_ref, shifted_ref, out_ref, weight_ref, mass_ref = refs[count:]
+    exp_ref, shifted_ref = refs[count : count + 2]
+    weight_ref, mass_ref = refs[count + 2 : count + 4]
     mass = weigh(count, stats, exp_ref, weight_ref)
     mass_ref[...] = mass
-    sum_block(doms, width, distance, weight_ref, shifted_ref, mass, (), out_ref)
-
-
-def next_sums_kernel(doms, width, distance, weight_ref, shifted_ref, mass_ref, done_ref, *refs):
-    received, out_ref = refs[:-1], refs[-1]
-    sum_block(doms, width, distance, weight_ref, shifted_ref, mass_ref[...], received, out_ref)
+    for block, out_ref in zip(blocks, refs[count + 4 :]):
+        store_block(width, block_sums(doms, width, block, weight_ref, shifted_ref), mass[:, :1], out_ref)
+
+
+def rest_sums_kernel(doms, width, blocks, weight_ref, shifted_ref, mass_ref, *refs):
+    for block, out_ref in zip(blocks, refs[-len(blocks) :]):
+        value = block_sums(doms, width, block, weight_ref, shifted_ref)
+        store_block(width, value, mass_ref[:, :1], out_ref)
+
+
+def add_kernel(width, *refs):
+    out_ref = refs[-1]
+    padded = -(-out_ref.shape[1] // LANES) * LANES
+    total, mass = None, None
+    for ref in refs[:-1]:
+        value = pad_columns(ref[...].astype(jnp.float32), padded)
+        total = value if total is None else total + value
+        tail = received_mass(width, ref)
+        mass = tail if mass is None else mass + tail
+    store_block(width, total, mass, out_ref)
 
 
 def final_kernel(width, own_ref, *refs):
@@ -474,50 +488,62 @@
         4 * rows * COLS,
         packed, classes_on_chip, phases_on_chip, scales,
     )
-    shifted, exps, stats = call(
-        functools.partial(rest_kernel, count),
-        [shifted_shape, exp_shape, stats_shape],
-        [],
-        work * (count - 1),
-        4 * (count - 1) * rows * COLS,
-        *others, table_on_chip, scales, rotated, norm, stats_own, shifted, exps,
-        aliases={count + 4: 0, count + 5: 1},
-        chip=(count + 4, count + 5),
-    )
+    stats = stats_own
+    for chunks in ([1], list(range(2, count))):
+        shifted, exps, stats = call(
+            functools.partial(rest_kernel, count, chunks),
+            [shifted_shape, exp_shape, stats_shape],
+            [],
+            work * len(chunks),
+            4 * len(chunks) * rows * COLS,
+            *[others[b - 1] for b in chunks],
+            table_on_chip, scales, rotated, norm, stats, shifted, exps,
+            aliases={len(chunks) + 5: 0, len(chunks) + 6: 1},
+            chip=(len(chunks) + 5, len(chunks) + 6),
+        )
     all_stats = [stats] + [exchange(stats, "cls", distance) for distance in range(1, count)]
-    low_bit = lambda b: b & -b if b else doms
-    order = sorted(range(doms), key=lambda b: (low_bit(b), -b))
+    low_bit = lambda b: b & -b
+    early = list(range(doms - 1, 1, -2))
+    order = early + sorted(range(2, doms, 2), key=lambda b: (low_bit(b), -b)) + [1]
     extents = {b: width + 3 + (doms - 1 - place) * growth for place, b in enumerate(order)}
-    first = order[0]
-    before, weights, mass = call(
-        functools.partial(first_sums_kernel, count, doms, width, first),
-        [
-            shape((classes, extents[first]), bf16),
-            shape((ROTS * classes, count * rows), bf16),
-            shape((classes, LANES), f32),
-        ],
+    late = [1] + list(range(0, doms, 2))
+    weights, mass, *made = call(
+        functools.partial(first_sums_kernel, count, doms, width, early),
+        [shape((ROTS * classes, count * rows), bf16), shape((classes, LANES), f32)]
+        + [shape((classes, extents[b]), bf16) for b in early],
         [],
         2 * count * rows * COLS * ROTS * classes // doms,
         4 * count * rows * width,
         *all_stats, exps, shifted,
         chip=(count, count + 1),
     )
-    incoming = {b: [] for b in order}
-    incoming[first ^ low_bit(first)].append(exchange(before, "dom", low_bit(first)))
-    for block in order[1:]:
-        arrived = incoming[block] if block else []
-        (before,) = call(
-            functools.partial(next_sums_kernel, doms, width, block),
-            [shape((classes, extents[block]), bf16 if block else f32)],
+    incoming = {b: [] for b in range(doms)}
+    for b, block in zip(early, made):
+        incoming[b ^ 1].append(exchange(block, "dom", 1))
+    rest = call(
+        functools.partial(rest_sums_kernel, doms, width, late),
+        [
+            shape((classes, extents.get(b, width + 3)), bf16 if b == 1 else f32) for b in late
+        ],
+        [],
+        1024,
+        1024,
+        weights, shifted, mass, *made,
+        chip=(1,),
+    )
+    blocks = dict(zip(late, rest))
+    for b in order[len(early) : -1]:
+        (block,) = call(
+            functools.partial(add_kernel, width),
+            [shape((classes, extents[b]), bf16)],
             [],
             1024,
             1024,
-            weights, shifted, mass, before, *arrived,
-            chip=(1,),
-        )
-        if block:
-            incoming[block ^ low_bit(block)].append(exchange(before, "dom", low_bit(block)))
-    own, received = before, incoming[0]
+            blocks[b], *incoming[b],
+        )
+        incoming[b ^ low_bit(b)].append(exchange(block, "dom", low_bit(b)))
+    incoming[0].append(exchange(blocks[1], "dom", 1))
+    own, received = blocks[0], incoming[0]
     class_sums, class_weights = call(
         functools.partial(final_kernel, width),
         [shape((classes, width), f32), shape((1, classes), f32)],

time: 32.4 us -> 32.7 us (level)
  starting transfers between devices: 9.98 us -> 11 us
  waiting for transfers between devices: 7.56 us -> 6.74 us
    ppermute x9, starting transfers between devices: 9.98 us -> 11 us  [exchange(): lax.ppermute(array, axis, [(i, i ^ distance) for i in range(lax.axis_size...]
    ppermute x9, waiting for transfers between devices: 7.56 us -> 6.74 us  [exchange(): lax.ppermute(array, axis, [(i, i ^ distance) for i in range(lax.axis_size...]
  transfers between devices with their start and end apart: 9 -> 9, of which waited for: 5 -> 3; matrix products, arithmetic and copies ran while one was open for 0% -> 0% of each run, Pallas kernels for 20% -> 23%
where the time goes in v6:
time: 32.7 us; the launch traced here: 32.5 us
  Pallas kernels  14.1 us (43%)
  starting transfers between devices  11 us (34%)
  waiting for transfers between devices  6.74 us (21%)
  between operations  0.68 us (2%)
    pallas_call x8, Pallas kernels, call(): pl.pallas_call(kernel, out_shape=[pltpu.VMEM(s.shape, s.dtype) if pinned...  14.1 us
    ppermute x9, starting transfers between devices, exchange(): lax.ppermute(array, axis, [(i, i ^ distance) for i in range(lax.axis_size...  11 us
    ppermute x9, waiting for transfers between devices, exchange(): lax.ppermute(array, axis, [(i, i ^ distance) for i in range(lax.axis_size...  6.74 us
  transfers between devices with their start and end apart: 9, of which 3 were waited for; matrix products, arithmetic and copies ran while one was open for 0% of the time, Pallas kernels for 23%

profile of v6, /device:TPU:0, one launch (start us, length us, event | category | flops | bytes accessed | tf_op | source)
XLA Modules:
  0.0 32.5 jit_solution(10955750144052549923)
XLA Ops:
  0.6 1.3 %shard_map.86 = (bf16[16,2432]{1,0:T(8,128)(2,1)S(1)}, bf16[64,2304]{1,0:T(8,128)(2,1)S(1)}, f32[1,64]{1,0:T(1,128)S(1)}, f32[48,2304]{1,0:T(8,128)S(1)}) custom-call(bf16[16,2304]{1,0:T(8,128)(2,1)} %particle_hbm.1, s32[16,16]{1,0:T(8,128)} %index_hbm.1, s32[1,16]{1,0:T(1,128)} %bitcast.4, s32[1,16]{1,0:T(1,128)} %bitcast.5, bf16[64,2304]{1,0:T(8,128)(2,1)} %class_hbm.1, ...), custom_call_target="tpu_custom_call" | custom-call | flops 36864 | bytes 147456 | tf_op jit(solution)/shard_map/pallas_call | solution.py:425
  1.9 0.5 %collective-permute-start.2 = (bf16[16,2432]{1,0:T(8,128)(2,1)S(1)}, bf16[16,2432]{1,0:T(8,128)(2,1)S(1)}, u32[]{:S(2)}, u32[]{:S(2)}) collective-permute-start(bf16[16,2432]{1,0:T(8,128)(2,1)S(1)} %get-tuple-element.26.block_ref), channel_id=1, source_target_pairs={{0,1},{1,0},{2,3},{3,2},{4,5},{5,4},{6,7},{7,6},{8,9},{9,8},{10,11... | collective-permute-start | bytes 233480 | tf_op jit(solution)/shard_map/ppermute | solution.py:81
  2.4 2.6 %collective-permute-start = (bf16[16,2432]{1,0:T(8,128)(2,1)S(1)}, bf16[16,2432]{1,0:T(8,128)(2,1)S(1)}, u32[]{:S(2)}, u32[]{:S(2)}) collective-permute-start(bf16[16,2432]{1,0:T(8,128)(2,1)S(1)} %get-tuple-element.26.block_ref), channel_id=1, source_target_pairs={{0,2},{1,3},{2,0},{3,1},{4,6},{5,7},{6,4},{7,5},{8,10},{9,11},{10,... | collective-permute-start | bytes 233480 | tf_op jit(solution)/shard_map/ppermute | solution.py:81
  5.0 0.1 collective-permute-start.1
  5.1 2.5 %shard_map.87 = (bf16[1024,2304]{1,0:T(8,128)(2,1)S(1)}, f32[512,1024]{1,0:T(8,128)S(1)}, f32[16,128]{1,0:T(8,128)S(1)}, bf16[512,2304]{1,0:T(8,128)(2,1)S(1)}, ...) custom-call(bf16[16,2432]{1,0:T(8,128)(2,1)S(1)} %get-tuple-element.26.block_ref, ...), custom_call_target="tpu_custom_call" | custom-call | flops 905969664 | bytes 2359296 | tf_op jit(solution)/shard_map/pallas_call | solution.py:425
  7.6 0.0 collective-permute-done.2.refs_0_
  7.6 2.0 %shard_map.88 = (bf16[1024,2304]{1,0:T(8,128)(2,1)S(1)}, f32[512,1024]{1,0:T(8,128)S(1)}, f32[16,128]{1,0:T(8,128)S(1)}) custom-call(bf16[16,2432]{1,0:T(8,128)(2,1)S(1)} %collective-permute-done.2.refs_0_, bf16[256,2304]{1,0:T(8,128)(2,1)S(1)} %get-tuple-element.30.refs_1_.refs_2_, ...), custom_call_target="tpu_custom_call", output_to_operand_aliasing={{0}: (6, {}), {1}: (7, {})} | custom-call | flops 905969664 | bytes 2359296 | tf_op jit(solution)/shard_map/pallas_call | solution.py:425
  9.6 0.0 collective-permute-done.refs_0_
  9.6 0.0 collective-permute-done.1.refs_1_
  9.6 3.0 %shard_map.89 = (bf16[1024,2304]{1,0:T(8,128)(2,1)S(1)}, f32[512,1024]{1,0:T(8,128)S(1)}, f32[16,128]{1,0:T(8,128)S(1)}) custom-call(bf16[16,2432]{1,0:T(8,128)(2,1)S(1)} %collective-permute-done.refs_0_, bf16[16,2432]{1,0:T(8,128)(2,1)S(1)} %collective-permute-done.1.refs_1_, ...), custom_call_target="tpu_custom_call", output_to_operand_aliasing={{0}: (7, {}), {1}: (8, {})} | custom-call | flops 1811939328 | bytes 4718592 | tf_op jit(solution)/shard_map/pallas_call | solution.py:425
  12.7 0.1 collective-permute-start.3
  12.8 1.9 %collective-permute-start.4 = (f32[16,128]{1,0:T(8,128)S(1)}, f32[16,128]{1,0:T(8,128)S(1)}, u32[]{:S(2)}, u32[]{:S(2)}) collective-permute-start(f32[16,128]{1,0:T(8,128)S(1)} %get-tuple-element.39.refs_0_), channel_id=1, source_target_pairs={{0,2},{1,3},{2,0},{3,1},{4,6},{5,7},{6,4},{7,5},{8,10},{9,11},{10,... | collective-permute-start | bytes 24584 | tf_op jit(solution)/shard_map/ppermute | solution.py:81
  14.7 0.0 collective-permute-start.5
  14.7 0.0 collective-permute-done.3.refs_1_
  14.7 1.7 %collective-permute-done.4.refs_2_ = f32[16,128]{1,0:T(8,128)S(1)} collective-permute-done((f32[16,128]{1,0:T(8,128)S(1)}, f32[16,128]{1,0:T(8,128)S(1)}, u32[]{:S(2)}, u32[]{:S(2)}) %collective-permute-start.4) | collective-permute-done | bytes 8224 | tf_op jit(solution)/shard_map/ppermute | solution.py:81
  16.5 1.4 %collective-permute-done.5.refs_3_ = f32[16,128]{1,0:T(8,128)S(1)} collective-permute-done((f32[16,128]{1,0:T(8,128)S(1)}, f32[16,128]{1,0:T(8,128)S(1)}, u32[]{:S(2)}, u32[]{:S(2)}) %collective-permute-start.5) | collective-permute-done | bytes 8224 | tf_op jit(solution)/shard_map/ppermute | solution.py:81
  17.8 1.5 %shard_map.90 = (bf16[512,1024]{1,0:T(8,128)(2,1)S(1)}, f32[64,128]{1,0:T(8,128)S(1)}, bf16[64,639]{1,0:T(8,128)(2,1)S(1)}) custom-call(f32[16,128]{1,0:T(8,128)S(1)} %get-tuple-element.39.refs_0_, f32[16,128]{1,0:T(8,128)S(1)} %collective-permute-done.3.refs_1_, f32[16,128]{1,0:T(8,128)S(1)} %collective-permute-done.4.refs_2_, ...), custom_call_target="tpu_custom_call" | custom-call | flops 603979776 | bytes 2359296 | tf_op jit(solution)/shard_map/pallas_call | solution.py:425
  19.3 1.6 %collective-permute-start.6 = (bf16[64,639]{1,0:T(8,128)(2,1)S(1)}, bf16[64,639]{1,0:T(8,128)(2,1)S(1)}, u32[]{:S(2)}, u32[]{:S(2)}) collective-permute-start(bf16[64,639]{1,0:T(8,128)(2,1)S(1)} %get-tuple-element.44.refs_0_), channel_id=1, source_target_pairs={{0,4},{4,0},{8,12},{12,8},{1,5},{5,1},{9,13},{13,9},{2,6},{6,2},{1... | collective-permute-start | bytes 245384 | tf_op jit(solution)/shard_map/ppermute | solution.py:81
  21.0 2.9 %shard_map.91 = (bf16[64,599]{1,0:T(8,128)(2,1)S(1)}, f32[64,579]{1,0:T(8,128)S(1)}, f32[64,619]{1,0:T(8,128)S(1)}) custom-call(bf16[512,1024]{1,0:T(8,128)(2,1)S(1)} %get-tuple-element.42.weight_ref, bf16[1024,2304]{1,0:T(8,128)(2,1)S(1)} %get-tuple-element.41.refs_5_.shifted_ref, f32[64,128]{1,0:T(8,128)S(1)} %get-tuple-element.43.mass_ref, ...), custom_call_target="tpu_custom_call" | custom-call | flops 1024 | bytes 1024 | tf_op jit(solution)/shard_map/pallas_call | solution.py:425
  23.9 0.0 collective-permute-done.6.refs_1_
  23.9 0.1 shard_map.92
  24.0 2.7 %collective-permute-start.7 = (bf16[64,619]{1,0:T(8,128)(2,1)S(1)}, bf16[64,619]{1,0:T(8,128)(2,1)S(1)}, u32[]{:S(2)}, u32[]{:S(2)}) collective-permute-start(bf16[64,619]{1,0:T(8,128)(2,1)S(1)} %shard_map.92), channel_id=1, source_target_pairs={{0,8},{4,12},{8,0},{12,4},{1,9},{5,13},{9,1},{13,5},{2,10},{6,14},... | collective-permute-start | bytes 237704 | tf_op jit(solution)/shard_map/ppermute | solution.py:81
  26.7 1.5 %collective-permute-start.8 = (bf16[64,599]{1,0:T(8,128)(2,1)S(1)}, bf16[64,599]{1,0:T(8,128)(2,1)S(1)}, u32[]{:S(2)}, u32[]{:S(2)}) collective-permute-start(bf16[64,599]{1,0:T(8,128)(2,1)S(1)} %get-tuple-element.47), channel_id=1, source_target_pairs={{0,4},{4,0},{8,12},{12,8},{1,5},{5,1},{9,13},{13,9},{2,6},{6,2},{1... | collective-permute-start | bytes 230024 | tf_op jit(solution)/shard_map/ppermute | solution.py:81
  28.2 3.6 %collective-permute-done.8.refs_1_ = bf16[64,599]{1,0:T(8,128)(2,1)S(1)} collective-permute-done((bf16[64,599]{1,0:T(8,128)(2,1)S(1)}, bf16[64,599]{1,0:T(8,128)(2,1)S(1)}, u32[]{:S(2)}, u32[]{:S(2)}) %collective-permute-start.8) | collective-permute-done | bytes 76704 | tf_op jit(solution)/shard_map/ppermute | solution.py:81
  31.8 0.0 collective-permute-done.7.refs_0_
  31.8 0.7 %shard_map.93 = (f32[64,576]{1,0:T(8,128)}, f32[1,64]{1,0:T(1,128)}) custom-call(f32[64,579]{1,0:T(8,128)S(1)} %get-tuple-element.45.own_ref, bf16[64,619]{1,0:T(8,128)(2,1)S(1)} %collective-permute-done.7.refs_0_, bf16[64,599]{1,0:T(8,128)(2,1)S(1)} %collective-permute-done.8.refs_1_), custom_call_target="tpu_custom_call" | custom-call | flops 163840 | bytes 655360 | tf_op jit(solution)/shard_map/pallas_call | solution.py:425
Async XLA Ops:
  1.9 5.7 %collective-permute-start.2 = (bf16[16,2432]{1,0:T(8,128)(2,1)S(1)}, bf16[16,2432]{1,0:T(8,128)(2,1)S(1)}, u32[]{:S(2)}, u32[]{:S(2)}) collective-permute-start(bf16[16,2432]{1,0:T(8,128)(2,1)S(1)} %get-tuple-element.26.block_ref), channel_id=1, source_target_pairs={{0,1},{1,0},{2,3},{3,2},{4,5},{5,4},{6,7},{7,6},{8,9},{9,8},{10,11... | collective-permute-start | bytes 233480 | tf_op jit(solution)/shard_map/ppermute | solution.py:81
  2.4 7.2 %collective-permute-start = (bf16[16,2432]{1,0:T(8,128)(2,1)S(1)}, bf16[16,2432]{1,0:T(8,128)(2,1)S(1)}, u32[]{:S(2)}, u32[]{:S(2)}) collective-permute-start(bf16[16,2432]{1,0:T(8,128)(2,1)S(1)} %get-tuple-element.26.block_ref), channel_id=1, source_target_pairs={{0,2},{1,3},{2,0},{3,1},{4,6},{5,7},{6,4},{7,5},{8,10},{9,11},{10,... | collective-permute-start | bytes 233480 | tf_op jit(solution)/shard_map/ppermute | solution.py:81
  5.0 4.6 %collective-permute-start.1 = (bf16[16,2432]{1,0:T(8,128)(2,1)S(1)}, bf16[16,2432]{1,0:T(8,128)(2,1)S(1)}, u32[]{:S(2)}, u32[]{:S(2)}) collective-permute-start(bf16[16,2432]{1,0:T(8,128)(2,1)S(1)} %get-tuple-element.26.block_ref), channel_id=1, source_target_pairs={{0,3},{1,2},{2,1},{3,0},{4,7},{5,6},{6,5},{7,4},{8,11},{9,10},{10,... | collective-permute-start | bytes 233480 | tf_op jit(solution)/shard_map/ppermute | solution.py:81
  12.7 2.1 %collective-permute-start.3 = (f32[16,128]{1,0:T(8,128)S(1)}, f32[16,128]{1,0:T(8,128)S(1)}, u32[]{:S(2)}, u32[]{:S(2)}) collective-permute-start(f32[16,128]{1,0:T(8,128)S(1)} %get-tuple-element.39.refs_0_), channel_id=1, source_target_pairs={{0,1},{1,0},{2,3},{3,2},{4,5},{5,4},{6,7},{7,6},{8,9},{9,8},{10,11... | collective-permute-start | bytes 24584 | tf_op jit(solution)/shard_map/ppermute | solution.py:81
  12.8 3.7 %collective-permute-start.4 = (f32[16,128]{1,0:T(8,128)S(1)}, f32[16,128]{1,0:T(8,128)S(1)}, u32[]{:S(2)}, u32[]{:S(2)}) collective-permute-start(f32[16,128]{1,0:T(8,128)S(1)} %get-tuple-element.39.refs_0_), channel_id=1, source_target_pairs={{0,2},{1,3},{2,0},{3,1},{4,6},{5,7},{6,4},{7,5},{8,10},{9,11},{10,... | collective-permute-start | bytes 24584 | tf_op jit(solution)/shard_map/ppermute | solution.py:81
  14.7 3.1 %collective-permute-start.5 = (f32[16,128]{1,0:T(8,128)S(1)}, f32[16,128]{1,0:T(8,128)S(1)}, u32[]{:S(2)}, u32[]{:S(2)}) collective-permute-start(f32[16,128]{1,0:T(8,128)S(1)} %get-tuple-element.39.refs_0_), channel_id=1, source_target_pairs={{0,3},{1,2},{2,1},{3,0},{4,7},{5,6},{6,5},{7,4},{8,11},{9,10},{10,... | collective-permute-start | bytes 24584 | tf_op jit(solution)/shard_map/ppermute | solution.py:81
  19.3 4.6 %collective-permute-start.6 = (bf16[64,639]{1,0:T(8,128)(2,1)S(1)}, bf16[64,639]{1,0:T(8,128)(2,1)S(1)}, u32[]{:S(2)}, u32[]{:S(2)}) collective-permute-start(bf16[64,639]{1,0:T(8,128)(2,1)S(1)} %get-tuple-element.44.refs_0_), channel_id=1, source_target_pairs={{0,4},{4,0},{8,12},{12,8},{1,5},{5,1},{9,13},{13,9},{2,6},{6,2},{1... | collective-permute-start | bytes 245384 | tf_op jit(solution)/shard_map/ppermute | solution.py:81
  24.0 7.8 %collective-permute-start.7 = (bf16[64,619]{1,0:T(8,128)(2,1)S(1)}, bf16[64,619]{1,0:T(8,128)(2,1)S(1)}, u32[]{:S(2)}, u32[]{:S(2)}) collective-permute-start(bf16[64,619]{1,0:T(8,128)(2,1)S(1)} %shard_map.92), channel_id=1, source_target_pairs={{0,8},{4,12},{8,0},{12,4},{1,9},{5,13},{9,1},{13,5},{2,10},{6,14},... | collective-permute-start | bytes 237704 | tf_op jit(solution)/shard_map/ppermute | solution.py:81
  26.7 5.1 %collective-permute-start.8 = (bf16[64,599]{1,0:T(8,128)(2,1)S(1)}, bf16[64,599]{1,0:T(8,128)(2,1)S(1)}, u32[]{:S(2)}, u32[]{:S(2)}) collective-permute-start(bf16[64,599]{1,0:T(8,128)(2,1)S(1)} %get-tuple-element.47), channel_id=1, source_target_pairs={{0,4},{4,0},{8,12},{12,8},{1,5},{5,1},{9,13},{13,9},{2,6},{6,2},{1... | collective-permute-start | bytes 230024 | tf_op jit(solution)/shard_map/ppermute | solution.py:81

commit v7 on v6

--- a/solution.py
+++ b/solution.py
@@ -236,34 +236,9 @@
     return highest, total, scale[:, :LANES]
 
 
-def own_kernel(
-    count, block_ref, class_ref, rows_ref, scale_ref,
-    shifted_ref, exp_ref, stats_ref, rotated_ref, norm_ref, table_ref,
-):
-    build_table(rows_ref, table_ref)
-    rotate_classes(class_ref, rotated_ref, norm_ref)
+def score_blocks(count, chunks, blocks, table_ref, scale_ref, rotated_ref, norm_ref, shifted_ref, exp_ref, stats_ref):
     classes = norm_ref.shape[0]
     rows = exp_ref.shape[1] // count
-
-    def out(rotation, value):
-        exp_ref[rotation * classes : (rotation + 1) * classes, 0:rows] = value
-
-    highest, total, scale = score_block(
-        block_ref, table_ref, scale_ref, rotated_ref, norm_ref, shifted_ref.at[0:rows, :], out
-    )
-    stats_ref[...] = jnp.zeros_like(stats_ref)
-    stats_ref[0:1, :] = highest
-    stats_ref[1:2, :] = total
-    stats_ref[2 * count : 2 * count + 1, :] = scale
-
-
-def rest_kernel(count, chunks, *refs):
-    blocks, refs = refs[: len(chunks)], refs[len(chunks) :]
-    table_ref, scale_ref, rotated_ref, norm_ref, own_ref = refs[:5]
-    shifted_ref, exp_ref, stats_ref = refs[7:]
-    classes = norm_ref.shape[0]
-    rows = exp_ref.shape[1] // count
-    stats_ref[...] = own_ref[...]
     for block, block_ref in zip(chunks, blocks):
         part = slice(block * rows, (block + 1) * rows)
 
@@ -271,26 +246,62 @@
             exp_ref[rotation * classes : (rotation + 1) * classes, part] = value
 
         highest, total, scale = score_block(
-            block_ref, table_ref, scale_ref, rotated_ref, norm_ref,
-            shifted_ref.at[part, :], out,
+            block_ref, table_ref, scale_ref, rotated_ref, norm_ref, shifted_ref.at[part, :], out
         )
         stats_ref[2 * block : 2 * block + 1, :] = highest
         stats_ref[2 * block + 1 : 2 * block + 2, :] = total
         stats_ref[2 * count + block : 2 * count + block + 1, :] = scale
 
 
-def weigh(count, stats, exp_ref, weight_ref):
+def first_kernel(count, chunks, *refs):
+    blocks, refs = refs[: len(chunks)], refs[len(chunks) :]
+    class_ref, rows_ref, scale_ref = refs[:3]
+    shifted_ref, exp_ref, stats_ref, rotated_ref, norm_ref, table_ref = refs[3:]
+    build_table(rows_ref, table_ref)
+    rotate_classes(class_ref, rotated_ref, norm_ref)
+    stats_ref[...] = jnp.zeros_like(stats_ref)
+    score_blocks(
+        count, chunks, blocks, table_ref, scale_ref, rotated_ref, norm_ref,
+        shifted_ref, exp_ref, stats_ref,
+    )
+
+
+def rest_kernel(count, chunks, *refs):
+    blocks, refs = refs[: len(chunks)], refs[len(chunks) :]
+    table_ref, scale_ref, rotated_ref, norm_ref, before_ref = refs[:5]
+    shifted_ref, exp_ref, stats_ref = refs[7:]
+    stats_ref[...] = before_ref[...]
+    score_blocks(
+        count, chunks, blocks, table_ref, scale_ref, rotated_ref, norm_ref,
+        shifted_ref, exp_ref, stats_ref,
+    )
+
+
+def merged(mine, other, block, distance):
+    twin = block ^ distance
+    high, other_high = mine[2 * block : 2 * block + 1, :], other[2 * twin : 2 * twin + 1, :]
+    top = jnp.maximum(high, other_high)
+    total = mine[2 * block + 1 : 2 * block + 2, :] * jnp.exp(high - top)
+    return top, total + other[2 * twin + 1 : 2 * twin + 2, :] * jnp.exp(other_high - top)
+
+
+def merge_kernel(count, distance, mine, other, out_ref):
+    out_ref[...] = jnp.zeros_like(out_ref)
+    for block in range(count):
+        top, total = merged(mine, other, block, distance)
+        out_ref[2 * block : 2 * block + 1, :] = top
+        out_ref[2 * block + 1 : 2 * block + 2, :] = total
+
+
+def weigh(count, stats_ref, mine, other, exp_ref, weight_ref):
     rows = exp_ref.shape[1] // count
     repeat = rows // LANES
     classes = weight_ref.shape[0] // ROTS
     mass = jnp.zeros((classes, rows), jnp.float32)
     for block in range(count):
-        highs = [stats[c][2 * (c ^ block) : 2 * (c ^ block) + 1, :] for c in range(count)]
-        lows = [stats[c][2 * (c ^ block) + 1 : 2 * (c ^ block) + 2, :] for c in range(count)]
-        top = functools.reduce(jnp.maximum, highs)
-        total = functools.reduce(jnp.add, [l * jnp.exp(h - top) for h, l in zip(highs, lows)])
-        factor = jnp.exp(highs[0] - top) / total
-        scale = stats[0][2 * count + block : 2 * count + block + 1, :]
+        top, total = merged(mine, other, block, count // 2)
+        factor = jnp.exp(stats_ref[2 * block : 2 * block + 1, :] - top) / total
+        scale = stats_ref[2 * count + block : 2 * count + block + 1, :]
         factor = jnp.concatenate([factor] * repeat, axis=1)
         scale = jnp.concatenate([scale] * repeat, axis=1)
         part = slice(block * rows, (block + 1) * rows)
@@ -373,12 +384,10 @@
 
 
 def first_sums_kernel(count, doms, width, blocks, *refs):
-    stats = refs[:count]
-    exp_ref, shifted_ref = refs[count : count + 2]
-    weight_ref, mass_ref = refs[count + 2 : count + 4]
-    mass = weigh(count, stats, exp_ref, weight_ref)
+    stats_ref, mine, other, exp_ref, shifted_ref, weight_ref, mass_ref = refs[:7]
+    mass = weigh(count, stats_ref, mine, other, exp_ref, weight_ref)
     mass_ref[...] = mass
-    for block, out_ref in zip(blocks, refs[count + 4 :]):
+    for block, out_ref in zip(blocks, refs[7:]):
         store_block(width, block_sums(doms, width, block, weight_ref, shifted_ref), mass[:, :1], out_ref)
 
 
@@ -467,14 +476,15 @@
         class_spectra, group_scale[None, :], phases,
         hbm=(0, 1, 2, 3, 4, 5, 6),
     )
-    others = [exchange(packed, "cls", distance) for distance in range(1, count)]
+    chunks = [packed] + [exchange(packed, "cls", distance) for distance in range(1, count)]
     stat_rows = -(-3 * count // 8) * 8
     work = 2 * rows * COLS * (ROTS * classes + 256)
     stats_shape = shape((stat_rows, LANES), f32)
     shifted_shape = shape((count * rows, COLS), bf16)
     exp_shape = shape((ROTS * classes, count * rows), f32)
-    shifted, exps, stats_own, rotated, norm, table_on_chip = call(
-        functools.partial(own_kernel, count),
+    near, far = [0, 1], list(range(2, count))
+    shifted, exps, stats, rotated, norm, table = call(
+        functools.partial(first_kernel, count, near),
         [
             shifted_shape,
             exp_shape,
@@ -484,27 +494,36 @@
             shape((2 * LANES, COLS), bf16),
         ],
         [],
-        work,
-        4 * rows * COLS,
-        packed, classes_on_chip, phases_on_chip, scales,
-    )
-    stats = stats_own
-    for chunks in ([1], list(range(2, count))):
-        shifted, exps, stats = call(
-            functools.partial(rest_kernel, count, chunks),
-            [shifted_shape, exp_shape, stats_shape],
+        work * len(near),
+        4 * len(near) * rows * COLS,
+        *[chunks[b] for b in near], classes_on_chip, phases_on_chip, scales,
+    )
+    shifted, exps, stats = call(
+        functools.partial(rest_kernel, count, far),
+        [shifted_shape, exp_shape, stats_shape],
+        [],
+        work * len(far),
+        4 * len(far) * rows * COLS,
+        *[chunks[b] for b in far], table, scales, rotated, norm, stats, shifted, exps,
+        aliases={len(far) + 5: 0, len(far) + 6: 1},
+        chip=(len(far) + 5, len(far) + 6),
+    )
+    mine, distance = stats, 1
+    other = exchange(mine, "cls", distance)
+    while 2 * distance < count:
+        (mine,) = call(
+            functools.partial(merge_kernel, count, distance),
+            [shape((-(-2 * count // 8) * 8, LANES), f32)],
             [],
-            work * len(chunks),
-            4 * len(chunks) * rows * COLS,
-            *[others[b - 1] for b in chunks],
-            table_on_chip, scales, rotated, norm, stats, shifted, exps,
-            aliases={len(chunks) + 5: 0, len(chunks) + 6: 1},
-            chip=(len(chunks) + 5, len(chunks) + 6),
-        )
-    all_stats = [stats] + [exchange(stats, "cls", distance) for distance in range(1, count)]
+            1024,
+            1024,
+            mine, other,
+        )
+        distance *= 2
+        other = exchange(mine, "cls", distance)
     low_bit = lambda b: b & -b
     early = list(range(doms - 1, 1, -2))
-    order = early + sorted(range(2, doms, 2), key=lambda b: (low_bit(b), -b)) + [1]
+    order = early + [1] + sorted(range(2, doms, 2), key=lambda b: (low_bit(b), -b))
     extents = {b: width + 3 + (doms - 1 - place) * growth for place, b in enumerate(order)}
     late = [1] + list(range(0, doms, 2))
     weights, mass, *made = call(
@@ -514,8 +533,8 @@
         [],
         2 * count * rows * COLS * ROTS * classes // doms,
         4 * count * rows * width,
-        *all_stats, exps, shifted,
-        chip=(count, count + 1),
+        stats, mine, other, exps, shifted,
+        chip=(3, 4),
     )
     incoming = {b: [] for b in range(doms)}
     for b, block in zip(early, made):
@@ -532,7 +551,8 @@
         chip=(1,),
     )
     blocks = dict(zip(late, rest))
-    for b in order[len(early) : -1]:
+    incoming[0].append(exchange(blocks[1], "dom", 1))
+    for b in order[len(early) + 1 :]:
         (block,) = call(
             functools.partial(add_kernel, width),
             [shape((classes, extents[b]), bf16)],
@@ -542,7 +562,6 @@
             blocks[b], *incoming[b],
         )
         incoming[b ^ low_bit(b)].append(exchange(block, "dom", low_bit(b)))
-    incoming[0].append(exchange(blocks[1], "dom", 1))
     own, received = blocks[0], incoming[0]
     class_sums, class_weights = call(
         functools.partial(final_kernel, width),

time: 32.7 us -> 30.8 us (0.942)
  Pallas kernels: 14.1 us -> 13 us
  starting transfers between devices: 11 us -> 9.94 us
    pallas_call x8, Pallas kernels: 14.1 us -> 13 us  [call(): pl.pallas_call(kernel, out_shape=[pltpu.VMEM(s.shape, s.dtype) if pinned...]
    ppermute x9 -> x8, starting transfers between devices: 11 us -> 9.94 us  [exchange(): lax.ppermute(array, axis, [(i, i ^ distance) for i in range(lax.axis_size...]
    ppermute x9 -> x8, waiting for transfers between devices: 6.74 us -> 7 us  [exchange(): lax.ppermute(array, axis, [(i, i ^ distance) for i in range(lax.axis_size...]
  transfers between devices with their start and end apart: 9 -> 8, of which waited for: 3 -> 5; matrix products, arithmetic and copies ran while one was open for 0% -> 0% of each run, Pallas kernels for 23% -> 21%
where the time goes in v7:
time: 30.8 us; the launch traced here: 30.6 us
  Pallas kernels  13 us (42%)
  starting transfers between devices  9.94 us (32%)
  waiting for transfers between devices  7 us (23%)
  between operations  0.67 us (2%)
    pallas_call x8, Pallas kernels, call(): pl.pallas_call(kernel, out_shape=[pltpu.VMEM(s.shape, s.dtype) if pinned...  13 us
    ppermute x8, starting transfers between devices, exchange(): lax.ppermute(array, axis, [(i, i ^ distance) for i in range(lax.axis_size...  9.94 us
    ppermute x8, waiting for transfers between devices, exchange(): lax.ppermute(array, axis, [(i, i ^ distance) for i in range(lax.axis_size...  7 us
  transfers between devices with their start and end apart: 8, of which 5 were waited for; matrix products, arithmetic and copies ran while one was open for 0% of the time, Pallas kernels for 21%

profile of v7, /device:TPU:0, one launch (start us, length us, event | category | flops | bytes accessed | tf_op | source)
XLA Modules:
  0.0 30.6 jit_solution(8566209480823512059)
XLA Ops:
  0.6 1.3 %shard_map.86 = (bf16[16,2432]{1,0:T(8,128)(2,1)S(1)}, bf16[64,2304]{1,0:T(8,128)(2,1)S(1)}, f32[1,64]{1,0:T(1,128)S(1)}, f32[48,2304]{1,0:T(8,128)S(1)}) custom-call(bf16[16,2304]{1,0:T(8,128)(2,1)} %particle_hbm.1, s32[16,16]{1,0:T(8,128)} %index_hbm.1, s32[1,16]{1,0:T(1,128)} %bitcast.4, s32[1,16]{1,0:T(1,128)} %bitcast.5, bf16[64,2304]{1,0:T(8,128)(2,1)} %class_hbm.1, ...), custom_call_target="tpu_custom_call" | custom-call | flops 36864 | bytes 147456 | tf_op jit(solution)/shard_map/pallas_call | solution.py:434
  1.9 0.5 %collective-permute-start.2 = (bf16[16,2432]{1,0:T(8,128)(2,1)S(1)}, bf16[16,2432]{1,0:T(8,128)(2,1)S(1)}, u32[]{:S(2)}, u32[]{:S(2)}) collective-permute-start(bf16[16,2432]{1,0:T(8,128)(2,1)S(1)} %get-tuple-element.23.refs_0_), channel_id=1, source_target_pairs={{0,1},{1,0},{2,3},{3,2},{4,5},{5,4},{6,7},{7,6},{8,9},{9,8},{10,11... | collective-permute-start | bytes 233480 | tf_op jit(solution)/shard_map/ppermute | solution.py:81
  2.4 2.6 %collective-permute-start.1 = (bf16[16,2432]{1,0:T(8,128)(2,1)S(1)}, bf16[16,2432]{1,0:T(8,128)(2,1)S(1)}, u32[]{:S(2)}, u32[]{:S(2)}) collective-permute-start(bf16[16,2432]{1,0:T(8,128)(2,1)S(1)} %get-tuple-element.23.refs_0_), channel_id=1, source_target_pairs={{0,3},{1,2},{2,1},{3,0},{4,7},{5,6},{6,5},{7,4},{8,11},{9,10},{10,... | collective-permute-start | bytes 233480 | tf_op jit(solution)/shard_map/ppermute | solution.py:81
  5.0 0.0 collective-permute-start
  5.1 0.0 collective-permute-done.2.refs_1_
  5.1 3.4 %shard_map.87 = (bf16[1024,2304]{1,0:T(8,128)(2,1)S(1)}, f32[512,1024]{1,0:T(8,128)S(1)}, f32[16,128]{1,0:T(8,128)S(1)}, bf16[512,2304]{1,0:T(8,128)(2,1)S(1)}, ...) custom-call(bf16[16,2432]{1,0:T(8,128)(2,1)S(1)} %get-tuple-element.23.refs_0_, ...), custom_call_target="tpu_custom_call" | custom-call | flops 1811939328 | bytes 4718592 | tf_op jit(solution)/shard_map/pallas_call | solution.py:434
  8.5 0.0 collective-permute-done.1.refs_1_
  8.5 1.1 %collective-permute-done.refs_0_ = bf16[16,2432]{1,0:T(8,128)(2,1)S(1)} collective-permute-done((bf16[16,2432]{1,0:T(8,128)(2,1)S(1)}, bf16[16,2432]{1,0:T(8,128)(2,1)S(1)}, u32[]{:S(2)}, u32[]{:S(2)}) %collective-permute-start) | collective-permute-done | bytes 77856 | tf_op jit(solution)/shard_map/ppermute | solution.py:81
  9.6 3.0 %shard_map.88 = (bf16[1024,2304]{1,0:T(8,128)(2,1)S(1)}, f32[512,1024]{1,0:T(8,128)S(1)}, f32[16,128]{1,0:T(8,128)S(1)}) custom-call(bf16[16,2432]{1,0:T(8,128)(2,1)S(1)} %collective-permute-done.refs_0_, bf16[16,2432]{1,0:T(8,128)(2,1)S(1)} %collective-permute-done.1.refs_1_, ...), custom_call_target="tpu_custom_call", output_to_operand_aliasing={{0}: (7, {}), {1}: (8, {})} | custom-call | flops 1811939328 | bytes 4718592 | tf_op jit(solution)/shard_map/pallas_call | solution.py:434
  12.6 0.0 collective-permute-start.3
  12.6 1.2 %collective-permute-done.3.other = f32[16,128]{1,0:T(8,128)S(1)} collective-permute-done((f32[16,128]{1,0:T(8,128)S(1)}, f32[16,128]{1,0:T(8,128)S(1)}, u32[]{:S(2)}, u32[]{:S(2)}) %collective-permute-start.3) | collective-permute-done | bytes 8224 | tf_op jit(solution)/shard_map/ppermute | solution.py:81
  13.8 1.8 %collective-permute-start.4 = (f32[8,128]{1,0:T(8,128)S(1)}, f32[8,128]{1,0:T(8,128)S(1)}, u32[]{:S(2)}, u32[]{:S(2)}) collective-permute-start(f32[8,128]{1,0:T(8,128)S(1)} %shard_map.89.refs_1_), channel_id=1, source_target_pairs={{0,2},{1,3},{2,0},{3,1},{4,6},{5,7},{6,4},{7,5},{8,10},{9,11},{10,... | collective-permute-start | bytes 12296 | tf_op jit(solution)/shard_map/ppermute | solution.py:81
  15.6 1.9 %collective-permute-done.4.refs_2_ = f32[8,128]{1,0:T(8,128)S(1)} collective-permute-done((f32[8,128]{1,0:T(8,128)S(1)}, f32[8,128]{1,0:T(8,128)S(1)}, u32[]{:S(2)}, u32[]{:S(2)}) %collective-permute-start.4) | collective-permute-done | bytes 4128 | tf_op jit(solution)/shard_map/ppermute | solution.py:81
  17.5 1.5 %shard_map.90 = (bf16[512,1024]{1,0:T(8,128)(2,1)S(1)}, f32[64,128]{1,0:T(8,128)S(1)}, bf16[64,639]{1,0:T(8,128)(2,1)S(1)}) custom-call(f32[16,128]{1,0:T(8,128)S(1)} %get-tuple-element.33.mine.refs_0_, f32[8,128]{1,0:T(8,128)S(1)} %shard_map.89.refs_1_, f32[8,128]{1,0:T(8,128)S(1)} %collective-permute-done.4.refs_2_, ...), custom_call_target="tpu_custom_call" | custom-call | flops 603979776 | bytes 2359296 | tf_op jit(solution)/shard_map/pallas_call | solution.py:434
  19.0 1.9 %collective-permute-start.6 = (bf16[64,639]{1,0:T(8,128)(2,1)S(1)}, bf16[64,639]{1,0:T(8,128)(2,1)S(1)}, u32[]{:S(2)}, u32[]{:S(2)}) collective-permute-start(bf16[64,639]{1,0:T(8,128)(2,1)S(1)} %get-tuple-element.38.refs_0_), channel_id=1, source_target_pairs={{0,4},{4,0},{8,12},{12,8},{1,5},{5,1},{9,13},{13,9},{2,6},{6,2},{1... | collective-permute-start | bytes 245384 | tf_op jit(solution)/shard_map/ppermute | solution.py:81
  20.9 3.0 %shard_map.91 = (bf16[64,619]{1,0:T(8,128)(2,1)S(1)}, f32[64,579]{1,0:T(8,128)S(1)}, f32[64,599]{1,0:T(8,128)S(1)}) custom-call(bf16[512,1024]{1,0:T(8,128)(2,1)S(1)} %get-tuple-element.36.weight_ref, bf16[1024,2304]{1,0:T(8,128)(2,1)S(1)} %get-tuple-element.35.refs_4_.shifted_ref, f32[64,128]{1,0:T(8,128)S(1)} %get-tuple-element.37.mass_ref, ...), custom_call_target="tpu_custom_call" | custom-call | flops 1024 | bytes 1024 | tf_op jit(solution)/shard_map/pallas_call | solution.py:434
  23.8 0.3 collective-permute-start.5
  24.1 0.0 collective-permute-done.6.refs_1_
  24.1 0.1 shard_map.92
  24.2 2.9 %collective-permute-start.7 = (bf16[64,599]{1,0:T(8,128)(2,1)S(1)}, bf16[64,599]{1,0:T(8,128)(2,1)S(1)}, u32[]{:S(2)}, u32[]{:S(2)}) collective-permute-start(bf16[64,599]{1,0:T(8,128)(2,1)S(1)} %shard_map.92), channel_id=1, source_target_pairs={{0,8},{4,12},{8,0},{12,4},{1,9},{5,13},{9,1},{13,5},{2,10},{6,14},... | collective-permute-start | bytes 230024 | tf_op jit(solution)/shard_map/ppermute | solution.py:81
  27.1 1.2 %collective-permute-done.5.refs_0_ = bf16[64,619]{1,0:T(8,128)(2,1)S(1)} collective-permute-done((bf16[64,619]{1,0:T(8,128)(2,1)S(1)}, bf16[64,619]{1,0:T(8,128)(2,1)S(1)}, u32[]{:S(2)}, u32[]{:S(2)}) %collective-permute-start.5) | collective-permute-done | bytes 79264 | tf_op jit(solution)/shard_map/ppermute | solution.py:81
  28.3 1.5 %collective-permute-done.7.refs_1_ = bf16[64,599]{1,0:T(8,128)(2,1)S(1)} collective-permute-done((bf16[64,599]{1,0:T(8,128)(2,1)S(1)}, bf16[64,599]{1,0:T(8,128)(2,1)S(1)}, u32[]{:S(2)}, u32[]{:S(2)}) %collective-permute-start.7) | collective-permute-done | bytes 76704 | tf_op jit(solution)/shard_map/ppermute | solution.py:81
  29.9 0.7 %shard_map.93 = (f32[64,576]{1,0:T(8,128)}, f32[1,64]{1,0:T(1,128)}) custom-call(f32[64,579]{1,0:T(8,128)S(1)} %get-tuple-element.39.own_ref, bf16[64,619]{1,0:T(8,128)(2,1)S(1)} %collective-permute-done.5.refs_0_, bf16[64,599]{1,0:T(8,128)(2,1)S(1)} %collective-permute-done.7.refs_1_), custom_call_target="tpu_custom_call" | custom-call | flops 163840 | bytes 655360 | tf_op jit(solution)/shard_map/pallas_call | solution.py:434
  (1 shorter events, 0.0 us)
Async XLA Ops:
  1.9 3.2 %collective-permute-start.2 = (bf16[16,2432]{1,0:T(8,128)(2,1)S(1)}, bf16[16,2432]{1,0:T(8,128)(2,1)S(1)}, u32[]{:S(2)}, u32[]{:S(2)}) collective-permute-start(bf16[16,2432]{1,0:T(8,128)(2,1)S(1)} %get-tuple-element.23.refs_0_), channel_id=1, source_target_pairs={{0,1},{1,0},{2,3},{3,2},{4,5},{5,4},{6,7},{7,6},{8,9},{9,8},{10,11... | collective-permute-start | bytes 233480 | tf_op jit(solution)/shard_map/ppermute | solution.py:81
  2.4 6.0 %collective-permute-start.1 = (bf16[16,2432]{1,0:T(8,128)(2,1)S(1)}, bf16[16,2432]{1,0:T(8,128)(2,1)S(1)}, u32[]{:S(2)}, u32[]{:S(2)}) collective-permute-start(bf16[16,2432]{1,0:T(8,128)(2,1)S(1)} %get-tuple-element.23.refs_0_), channel_id=1, source_target_pairs={{0,3},{1,2},{2,1},{3,0},{4,7},{5,6},{6,5},{7,4},{8,11},{9,10},{10,... | collective-permute-start | bytes 233480 | tf_op jit(solution)/shard_map/ppermute | solution.py:81
  5.0 4.6 %collective-permute-start = (bf16[16,2432]{1,0:T(8,128)(2,1)S(1)}, bf16[16,2432]{1,0:T(8,128)(2,1)S(1)}, u32[]{:S(2)}, u32[]{:S(2)}) collective-permute-start(bf16[16,2432]{1,0:T(8,128)(2,1)S(1)} %get-tuple-element.23.refs_0_), channel_id=1, source_target_pairs={{0,2},{1,3},{2,0},{3,1},{4,6},{5,7},{6,4},{7,5},{8,10},{9,11},{10,... | collective-permute-start | bytes 233480 | tf_op jit(solution)/shard_map/ppermute | solution.py:81
  12.6 1.2 %collective-permute-start.3 = (f32[16,128]{1,0:T(8,128)S(1)}, f32[16,128]{1,0:T(8,128)S(1)}, u32[]{:S(2)}, u32[]{:S(2)}) collective-permute-start(f32[16,128]{1,0:T(8,128)S(1)} %get-tuple-element.33.mine.refs_0_), channel_id=1, source_target_pairs={{0,1},{1,0},{2,3},{3,2},{4,5},{5,4},{6,7},{7,6},{8,9},{9,8},{10,11... | collective-permute-start | bytes 24584 | tf_op jit(solution)/shard_map/ppermute | solution.py:81
  13.8 3.7 %collective-permute-start.4 = (f32[8,128]{1,0:T(8,128)S(1)}, f32[8,128]{1,0:T(8,128)S(1)}, u32[]{:S(2)}, u32[]{:S(2)}) collective-permute-start(f32[8,128]{1,0:T(8,128)S(1)} %shard_map.89.refs_1_), channel_id=1, source_target_pairs={{0,2},{1,3},{2,0},{3,1},{4,6},{5,7},{6,4},{7,5},{8,10},{9,11},{10,... | collective-permute-start | bytes 12296 | tf_op jit(solution)/shard_map/ppermute | solution.py:81
  19.0 5.1 %collective-permute-start.6 = (bf16[64,639]{1,0:T(8,128)(2,1)S(1)}, bf16[64,639]{1,0:T(8,128)(2,1)S(1)}, u32[]{:S(2)}, u32[]{:S(2)}) collective-permute-start(bf16[64,639]{1,0:T(8,128)(2,1)S(1)} %get-tuple-element.38.refs_0_), channel_id=1, source_target_pairs={{0,4},{4,0},{8,12},{12,8},{1,5},{5,1},{9,13},{13,9},{2,6},{6,2},{1... | collective-permute-start | bytes 245384 | tf_op jit(solution)/shard_map/ppermute | solution.py:81
  23.8 4.5 %collective-permute-start.5 = (bf16[64,619]{1,0:T(8,128)(2,1)S(1)}, bf16[64,619]{1,0:T(8,128)(2,1)S(1)}, u32[]{:S(2)}, u32[]{:S(2)}) collective-permute-start(bf16[64,619]{1,0:T(8,128)(2,1)S(1)} %get-tuple-element.40), channel_id=1, source_target_pairs={{0,4},{4,0},{8,12},{12,8},{1,5},{5,1},{9,13},{13,9},{2,6},{6,2},{1... | collective-permute-start | bytes 237704 | tf_op jit(solution)/shard_map/ppermute | solution.py:81
  24.2 5.6 %collective-permute-start.7 = (bf16[64,599]{1,0:T(8,128)(2,1)S(1)}, bf16[64,599]{1,0:T(8,128)(2,1)S(1)}, u32[]{:S(2)}, u32[]{:S(2)}) collective-permute-start(bf16[64,599]{1,0:T(8,128)(2,1)S(1)} %shard_map.92), channel_id=1, source_target_pairs={{0,8},{4,12},{8,0},{12,4},{1,9},{5,13},{9,1},{13,5},{2,10},{6,14},... | collective-permute-start | bytes 230024 | tf_op jit(solution)/shard_map/ppermute | solution.py:81

commit v8 on v7

--- a/solution.py
+++ b/solution.py
@@ -25,7 +25,33 @@
 VMEM_LIMIT = 20 * 1024 * 1024
 
 
-def phase_rows():
+def column_layout(doms):
+    width = COLS // doms
+    main = width - ANG
+    half = doms // 2
+    if width % ANG or main <= 0 or main % LANES or half * ANG % LANES:
+        step = 3 * LANES
+        segments = [(start, HALF + start, step) for start in range(0, HALF, step)]
+        return list(range(COLS // ANG)), segments, 0
+    per = width // ANG
+    groups = [per * dom + group for dom in range(doms) for group in range(per - 1)]
+    groups += [per * dom + per - 1 for dom in range(doms)]
+    segments = [(dom * main, (half + dom) * main, main) for dom in range(half)]
+    segments.append((doms * main, doms * main + half * ANG, half * ANG))
+    return groups, segments, main
+
+
+def tile_of(groups, tile, read):
+    low, high = groups[2 * tile], groups[2 * tile + 1]
+    if low % 2 == 0 and high == low + 1:
+        return read(low // 2)
+    first, second = read(low // 2), read(high // 2)
+    first = pltpu.roll(first, ANG, 1) if low % 2 else first
+    second = second if high % 2 else pltpu.roll(second, ANG, 1)
+    return jnp.where(lane_index(first.shape) < ANG, first, second)
+
+
+def phase_rows(groups):
     angles = np.arange(ANG) * (2.0 * math.pi / ANG)
     radius = np.arange(CYCLES) + 1.0
     fx = (radius[:, None] * np.cos(angles)[None, :]).reshape(-1)
@@ -38,14 +64,14 @@
     values = np.zeros((48, COLS), np.float32)
     for start, phase in ((0, along_x), (16, along_y), (32, both)):
         values[start : start + len(phase)] = np.concatenate([np.cos(phase), np.sin(phase)], axis=1)
-    return values
-
-
-def build_table(rows_ref, table_ref):
-    width = 3 * LANES
-    for start in range(0, HALF, width):
-        real = slice(start, start + width)
-        imag = slice(HALF + start, HALF + start + width)
+    columns = np.concatenate([np.arange(ANG) + ANG * group for group in groups])
+    return values[:, columns]
+
+
+def build_table(segments, rows_ref, table_ref):
+    for real_start, imag_start, width in segments:
+        real = slice(real_start, real_start + width)
+        imag = slice(imag_start, imag_start + width)
 
         def product(block, row):
             c, s = rows_ref[block : block + SUB, real], rows_ref[block : block + SUB, imag]
@@ -85,13 +111,15 @@
     return lax.broadcasted_iota(jnp.int32, shape, len(shape) - 1)
 
 
-def rotate_classes(class_ref, rotated_ref, norm_ref):
+def rotate_classes(groups, class_ref, rotated_ref, norm_ref):
     classes = class_ref.shape[0]
     total = jnp.zeros((classes, LANES), jnp.float32)
     lane = lane_index((classes, LANES)) % ANG
     for tile in range(COLS // LANES):
         columns = slice(tile * LANES, (tile + 1) * LANES)
-        value = class_ref[:, columns]
+        value = tile_of(
+            groups, tile, lambda k: class_ref[:, k * LANES : (k + 1) * LANES]
+        )
         wide = value.astype(jnp.float32)
         total = total + wide * wide
         other = pltpu.roll(value, ANG, 1)
@@ -130,8 +158,8 @@
 
 
 def pack_kernel(
-    particle_hbm, index_hbm, prior_hbm, group_hbm, class_hbm, scale_hbm, rows_hbm,
-    packed_ref, class_ref, scale_ref, rows_ref, index_ref, prior_ref, group_ref, sems,
+    groups, particle_hbm, index_hbm, prior_hbm, group_hbm, class_hbm, scale_hbm, rows_hbm,
+    packed_ref, class_ref, scale_ref, rows_ref, particle_ref, index_ref, prior_ref, group_ref, sems,
 ):
     particles, candidates = index_ref.shape
     copies = [
@@ -141,7 +169,7 @@
                 (index_hbm, index_ref),
                 (prior_hbm, prior_ref),
                 (group_hbm, group_ref),
-                (particle_hbm, packed_ref.at[:, pl.ds(0, COLS)]),
+                (particle_hbm, particle_ref),
                 (class_hbm, class_ref),
                 (scale_hbm, scale_ref),
                 (rows_hbm, rows_ref),
@@ -161,11 +189,16 @@
     group = to_column(group_ref[...].astype(jnp.float32))
     meta = jnp.where(lane == candidates, prior, jnp.where(lane == candidates + 1, group, index))
     packed_ref[:, COLS:] = meta.astype(jnp.bfloat16)
-    for copy in copies[3:]:
+    copies[3].wait()
+    for tile in range(COLS // LANES):
+        packed_ref[:, tile * LANES : (tile + 1) * LANES] = tile_of(
+            groups, tile, lambda k: particle_ref[:, k * LANES : (k + 1) * LANES]
+        )
+    for copy in copies[4:]:
         copy.wait()
 
 
-def score_block(block_ref, table_ref, scale_ref, rotated_ref, norm_ref, shifted_ref, out):
+def score_block(segments, block_ref, table_ref, scale_ref, rotated_ref, norm_ref, shifted_ref, out):
     particles = block_ref.shape[0]
     classes = norm_ref.shape[0]
     candidates = shifted_ref.shape[0] // particles
@@ -191,10 +224,9 @@
     )
     scale = to_lanes(scale_column, rows)
     prior = to_lanes(meta[:, candidates : candidates + 1], rows)
-    width = 3 * LANES
-    for start in range(0, HALF, width):
-        real_columns = slice(start, start + width)
-        imag_columns = slice(HALF + start, HALF + start + width)
+    for real_start, imag_start, width in segments:
+        real_columns = slice(real_start, real_start + width)
+        imag_columns = slice(imag_start, imag_start + width)
         cosine = jnp.dot(hot, table_ref[:, real_columns], preferred_element_type=jnp.float32)
         sine = jnp.dot(hot, table_ref[:, imag_columns], preferred_element_type=jnp.float32)
         real = block_ref[:, real_columns].astype(jnp.float32)
@@ -236,7 +268,7 @@
     return highest, total, scale[:, :LANES]
 
 
-def score_blocks(count, chunks, blocks, table_ref, scale_ref, rotated_ref, norm_ref, shifted_ref, exp_ref, stats_ref):
+def score_blocks(count, segments, chunks, blocks, table_ref, scale_ref, rotated_ref, norm_ref, shifted_ref, exp_ref, stats_ref):
     classes = norm_ref.shape[0]
     rows = exp_ref.shape[1] // count
     for block, block_ref in zip(chunks, blocks):
@@ -246,33 +278,34 @@
             exp_ref[rotation * classes : (rotation + 1) * classes, part] = value
 
         highest, total, scale = score_block(
-            block_ref, table_ref, scale_ref, rotated_ref, norm_ref, shifted_ref.at[part, :], out
+            segments, block_ref, table_ref, scale_ref, rotated_ref, norm_ref,
+            shifted_ref.at[part, :], out,
         )
         stats_ref[2 * block : 2 * block + 1, :] = highest
         stats_ref[2 * block + 1 : 2 * block + 2, :] = total
         stats_ref[2 * count + block : 2 * count + block + 1, :] = scale
 
 
-def first_kernel(count, chunks, *refs):
+def first_kernel(count, groups, segments, chunks, *refs):
     blocks, refs = refs[: len(chunks)], refs[len(chunks) :]
     class_ref, rows_ref, scale_ref = refs[:3]
     shifted_ref, exp_ref, stats_ref, rotated_ref, norm_ref, table_ref = refs[3:]
-    build_table(rows_ref, table_ref)
-    rotate_classes(class_ref, rotated_ref, norm_ref)
+    build_table(segments, rows_ref, table_ref)
+    rotate_classes(groups, class_ref, rotated_ref, norm_ref)
     stats_ref[...] = jnp.zeros_like(stats_ref)
     score_blocks(
-        count, chunks, blocks, table_ref, scale_ref, rotated_ref, norm_ref,
+        count, segments, chunks, blocks, table_ref, scale_ref, rotated_ref, norm_ref,
         shifted_ref, exp_ref, stats_ref,
     )
 
 
-def rest_kernel(count, chunks, *refs):
+def rest_kernel(count, segments, chunks, *refs):
     blocks, refs = refs[: len(chunks)], refs[len(chunks) :]
     table_ref, scale_ref, rotated_ref, norm_ref, before_ref = refs[:5]
     shifted_ref, exp_ref, stats_ref = refs[7:]
     stats_ref[...] = before_ref[...]
     score_blocks(
-        count, chunks, blocks, table_ref, scale_ref, rotated_ref, norm_ref,
+        count, segments, chunks, blocks, table_ref, scale_ref, rotated_ref, norm_ref,
         shifted_ref, exp_ref, stats_ref,
     )
 
@@ -313,47 +346,61 @@
     return jnp.broadcast_to(jnp.sum(mass, axis=1, keepdims=True), (classes, LANES))
 
 
-def block_sums(doms, width, distance, weight_ref, shifted_ref):
+def window_sums(weight_ref, shifted_ref, start, wide):
+    classes = weight_ref.shape[0] // ROTS
+    product = jnp.dot(
+        weight_ref[...], shifted_ref[:, pl.ds(start, wide)], preferred_element_type=jnp.float32
+    )
+    lane = lane_index((classes, LANES)) % ANG
+    tiles = []
+    for part in range(0, wide, LANES):
+        inside = product[:classes, part : part + LANES]
+        wrapped = None
+        for rotation in range(1, ROTS):
+            offset = ANG_STEP * rotation % ANG
+            turned = pltpu.roll(
+                product[rotation * classes : (rotation + 1) * classes, part : part + LANES],
+                LANES - offset,
+                1,
+            )
+            within = lane < ANG - offset
+            inside = inside + jnp.where(within, turned, 0.0)
+            over = jnp.where(within, 0.0, turned)
+            wrapped = over if wrapped is None else wrapped + over
+        tiles.append(inside + pltpu.roll(wrapped, ANG, 1))
+    return tiles
+
+
+def block_sums(doms, width, main, distance, weight_ref, shifted_ref, tails_ref):
     classes = weight_ref.shape[0] // ROTS
     padded = -(-(width + 3) // LANES) * LANES
     place = lax.axis_index("dom") ^ distance
-    first = place * width
-    shifts = sorted({width * dom % LANES for dom in range(doms)})
-    span = -(-(shifts[-1] + width) // LANES) * LANES
+    first = place * (main or width)
+    shifts = [0] if main else sorted({width * dom % LANES for dom in range(doms)})
+    span = main or -(-(shifts[-1] + width) // LANES) * LANES
     base = first // LANES * LANES
     tiles = []
     for start in range(0, span, 2 * LANES):
-        wide = min(2 * LANES, span - start)
-        columns = pl.ds(pl.multiple_of(base + start, LANES), wide)
-        product = jnp.dot(
-            weight_ref[...], shifted_ref[:, columns], preferred_element_type=jnp.float32
-        )
-        for part in range(0, wide, LANES):
-            lane = lane_index((classes, LANES)) % ANG
-            inside = product[:classes, part : part + LANES]
-            wrapped = None
-            for rotation in range(1, ROTS):
-                offset = ANG_STEP * rotation % ANG
-                turned = pltpu.roll(
-                    product[rotation * classes : (rotation + 1) * classes, part : part + LANES],
-                    LANES - offset,
-                    1,
-                )
-                within = lane < ANG - offset
-                inside = inside + jnp.where(within, turned, 0.0)
-                over = jnp.where(within, 0.0, turned)
-                wrapped = over if wrapped is None else wrapped + over
-            tiles.append(inside + pltpu.roll(wrapped, ANG, 1))
+        tiles += window_sums(
+            weight_ref,
+            shifted_ref,
+            pl.multiple_of(base + start, LANES),
+            min(2 * LANES, span - start),
+        )
+    if main:
+        tail = None
+        for dom in range(doms):
+            part = dom * ANG // LANES * LANES
+            piece = tails_ref[:, part : part + LANES]
+            piece = pltpu.roll(piece, ANG, 1) if dom % 2 else piece
+            tail = piece if tail is None else jnp.where(place == dom, piece, tail)
+        tiles.append(tail)
     total = jnp.concatenate(tiles, axis=1)
     aligned = total
     for shift in shifts:
         if shift:
             aligned = jnp.where(first - base == shift, pltpu.roll(total, span - shift, 1), aligned)
-    if span < padded:
-        aligned = jnp.concatenate(
-            [aligned, jnp.zeros((classes, padded - span), jnp.float32)], axis=1
-        )
-    return aligned[:, :padded]
+    return pad_columns(aligned, padded)
 
 
 def store_block(width, value, mass, out_ref):
@@ -383,17 +430,22 @@
     return jnp.sum(tail, axis=1, keepdims=True)
 
 
-def first_sums_kernel(count, doms, width, blocks, *refs):
-    stats_ref, mine, other, exp_ref, shifted_ref, weight_ref, mass_ref = refs[:7]
+def first_sums_kernel(count, doms, width, main, blocks, *refs):
+    stats_ref, mine, other, exp_ref, shifted_ref, weight_ref, mass_ref, tails_ref = refs[:8]
     mass = weigh(count, stats_ref, mine, other, exp_ref, weight_ref)
     mass_ref[...] = mass
-    for block, out_ref in zip(blocks, refs[7:]):
-        store_block(width, block_sums(doms, width, block, weight_ref, shifted_ref), mass[:, :1], out_ref)
-
-
-def rest_sums_kernel(doms, width, blocks, weight_ref, shifted_ref, mass_ref, *refs):
+    tails_ref[...] = jnp.zeros_like(tails_ref)
+    for start in range(0, doms * ANG if main else 0, 2 * LANES):
+        tiles = window_sums(weight_ref, shifted_ref, doms * main + start, 2 * LANES)
+        tails_ref[:, start : start + 2 * LANES] = jnp.concatenate(tiles, axis=1)
+    for block, out_ref in zip(blocks, refs[8:]):
+        value = block_sums(doms, width, main, block, weight_ref, shifted_ref, tails_ref)
+        store_block(width, value, mass[:, :1], out_ref)
+
+
+def rest_sums_kernel(doms, width, main, blocks, weight_ref, shifted_ref, mass_ref, tails_ref, *refs):
     for block, out_ref in zip(blocks, refs[-len(blocks) :]):
-        value = block_sums(doms, width, block, weight_ref, shifted_ref)
+        value = block_sums(doms, width, main, block, weight_ref, shifted_ref, tails_ref)
         store_block(width, value, mass_ref[:, :1], out_ref)
 
 
@@ -455,9 +507,10 @@
     f32, bf16 = jnp.float32, jnp.bfloat16
     shape = jax.ShapeDtypeStruct
 
-    phases = jnp.asarray(phase_rows())
+    groups, segments, main = column_layout(doms)
+    phases = jnp.asarray(phase_rows(groups))
     packed, classes_on_chip, scales, phases_on_chip = call(
-        pack_kernel,
+        functools.partial(pack_kernel, groups),
         [
             shape((particles, COLS + META), bf16),
             shape(class_spectra.shape, bf16),
@@ -465,6 +518,7 @@
             shape(phases.shape, f32),
         ],
         [
+            pltpu.VMEM((particles, COLS), bf16),
             pltpu.VMEM((particles, candidates), jnp.int32),
             pltpu.VMEM((1, particles), jnp.int32),
             pltpu.VMEM((1, particles), jnp.int32),
@@ -484,7 +538,7 @@
     exp_shape = shape((ROTS * classes, count * rows), f32)
     near, far = [0, 1], list(range(2, count))
     shifted, exps, stats, rotated, norm, table = call(
-        functools.partial(first_kernel, count, near),
+        functools.partial(first_kernel, count, groups, segments, near),
         [
             shifted_shape,
             exp_shape,
@@ -499,7 +553,7 @@
         *[chunks[b] for b in near], classes_on_chip, phases_on_chip, scales,
     )
     shifted, exps, stats = call(
-        functools.partial(rest_kernel, count, far),
+        functools.partial(rest_kernel, count, segments, far),
         [shifted_shape, exp_shape, stats_shape],
         [],
         work * len(far),
@@ -522,13 +576,17 @@
         distance *= 2
         other = exchange(mine, "cls", distance)
     low_bit = lambda b: b & -b
-    early = list(range(doms - 1, 1, -2))
-    order = early + [1] + sorted(range(2, doms, 2), key=lambda b: (low_bit(b), -b))
+    early = list(range(doms - 1, 0, -2))
+    order = early + sorted(range(2, doms, 2), key=lambda b: (low_bit(b), -b))
     extents = {b: width + 3 + (doms - 1 - place) * growth for place, b in enumerate(order)}
-    late = [1] + list(range(0, doms, 2))
-    weights, mass, *made = call(
-        functools.partial(first_sums_kernel, count, doms, width, early),
-        [shape((ROTS * classes, count * rows), bf16), shape((classes, LANES), f32)]
+    late = list(range(0, doms, 2))
+    weights, mass, tails, *made = call(
+        functools.partial(first_sums_kernel, count, doms, width, main, early),
+        [
+            shape((ROTS * classes, count * rows), bf16),
+            shape((classes, LANES), f32),
+            shape((classes, doms * ANG if main else LANES), f32),
+        ]
         + [shape((classes, extents[b]), bf16) for b in early],
         [],
         2 * count * rows * COLS * ROTS * classes // doms,
@@ -540,19 +598,16 @@
     for b, block in zip(early, made):
         incoming[b ^ 1].append(exchange(block, "dom", 1))
     rest = call(
-        functools.partial(rest_sums_kernel, doms, width, late),
-        [
-            shape((classes, extents.get(b, width + 3)), bf16 if b == 1 else f32) for b in late
-        ],
+        functools.partial(rest_sums_kernel, doms, width, main, late),
+        [shape((classes, width + 3), f32) for b in late],
         [],
         1024,
         1024,
-        weights, shifted, mass, *made,
+        weights, shifted, mass, tails, *made,
         chip=(1,),
     )
     blocks = dict(zip(late, rest))
-    incoming[0].append(exchange(blocks[1], "dom", 1))
-    for b in order[len(early) + 1 :]:
+    for b in order[len(early) :]:
         (block,) = call(
             functools.partial(add_kernel, width),
             [shape((classes, extents[b]), bf16)],

time: 30.8 us -> 30.8 us (level)
  waiting for transfers between devices: 7 us -> 8.35 us
  Pallas kernels: 13 us -> 11.8 us
    ppermute x8, waiting for transfers between devices: 7 us -> 8.35 us  [exchange(): lax.ppermute(array, axis, [(i, i ^ distance) for i in range(lax.axis_size...]
    pallas_call x8, Pallas kernels: 13 us -> 11.8 us  [call(): pl.pallas_call(kernel, out_shape=[pltpu.VMEM(s.shape, s.dtype) if pinned...]
  transfers between devices with their start and end apart: 8 -> 8, of which waited for: 5 -> 5; matrix products, arithmetic and copies ran while one was open for 0% -> 0% of each run, Pallas kernels for 21% -> 16%
where the time goes in v8:
time: 30.8 us; the launch traced here: 30.6 us
  Pallas kernels  11.8 us (38%)
  starting transfers between devices  9.7 us (31%)
  waiting for transfers between devices  8.35 us (27%)
  between operations  0.67 us (2%)
    pallas_call x8, Pallas kernels, call(): pl.pallas_call(kernel, out_shape=[pltpu.VMEM(s.shape, s.dtype) if pinned...  11.8 us
    ppermute x8, starting transfers between devices, exchange(): lax.ppermute(array, axis, [(i, i ^ distance) for i in range(lax.axis_size...  9.7 us
    ppermute x8, waiting for transfers between devices, exchange(): lax.ppermute(array, axis, [(i, i ^ distance) for i in range(lax.axis_size...  8.35 us
  transfers between devices with their start and end apart: 8, of which 5 were waited for; matrix products, arithmetic and copies ran while one was open for 0% of the time, Pallas kernels for 16%

profile of v8, /device:TPU:0, one launch (start us, length us, event | category | flops | bytes accessed | tf_op | source)
XLA Modules:
  0.0 30.6 jit_solution(5305033336038148059)
XLA Ops:
  0.6 1.3 %shard_map.86 = (bf16[16,2432]{1,0:T(8,128)(2,1)S(1)}, bf16[64,2304]{1,0:T(8,128)(2,1)S(1)}, f32[1,64]{1,0:T(1,128)S(1)}, f32[48,2304]{1,0:T(8,128)S(1)}) custom-call(bf16[16,2304]{1,0:T(8,128)(2,1)} %particle_hbm.1, s32[16,16]{1,0:T(8,128)} %index_hbm.1, s32[1,16]{1,0:T(1,128)} %bitcast.4, s32[1,16]{1,0:T(1,128)} %bitcast.5, bf16[64,2304]{1,0:T(8,128)(2,1)} %class_hbm.1, ...), custom_call_target="tpu_custom_call" | custom-call | flops 36864 | bytes 147456 | tf_op jit(solution)/shard_map/pallas_call | solution.py:486
  1.9 0.5 %collective-permute-start.2 = (bf16[16,2432]{1,0:T(8,128)(2,1)S(1)}, bf16[16,2432]{1,0:T(8,128)(2,1)S(1)}, u32[]{:S(2)}, u32[]{:S(2)}) collective-permute-start(bf16[16,2432]{1,0:T(8,128)(2,1)S(1)} %get-tuple-element.24.refs_0_), channel_id=1, source_target_pairs={{0,1},{1,0},{2,3},{3,2},{4,5},{5,4},{6,7},{7,6},{8,9},{9,8},{10,11... | collective-permute-start | bytes 233480 | tf_op jit(solution)/shard_map/ppermute | solution.py:107
  2.4 2.6 %collective-permute-start.1 = (bf16[16,2432]{1,0:T(8,128)(2,1)S(1)}, bf16[16,2432]{1,0:T(8,128)(2,1)S(1)}, u32[]{:S(2)}, u32[]{:S(2)}) collective-permute-start(bf16[16,2432]{1,0:T(8,128)(2,1)S(1)} %get-tuple-element.24.refs_0_), channel_id=1, source_target_pairs={{0,3},{1,2},{2,1},{3,0},{4,7},{5,6},{6,5},{7,4},{8,11},{9,10},{10,... | collective-permute-start | bytes 233480 | tf_op jit(solution)/shard_map/ppermute | solution.py:107
  5.0 0.0 collective-permute-start
  5.1 0.0 collective-permute-done.2.refs_1_
  5.1 3.3 %shard_map.87 = (bf16[1024,2304]{1,0:T(8,128)(2,1)S(1)}, f32[512,1024]{1,0:T(8,128)S(1)}, f32[16,128]{1,0:T(8,128)S(1)}, bf16[512,2304]{1,0:T(8,128)(2,1)S(1)}, ...) custom-call(bf16[16,2432]{1,0:T(8,128)(2,1)S(1)} %get-tuple-element.24.refs_0_, ...), custom_call_target="tpu_custom_call" | custom-call | flops 1811939328 | bytes 4718592 | tf_op jit(solution)/shard_map/pallas_call | solution.py:486
  8.4 0.0 collective-permute-done.1.refs_1_
  8.4 1.2 %collective-permute-done.refs_0_ = bf16[16,2432]{1,0:T(8,128)(2,1)S(1)} collective-permute-done((bf16[16,2432]{1,0:T(8,128)(2,1)S(1)}, bf16[16,2432]{1,0:T(8,128)(2,1)S(1)}, u32[]{:S(2)}, u32[]{:S(2)}) %collective-permute-start) | collective-permute-done | bytes 77856 | tf_op jit(solution)/shard_map/ppermute | solution.py:107
  9.6 2.8 %shard_map.88 = (bf16[1024,2304]{1,0:T(8,128)(2,1)S(1)}, f32[512,1024]{1,0:T(8,128)S(1)}, f32[16,128]{1,0:T(8,128)S(1)}) custom-call(bf16[16,2432]{1,0:T(8,128)(2,1)S(1)} %collective-permute-done.refs_0_, bf16[16,2432]{1,0:T(8,128)(2,1)S(1)} %collective-permute-done.1.refs_1_, ...), custom_call_target="tpu_custom_call", output_to_operand_aliasing={{0}: (7, {}), {1}: (8, {})} | custom-call | flops 1811939328 | bytes 4718592 | tf_op jit(solution)/shard_map/pallas_call | solution.py:486
  12.4 0.0 collective-permute-start.3
  12.4 1.2 %collective-permute-done.3.other = f32[16,128]{1,0:T(8,128)S(1)} collective-permute-done((f32[16,128]{1,0:T(8,128)S(1)}, f32[16,128]{1,0:T(8,128)S(1)}, u32[]{:S(2)}, u32[]{:S(2)}) %collective-permute-start.3) | collective-permute-done | bytes 8224 | tf_op jit(solution)/shard_map/ppermute | solution.py:107
  13.6 1.8 %collective-permute-start.4 = (f32[8,128]{1,0:T(8,128)S(1)}, f32[8,128]{1,0:T(8,128)S(1)}, u32[]{:S(2)}, u32[]{:S(2)}) collective-permute-start(f32[8,128]{1,0:T(8,128)S(1)} %shard_map.89.refs_1_), channel_id=1, source_target_pairs={{0,2},{1,3},{2,0},{3,1},{4,6},{5,7},{6,4},{7,5},{8,10},{9,11},{10,... | collective-permute-start | bytes 12296 | tf_op jit(solution)/shard_map/ppermute | solution.py:107
  15.4 1.9 %collective-permute-done.4.refs_2_ = f32[8,128]{1,0:T(8,128)S(1)} collective-permute-done((f32[8,128]{1,0:T(8,128)S(1)}, f32[8,128]{1,0:T(8,128)S(1)}, u32[]{:S(2)}, u32[]{:S(2)}) %collective-permute-start.4) | collective-permute-done | bytes 4128 | tf_op jit(solution)/shard_map/ppermute | solution.py:107
  17.3 2.1 %shard_map.90 = (bf16[512,1024]{1,0:T(8,128)(2,1)S(1)}, f32[64,128]{1,0:T(8,128)S(1)}, f32[64,256]{1,0:T(8,128)S(1)}, bf16[64,639]{1,0:T(8,128)(2,1)S(1)}, bf16[64,619]{1,0:T(8,128)(2,1)S(1)}) custom-call(f32[16,128]{1,0:T(8,128)S(1)} %get-tuple-element.34.mine.refs_0_, f32[8,128]{1,0:T(8,128)S(1)} %shard_map.89.refs_1_, ...), custom_call_target="tpu_custom_call" | custom-call | flops 603979776 | bytes 2359296 | tf_op jit(solution)/shard_map/pallas_call | solution.py:486
  19.3 1.9 %collective-permute-start.6 = (bf16[64,639]{1,0:T(8,128)(2,1)S(1)}, bf16[64,639]{1,0:T(8,128)(2,1)S(1)}, u32[]{:S(2)}, u32[]{:S(2)}) collective-permute-start(bf16[64,639]{1,0:T(8,128)(2,1)S(1)} %get-tuple-element.40.refs_0_), channel_id=1, source_target_pairs={{0,4},{4,0},{8,12},{12,8},{1,5},{5,1},{9,13},{13,9},{2,6},{6,2},{1... | collective-permute-start | bytes 245384 | tf_op jit(solution)/shard_map/ppermute | solution.py:107
  21.2 0.2 collective-permute-start.5
  21.4 1.6 %shard_map.91 = (f32[64,579]{1,0:T(8,128)S(1)}, f32[64,579]{1,0:T(8,128)S(1)}) custom-call(bf16[512,1024]{1,0:T(8,128)(2,1)S(1)} %get-tuple-element.37.weight_ref, bf16[1024,2304]{1,0:T(8,128)(2,1)S(1)} %get-tuple-element.36.refs_4_.shifted_ref, f32[64,128]{1,0:T(8,128)S(1)} %get-tuple-element.38.mass_ref, f32[64,256]{1,0:T(8,128)S(1)} %get-tuple-element.39.tails_ref, ...), custom_call_target="tpu_custom_call" | custom-call | flops 1024 | bytes 1024 | tf_op jit(solution)/shard_map/pallas_call | solution.py:486
  23.0 1.3 %collective-permute-done.6.refs_1_ = bf16[64,639]{1,0:T(8,128)(2,1)S(1)} collective-permute-done((bf16[64,639]{1,0:T(8,128)(2,1)S(1)}, bf16[64,639]{1,0:T(8,128)(2,1)S(1)}, u32[]{:S(2)}, u32[]{:S(2)}) %collective-permute-start.6) | collective-permute-done | bytes 81824 | tf_op jit(solution)/shard_map/ppermute | solution.py:107
  24.3 0.1 shard_map.92
  24.4 2.7 %collective-permute-start.7 = (bf16[64,599]{1,0:T(8,128)(2,1)S(1)}, bf16[64,599]{1,0:T(8,128)(2,1)S(1)}, u32[]{:S(2)}, u32[]{:S(2)}) collective-permute-start(bf16[64,599]{1,0:T(8,128)(2,1)S(1)} %shard_map.92), channel_id=1, source_target_pairs={{0,8},{4,12},{8,0},{12,4},{1,9},{5,13},{9,1},{13,5},{2,10},{6,14},... | collective-permute-start | bytes 230024 | tf_op jit(solution)/shard_map/ppermute | solution.py:107
  27.1 0.0 collective-permute-done.5.refs_0_
  27.1 2.8 %collective-permute-done.7.refs_1_ = bf16[64,599]{1,0:T(8,128)(2,1)S(1)} collective-permute-done((bf16[64,599]{1,0:T(8,128)(2,1)S(1)}, bf16[64,599]{1,0:T(8,128)(2,1)S(1)}, u32[]{:S(2)}, u32[]{:S(2)}) %collective-permute-start.7) | collective-permute-done | bytes 76704 | tf_op jit(solution)/shard_map/ppermute | solution.py:107
  29.8 0.7 %shard_map.93 = (f32[64,576]{1,0:T(8,128)}, f32[1,64]{1,0:T(1,128)}) custom-call(f32[64,579]{1,0:T(8,128)S(1)} %get-tuple-element.42.own_ref, bf16[64,619]{1,0:T(8,128)(2,1)S(1)} %collective-permute-done.5.refs_0_, bf16[64,599]{1,0:T(8,128)(2,1)S(1)} %collective-permute-done.7.refs_1_), custom_call_target="tpu_custom_call" | custom-call | flops 163840 | bytes 655360 | tf_op jit(solution)/shard_map/pallas_call | solution.py:486
  (1 shorter events, 0.0 us)
Async XLA Ops:
  1.9 3.2 %collective-permute-start.2 = (bf16[16,2432]{1,0:T(8,128)(2,1)S(1)}, bf16[16,2432]{1,0:T(8,128)(2,1)S(1)}, u32[]{:S(2)}, u32[]{:S(2)}) collective-permute-start(bf16[16,2432]{1,0:T(8,128)(2,1)S(1)} %get-tuple-element.24.refs_0_), channel_id=1, source_target_pairs={{0,1},{1,0},{2,3},{3,2},{4,5},{5,4},{6,7},{7,6},{8,9},{9,8},{10,11... | collective-permute-start | bytes 233480 | tf_op jit(solution)/shard_map/ppermute | solution.py:107
  2.4 6.0 %collective-permute-start.1 = (bf16[16,2432]{1,0:T(8,128)(2,1)S(1)}, bf16[16,2432]{1,0:T(8,128)(2,1)S(1)}, u32[]{:S(2)}, u32[]{:S(2)}) collective-permute-start(bf16[16,2432]{1,0:T(8,128)(2,1)S(1)} %get-tuple-element.24.refs_0_), channel_id=1, source_target_pairs={{0,3},{1,2},{2,1},{3,0},{4,7},{5,6},{6,5},{7,4},{8,11},{9,10},{10,... | collective-permute-start | bytes 233480 | tf_op jit(solution)/shard_map/ppermute | solution.py:107
  5.0 4.6 %collective-permute-start = (bf16[16,2432]{1,0:T(8,128)(2,1)S(1)}, bf16[16,2432]{1,0:T(8,128)(2,1)S(1)}, u32[]{:S(2)}, u32[]{:S(2)}) collective-permute-start(bf16[16,2432]{1,0:T(8,128)(2,1)S(1)} %get-tuple-element.24.refs_0_), channel_id=1, source_target_pairs={{0,2},{1,3},{2,0},{3,1},{4,6},{5,7},{6,4},{7,5},{8,10},{9,11},{10,... | collective-permute-start | bytes 233480 | tf_op jit(solution)/shard_map/ppermute | solution.py:107
  12.4 1.2 %collective-permute-start.3 = (f32[16,128]{1,0:T(8,128)S(1)}, f32[16,128]{1,0:T(8,128)S(1)}, u32[]{:S(2)}, u32[]{:S(2)}) collective-permute-start(f32[16,128]{1,0:T(8,128)S(1)} %get-tuple-element.34.mine.refs_0_), channel_id=1, source_target_pairs={{0,1},{1,0},{2,3},{3,2},{4,5},{5,4},{6,7},{7,6},{8,9},{9,8},{10,11... | collective-permute-start | bytes 24584 | tf_op jit(solution)/shard_map/ppermute | solution.py:107
  13.6 3.7 %collective-permute-start.4 = (f32[8,128]{1,0:T(8,128)S(1)}, f32[8,128]{1,0:T(8,128)S(1)}, u32[]{:S(2)}, u32[]{:S(2)}) collective-permute-start(f32[8,128]{1,0:T(8,128)S(1)} %shard_map.89.refs_1_), channel_id=1, source_target_pairs={{0,2},{1,3},{2,0},{3,1},{4,6},{5,7},{6,4},{7,5},{8,10},{9,11},{10,... | collective-permute-start | bytes 12296 | tf_op jit(solution)/shard_map/ppermute | solution.py:107
  19.3 5.0 %collective-permute-start.6 = (bf16[64,639]{1,0:T(8,128)(2,1)S(1)}, bf16[64,639]{1,0:T(8,128)(2,1)S(1)}, u32[]{:S(2)}, u32[]{:S(2)}) collective-permute-start(bf16[64,639]{1,0:T(8,128)(2,1)S(1)} %get-tuple-element.40.refs_0_), channel_id=1, source_target_pairs={{0,4},{4,0},{8,12},{12,8},{1,5},{5,1},{9,13},{13,9},{2,6},{6,2},{1... | collective-permute-start | bytes 245384 | tf_op jit(solution)/shard_map/ppermute | solution.py:107
  21.2 5.9 %collective-permute-start.5 = (bf16[64,619]{1,0:T(8,128)(2,1)S(1)}, bf16[64,619]{1,0:T(8,128)(2,1)S(1)}, u32[]{:S(2)}, u32[]{:S(2)}) collective-permute-start(bf16[64,619]{1,0:T(8,128)(2,1)S(1)} %get-tuple-element.41.refs_1_), channel_id=1, source_target_pairs={{0,4},{4,0},{8,12},{12,8},{1,5},{5,1},{9,13},{13,9},{2,6},{6,2},{1... | collective-permute-start | bytes 237704 | tf_op jit(solution)/shard_map/ppermute | solution.py:107
  24.4 5.4 %collective-permute-start.7 = (bf16[64,599]{1,0:T(8,128)(2,1)S(1)}, bf16[64,599]{1,0:T(8,128)(2,1)S(1)}, u32[]{:S(2)}, u32[]{:S(2)}) collective-permute-start(bf16[64,599]{1,0:T(8,128)(2,1)S(1)} %shard_map.92), channel_id=1, source_target_pairs={{0,8},{4,12},{8,0},{12,4},{1,9},{5,13},{9,1},{13,5},{2,10},{6,14},... | collective-permute-start | bytes 230024 | tf_op jit(solution)/shard_map/ppermute | solution.py:107

commit v9 on v8

--- a/solution.py
+++ b/solution.py
@@ -449,18 +449,6 @@
         store_block(width, value, mass_ref[:, :1], out_ref)
 
 
-def add_kernel(width, *refs):
-    out_ref = refs[-1]
-    padded = -(-out_ref.shape[1] // LANES) * LANES
-    total, mass = None, None
-    for ref in refs[:-1]:
-        value = pad_columns(ref[...].astype(jnp.float32), padded)
-        total = value if total is None else total + value
-        tail = received_mass(width, ref)
-        mass = tail if mass is None else mass + tail
-    store_block(width, total, mass, out_ref)
-
-
 def final_kernel(width, own_ref, *refs):
     received, sums_ref, weights_ref = refs[:-2], refs[-2], refs[-1]
     total, mass = None, None
@@ -575,11 +563,8 @@
         )
         distance *= 2
         other = exchange(mine, "cls", distance)
-    low_bit = lambda b: b & -b
-    early = list(range(doms - 1, 0, -2))
-    order = early + sorted(range(2, doms, 2), key=lambda b: (low_bit(b), -b))
-    extents = {b: width + 3 + (doms - 1 - place) * growth for place, b in enumerate(order)}
-    late = list(range(0, doms, 2))
+    early, late = [doms - 1], list(range(doms - 2, -1, -1))
+    extents = {b: width + 3 + b * growth for b in range(doms)}
     weights, mass, tails, *made = call(
         functools.partial(first_sums_kernel, count, doms, width, main, early),
         [
@@ -594,30 +579,18 @@
         stats, mine, other, exps, shifted,
         chip=(3, 4),
     )
-    incoming = {b: [] for b in range(doms)}
-    for b, block in zip(early, made):
-        incoming[b ^ 1].append(exchange(block, "dom", 1))
     rest = call(
         functools.partial(rest_sums_kernel, doms, width, main, late),
-        [shape((classes, width + 3), f32) for b in late],
+        [shape((classes, extents[b]), bf16 if b else f32) for b in late],
         [],
         1024,
         1024,
         weights, shifted, mass, tails, *made,
         chip=(1,),
     )
-    blocks = dict(zip(late, rest))
-    for b in order[len(early) :]:
-        (block,) = call(
-            functools.partial(add_kernel, width),
-            [shape((classes, extents[b]), bf16)],
-            [],
-            1024,
-            1024,
-            blocks[b], *incoming[b],
-        )
-        incoming[b ^ low_bit(b)].append(exchange(block, "dom", low_bit(b)))
-    own, received = blocks[0], incoming[0]
+    blocks = dict(zip(early + late, [*made, *rest]))
+    own = blocks[0]
+    received = [exchange(blocks[b], "dom", b) for b in range(doms - 1, 0, -1)]
     class_sums, class_weights = call(
         functools.partial(final_kernel, width),
         [shape((classes, width), f32), shape((1, classes), f32)],

time: 30.8 us -> 31.5 us (1.023)
  waiting for transfers between devices: 8.35 us -> 9.42 us
    ppermute x8, waiting for transfers between devices: 8.35 us -> 9.42 us  [exchange(): lax.ppermute(array, axis, [(i, i ^ distance) for i in range(lax.axis_size...]
    pallas_call x8 -> x7, Pallas kernels: 11.8 us -> 11.7 us  [call(): pl.pallas_call(kernel, out_shape=[pltpu.VMEM(s.shape, s.dtype) if pinned...]
  transfers between devices with their start and end apart: 8 -> 8, of which waited for: 5 -> 5; matrix products, arithmetic and copies ran while one was open for 0% -> 0% of each run, Pallas kernels for 16% -> 17%
where the time goes in v9:
time: 31.5 us; the launch traced here: 31.3 us
  Pallas kernels  11.7 us (37%)
  starting transfers between devices  9.48 us (30%)
  waiting for transfers between devices  9.42 us (30%)
  between operations  0.67 us (2%)
    pallas_call x7, Pallas kernels, call(): pl.pallas_call(kernel, out_shape=[pltpu.VMEM(s.shape, s.dtype) if pinned...  11.7 us
    ppermute x8, starting transfers between devices, exchange(): lax.ppermute(array, axis, [(i, i ^ distance) for i in range(lax.axis_size...  9.48 us
    ppermute x8, waiting for transfers between devices, exchange(): lax.ppermute(array, axis, [(i, i ^ distance) for i in range(lax.axis_size...  9.42 us
  transfers between devices with their start and end apart: 8, of which 5 were waited for; matrix products, arithmetic and copies ran while one was open for 0% of the time, Pallas kernels for 17%

profile of v9, /device:TPU:0, one launch (start us, length us, event | category | flops | bytes accessed | tf_op | source)
XLA Modules:
  0.0 31.3 jit_solution(13485628261775891182)
XLA Ops:
  0.6 1.3 %shard_map.86 = (bf16[16,2432]{1,0:T(8,128)(2,1)S(1)}, bf16[64,2304]{1,0:T(8,128)(2,1)S(1)}, f32[1,64]{1,0:T(1,128)S(1)}, f32[48,2304]{1,0:T(8,128)S(1)}) custom-call(bf16[16,2304]{1,0:T(8,128)(2,1)} %particle_hbm.1, s32[16,16]{1,0:T(8,128)} %index_hbm.1, s32[1,16]{1,0:T(1,128)} %bitcast.4, s32[1,16]{1,0:T(1,128)} %bitcast.5, bf16[64,2304]{1,0:T(8,128)(2,1)} %class_hbm.1, ...), custom_call_target="tpu_custom_call" | custom-call | flops 36864 | bytes 147456 | tf_op jit(solution)/shard_map/pallas_call | solution.py:474
  1.9 0.5 %collective-permute-start.2 = (bf16[16,2432]{1,0:T(8,128)(2,1)S(1)}, bf16[16,2432]{1,0:T(8,128)(2,1)S(1)}, u32[]{:S(2)}, u32[]{:S(2)}) collective-permute-start(bf16[16,2432]{1,0:T(8,128)(2,1)S(1)} %get-tuple-element.24.refs_0_), channel_id=1, source_target_pairs={{0,1},{1,0},{2,3},{3,2},{4,5},{5,4},{6,7},{7,6},{8,9},{9,8},{10,11... | collective-permute-start | bytes 233480 | tf_op jit(solution)/shard_map/ppermute | solution.py:107
  2.4 2.6 %collective-permute-start.1 = (bf16[16,2432]{1,0:T(8,128)(2,1)S(1)}, bf16[16,2432]{1,0:T(8,128)(2,1)S(1)}, u32[]{:S(2)}, u32[]{:S(2)}) collective-permute-start(bf16[16,2432]{1,0:T(8,128)(2,1)S(1)} %get-tuple-element.24.refs_0_), channel_id=1, source_target_pairs={{0,3},{1,2},{2,1},{3,0},{4,7},{5,6},{6,5},{7,4},{8,11},{9,10},{10,... | collective-permute-start | bytes 233480 | tf_op jit(solution)/shard_map/ppermute | solution.py:107
  5.0 0.0 collective-permute-start
  5.1 0.0 collective-permute-done.2.refs_1_
  5.1 3.3 %shard_map.87 = (bf16[1024,2304]{1,0:T(8,128)(2,1)S(1)}, f32[512,1024]{1,0:T(8,128)S(1)}, f32[16,128]{1,0:T(8,128)S(1)}, bf16[512,2304]{1,0:T(8,128)(2,1)S(1)}, ...) custom-call(bf16[16,2432]{1,0:T(8,128)(2,1)S(1)} %get-tuple-element.24.refs_0_, ...), custom_call_target="tpu_custom_call" | custom-call | flops 1811939328 | bytes 4718592 | tf_op jit(solution)/shard_map/pallas_call | solution.py:474
  8.4 0.0 collective-permute-done.1.refs_1_
  8.4 1.2 %collective-permute-done.refs_0_ = bf16[16,2432]{1,0:T(8,128)(2,1)S(1)} collective-permute-done((bf16[16,2432]{1,0:T(8,128)(2,1)S(1)}, bf16[16,2432]{1,0:T(8,128)(2,1)S(1)}, u32[]{:S(2)}, u32[]{:S(2)}) %collective-permute-start) | collective-permute-done | bytes 77856 | tf_op jit(solution)/shard_map/ppermute | solution.py:107
  9.6 2.8 %shard_map.88 = (bf16[1024,2304]{1,0:T(8,128)(2,1)S(1)}, f32[512,1024]{1,0:T(8,128)S(1)}, f32[16,128]{1,0:T(8,128)S(1)}) custom-call(bf16[16,2432]{1,0:T(8,128)(2,1)S(1)} %collective-permute-done.refs_0_, bf16[16,2432]{1,0:T(8,128)(2,1)S(1)} %collective-permute-done.1.refs_1_, ...), custom_call_target="tpu_custom_call", output_to_operand_aliasing={{0}: (7, {}), {1}: (8, {})} | custom-call | flops 1811939328 | bytes 4718592 | tf_op jit(solution)/shard_map/pallas_call | solution.py:474
  12.4 0.0 collective-permute-start.3
  12.4 1.2 %collective-permute-done.3.other = f32[16,128]{1,0:T(8,128)S(1)} collective-permute-done((f32[16,128]{1,0:T(8,128)S(1)}, f32[16,128]{1,0:T(8,128)S(1)}, u32[]{:S(2)}, u32[]{:S(2)}) %collective-permute-start.3) | collective-permute-done | bytes 8224 | tf_op jit(solution)/shard_map/ppermute | solution.py:107
  13.6 1.8 %collective-permute-start.4 = (f32[8,128]{1,0:T(8,128)S(1)}, f32[8,128]{1,0:T(8,128)S(1)}, u32[]{:S(2)}, u32[]{:S(2)}) collective-permute-start(f32[8,128]{1,0:T(8,128)S(1)} %shard_map.89.refs_1_), channel_id=1, source_target_pairs={{0,2},{1,3},{2,0},{3,1},{4,6},{5,7},{6,4},{7,5},{8,10},{9,11},{10,... | collective-permute-start | bytes 12296 | tf_op jit(solution)/shard_map/ppermute | solution.py:107
  15.4 1.9 %collective-permute-done.4.refs_2_ = f32[8,128]{1,0:T(8,128)S(1)} collective-permute-done((f32[8,128]{1,0:T(8,128)S(1)}, f32[8,128]{1,0:T(8,128)S(1)}, u32[]{:S(2)}, u32[]{:S(2)}) %collective-permute-start.4) | collective-permute-done | bytes 4128 | tf_op jit(solution)/shard_map/ppermute | solution.py:107
  17.3 1.5 %shard_map.90 = (bf16[512,1024]{1,0:T(8,128)(2,1)S(1)}, f32[64,128]{1,0:T(8,128)S(1)}, f32[64,256]{1,0:T(8,128)S(1)}, bf16[64,639]{1,0:T(8,128)(2,1)S(1)}) custom-call(f32[16,128]{1,0:T(8,128)S(1)} %get-tuple-element.34.mine.refs_0_, f32[8,128]{1,0:T(8,128)S(1)} %shard_map.89.refs_1_, f32[8,128]{1,0:T(8,128)S(1)} %collective-permute-done.4.refs_2_, ...), custom_call_target="tpu_custom_call" | custom-call | flops 603979776 | bytes 2359296 | tf_op jit(solution)/shard_map/pallas_call | solution.py:474
  18.7 3.9 %collective-permute-start.5 = (bf16[64,639]{1,0:T(8,128)(2,1)S(1)}, bf16[64,639]{1,0:T(8,128)(2,1)S(1)}, u32[]{:S(2)}, u32[]{:S(2)}) collective-permute-start(bf16[64,639]{1,0:T(8,128)(2,1)S(1)} %get-tuple-element.40.refs_0_), channel_id=1, source_target_pairs={{0,12},{4,8},{8,4},{12,0},{1,13},{5,9},{9,5},{13,1},{2,14},{6,10},... | collective-permute-start | bytes 245384 | tf_op jit(solution)/shard_map/ppermute | solution.py:107
  22.6 2.1 %shard_map.91 = (bf16[64,619]{1,0:T(8,128)(2,1)S(1)}, bf16[64,599]{1,0:T(8,128)(2,1)S(1)}, f32[64,579]{1,0:T(8,128)S(1)}) custom-call(bf16[512,1024]{1,0:T(8,128)(2,1)S(1)} %get-tuple-element.37.weight_ref, bf16[1024,2304]{1,0:T(8,128)(2,1)S(1)} %get-tuple-element.36.refs_4_.shifted_ref, f32[64,128]{1,0:T(8,128)S(1)} %get-tuple-element.38.mass_ref, ...), custom_call_target="tpu_custom_call" | custom-call | flops 1024 | bytes 1024 | tf_op jit(solution)/shard_map/pallas_call | solution.py:474
  24.8 0.1 collective-permute-start.6
  24.8 0.6 %collective-permute-start.7 = (bf16[64,599]{1,0:T(8,128)(2,1)S(1)}, bf16[64,599]{1,0:T(8,128)(2,1)S(1)}, u32[]{:S(2)}, u32[]{:S(2)}) collective-permute-start(bf16[64,599]{1,0:T(8,128)(2,1)S(1)} %get-tuple-element.43), channel_id=1, source_target_pairs={{0,4},{4,0},{8,12},{12,8},{1,5},{5,1},{9,13},{13,9},{2,6},{6,2},{1... | collective-permute-start | bytes 230024 | tf_op jit(solution)/shard_map/ppermute | solution.py:107
  25.4 4.0 %collective-permute-done.7.refs_2_ = bf16[64,599]{1,0:T(8,128)(2,1)S(1)} collective-permute-done((bf16[64,599]{1,0:T(8,128)(2,1)S(1)}, bf16[64,599]{1,0:T(8,128)(2,1)S(1)}, u32[]{:S(2)}, u32[]{:S(2)}) %collective-permute-start.7) | collective-permute-done | bytes 76704 | tf_op jit(solution)/shard_map/ppermute | solution.py:107
  29.4 1.1 %collective-permute-done.6.refs_1_ = bf16[64,619]{1,0:T(8,128)(2,1)S(1)} collective-permute-done((bf16[64,619]{1,0:T(8,128)(2,1)S(1)}, bf16[64,619]{1,0:T(8,128)(2,1)S(1)}, u32[]{:S(2)}, u32[]{:S(2)}) %collective-permute-start.6) | collective-permute-done | bytes 79264 | tf_op jit(solution)/shard_map/ppermute | solution.py:107
  30.5 0.0 collective-permute-done.5.refs_0_
  30.5 0.7 %shard_map.92 = (f32[64,576]{1,0:T(8,128)}, f32[1,64]{1,0:T(1,128)}) custom-call(f32[64,579]{1,0:T(8,128)S(1)} %get-tuple-element.41.own_ref, bf16[64,639]{1,0:T(8,128)(2,1)S(1)} %collective-permute-done.5.refs_0_, bf16[64,619]{1,0:T(8,128)(2,1)S(1)} %collective-permute-done.6.refs_1_, bf16[64,599]{1,0:T(8,128)(2,1)S(1)} %collective-permute-done.7.refs_2_), custom_call_target="tpu_custom_call" | custom-call | flops 163840 | bytes 655360 | tf_op jit(solution)/shard_map/pallas_call | solution.py:474
  (1 shorter events, 0.0 us)
Async XLA Ops:
  1.9 3.2 %collective-permute-start.2 = (bf16[16,2432]{1,0:T(8,128)(2,1)S(1)}, bf16[16,2432]{1,0:T(8,128)(2,1)S(1)}, u32[]{:S(2)}, u32[]{:S(2)}) collective-permute-start(bf16[16,2432]{1,0:T(8,128)(2,1)S(1)} %get-tuple-element.24.refs_0_), channel_id=1, source_target_pairs={{0,1},{1,0},{2,3},{3,2},{4,5},{5,4},{6,7},{7,6},{8,9},{9,8},{10,11... | collective-permute-start | bytes 233480 | tf_op jit(solution)/shard_map/ppermute | solution.py:107
  2.4 6.0 %collective-permute-start.1 = (bf16[16,2432]{1,0:T(8,128)(2,1)S(1)}, bf16[16,2432]{1,0:T(8,128)(2,1)S(1)}, u32[]{:S(2)}, u32[]{:S(2)}) collective-permute-start(bf16[16,2432]{1,0:T(8,128)(2,1)S(1)} %get-tuple-element.24.refs_0_), channel_id=1, source_target_pairs={{0,3},{1,2},{2,1},{3,0},{4,7},{5,6},{6,5},{7,4},{8,11},{9,10},{10,... | collective-permute-start | bytes 233480 | tf_op jit(solution)/shard_map/ppermute | solution.py:107
  5.0 4.6 %collective-permute-start = (bf16[16,2432]{1,0:T(8,128)(2,1)S(1)}, bf16[16,2432]{1,0:T(8,128)(2,1)S(1)}, u32[]{:S(2)}, u32[]{:S(2)}) collective-permute-start(bf16[16,2432]{1,0:T(8,128)(2,1)S(1)} %get-tuple-element.24.refs_0_), channel_id=1, source_target_pairs={{0,2},{1,3},{2,0},{3,1},{4,6},{5,7},{6,4},{7,5},{8,10},{9,11},{10,... | collective-permute-start | bytes 233480 | tf_op jit(solution)/shard_map/ppermute | solution.py:107
  12.4 1.2 %collective-permute-start.3 = (f32[16,128]{1,0:T(8,128)S(1)}, f32[16,128]{1,0:T(8,128)S(1)}, u32[]{:S(2)}, u32[]{:S(2)}) collective-permute-start(f32[16,128]{1,0:T(8,128)S(1)} %get-tuple-element.34.mine.refs_0_), channel_id=1, source_target_pairs={{0,1},{1,0},{2,3},{3,2},{4,5},{5,4},{6,7},{7,6},{8,9},{9,8},{10,11... | collective-permute-start | bytes 24584 | tf_op jit(solution)/shard_map/ppermute | solution.py:107
  13.6 3.7 %collective-permute-start.4 = (f32[8,128]{1,0:T(8,128)S(1)}, f32[8,128]{1,0:T(8,128)S(1)}, u32[]{:S(2)}, u32[]{:S(2)}) collective-permute-start(f32[8,128]{1,0:T(8,128)S(1)} %shard_map.89.refs_1_), channel_id=1, source_target_pairs={{0,2},{1,3},{2,0},{3,1},{4,6},{5,7},{6,4},{7,5},{8,10},{9,11},{10,... | collective-permute-start | bytes 12296 | tf_op jit(solution)/shard_map/ppermute | solution.py:107
  18.7 11.8 %collective-permute-start.5 = (bf16[64,639]{1,0:T(8,128)(2,1)S(1)}, bf16[64,639]{1,0:T(8,128)(2,1)S(1)}, u32[]{:S(2)}, u32[]{:S(2)}) collective-permute-start(bf16[64,639]{1,0:T(8,128)(2,1)S(1)} %get-tuple-element.40.refs_0_), channel_id=1, source_target_pairs={{0,12},{4,8},{8,4},{12,0},{1,13},{5,9},{9,5},{13,1},{2,14},{6,10},... | collective-permute-start | bytes 245384 | tf_op jit(solution)/shard_map/ppermute | solution.py:107
  24.8 5.8 %collective-permute-start.6 = (bf16[64,619]{1,0:T(8,128)(2,1)S(1)}, bf16[64,619]{1,0:T(8,128)(2,1)S(1)}, u32[]{:S(2)}, u32[]{:S(2)}) collective-permute-start(bf16[64,619]{1,0:T(8,128)(2,1)S(1)} %get-tuple-element.42), channel_id=1, source_target_pairs={{0,8},{4,12},{8,0},{12,4},{1,9},{5,13},{9,1},{13,5},{2,10},{6,14},... | collective-permute-start | bytes 237704 | tf_op jit(solution)/shard_map/ppermute | solution.py:107
  24.8 4.6 %collective-permute-start.7 = (bf16[64,599]{1,0:T(8,128)(2,1)S(1)}, bf16[64,599]{1,0:T(8,128)(2,1)S(1)}, u32[]{:S(2)}, u32[]{:S(2)}) collective-permute-start(bf16[64,599]{1,0:T(8,128)(2,1)S(1)} %get-tuple-element.43), channel_id=1, source_target_pairs={{0,4},{4,0},{8,12},{12,8},{1,5},{5,1},{9,13},{13,9},{2,6},{6,2},{1... | collective-permute-start | bytes 230024 | tf_op jit(solution)/shard_map/ppermute | solution.py:107

commit v10 on v9

--- a/solution.py
+++ b/solution.py
@@ -563,7 +563,7 @@
         )
         distance *= 2
         other = exchange(mine, "cls", distance)
-    early, late = [doms - 1], list(range(doms - 2, -1, -1))
+    early, late = list(range(doms - 1, 0, -1)), [0]
     extents = {b: width + 3 + b * growth for b in range(doms)}
     weights, mass, tails, *made = call(
         functools.partial(first_sums_kernel, count, doms, width, main, early),

time: 31.5 us -> 31.2 us (level)
  waiting for transfers between devices: 9.42 us -> 8.9 us
    ppermute x8, waiting for transfers between devices: 9.42 us -> 8.9 us  [exchange(): lax.ppermute(array, axis, [(i, i ^ distance) for i in range(lax.axis_size...]
  transfers between devices with their start and end apart: 8 -> 8, of which waited for: 5 -> 5; matrix products, arithmetic and copies ran while one was open for 0% -> 0% of each run, Pallas kernels for 17% -> 14%
where the time goes in v10:
time: 31.2 us; the launch traced here: 31 us
  Pallas kernels  11.9 us (38%)
  starting transfers between devices  9.49 us (30%)
  waiting for transfers between devices  8.9 us (29%)
  between operations  0.67 us (2%)
    pallas_call x7, Pallas kernels, call(): pl.pallas_call(kernel, out_shape=[pltpu.VMEM(s.shape, s.dtype) if pinned...  11.9 us
    ppermute x8, starting transfers between devices, exchange(): lax.ppermute(array, axis, [(i, i ^ distance) for i in range(lax.axis_size...  9.49 us
    ppermute x8, waiting for transfers between devices, exchange(): lax.ppermute(array, axis, [(i, i ^ distance) for i in range(lax.axis_size...  8.9 us
  transfers between devices with their start and end apart: 8, of which 5 were waited for; matrix products, arithmetic and copies ran while one was open for 0% of the time, Pallas kernels for 14%

profile of v10, /device:TPU:0, one launch (start us, length us, event | category | flops | bytes accessed | tf_op | source)
XLA Modules:
  0.0 31.0 jit_solution(5651465522823459736)
XLA Ops:
  0.6 1.3 %shard_map.86 = (bf16[16,2432]{1,0:T(8,128)(2,1)S(1)}, bf16[64,2304]{1,0:T(8,128)(2,1)S(1)}, f32[1,64]{1,0:T(1,128)S(1)}, f32[48,2304]{1,0:T(8,128)S(1)}) custom-call(bf16[16,2304]{1,0:T(8,128)(2,1)} %particle_hbm.1, s32[16,16]{1,0:T(8,128)} %index_hbm.1, s32[1,16]{1,0:T(1,128)} %bitcast.4, s32[1,16]{1,0:T(1,128)} %bitcast.5, bf16[64,2304]{1,0:T(8,128)(2,1)} %class_hbm.1, ...), custom_call_target="tpu_custom_call" | custom-call | flops 36864 | bytes 147456 | tf_op jit(solution)/shard_map/pallas_call | solution.py:474
  1.9 0.5 %collective-permute-start.2 = (bf16[16,2432]{1,0:T(8,128)(2,1)S(1)}, bf16[16,2432]{1,0:T(8,128)(2,1)S(1)}, u32[]{:S(2)}, u32[]{:S(2)}) collective-permute-start(bf16[16,2432]{1,0:T(8,128)(2,1)S(1)} %get-tuple-element.23.refs_0_), channel_id=1, source_target_pairs={{0,1},{1,0},{2,3},{3,2},{4,5},{5,4},{6,7},{7,6},{8,9},{9,8},{10,11... | collective-permute-start | bytes 233480 | tf_op jit(solution)/shard_map/ppermute | solution.py:107
  2.4 2.6 %collective-permute-start.1 = (bf16[16,2432]{1,0:T(8,128)(2,1)S(1)}, bf16[16,2432]{1,0:T(8,128)(2,1)S(1)}, u32[]{:S(2)}, u32[]{:S(2)}) collective-permute-start(bf16[16,2432]{1,0:T(8,128)(2,1)S(1)} %get-tuple-element.23.refs_0_), channel_id=1, source_target_pairs={{0,3},{1,2},{2,1},{3,0},{4,7},{5,6},{6,5},{7,4},{8,11},{9,10},{10,... | collective-permute-start | bytes 233480 | tf_op jit(solution)/shard_map/ppermute | solution.py:107
  5.0 0.0 collective-permute-start
  5.1 0.0 collective-permute-done.2.refs_1_
  5.1 3.3 %shard_map.87 = (bf16[1024,2304]{1,0:T(8,128)(2,1)S(1)}, f32[512,1024]{1,0:T(8,128)S(1)}, f32[16,128]{1,0:T(8,128)S(1)}, bf16[512,2304]{1,0:T(8,128)(2,1)S(1)}, ...) custom-call(bf16[16,2432]{1,0:T(8,128)(2,1)S(1)} %get-tuple-element.23.refs_0_, ...), custom_call_target="tpu_custom_call" | custom-call | flops 1811939328 | bytes 4718592 | tf_op jit(solution)/shard_map/pallas_call | solution.py:474
  8.4 0.0 collective-permute-done.1.refs_1_
  8.4 1.2 %collective-permute-done.refs_0_ = bf16[16,2432]{1,0:T(8,128)(2,1)S(1)} collective-permute-done((bf16[16,2432]{1,0:T(8,128)(2,1)S(1)}, bf16[16,2432]{1,0:T(8,128)(2,1)S(1)}, u32[]{:S(2)}, u32[]{:S(2)}) %collective-permute-start) | collective-permute-done | bytes 77856 | tf_op jit(solution)/shard_map/ppermute | solution.py:107
  9.6 2.8 %shard_map.88 = (bf16[1024,2304]{1,0:T(8,128)(2,1)S(1)}, f32[512,1024]{1,0:T(8,128)S(1)}, f32[16,128]{1,0:T(8,128)S(1)}) custom-call(bf16[16,2432]{1,0:T(8,128)(2,1)S(1)} %collective-permute-done.refs_0_, bf16[16,2432]{1,0:T(8,128)(2,1)S(1)} %collective-permute-done.1.refs_1_, ...), custom_call_target="tpu_custom_call", output_to_operand_aliasing={{0}: (7, {}), {1}: (8, {})} | custom-call | flops 1811939328 | bytes 4718592 | tf_op jit(solution)/shard_map/pallas_call | solution.py:474
  12.4 0.0 collective-permute-start.3
  12.4 1.2 %collective-permute-done.3.other = f32[16,128]{1,0:T(8,128)S(1)} collective-permute-done((f32[16,128]{1,0:T(8,128)S(1)}, f32[16,128]{1,0:T(8,128)S(1)}, u32[]{:S(2)}, u32[]{:S(2)}) %collective-permute-start.3) | collective-permute-done | bytes 8224 | tf_op jit(solution)/shard_map/ppermute | solution.py:107
  13.6 1.8 %collective-permute-start.4 = (f32[8,128]{1,0:T(8,128)S(1)}, f32[8,128]{1,0:T(8,128)S(1)}, u32[]{:S(2)}, u32[]{:S(2)}) collective-permute-start(f32[8,128]{1,0:T(8,128)S(1)} %shard_map.89.refs_1_), channel_id=1, source_target_pairs={{0,2},{1,3},{2,0},{3,1},{4,6},{5,7},{6,4},{7,5},{8,10},{9,11},{10,... | collective-permute-start | bytes 12296 | tf_op jit(solution)/shard_map/ppermute | solution.py:107
  15.4 1.9 %collective-permute-done.4.refs_2_ = f32[8,128]{1,0:T(8,128)S(1)} collective-permute-done((f32[8,128]{1,0:T(8,128)S(1)}, f32[8,128]{1,0:T(8,128)S(1)}, u32[]{:S(2)}, u32[]{:S(2)}) %collective-permute-start.4) | collective-permute-done | bytes 4128 | tf_op jit(solution)/shard_map/ppermute | solution.py:107
  17.3 2.8 %shard_map.90 = (bf16[512,1024]{1,0:T(8,128)(2,1)S(1)}, f32[64,128]{1,0:T(8,128)S(1)}, f32[64,256]{1,0:T(8,128)S(1)}, bf16[64,639]{1,0:T(8,128)(2,1)S(1)}, bf16[...) custom-call(f32[16,128]{1,0:T(8,128)S(1)} %get-tuple-element.33.mine.refs_0_, f32[8,128]{1,0:T(8,128)S(1)} %shard_map.89.refs_1_, ...), custom_call_target="tpu_custom_call" | custom-call | flops 603979776 | bytes 2359296 | tf_op jit(solution)/shard_map/pallas_call | solution.py:474
  20.1 3.9 %collective-permute-start.5 = (bf16[64,639]{1,0:T(8,128)(2,1)S(1)}, bf16[64,639]{1,0:T(8,128)(2,1)S(1)}, u32[]{:S(2)}, u32[]{:S(2)}) collective-permute-start(bf16[64,639]{1,0:T(8,128)(2,1)S(1)} %get-tuple-element.39.refs_0_), channel_id=1, source_target_pairs={{0,12},{4,8},{8,4},{12,0},{1,13},{5,9},{9,5},{13,1},{2,14},{6,10},... | collective-permute-start | bytes 245384 | tf_op jit(solution)/shard_map/ppermute | solution.py:107
  24.0 0.0 collective-permute-start.6
  24.0 0.6 %collective-permute-start.7 = (bf16[64,599]{1,0:T(8,128)(2,1)S(1)}, bf16[64,599]{1,0:T(8,128)(2,1)S(1)}, u32[]{:S(2)}, u32[]{:S(2)}) collective-permute-start(bf16[64,599]{1,0:T(8,128)(2,1)S(1)} %get-tuple-element.41.refs_2_), channel_id=1, source_target_pairs={{0,4},{4,0},{8,12},{12,8},{1,5},{5,1},{9,13},{13,9},{2,6},{6,2},{1... | collective-permute-start | bytes 230024 | tf_op jit(solution)/shard_map/ppermute | solution.py:107
  24.7 1.0 %shard_map.91.own_ref = f32[64,579]{1,0:T(8,128)S(1)} custom-call(bf16[512,1024]{1,0:T(8,128)(2,1)S(1)} %get-tuple-element.36.weight_ref, bf16[1024,2304]{1,0:T(8,128)(2,1)S(1)} %get-tuple-element.35.refs_4_.shifted_ref, f32[64,128]{1,0:T(8,128)S(1)} %get-tuple-element.37.mass_ref, f32[64,256]{1,0:T(8,128)S(1)} %get-tuple-element.38.tails_ref, ...), custom_call_target="tpu_custom_call" | custom-call | flops 1024 | bytes 1024 | tf_op jit(solution)/shard_map/pallas_call | solution.py:474
  25.7 3.1 %collective-permute-done.7.refs_2_ = bf16[64,599]{1,0:T(8,128)(2,1)S(1)} collective-permute-done((bf16[64,599]{1,0:T(8,128)(2,1)S(1)}, bf16[64,599]{1,0:T(8,128)(2,1)S(1)}, u32[]{:S(2)}, u32[]{:S(2)}) %collective-permute-start.7) | collective-permute-done | bytes 76704 | tf_op jit(solution)/shard_map/ppermute | solution.py:107
  28.7 1.5 %collective-permute-done.6.refs_1_ = bf16[64,619]{1,0:T(8,128)(2,1)S(1)} collective-permute-done((bf16[64,619]{1,0:T(8,128)(2,1)S(1)}, bf16[64,619]{1,0:T(8,128)(2,1)S(1)}, u32[]{:S(2)}, u32[]{:S(2)}) %collective-permute-start.6) | collective-permute-done | bytes 79264 | tf_op jit(solution)/shard_map/ppermute | solution.py:107
  30.2 0.0 collective-permute-done.5.refs_0_
  30.2 0.7 %shard_map.92 = (f32[64,576]{1,0:T(8,128)}, f32[1,64]{1,0:T(1,128)}) custom-call(f32[64,579]{1,0:T(8,128)S(1)} %shard_map.91.own_ref, bf16[64,639]{1,0:T(8,128)(2,1)S(1)} %collective-permute-done.5.refs_0_, bf16[64,619]{1,0:T(8,128)(2,1)S(1)} %collective-permute-done.6.refs_1_, bf16[64,599]{1,0:T(8,128)(2,1)S(1)} %collective-permute-done.7.refs_2_), custom_call_target="tpu_custom_call" | custom-call | flops 163840 | bytes 655360 | tf_op jit(solution)/shard_map/pallas_call | solution.py:474
  (1 shorter events, 0.0 us)
Async XLA Ops:
  1.9 3.2 %collective-permute-start.2 = (bf16[16,2432]{1,0:T(8,128)(2,1)S(1)}, bf16[16,2432]{1,0:T(8,128)(2,1)S(1)}, u32[]{:S(2)}, u32[]{:S(2)}) collective-permute-start(bf16[16,2432]{1,0:T(8,128)(2,1)S(1)} %get-tuple-element.23.refs_0_), channel_id=1, source_target_pairs={{0,1},{1,0},{2,3},{3,2},{4,5},{5,4},{6,7},{7,6},{8,9},{9,8},{10,11... | collective-permute-start | bytes 233480 | tf_op jit(solution)/shard_map/ppermute | solution.py:107
  2.4 6.0 %collective-permute-start.1 = (bf16[16,2432]{1,0:T(8,128)(2,1)S(1)}, bf16[16,2432]{1,0:T(8,128)(2,1)S(1)}, u32[]{:S(2)}, u32[]{:S(2)}) collective-permute-start(bf16[16,2432]{1,0:T(8,128)(2,1)S(1)} %get-tuple-element.23.refs_0_), channel_id=1, source_target_pairs={{0,3},{1,2},{2,1},{3,0},{4,7},{5,6},{6,5},{7,4},{8,11},{9,10},{10,... | collective-permute-start | bytes 233480 | tf_op jit(solution)/shard_map/ppermute | solution.py:107
  5.0 4.6 %collective-permute-start = (bf16[16,2432]{1,0:T(8,128)(2,1)S(1)}, bf16[16,2432]{1,0:T(8,128)(2,1)S(1)}, u32[]{:S(2)}, u32[]{:S(2)}) collective-permute-start(bf16[16,2432]{1,0:T(8,128)(2,1)S(1)} %get-tuple-element.23.refs_0_), channel_id=1, source_target_pairs={{0,2},{1,3},{2,0},{3,1},{4,6},{5,7},{6,4},{7,5},{8,10},{9,11},{10,... | collective-permute-start | bytes 233480 | tf_op jit(solution)/shard_map/ppermute | solution.py:107
  12.4 1.2 %collective-permute-start.3 = (f32[16,128]{1,0:T(8,128)S(1)}, f32[16,128]{1,0:T(8,128)S(1)}, u32[]{:S(2)}, u32[]{:S(2)}) collective-permute-start(f32[16,128]{1,0:T(8,128)S(1)} %get-tuple-element.33.mine.refs_0_), channel_id=1, source_target_pairs={{0,1},{1,0},{2,3},{3,2},{4,5},{5,4},{6,7},{7,6},{8,9},{9,8},{10,11... | collective-permute-start | bytes 24584 | tf_op jit(solution)/shard_map/ppermute | solution.py:107
  13.6 3.7 %collective-permute-start.4 = (f32[8,128]{1,0:T(8,128)S(1)}, f32[8,128]{1,0:T(8,128)S(1)}, u32[]{:S(2)}, u32[]{:S(2)}) collective-permute-start(f32[8,128]{1,0:T(8,128)S(1)} %shard_map.89.refs_1_), channel_id=1, source_target_pairs={{0,2},{1,3},{2,0},{3,1},{4,6},{5,7},{6,4},{7,5},{8,10},{9,11},{10,... | collective-permute-start | bytes 12296 | tf_op jit(solution)/shard_map/ppermute | solution.py:107
  20.1 10.1 %collective-permute-start.5 = (bf16[64,639]{1,0:T(8,128)(2,1)S(1)}, bf16[64,639]{1,0:T(8,128)(2,1)S(1)}, u32[]{:S(2)}, u32[]{:S(2)}) collective-permute-start(bf16[64,639]{1,0:T(8,128)(2,1)S(1)} %get-tuple-element.39.refs_0_), channel_id=1, source_target_pairs={{0,12},{4,8},{8,4},{12,0},{1,13},{5,9},{9,5},{13,1},{2,14},{6,10},... | collective-permute-start | bytes 245384 | tf_op jit(solution)/shard_map/ppermute | solution.py:107
  24.0 6.2 %collective-permute-start.6 = (bf16[64,619]{1,0:T(8,128)(2,1)S(1)}, bf16[64,619]{1,0:T(8,128)(2,1)S(1)}, u32[]{:S(2)}, u32[]{:S(2)}) collective-permute-start(bf16[64,619]{1,0:T(8,128)(2,1)S(1)} %get-tuple-element.40.refs_1_), channel_id=1, source_target_pairs={{0,8},{4,12},{8,0},{12,4},{1,9},{5,13},{9,1},{13,5},{2,10},{6,14},... | collective-permute-start | bytes 237704 | tf_op jit(solution)/shard_map/ppermute | solution.py:107
  24.0 4.7 %collective-permute-start.7 = (bf16[64,599]{1,0:T(8,128)(2,1)S(1)}, bf16[64,599]{1,0:T(8,128)(2,1)S(1)}, u32[]{:S(2)}, u32[]{:S(2)}) collective-permute-start(bf16[64,599]{1,0:T(8,128)(2,1)S(1)} %get-tuple-element.41.refs_2_), channel_id=1, source_target_pairs={{0,4},{4,0},{8,12},{12,8},{1,5},{5,1},{9,13},{13,9},{2,6},{6,2},{1... | collective-permute-start | bytes 230024 | tf_op jit(solution)/shard_map/ppermute | solution.py:107

commit v11 on v8

--- a/solution.py
+++ b/solution.py
@@ -576,10 +576,10 @@
         distance *= 2
         other = exchange(mine, "cls", distance)
     low_bit = lambda b: b & -b
-    early = list(range(doms - 1, 0, -2))
-    order = early + sorted(range(2, doms, 2), key=lambda b: (low_bit(b), -b))
+    early = list(range(doms - 1, 1, -2))
+    order = early + [1] + sorted(range(2, doms, 2), key=lambda b: (low_bit(b), -b))
     extents = {b: width + 3 + (doms - 1 - place) * growth for place, b in enumerate(order)}
-    late = list(range(0, doms, 2))
+    late = [1] + list(range(0, doms, 2))
     weights, mass, tails, *made = call(
         functools.partial(first_sums_kernel, count, doms, width, main, early),
         [
@@ -599,7 +599,9 @@
         incoming[b ^ 1].append(exchange(block, "dom", 1))
     rest = call(
         functools.partial(rest_sums_kernel, doms, width, main, late),
-        [shape((classes, width + 3), f32) for b in late],
+        [
+            shape((classes, extents.get(b, width + 3)), bf16 if b == 1 else f32) for b in late
+        ],
         [],
         1024,
         1024,
@@ -607,7 +609,8 @@
         chip=(1,),
     )
     blocks = dict(zip(late, rest))
-    for b in order[len(early) :]:
+    incoming[0].append(exchange(blocks[1], "dom", 1))
+    for b in order[len(early) + 1 :]:
         (block,) = call(
             functools.partial(add_kernel, width),
             [shape((classes, extents[b]), bf16)],

time: 30.8 us -> 29.7 us (0.964)
  waiting for transfers between devices: 8.35 us -> 7.12 us
    ppermute x8, waiting for transfers between devices: 8.35 us -> 7.12 us  [exchange(): lax.ppermute(array, axis, [(i, i ^ distance) for i in range(lax.axis_size...]
  transfers between devices with their start and end apart: 8 -> 8, of which waited for: 5 -> 6; matrix products, arithmetic and copies ran while one was open for 0% -> 0% of each run, Pallas kernels for 16% -> 19%
where the time goes in v11:
time: 29.7 us; the launch traced here: 29.5 us
  Pallas kernels  11.8 us (40%)
  starting transfers between devices  9.94 us (33%)
  waiting for transfers between devices  7.12 us (24%)
  between operations  0.67 us (2%)
    pallas_call x8, Pallas kernels, call(): pl.pallas_call(kernel, out_shape=[pltpu.VMEM(s.shape, s.dtype) if pinned...  11.8 us
    ppermute x8, starting transfers between devices, exchange(): lax.ppermute(array, axis, [(i, i ^ distance) for i in range(lax.axis_size...  9.94 us
    ppermute x8, waiting for transfers between devices, exchange(): lax.ppermute(array, axis, [(i, i ^ distance) for i in range(lax.axis_size...  7.12 us
  transfers between devices with their start and end apart: 8, of which 6 were waited for; matrix products, arithmetic and copies ran while one was open for 0% of the time, Pallas kernels for 19%

profile of v11, /device:TPU:0, one launch (start us, length us, event | category | flops | bytes accessed | tf_op | source)
XLA Modules:
  0.0 29.5 jit_solution(14170597923754444199)
XLA Ops:
  0.6 1.3 %shard_map.86 = (bf16[16,2432]{1,0:T(8,128)(2,1)S(1)}, bf16[64,2304]{1,0:T(8,128)(2,1)S(1)}, f32[1,64]{1,0:T(1,128)S(1)}, f32[48,2304]{1,0:T(8,128)S(1)}) custom-call(bf16[16,2304]{1,0:T(8,128)(2,1)} %particle_hbm.1, s32[16,16]{1,0:T(8,128)} %index_hbm.1, s32[1,16]{1,0:T(1,128)} %bitcast.4, s32[1,16]{1,0:T(1,128)} %bitcast.5, bf16[64,2304]{1,0:T(8,128)(2,1)} %class_hbm.1, ...), custom_call_target="tpu_custom_call" | custom-call | flops 36864 | bytes 147456 | tf_op jit(solution)/shard_map/pallas_call | solution.py:486
  1.9 0.5 %collective-permute-start.2 = (bf16[16,2432]{1,0:T(8,128)(2,1)S(1)}, bf16[16,2432]{1,0:T(8,128)(2,1)S(1)}, u32[]{:S(2)}, u32[]{:S(2)}) collective-permute-start(bf16[16,2432]{1,0:T(8,128)(2,1)S(1)} %get-tuple-element.24.refs_0_), channel_id=1, source_target_pairs={{0,1},{1,0},{2,3},{3,2},{4,5},{5,4},{6,7},{7,6},{8,9},{9,8},{10,11... | collective-permute-start | bytes 233480 | tf_op jit(solution)/shard_map/ppermute | solution.py:107
  2.4 2.6 %collective-permute-start.1 = (bf16[16,2432]{1,0:T(8,128)(2,1)S(1)}, bf16[16,2432]{1,0:T(8,128)(2,1)S(1)}, u32[]{:S(2)}, u32[]{:S(2)}) collective-permute-start(bf16[16,2432]{1,0:T(8,128)(2,1)S(1)} %get-tuple-element.24.refs_0_), channel_id=1, source_target_pairs={{0,3},{1,2},{2,1},{3,0},{4,7},{5,6},{6,5},{7,4},{8,11},{9,10},{10,... | collective-permute-start | bytes 233480 | tf_op jit(solution)/shard_map/ppermute | solution.py:107
  5.0 0.0 collective-permute-start
  5.1 0.0 collective-permute-done.2.refs_1_
  5.1 3.3 %shard_map.87 = (bf16[1024,2304]{1,0:T(8,128)(2,1)S(1)}, f32[512,1024]{1,0:T(8,128)S(1)}, f32[16,128]{1,0:T(8,128)S(1)}, bf16[512,2304]{1,0:T(8,128)(2,1)S(1)}, ...) custom-call(bf16[16,2432]{1,0:T(8,128)(2,1)S(1)} %get-tuple-element.24.refs_0_, ...), custom_call_target="tpu_custom_call" | custom-call | flops 1811939328 | bytes 4718592 | tf_op jit(solution)/shard_map/pallas_call | solution.py:486
  8.4 0.0 collective-permute-done.1.refs_1_
  8.4 1.2 %collective-permute-done.refs_0_ = bf16[16,2432]{1,0:T(8,128)(2,1)S(1)} collective-permute-done((bf16[16,2432]{1,0:T(8,128)(2,1)S(1)}, bf16[16,2432]{1,0:T(8,128)(2,1)S(1)}, u32[]{:S(2)}, u32[]{:S(2)}) %collective-permute-start) | collective-permute-done | bytes 77856 | tf_op jit(solution)/shard_map/ppermute | solution.py:107
  9.6 2.8 %shard_map.88 = (bf16[1024,2304]{1,0:T(8,128)(2,1)S(1)}, f32[512,1024]{1,0:T(8,128)S(1)}, f32[16,128]{1,0:T(8,128)S(1)}) custom-call(bf16[16,2432]{1,0:T(8,128)(2,1)S(1)} %collective-permute-done.refs_0_, bf16[16,2432]{1,0:T(8,128)(2,1)S(1)} %collective-permute-done.1.refs_1_, ...), custom_call_target="tpu_custom_call", output_to_operand_aliasing={{0}: (7, {}), {1}: (8, {})} | custom-call | flops 1811939328 | bytes 4718592 | tf_op jit(solution)/shard_map/pallas_call | solution.py:486
  12.4 0.0 collective-permute-start.3
  12.4 1.2 %collective-permute-done.3.other = f32[16,128]{1,0:T(8,128)S(1)} collective-permute-done((f32[16,128]{1,0:T(8,128)S(1)}, f32[16,128]{1,0:T(8,128)S(1)}, u32[]{:S(2)}, u32[]{:S(2)}) %collective-permute-start.3) | collective-permute-done | bytes 8224 | tf_op jit(solution)/shard_map/ppermute | solution.py:107
  13.6 1.8 %collective-permute-start.4 = (f32[8,128]{1,0:T(8,128)S(1)}, f32[8,128]{1,0:T(8,128)S(1)}, u32[]{:S(2)}, u32[]{:S(2)}) collective-permute-start(f32[8,128]{1,0:T(8,128)S(1)} %shard_map.89.refs_1_), channel_id=1, source_target_pairs={{0,2},{1,3},{2,0},{3,1},{4,6},{5,7},{6,4},{7,5},{8,10},{9,11},{10,... | collective-permute-start | bytes 12296 | tf_op jit(solution)/shard_map/ppermute | solution.py:107
  15.4 1.9 %collective-permute-done.4.refs_2_ = f32[8,128]{1,0:T(8,128)S(1)} collective-permute-done((f32[8,128]{1,0:T(8,128)S(1)}, f32[8,128]{1,0:T(8,128)S(1)}, u32[]{:S(2)}, u32[]{:S(2)}) %collective-permute-start.4) | collective-permute-done | bytes 4128 | tf_op jit(solution)/shard_map/ppermute | solution.py:107
  17.3 1.5 %shard_map.90 = (bf16[512,1024]{1,0:T(8,128)(2,1)S(1)}, f32[64,128]{1,0:T(8,128)S(1)}, f32[64,256]{1,0:T(8,128)S(1)}, bf16[64,639]{1,0:T(8,128)(2,1)S(1)}) custom-call(f32[16,128]{1,0:T(8,128)S(1)} %get-tuple-element.34.mine.refs_0_, f32[8,128]{1,0:T(8,128)S(1)} %shard_map.89.refs_1_, f32[8,128]{1,0:T(8,128)S(1)} %collective-permute-done.4.refs_2_, ...), custom_call_target="tpu_custom_call" | custom-call | flops 603979776 | bytes 2359296 | tf_op jit(solution)/shard_map/pallas_call | solution.py:486
  18.7 1.9 %collective-permute-start.6 = (bf16[64,639]{1,0:T(8,128)(2,1)S(1)}, bf16[64,639]{1,0:T(8,128)(2,1)S(1)}, u32[]{:S(2)}, u32[]{:S(2)}) collective-permute-start(bf16[64,639]{1,0:T(8,128)(2,1)S(1)} %get-tuple-element.40.refs_0_), channel_id=1, source_target_pairs={{0,4},{4,0},{8,12},{12,8},{1,5},{5,1},{9,13},{13,9},{2,6},{6,2},{1... | collective-permute-start | bytes 245384 | tf_op jit(solution)/shard_map/ppermute | solution.py:107
  20.6 2.2 %shard_map.91 = (bf16[64,619]{1,0:T(8,128)(2,1)S(1)}, f32[64,579]{1,0:T(8,128)S(1)}, f32[64,599]{1,0:T(8,128)S(1)}) custom-call(bf16[512,1024]{1,0:T(8,128)(2,1)S(1)} %get-tuple-element.37.weight_ref, bf16[1024,2304]{1,0:T(8,128)(2,1)S(1)} %get-tuple-element.36.refs_4_.shifted_ref, f32[64,128]{1,0:T(8,128)S(1)} %get-tuple-element.38.mass_ref, ...), custom_call_target="tpu_custom_call" | custom-call | flops 1024 | bytes 1024 | tf_op jit(solution)/shard_map/pallas_call | solution.py:486
  22.8 0.3 collective-permute-start.5
  23.0 0.2 collective-permute-done.6.refs_1_
  23.2 0.1 shard_map.92
  23.4 2.9 %collective-permute-start.7 = (bf16[64,599]{1,0:T(8,128)(2,1)S(1)}, bf16[64,599]{1,0:T(8,128)(2,1)S(1)}, u32[]{:S(2)}, u32[]{:S(2)}) collective-permute-start(bf16[64,599]{1,0:T(8,128)(2,1)S(1)} %shard_map.92), channel_id=1, source_target_pairs={{0,8},{4,12},{8,0},{12,4},{1,9},{5,13},{9,1},{13,5},{2,10},{6,14},... | collective-permute-start | bytes 230024 | tf_op jit(solution)/shard_map/ppermute | solution.py:107
  26.2 1.0 %collective-permute-done.5.refs_0_ = bf16[64,619]{1,0:T(8,128)(2,1)S(1)} collective-permute-done((bf16[64,619]{1,0:T(8,128)(2,1)S(1)}, bf16[64,619]{1,0:T(8,128)(2,1)S(1)}, u32[]{:S(2)}, u32[]{:S(2)}) %collective-permute-start.5) | collective-permute-done | bytes 79264 | tf_op jit(solution)/shard_map/ppermute | solution.py:107
  27.3 1.6 %collective-permute-done.7.refs_1_ = bf16[64,599]{1,0:T(8,128)(2,1)S(1)} collective-permute-done((bf16[64,599]{1,0:T(8,128)(2,1)S(1)}, bf16[64,599]{1,0:T(8,128)(2,1)S(1)}, u32[]{:S(2)}, u32[]{:S(2)}) %collective-permute-start.7) | collective-permute-done | bytes 76704 | tf_op jit(solution)/shard_map/ppermute | solution.py:107
  28.8 0.7 %shard_map.93 = (f32[64,576]{1,0:T(8,128)}, f32[1,64]{1,0:T(1,128)}) custom-call(f32[64,579]{1,0:T(8,128)S(1)} %get-tuple-element.41.own_ref, bf16[64,619]{1,0:T(8,128)(2,1)S(1)} %collective-permute-done.5.refs_0_, bf16[64,599]{1,0:T(8,128)(2,1)S(1)} %collective-permute-done.7.refs_1_), custom_call_target="tpu_custom_call" | custom-call | flops 163840 | bytes 655360 | tf_op jit(solution)/shard_map/pallas_call | solution.py:486
  (1 shorter events, 0.0 us)
Async XLA Ops:
  1.9 3.2 %collective-permute-start.2 = (bf16[16,2432]{1,0:T(8,128)(2,1)S(1)}, bf16[16,2432]{1,0:T(8,128)(2,1)S(1)}, u32[]{:S(2)}, u32[]{:S(2)}) collective-permute-start(bf16[16,2432]{1,0:T(8,128)(2,1)S(1)} %get-tuple-element.24.refs_0_), channel_id=1, source_target_pairs={{0,1},{1,0},{2,3},{3,2},{4,5},{5,4},{6,7},{7,6},{8,9},{9,8},{10,11... | collective-permute-start | bytes 233480 | tf_op jit(solution)/shard_map/ppermute | solution.py:107
  2.4 6.0 %collective-permute-start.1 = (bf16[16,2432]{1,0:T(8,128)(2,1)S(1)}, bf16[16,2432]{1,0:T(8,128)(2,1)S(1)}, u32[]{:S(2)}, u32[]{:S(2)}) collective-permute-start(bf16[16,2432]{1,0:T(8,128)(2,1)S(1)} %get-tuple-element.24.refs_0_), channel_id=1, source_target_pairs={{0,3},{1,2},{2,1},{3,0},{4,7},{5,6},{6,5},{7,4},{8,11},{9,10},{10,... | collective-permute-start | bytes 233480 | tf_op jit(solution)/shard_map/ppermute | solution.py:107
  5.0 4.6 %collective-permute-start = (bf16[16,2432]{1,0:T(8,128)(2,1)S(1)}, bf16[16,2432]{1,0:T(8,128)(2,1)S(1)}, u32[]{:S(2)}, u32[]{:S(2)}) collective-permute-start(bf16[16,2432]{1,0:T(8,128)(2,1)S(1)} %get-tuple-element.24.refs_0_), channel_id=1, source_target_pairs={{0,2},{1,3},{2,0},{3,1},{4,6},{5,7},{6,4},{7,5},{8,10},{9,11},{10,... | collective-permute-start | bytes 233480 | tf_op jit(solution)/shard_map/ppermute | solution.py:107
  12.4 1.2 %collective-permute-start.3 = (f32[16,128]{1,0:T(8,128)S(1)}, f32[16,128]{1,0:T(8,128)S(1)}, u32[]{:S(2)}, u32[]{:S(2)}) collective-permute-start(f32[16,128]{1,0:T(8,128)S(1)} %get-tuple-element.34.mine.refs_0_), channel_id=1, source_target_pairs={{0,1},{1,0},{2,3},{3,2},{4,5},{5,4},{6,7},{7,6},{8,9},{9,8},{10,11... | collective-permute-start | bytes 24584 | tf_op jit(solution)/shard_map/ppermute | solution.py:107
  13.6 3.7 %collective-permute-start.4 = (f32[8,128]{1,0:T(8,128)S(1)}, f32[8,128]{1,0:T(8,128)S(1)}, u32[]{:S(2)}, u32[]{:S(2)}) collective-permute-start(f32[8,128]{1,0:T(8,128)S(1)} %shard_map.89.refs_1_), channel_id=1, source_target_pairs={{0,2},{1,3},{2,0},{3,1},{4,6},{5,7},{6,4},{7,5},{8,10},{9,11},{10,... | collective-permute-start | bytes 12296 | tf_op jit(solution)/shard_map/ppermute | solution.py:107
  18.7 4.5 %collective-permute-start.6 = (bf16[64,639]{1,0:T(8,128)(2,1)S(1)}, bf16[64,639]{1,0:T(8,128)(2,1)S(1)}, u32[]{:S(2)}, u32[]{:S(2)}) collective-permute-start(bf16[64,639]{1,0:T(8,128)(2,1)S(1)} %get-tuple-element.40.refs_0_), channel_id=1, source_target_pairs={{0,4},{4,0},{8,12},{12,8},{1,5},{5,1},{9,13},{13,9},{2,6},{6,2},{1... | collective-permute-start | bytes 245384 | tf_op jit(solution)/shard_map/ppermute | solution.py:107
  22.8 4.5 %collective-permute-start.5 = (bf16[64,619]{1,0:T(8,128)(2,1)S(1)}, bf16[64,619]{1,0:T(8,128)(2,1)S(1)}, u32[]{:S(2)}, u32[]{:S(2)}) collective-permute-start(bf16[64,619]{1,0:T(8,128)(2,1)S(1)} %get-tuple-element.42), channel_id=1, source_target_pairs={{0,4},{4,0},{8,12},{12,8},{1,5},{5,1},{9,13},{13,9},{2,6},{6,2},{1... | collective-permute-start | bytes 237704 | tf_op jit(solution)/shard_map/ppermute | solution.py:107
  23.4 5.5 %collective-permute-start.7 = (bf16[64,599]{1,0:T(8,128)(2,1)S(1)}, bf16[64,599]{1,0:T(8,128)(2,1)S(1)}, u32[]{:S(2)}, u32[]{:S(2)}) collective-permute-start(bf16[64,599]{1,0:T(8,128)(2,1)S(1)} %shard_map.92), channel_id=1, source_target_pairs={{0,8},{4,12},{8,0},{12,4},{1,9},{5,13},{9,1},{13,5},{2,10},{6,14},... | collective-permute-start | bytes 230024 | tf_op jit(solution)/shard_map/ppermute | solution.py:107

commit v12 on v11

--- a/solution.py
+++ b/solution.py
@@ -530,13 +530,15 @@
         class_spectra, group_scale[None, :], phases,
         hbm=(0, 1, 2, 3, 4, 5, 6),
     )
-    chunks = [packed] + [exchange(packed, "cls", distance) for distance in range(1, count)]
+    chunks = {0: packed, 1: exchange(packed, "cls", 1)}
+    for b in range(2, count, 2):
+        chunks[b] = exchange(packed, "cls", b)
     stat_rows = -(-3 * count // 8) * 8
     work = 2 * rows * COLS * (ROTS * classes + 256)
     stats_shape = shape((stat_rows, LANES), f32)
     shifted_shape = shape((count * rows, COLS), bf16)
     exp_shape = shape((ROTS * classes, count * rows), f32)
-    near, far = [0, 1], list(range(2, count))
+    near = [0, 1]
     shifted, exps, stats, rotated, norm, table = call(
         functools.partial(first_kernel, count, groups, segments, near),
         [
@@ -552,16 +554,20 @@
         4 * len(near) * rows * COLS,
         *[chunks[b] for b in near], classes_on_chip, phases_on_chip, scales,
     )
-    shifted, exps, stats = call(
-        functools.partial(rest_kernel, count, segments, far),
-        [shifted_shape, exp_shape, stats_shape],
-        [],
-        work * len(far),
-        4 * len(far) * rows * COLS,
-        *[chunks[b] for b in far], table, scales, rotated, norm, stats, shifted, exps,
-        aliases={len(far) + 5: 0, len(far) + 6: 1},
-        chip=(len(far) + 5, len(far) + 6),
-    )
+    for b in range(2, count, 2):
+        arrived, stats = lax.optimization_barrier((chunks[b], stats))
+        chunks[b + 1] = exchange(arrived, "cls", 1)
+    for far in (list(range(2, count, 2)), list(range(3, count, 2))):
+        shifted, exps, stats = call(
+            functools.partial(rest_kernel, count, segments, far),
+            [shifted_shape, exp_shape, stats_shape],
+            [],
+            work * len(far),
+            4 * len(far) * rows * COLS,
+            *[chunks[b] for b in far], table, scales, rotated, norm, stats, shifted, exps,
+            aliases={len(far) + 5: 0, len(far) + 6: 1},
+            chip=(len(far) + 5, len(far) + 6),
+        )
     mine, distance = stats, 1
     other = exchange(mine, "cls", distance)
     while 2 * distance < count:

time: 29.7 us -> 29.3 us (0.987)
  waiting for transfers between devices: 7.12 us -> 6.03 us
  Pallas kernels: 11.8 us -> 12.5 us
    ppermute x8, waiting for transfers between devices: 7.12 us -> 6.03 us  [exchange(): lax.ppermute(array, axis, [(i, i ^ distance) for i in range(lax.axis_size...]
    pallas_call x8 -> x9, Pallas kernels: 11.8 us -> 12.5 us  [call(): pl.pallas_call(kernel, out_shape=[pltpu.VMEM(s.shape, s.dtype) if pinned...]
  transfers between devices with their start and end apart: 8 -> 8, of which waited for: 6 -> 5; matrix products, arithmetic and copies ran while one was open for 0% -> 0% of each run, Pallas kernels for 19% -> 25%
where the time goes in v12:
time: 29.3 us; the launch traced here: 29.1 us
  Pallas kernels  12.5 us (43%)
  starting transfers between devices  9.84 us (34%)
  waiting for transfers between devices  6.03 us (21%)
  between operations  0.67 us (2%)
    pallas_call x9, Pallas kernels, call(): pl.pallas_call(kernel, out_shape=[pltpu.VMEM(s.shape, s.dtype) if pinned...  12.5 us
    ppermute x8, starting transfers between devices, exchange(): lax.ppermute(array, axis, [(i, i ^ distance) for i in range(lax.axis_size...  9.84 us
    ppermute x8, waiting for transfers between devices, exchange(): lax.ppermute(array, axis, [(i, i ^ distance) for i in range(lax.axis_size...  6.03 us
  transfers between devices with their start and end apart: 8, of which 5 were waited for; matrix products, arithmetic and copies ran while one was open for 0% of the time, Pallas kernels for 25%

profile of v12, /device:TPU:0, one launch (start us, length us, event | category | flops | bytes accessed | tf_op | source)
XLA Modules:
  0.0 29.1 jit_solution(2434819707860769750)
XLA Ops:
  0.6 1.3 %shard_map.86 = (bf16[16,2432]{1,0:T(8,128)(2,1)S(1)}, bf16[64,2304]{1,0:T(8,128)(2,1)S(1)}, f32[1,64]{1,0:T(1,128)S(1)}, f32[48,2304]{1,0:T(8,128)S(1)}) custom-call(bf16[16,2304]{1,0:T(8,128)(2,1)} %particle_hbm.1, s32[16,16]{1,0:T(8,128)} %index_hbm.1, s32[1,16]{1,0:T(1,128)} %bitcast.4, s32[1,16]{1,0:T(1,128)} %bitcast.5, bf16[64,2304]{1,0:T(8,128)(2,1)} %class_hbm.1, ...), custom_call_target="tpu_custom_call" | custom-call | flops 36864 | bytes 147456 | tf_op jit(solution)/shard_map/pallas_call | solution.py:486
  1.9 0.5 %collective-permute-start.1 = (bf16[16,2432]{1,0:T(8,128)(2,1)S(1)}, bf16[16,2432]{1,0:T(8,128)(2,1)S(1)}, u32[]{:S(2)}, u32[]{:S(2)}) collective-permute-start(bf16[16,2432]{1,0:T(8,128)(2,1)S(1)} %get-tuple-element.29.refs_0_), channel_id=1, source_target_pairs={{0,1},{1,0},{2,3},{3,2},{4,5},{5,4},{6,7},{7,6},{8,9},{9,8},{10,11... | collective-permute-start | bytes 233480 | tf_op jit(solution)/shard_map/ppermute | solution.py:107
  2.4 2.6 %collective-permute-start = (bf16[16,2432]{1,0:T(8,128)(2,1)S(1)}, bf16[16,2432]{1,0:T(8,128)(2,1)S(1)}, u32[]{:S(2)}, u32[]{:S(2)}) collective-permute-start(bf16[16,2432]{1,0:T(8,128)(2,1)S(1)} %get-tuple-element.29.refs_0_), channel_id=1, source_target_pairs={{0,2},{1,3},{2,0},{3,1},{4,6},{5,7},{6,4},{7,5},{8,10},{9,11},{10,... | collective-permute-start | bytes 233480 | tf_op jit(solution)/shard_map/ppermute | solution.py:107
  5.0 0.0 collective-permute-done.1.refs_1_
  5.0 3.3 %shard_map.87 = (bf16[1024,2304]{1,0:T(8,128)(2,1)S(1)}, f32[512,1024]{1,0:T(8,128)S(1)}, f32[16,128]{1,0:T(8,128)S(1)}, bf16[512,2304]{1,0:T(8,128)(2,1)S(1)}, ...) custom-call(bf16[16,2432]{1,0:T(8,128)(2,1)S(1)} %get-tuple-element.29.refs_0_, ...), custom_call_target="tpu_custom_call" | custom-call | flops 1811939328 | bytes 4718592 | tf_op jit(solution)/shard_map/pallas_call | solution.py:486
  8.3 0.0 collective-permute-done.refs_0_
  8.3 0.2 collective-permute-start.2
  8.5 1.8 %shard_map.88 = (bf16[1024,2304]{1,0:T(8,128)(2,1)S(1)}, f32[512,1024]{1,0:T(8,128)S(1)}, f32[16,128]{1,0:T(8,128)S(1)}) custom-call(bf16[16,2432]{1,0:T(8,128)(2,1)S(1)} %collective-permute-done.refs_0_, bf16[256,2304]{1,0:T(8,128)(2,1)S(1)} %get-tuple-element.35.refs_1_, ...), custom_call_target="tpu_custom_call", output_to_operand_aliasing={{0}: (6, {}), {1}: (7, {})} | custom-call | flops 905969664 | bytes 2359296 | tf_op jit(solution)/shard_map/pallas_call | solution.py:486
  10.2 0.0 collective-permute-done.2.refs_0_
  10.2 1.8 %shard_map.89 = (bf16[1024,2304]{1,0:T(8,128)(2,1)S(1)}, f32[512,1024]{1,0:T(8,128)S(1)}, f32[16,128]{1,0:T(8,128)S(1)}) custom-call(bf16[16,2432]{1,0:T(8,128)(2,1)S(1)} %collective-permute-done.2.refs_0_, bf16[256,2304]{1,0:T(8,128)(2,1)S(1)} %get-tuple-element.35.refs_1_, ...), custom_call_target="tpu_custom_call", output_to_operand_aliasing={{0}: (6, {}), {1}: (7, {})} | custom-call | flops 905969664 | bytes 2359296 | tf_op jit(solution)/shard_map/pallas_call | solution.py:486
  12.0 0.3 %collective-permute-start.3 = (f32[16,128]{1,0:T(8,128)S(1)}, f32[16,128]{1,0:T(8,128)S(1)}, u32[]{:S(2)}, u32[]{:S(2)}) collective-permute-start(f32[16,128]{1,0:T(8,128)S(1)} %get-tuple-element.44.mine.refs_0_), channel_id=1, source_target_pairs={{0,1},{1,0},{2,3},{3,2},{4,5},{5,4},{6,7},{7,6},{8,9},{9,8},{10,11... | collective-permute-start | bytes 24584 | tf_op jit(solution)/shard_map/ppermute | solution.py:107
  12.3 0.8 %collective-permute-done.3.other = f32[16,128]{1,0:T(8,128)S(1)} collective-permute-done((f32[16,128]{1,0:T(8,128)S(1)}, f32[16,128]{1,0:T(8,128)S(1)}, u32[]{:S(2)}, u32[]{:S(2)}) %collective-permute-start.3) | collective-permute-done | bytes 8224 | tf_op jit(solution)/shard_map/ppermute | solution.py:107
  13.2 1.5 %collective-permute-start.4 = (f32[8,128]{1,0:T(8,128)S(1)}, f32[8,128]{1,0:T(8,128)S(1)}, u32[]{:S(2)}, u32[]{:S(2)}) collective-permute-start(f32[8,128]{1,0:T(8,128)S(1)} %shard_map.90.refs_1_), channel_id=1, source_target_pairs={{0,2},{1,3},{2,0},{3,1},{4,6},{5,7},{6,4},{7,5},{8,10},{9,11},{10,... | collective-permute-start | bytes 12296 | tf_op jit(solution)/shard_map/ppermute | solution.py:107
  14.7 2.2 %collective-permute-done.4.refs_2_ = f32[8,128]{1,0:T(8,128)S(1)} collective-permute-done((f32[8,128]{1,0:T(8,128)S(1)}, f32[8,128]{1,0:T(8,128)S(1)}, u32[]{:S(2)}, u32[]{:S(2)}) %collective-permute-start.4) | collective-permute-done | bytes 4128 | tf_op jit(solution)/shard_map/ppermute | solution.py:107
  16.9 1.5 %shard_map.91 = (bf16[512,1024]{1,0:T(8,128)(2,1)S(1)}, f32[64,128]{1,0:T(8,128)S(1)}, f32[64,256]{1,0:T(8,128)S(1)}, bf16[64,639]{1,0:T(8,128)(2,1)S(1)}) custom-call(f32[16,128]{1,0:T(8,128)S(1)} %get-tuple-element.44.mine.refs_0_, f32[8,128]{1,0:T(8,128)S(1)} %shard_map.90.refs_1_, f32[8,128]{1,0:T(8,128)S(1)} %collective-permute-done.4.refs_2_, ...), custom_call_target="tpu_custom_call" | custom-call | flops 603979776 | bytes 2359296 | tf_op jit(solution)/shard_map/pallas_call | solution.py:486
  18.3 1.7 %collective-permute-start.6 = (bf16[64,639]{1,0:T(8,128)(2,1)S(1)}, bf16[64,639]{1,0:T(8,128)(2,1)S(1)}, u32[]{:S(2)}, u32[]{:S(2)}) collective-permute-start(bf16[64,639]{1,0:T(8,128)(2,1)S(1)} %get-tuple-element.50.refs_0_), channel_id=1, source_target_pairs={{0,4},{4,0},{8,12},{12,8},{1,5},{5,1},{9,13},{13,9},{2,6},{6,2},{1... | collective-permute-start | bytes 245384 | tf_op jit(solution)/shard_map/ppermute | solution.py:107
  20.0 2.2 %shard_map.92 = (bf16[64,619]{1,0:T(8,128)(2,1)S(1)}, f32[64,579]{1,0:T(8,128)S(1)}, f32[64,599]{1,0:T(8,128)S(1)}) custom-call(bf16[512,1024]{1,0:T(8,128)(2,1)S(1)} %get-tuple-element.47.weight_ref, bf16[1024,2304]{1,0:T(8,128)(2,1)S(1)} %get-tuple-element.46.refs_4_.shifted_ref, f32[64,128]{1,0:T(8,128)S(1)} %get-tuple-element.48.mass_ref, ...), custom_call_target="tpu_custom_call" | custom-call | flops 1024 | bytes 1024 | tf_op jit(solution)/shard_map/pallas_call | solution.py:486
  22.1 0.5 %collective-permute-start.5 = (bf16[64,619]{1,0:T(8,128)(2,1)S(1)}, bf16[64,619]{1,0:T(8,128)(2,1)S(1)}, u32[]{:S(2)}, u32[]{:S(2)}) collective-permute-start(bf16[64,619]{1,0:T(8,128)(2,1)S(1)} %get-tuple-element.52), channel_id=1, source_target_pairs={{0,4},{4,0},{8,12},{12,8},{1,5},{5,1},{9,13},{13,9},{2,6},{6,2},{1... | collective-permute-start | bytes 237704 | tf_op jit(solution)/shard_map/ppermute | solution.py:107
  22.6 0.2 collective-permute-done.6.refs_1_
  22.8 0.1 shard_map.93
  23.0 2.7 %collective-permute-start.7 = (bf16[64,599]{1,0:T(8,128)(2,1)S(1)}, bf16[64,599]{1,0:T(8,128)(2,1)S(1)}, u32[]{:S(2)}, u32[]{:S(2)}) collective-permute-start(bf16[64,599]{1,0:T(8,128)(2,1)S(1)} %shard_map.93), channel_id=1, source_target_pairs={{0,8},{4,12},{8,0},{12,4},{1,9},{5,13},{9,1},{13,5},{2,10},{6,14},... | collective-permute-start | bytes 230024 | tf_op jit(solution)/shard_map/ppermute | solution.py:107
  25.6 1.1 %collective-permute-done.5.refs_0_ = bf16[64,619]{1,0:T(8,128)(2,1)S(1)} collective-permute-done((bf16[64,619]{1,0:T(8,128)(2,1)S(1)}, bf16[64,619]{1,0:T(8,128)(2,1)S(1)}, u32[]{:S(2)}, u32[]{:S(2)}) %collective-permute-start.5) | collective-permute-done | bytes 79264 | tf_op jit(solution)/shard_map/ppermute | solution.py:107
  26.7 1.7 %collective-permute-done.7.refs_1_ = bf16[64,599]{1,0:T(8,128)(2,1)S(1)} collective-permute-done((bf16[64,599]{1,0:T(8,128)(2,1)S(1)}, bf16[64,599]{1,0:T(8,128)(2,1)S(1)}, u32[]{:S(2)}, u32[]{:S(2)}) %collective-permute-start.7) | collective-permute-done | bytes 76704 | tf_op jit(solution)/shard_map/ppermute | solution.py:107
  28.4 0.7 %shard_map.94 = (f32[64,576]{1,0:T(8,128)}, f32[1,64]{1,0:T(1,128)}) custom-call(f32[64,579]{1,0:T(8,128)S(1)} %get-tuple-element.51.own_ref, bf16[64,619]{1,0:T(8,128)(2,1)S(1)} %collective-permute-done.5.refs_0_, bf16[64,599]{1,0:T(8,128)(2,1)S(1)} %collective-permute-done.7.refs_1_), custom_call_target="tpu_custom_call" | custom-call | flops 163840 | bytes 655360 | tf_op jit(solution)/shard_map/pallas_call | solution.py:486
  (1 shorter events, 0.0 us)
Async XLA Ops:
  1.9 3.1 %collective-permute-start.1 = (bf16[16,2432]{1,0:T(8,128)(2,1)S(1)}, bf16[16,2432]{1,0:T(8,128)(2,1)S(1)}, u32[]{:S(2)}, u32[]{:S(2)}) collective-permute-start(bf16[16,2432]{1,0:T(8,128)(2,1)S(1)} %get-tuple-element.29.refs_0_), channel_id=1, source_target_pairs={{0,1},{1,0},{2,3},{3,2},{4,5},{5,4},{6,7},{7,6},{8,9},{9,8},{10,11... | collective-permute-start | bytes 233480 | tf_op jit(solution)/shard_map/ppermute | solution.py:107
  2.4 5.9 %collective-permute-start = (bf16[16,2432]{1,0:T(8,128)(2,1)S(1)}, bf16[16,2432]{1,0:T(8,128)(2,1)S(1)}, u32[]{:S(2)}, u32[]{:S(2)}) collective-permute-start(bf16[16,2432]{1,0:T(8,128)(2,1)S(1)} %get-tuple-element.29.refs_0_), channel_id=1, source_target_pairs={{0,2},{1,3},{2,0},{3,1},{4,6},{5,7},{6,4},{7,5},{8,10},{9,11},{10,... | collective-permute-start | bytes 233480 | tf_op jit(solution)/shard_map/ppermute | solution.py:107
  8.3 1.9 %collective-permute-start.2 = (bf16[16,2432]{1,0:T(8,128)(2,1)S(1)}, bf16[16,2432]{1,0:T(8,128)(2,1)S(1)}, u32[]{:S(2)}, u32[]{:S(2)}) collective-permute-start(bf16[16,2432]{1,0:T(8,128)(2,1)S(1)} %collective-permute-done.refs_0_), channel_id=1, source_target_pairs={{0,1},{1,0},{2,3},{3,2},{4,5},{5,4},{6,7},{7,6},{8,9},{9,8},{10,11... | collective-permute-start | bytes 233480 | tf_op jit(solution)/shard_map/ppermute | solution.py:107
  12.0 1.2 %collective-permute-start.3 = (f32[16,128]{1,0:T(8,128)S(1)}, f32[16,128]{1,0:T(8,128)S(1)}, u32[]{:S(2)}, u32[]{:S(2)}) collective-permute-start(f32[16,128]{1,0:T(8,128)S(1)} %get-tuple-element.44.mine.refs_0_), channel_id=1, source_target_pairs={{0,1},{1,0},{2,3},{3,2},{4,5},{5,4},{6,7},{7,6},{8,9},{9,8},{10,11... | collective-permute-start | bytes 24584 | tf_op jit(solution)/shard_map/ppermute | solution.py:107
  13.2 3.7 %collective-permute-start.4 = (f32[8,128]{1,0:T(8,128)S(1)}, f32[8,128]{1,0:T(8,128)S(1)}, u32[]{:S(2)}, u32[]{:S(2)}) collective-permute-start(f32[8,128]{1,0:T(8,128)S(1)} %shard_map.90.refs_1_), channel_id=1, source_target_pairs={{0,2},{1,3},{2,0},{3,1},{4,6},{5,7},{6,4},{7,5},{8,10},{9,11},{10,... | collective-permute-start | bytes 12296 | tf_op jit(solution)/shard_map/ppermute | solution.py:107
  18.3 4.5 %collective-permute-start.6 = (bf16[64,639]{1,0:T(8,128)(2,1)S(1)}, bf16[64,639]{1,0:T(8,128)(2,1)S(1)}, u32[]{:S(2)}, u32[]{:S(2)}) collective-permute-start(bf16[64,639]{1,0:T(8,128)(2,1)S(1)} %get-tuple-element.50.refs_0_), channel_id=1, source_target_pairs={{0,4},{4,0},{8,12},{12,8},{1,5},{5,1},{9,13},{13,9},{2,6},{6,2},{1... | collective-permute-start | bytes 245384 | tf_op jit(solution)/shard_map/ppermute | solution.py:107
  22.1 4.5 %collective-permute-start.5 = (bf16[64,619]{1,0:T(8,128)(2,1)S(1)}, bf16[64,619]{1,0:T(8,128)(2,1)S(1)}, u32[]{:S(2)}, u32[]{:S(2)}) collective-permute-start(bf16[64,619]{1,0:T(8,128)(2,1)S(1)} %get-tuple-element.52), channel_id=1, source_target_pairs={{0,4},{4,0},{8,12},{12,8},{1,5},{5,1},{9,13},{13,9},{2,6},{6,2},{1... | collective-permute-start | bytes 237704 | tf_op jit(solution)/shard_map/ppermute | solution.py:107
  23.0 5.4 %collective-permute-start.7 = (bf16[64,599]{1,0:T(8,128)(2,1)S(1)}, bf16[64,599]{1,0:T(8,128)(2,1)S(1)}, u32[]{:S(2)}, u32[]{:S(2)}) collective-permute-start(bf16[64,599]{1,0:T(8,128)(2,1)S(1)} %shard_map.93), channel_id=1, source_target_pairs={{0,8},{4,12},{8,0},{12,4},{1,9},{5,13},{9,1},{13,5},{2,10},{6,14},... | collective-permute-start | bytes 230024 | tf_op jit(solution)/shard_map/ppermute | solution.py:107

commit v13 on v12

--- a/solution.py
+++ b/solution.py
@@ -332,7 +332,7 @@
     classes = weight_ref.shape[0] // ROTS
     mass = jnp.zeros((classes, rows), jnp.float32)
     for block in range(count):
-        top, total = merged(mine, other, block, count // 2)
+        top, total = merged(mine, other, block, count - 1)
         factor = jnp.exp(stats_ref[2 * block : 2 * block + 1, :] - top) / total
         scale = stats_ref[2 * count + block : 2 * count + block + 1, :]
         factor = jnp.concatenate([factor] * repeat, axis=1)
@@ -532,7 +532,7 @@
     )
     chunks = {0: packed, 1: exchange(packed, "cls", 1)}
     for b in range(2, count, 2):
-        chunks[b] = exchange(packed, "cls", b)
+        chunks[b + 1] = exchange(packed, "cls", b + 1)
     stat_rows = -(-3 * count // 8) * 8
     work = 2 * rows * COLS * (ROTS * classes + 256)
     stats_shape = shape((stat_rows, LANES), f32)
@@ -555,9 +555,9 @@
         *[chunks[b] for b in near], classes_on_chip, phases_on_chip, scales,
     )
     for b in range(2, count, 2):
-        arrived, stats = lax.optimization_barrier((chunks[b], stats))
-        chunks[b + 1] = exchange(arrived, "cls", 1)
-    for far in (list(range(2, count, 2)), list(range(3, count, 2))):
+        arrived, stats = lax.optimization_barrier((chunks[b + 1], stats))
+        chunks[b] = exchange(arrived, "cls", 1)
+    for far in (list(range(3, count, 2)), list(range(2, count, 2))):
         shifted, exps, stats = call(
             functools.partial(rest_kernel, count, segments, far),
             [shifted_shape, exp_shape, stats_shape],
@@ -570,7 +570,7 @@
         )
     mine, distance = stats, 1
     other = exchange(mine, "cls", distance)
-    while 2 * distance < count:
+    while distance + 1 < count:
         (mine,) = call(
             functools.partial(merge_kernel, count, distance),
             [shape((-(-2 * count // 8) * 8, LANES), f32)],
@@ -579,7 +579,7 @@
             1024,
             mine, other,
         )
-        distance *= 2
+        distance = 2 * distance + 1
         other = exchange(mine, "cls", distance)
     low_bit = lambda b: b & -b
     early = list(range(doms - 1, 1, -2))

time: 29.3 us -> 29.9 us (1.020)
  waiting for transfers between devices: 6.03 us -> 6.89 us
    ppermute x8, waiting for transfers between devices: 6.03 us -> 6.89 us  [exchange(): lax.ppermute(array, axis, [(i, i ^ distance) for i in range(lax.axis_size...]
where the time goes in v13:
time: 29.9 us; the launch traced here: 29.7 us
  Pallas kernels  12.5 us (42%)
  starting transfers between devices  9.58 us (32%)
  waiting for transfers between devices  6.89 us (23%)
  between operations  0.67 us (2%)
    pallas_call x9, Pallas kernels, call(): pl.pallas_call(kernel, out_shape=[pltpu.VMEM(s.shape, s.dtype) if pinned...  12.5 us
    ppermute x8, starting transfers between devices, exchange(): lax.ppermute(array, axis, [(i, i ^ distance) for i in range(lax.axis_size...  9.58 us
    ppermute x8, waiting for transfers between devices, exchange(): lax.ppermute(array, axis, [(i, i ^ distance) for i in range(lax.axis_size...  6.89 us
  transfers between devices with their start and end apart: 8, of which 5 were waited for; matrix products, arithmetic and copies ran while one was open for 0% of the time, Pallas kernels for 25%

profile of v13, /device:TPU:0, one launch (start us, length us, event | category | flops | bytes accessed | tf_op | source)
XLA Modules:
  0.0 29.7 jit_solution(12015906486759432378)
XLA Ops:
  0.6 1.3 %shard_map.86 = (bf16[16,2432]{1,0:T(8,128)(2,1)S(1)}, bf16[64,2304]{1,0:T(8,128)(2,1)S(1)}, f32[1,64]{1,0:T(1,128)S(1)}, f32[48,2304]{1,0:T(8,128)S(1)}) custom-call(bf16[16,2304]{1,0:T(8,128)(2,1)} %particle_hbm.1, s32[16,16]{1,0:T(8,128)} %index_hbm.1, s32[1,16]{1,0:T(1,128)} %bitcast.4, s32[1,16]{1,0:T(1,128)} %bitcast.5, bf16[64,2304]{1,0:T(8,128)(2,1)} %class_hbm.1, ...), custom_call_target="tpu_custom_call" | custom-call | flops 36864 | bytes 147456 | tf_op jit(solution)/shard_map/pallas_call | solution.py:486
  1.9 0.5 %collective-permute-start.1 = (bf16[16,2432]{1,0:T(8,128)(2,1)S(1)}, bf16[16,2432]{1,0:T(8,128)(2,1)S(1)}, u32[]{:S(2)}, u32[]{:S(2)}) collective-permute-start(bf16[16,2432]{1,0:T(8,128)(2,1)S(1)} %get-tuple-element.29.refs_0_), channel_id=1, source_target_pairs={{0,1},{1,0},{2,3},{3,2},{4,5},{5,4},{6,7},{7,6},{8,9},{9,8},{10,11... | collective-permute-start | bytes 233480 | tf_op jit(solution)/shard_map/ppermute | solution.py:107
  2.4 2.6 %collective-permute-start = (bf16[16,2432]{1,0:T(8,128)(2,1)S(1)}, bf16[16,2432]{1,0:T(8,128)(2,1)S(1)}, u32[]{:S(2)}, u32[]{:S(2)}) collective-permute-start(bf16[16,2432]{1,0:T(8,128)(2,1)S(1)} %get-tuple-element.29.refs_0_), channel_id=1, source_target_pairs={{0,3},{1,2},{2,1},{3,0},{4,7},{5,6},{6,5},{7,4},{8,11},{9,10},{10,... | collective-permute-start | bytes 233480 | tf_op jit(solution)/shard_map/ppermute | solution.py:107
  5.0 0.0 collective-permute-done.1.refs_1_
  5.0 3.3 %shard_map.87 = (bf16[1024,2304]{1,0:T(8,128)(2,1)S(1)}, f32[512,1024]{1,0:T(8,128)S(1)}, f32[16,128]{1,0:T(8,128)S(1)}, bf16[512,2304]{1,0:T(8,128)(2,1)S(1)}, ...) custom-call(bf16[16,2432]{1,0:T(8,128)(2,1)S(1)} %get-tuple-element.29.refs_0_, ...), custom_call_target="tpu_custom_call" | custom-call | flops 1811939328 | bytes 4718592 | tf_op jit(solution)/shard_map/pallas_call | solution.py:486
  8.3 0.0 collective-permute-done.refs_0_
  8.3 0.1 collective-permute-start.2
  8.4 1.8 %shard_map.88 = (bf16[1024,2304]{1,0:T(8,128)(2,1)S(1)}, f32[512,1024]{1,0:T(8,128)S(1)}, f32[16,128]{1,0:T(8,128)S(1)}) custom-call(bf16[16,2432]{1,0:T(8,128)(2,1)S(1)} %collective-permute-done.refs_0_, bf16[256,2304]{1,0:T(8,128)(2,1)S(1)} %get-tuple-element.35.refs_1_, ...), custom_call_target="tpu_custom_call", output_to_operand_aliasing={{0}: (6, {}), {1}: (7, {})} | custom-call | flops 905969664 | bytes 2359296 | tf_op jit(solution)/shard_map/pallas_call | solution.py:486
  10.2 0.0 collective-permute-done.2.refs_0_
  10.2 1.8 %shard_map.89 = (bf16[1024,2304]{1,0:T(8,128)(2,1)S(1)}, f32[512,1024]{1,0:T(8,128)S(1)}, f32[16,128]{1,0:T(8,128)S(1)}) custom-call(bf16[16,2432]{1,0:T(8,128)(2,1)S(1)} %collective-permute-done.2.refs_0_, bf16[256,2304]{1,0:T(8,128)(2,1)S(1)} %get-tuple-element.35.refs_1_, ...), custom_call_target="tpu_custom_call", output_to_operand_aliasing={{0}: (6, {}), {1}: (7, {})} | custom-call | flops 905969664 | bytes 2359296 | tf_op jit(solution)/shard_map/pallas_call | solution.py:486
  11.9 0.4 %collective-permute-start.3 = (f32[16,128]{1,0:T(8,128)S(1)}, f32[16,128]{1,0:T(8,128)S(1)}, u32[]{:S(2)}, u32[]{:S(2)}) collective-permute-start(f32[16,128]{1,0:T(8,128)S(1)} %get-tuple-element.44.mine.refs_0_), channel_id=1, source_target_pairs={{0,1},{1,0},{2,3},{3,2},{4,5},{5,4},{6,7},{7,6},{8,9},{9,8},{10,11... | collective-permute-start | bytes 24584 | tf_op jit(solution)/shard_map/ppermute | solution.py:107
  12.4 0.8 %collective-permute-done.3.other = f32[16,128]{1,0:T(8,128)S(1)} collective-permute-done((f32[16,128]{1,0:T(8,128)S(1)}, f32[16,128]{1,0:T(8,128)S(1)}, u32[]{:S(2)}, u32[]{:S(2)}) %collective-permute-start.3) | collective-permute-done | bytes 8224 | tf_op jit(solution)/shard_map/ppermute | solution.py:107
  13.2 1.2 %collective-permute-start.4 = (f32[8,128]{1,0:T(8,128)S(1)}, f32[8,128]{1,0:T(8,128)S(1)}, u32[]{:S(2)}, u32[]{:S(2)}) collective-permute-start(f32[8,128]{1,0:T(8,128)S(1)} %shard_map.90.refs_1_), channel_id=1, source_target_pairs={{0,3},{1,2},{2,1},{3,0},{4,7},{5,6},{6,5},{7,4},{8,11},{9,10},{10,... | collective-permute-start | bytes 12296 | tf_op jit(solution)/shard_map/ppermute | solution.py:107
  14.4 1.9 %collective-permute-done.4.refs_2_ = f32[8,128]{1,0:T(8,128)S(1)} collective-permute-done((f32[8,128]{1,0:T(8,128)S(1)}, f32[8,128]{1,0:T(8,128)S(1)}, u32[]{:S(2)}, u32[]{:S(2)}) %collective-permute-start.4) | collective-permute-done | bytes 4128 | tf_op jit(solution)/shard_map/ppermute | solution.py:107
  16.3 1.5 %shard_map.91 = (bf16[512,1024]{1,0:T(8,128)(2,1)S(1)}, f32[64,128]{1,0:T(8,128)S(1)}, f32[64,256]{1,0:T(8,128)S(1)}, bf16[64,639]{1,0:T(8,128)(2,1)S(1)}) custom-call(f32[16,128]{1,0:T(8,128)S(1)} %get-tuple-element.44.mine.refs_0_, f32[8,128]{1,0:T(8,128)S(1)} %shard_map.90.refs_1_, f32[8,128]{1,0:T(8,128)S(1)} %collective-permute-done.4.refs_2_, ...), custom_call_target="tpu_custom_call" | custom-call | flops 603979776 | bytes 2359296 | tf_op jit(solution)/shard_map/pallas_call | solution.py:486
  17.8 1.7 %collective-permute-start.6 = (bf16[64,639]{1,0:T(8,128)(2,1)S(1)}, bf16[64,639]{1,0:T(8,128)(2,1)S(1)}, u32[]{:S(2)}, u32[]{:S(2)}) collective-permute-start(bf16[64,639]{1,0:T(8,128)(2,1)S(1)} %get-tuple-element.50.refs_0_), channel_id=1, source_target_pairs={{0,4},{4,0},{8,12},{12,8},{1,5},{5,1},{9,13},{13,9},{2,6},{6,2},{1... | collective-permute-start | bytes 245384 | tf_op jit(solution)/shard_map/ppermute | solution.py:107
  19.5 2.2 %shard_map.92 = (bf16[64,619]{1,0:T(8,128)(2,1)S(1)}, f32[64,579]{1,0:T(8,128)S(1)}, f32[64,599]{1,0:T(8,128)S(1)}) custom-call(bf16[512,1024]{1,0:T(8,128)(2,1)S(1)} %get-tuple-element.47.weight_ref, bf16[1024,2304]{1,0:T(8,128)(2,1)S(1)} %get-tuple-element.46.refs_4_.shifted_ref, f32[64,128]{1,0:T(8,128)S(1)} %get-tuple-element.48.mass_ref, ...), custom_call_target="tpu_custom_call" | custom-call | flops 1024 | bytes 1024 | tf_op jit(solution)/shard_map/pallas_call | solution.py:486
  21.6 0.5 %collective-permute-start.5 = (bf16[64,619]{1,0:T(8,128)(2,1)S(1)}, bf16[64,619]{1,0:T(8,128)(2,1)S(1)}, u32[]{:S(2)}, u32[]{:S(2)}) collective-permute-start(bf16[64,619]{1,0:T(8,128)(2,1)S(1)} %get-tuple-element.52), channel_id=1, source_target_pairs={{0,4},{4,0},{8,12},{12,8},{1,5},{5,1},{9,13},{13,9},{2,6},{6,2},{1... | collective-permute-start | bytes 237704 | tf_op jit(solution)/shard_map/ppermute | solution.py:107
  22.1 0.5 %collective-permute-done.6.refs_1_ = bf16[64,639]{1,0:T(8,128)(2,1)S(1)} collective-permute-done((bf16[64,639]{1,0:T(8,128)(2,1)S(1)}, bf16[64,639]{1,0:T(8,128)(2,1)S(1)}, u32[]{:S(2)}, u32[]{:S(2)}) %collective-permute-start.6) | collective-permute-done | bytes 81824 | tf_op jit(solution)/shard_map/ppermute | solution.py:107
  22.6 0.1 shard_map.93
  22.7 2.7 %collective-permute-start.7 = (bf16[64,599]{1,0:T(8,128)(2,1)S(1)}, bf16[64,599]{1,0:T(8,128)(2,1)S(1)}, u32[]{:S(2)}, u32[]{:S(2)}) collective-permute-start(bf16[64,599]{1,0:T(8,128)(2,1)S(1)} %shard_map.93), channel_id=1, source_target_pairs={{0,8},{4,12},{8,0},{12,4},{1,9},{5,13},{9,1},{13,5},{2,10},{6,14},... | collective-permute-start | bytes 230024 | tf_op jit(solution)/shard_map/ppermute | solution.py:107
  25.3 1.7 %collective-permute-done.5.refs_0_ = bf16[64,619]{1,0:T(8,128)(2,1)S(1)} collective-permute-done((bf16[64,619]{1,0:T(8,128)(2,1)S(1)}, bf16[64,619]{1,0:T(8,128)(2,1)S(1)}, u32[]{:S(2)}, u32[]{:S(2)}) %collective-permute-start.5) | collective-permute-done | bytes 79264 | tf_op jit(solution)/shard_map/ppermute | solution.py:107
  27.0 2.0 %collective-permute-done.7.refs_1_ = bf16[64,599]{1,0:T(8,128)(2,1)S(1)} collective-permute-done((bf16[64,599]{1,0:T(8,128)(2,1)S(1)}, bf16[64,599]{1,0:T(8,128)(2,1)S(1)}, u32[]{:S(2)}, u32[]{:S(2)}) %collective-permute-start.7) | collective-permute-done | bytes 76704 | tf_op jit(solution)/shard_map/ppermute | solution.py:107
  29.0 0.7 %shard_map.94 = (f32[64,576]{1,0:T(8,128)}, f32[1,64]{1,0:T(1,128)}) custom-call(f32[64,579]{1,0:T(8,128)S(1)} %get-tuple-element.51.own_ref, bf16[64,619]{1,0:T(8,128)(2,1)S(1)} %collective-permute-done.5.refs_0_, bf16[64,599]{1,0:T(8,128)(2,1)S(1)} %collective-permute-done.7.refs_1_), custom_call_target="tpu_custom_call" | custom-call | flops 163840 | bytes 655360 | tf_op jit(solution)/shard_map/pallas_call | solution.py:486
  (1 shorter events, 0.0 us)
Async XLA Ops:
  1.9 3.1 %collective-permute-start.1 = (bf16[16,2432]{1,0:T(8,128)(2,1)S(1)}, bf16[16,2432]{1,0:T(8,128)(2,1)S(1)}, u32[]{:S(2)}, u32[]{:S(2)}) collective-permute-start(bf16[16,2432]{1,0:T(8,128)(2,1)S(1)} %get-tuple-element.29.refs_0_), channel_id=1, source_target_pairs={{0,1},{1,0},{2,3},{3,2},{4,5},{5,4},{6,7},{7,6},{8,9},{9,8},{10,11... | collective-permute-start | bytes 233480 | tf_op jit(solution)/shard_map/ppermute | solution.py:107
  2.4 5.9 %collective-permute-start = (bf16[16,2432]{1,0:T(8,128)(2,1)S(1)}, bf16[16,2432]{1,0:T(8,128)(2,1)S(1)}, u32[]{:S(2)}, u32[]{:S(2)}) collective-permute-start(bf16[16,2432]{1,0:T(8,128)(2,1)S(1)} %get-tuple-element.29.refs_0_), channel_id=1, source_target_pairs={{0,3},{1,2},{2,1},{3,0},{4,7},{5,6},{6,5},{7,4},{8,11},{9,10},{10,... | collective-permute-start | bytes 233480 | tf_op jit(solution)/shard_map/ppermute | solution.py:107
  8.3 1.8 %collective-permute-start.2 = (bf16[16,2432]{1,0:T(8,128)(2,1)S(1)}, bf16[16,2432]{1,0:T(8,128)(2,1)S(1)}, u32[]{:S(2)}, u32[]{:S(2)}) collective-permute-start(bf16[16,2432]{1,0:T(8,128)(2,1)S(1)} %collective-permute-done.refs_0_), channel_id=1, source_target_pairs={{0,1},{1,0},{2,3},{3,2},{4,5},{5,4},{6,7},{7,6},{8,9},{9,8},{10,11... | collective-permute-start | bytes 233480 | tf_op jit(solution)/shard_map/ppermute | solution.py:107
  11.9 1.3 %collective-permute-start.3 = (f32[16,128]{1,0:T(8,128)S(1)}, f32[16,128]{1,0:T(8,128)S(1)}, u32[]{:S(2)}, u32[]{:S(2)}) collective-permute-start(f32[16,128]{1,0:T(8,128)S(1)} %get-tuple-element.44.mine.refs_0_), channel_id=1, source_target_pairs={{0,1},{1,0},{2,3},{3,2},{4,5},{5,4},{6,7},{7,6},{8,9},{9,8},{10,11... | collective-permute-start | bytes 24584 | tf_op jit(solution)/shard_map/ppermute | solution.py:107
  13.2 3.1 %collective-permute-start.4 = (f32[8,128]{1,0:T(8,128)S(1)}, f32[8,128]{1,0:T(8,128)S(1)}, u32[]{:S(2)}, u32[]{:S(2)}) collective-permute-start(f32[8,128]{1,0:T(8,128)S(1)} %shard_map.90.refs_1_), channel_id=1, source_target_pairs={{0,3},{1,2},{2,1},{3,0},{4,7},{5,6},{6,5},{7,4},{8,11},{9,10},{10,... | collective-permute-start | bytes 12296 | tf_op jit(solution)/shard_map/ppermute | solution.py:107
  17.8 4.8 %collective-permute-start.6 = (bf16[64,639]{1,0:T(8,128)(2,1)S(1)}, bf16[64,639]{1,0:T(8,128)(2,1)S(1)}, u32[]{:S(2)}, u32[]{:S(2)}) collective-permute-start(bf16[64,639]{1,0:T(8,128)(2,1)S(1)} %get-tuple-element.50.refs_0_), channel_id=1, source_target_pairs={{0,4},{4,0},{8,12},{12,8},{1,5},{5,1},{9,13},{13,9},{2,6},{6,2},{1... | collective-permute-start | bytes 245384 | tf_op jit(solution)/shard_map/ppermute | solution.py:107
  21.6 5.4 %collective-permute-start.5 = (bf16[64,619]{1,0:T(8,128)(2,1)S(1)}, bf16[64,619]{1,0:T(8,128)(2,1)S(1)}, u32[]{:S(2)}, u32[]{:S(2)}) collective-permute-start(bf16[64,619]{1,0:T(8,128)(2,1)S(1)} %get-tuple-element.52), channel_id=1, source_target_pairs={{0,4},{4,0},{8,12},{12,8},{1,5},{5,1},{9,13},{13,9},{2,6},{6,2},{1... | collective-permute-start | bytes 237704 | tf_op jit(solution)/shard_map/ppermute | solution.py:107
  22.7 6.3 %collective-permute-start.7 = (bf16[64,599]{1,0:T(8,128)(2,1)S(1)}, bf16[64,599]{1,0:T(8,128)(2,1)S(1)}, u32[]{:S(2)}, u32[]{:S(2)}) collective-permute-start(bf16[64,599]{1,0:T(8,128)(2,1)S(1)} %shard_map.93), channel_id=1, source_target_pairs={{0,8},{4,12},{8,0},{12,4},{1,9},{5,13},{9,1},{13,5},{2,10},{6,14},... | collective-permute-start | bytes 230024 | tf_op jit(solution)/shard_map/ppermute | solution.py:107

commit v14 on v12

--- a/solution.py
+++ b/solution.py
@@ -198,12 +198,9 @@
         copy.wait()
 
 
-def score_block(segments, block_ref, table_ref, scale_ref, rotated_ref, norm_ref, shifted_ref, out):
+def match_block(segments, block_ref, table_ref, scale_ref, rotated_ref, shifted_ref):
     particles = block_ref.shape[0]
-    classes = norm_ref.shape[0]
     candidates = shifted_ref.shape[0] // particles
-    rows = particles * candidates
-    repeat = rows // LANES
     meta = block_ref[:, COLS : COLS + META].astype(jnp.float32)
     index = meta[:, :candidates].astype(jnp.int32)
     lane = lane_index((particles, LANES))
@@ -222,8 +219,8 @@
         axis=1,
         keepdims=True,
     )
-    scale = to_lanes(scale_column, rows)
-    prior = to_lanes(meta[:, candidates : candidates + 1], rows)
+    scale = to_lanes(scale_column, LANES)
+    prior = to_lanes(meta[:, candidates : candidates + 1], LANES)
     for real_start, imag_start, width in segments:
         real_columns = slice(real_start, real_start + width)
         imag_columns = slice(imag_start, imag_start + width)
@@ -242,14 +239,21 @@
         (((1,), (1,)), ((), ())),
         preferred_element_type=jnp.float32,
     )
+    return product, scale, prior
+
+
+def soften_block(product, scale, prior, norm_ref, particles, rows, out):
+    repeat = rows // LANES
     norm = jnp.concatenate([norm_ref[...]] * repeat, axis=1)
+    scale = jnp.concatenate([scale] * repeat, axis=1)
+    prior = jnp.concatenate([prior] * repeat, axis=1)
     half_square = 0.5 * scale * scale
     scores = []
     highest = None
     for rotation in range(ROTS):
         distance = jnp.abs(rotation - prior)
         score = (
-            scale * product[rotation * classes : (rotation + 1) * classes]
+            scale * product(rotation)
             - half_square * norm
             - ROT_PRIOR * (distance * distance)
         )
@@ -265,25 +269,43 @@
         added = jnp.sum(value, axis=0, keepdims=True)
         total = added if total is None else total + added
     total = fold_lanes(total, particles, jnp.add)
-    return highest, total, scale[:, :LANES]
-
-
-def score_blocks(count, segments, chunks, blocks, table_ref, scale_ref, rotated_ref, norm_ref, shifted_ref, exp_ref, stats_ref):
+    return highest, total
+
+
+def score_blocks(
+    count, segments, pending, chunks, last, blocks, table_ref, scale_ref, rotated_ref, norm_ref,
+    shifted_ref, exp_ref, stats_ref,
+):
     classes = norm_ref.shape[0]
     rows = exp_ref.shape[1] // count
+    particles = blocks[0].shape[0]
+
+    def soften(block, product):
+        part = slice(block * rows, (block + 1) * rows)
+
+        def out(rotation, value):
+            exp_ref[rotation * classes : (rotation + 1) * classes, part] = value
+
+        scale = stats_ref[2 * count + block : 2 * count + block + 1, :]
+        prior = stats_ref[3 * count + block : 3 * count + block + 1, :]
+        highest, total = soften_block(product, scale, prior, norm_ref, particles, rows, out)
+        stats_ref[2 * block : 2 * block + 1, :] = highest
+        stats_ref[2 * block + 1 : 2 * block + 2, :] = total
+
+    for block in pending:
+        part = slice(block * rows, (block + 1) * rows)
+        soften(block, lambda rotation: exp_ref[rotation * classes : (rotation + 1) * classes, part])
     for block, block_ref in zip(chunks, blocks):
         part = slice(block * rows, (block + 1) * rows)
-
-        def out(rotation, value):
-            exp_ref[rotation * classes : (rotation + 1) * classes, part] = value
-
-        highest, total, scale = score_block(
-            segments, block_ref, table_ref, scale_ref, rotated_ref, norm_ref,
-            shifted_ref.at[part, :], out,
-        )
-        stats_ref[2 * block : 2 * block + 1, :] = highest
-        stats_ref[2 * block + 1 : 2 * block + 2, :] = total
+        product, scale, prior = match_block(
+            segments, block_ref, table_ref, scale_ref, rotated_ref, shifted_ref.at[part, :]
+        )
         stats_ref[2 * count + block : 2 * count + block + 1, :] = scale
+        stats_ref[3 * count + block : 3 * count + block + 1, :] = prior
+        if block != chunks[-1] or last:
+            soften(block, lambda rotation: product[rotation * classes : (rotation + 1) * classes])
+        else:
+            exp_ref[0 : ROTS * classes, part] = product
 
 
 def first_kernel(count, groups, segments, chunks, *refs):
@@ -294,18 +316,18 @@
     rotate_classes(groups, class_ref, rotated_ref, norm_ref)
     stats_ref[...] = jnp.zeros_like(stats_ref)
     score_blocks(
-        count, segments, chunks, blocks, table_ref, scale_ref, rotated_ref, norm_ref,
+        count, segments, [], chunks, False, blocks, table_ref, scale_ref, rotated_ref, norm_ref,
         shifted_ref, exp_ref, stats_ref,
     )
 
 
-def rest_kernel(count, segments, chunks, *refs):
+def rest_kernel(count, segments, pending, chunks, last, *refs):
     blocks, refs = refs[: len(chunks)], refs[len(chunks) :]
     table_ref, scale_ref, rotated_ref, norm_ref, before_ref = refs[:5]
     shifted_ref, exp_ref, stats_ref = refs[7:]
     stats_ref[...] = before_ref[...]
     score_blocks(
-        count, segments, chunks, blocks, table_ref, scale_ref, rotated_ref, norm_ref,
+        count, segments, pending, chunks, last, blocks, table_ref, scale_ref, rotated_ref, norm_ref,
         shifted_ref, exp_ref, stats_ref,
     )
 
@@ -533,7 +555,7 @@
     chunks = {0: packed, 1: exchange(packed, "cls", 1)}
     for b in range(2, count, 2):
         chunks[b] = exchange(packed, "cls", b)
-    stat_rows = -(-3 * count // 8) * 8
+    stat_rows = -(-4 * count // 8) * 8
     work = 2 * rows * COLS * (ROTS * classes + 256)
     stats_shape = shape((stat_rows, LANES), f32)
     shifted_shape = shape((count * rows, COLS), bf16)
@@ -557,9 +579,10 @@
     for b in range(2, count, 2):
         arrived, stats = lax.optimization_barrier((chunks[b], stats))
         chunks[b + 1] = exchange(arrived, "cls", 1)
-    for far in (list(range(2, count, 2)), list(range(3, count, 2))):
+    evens, odds = list(range(2, count, 2)), list(range(3, count, 2))
+    for pending, far in ((near[-1:], evens), (evens[-1:], odds)):
         shifted, exps, stats = call(
-            functools.partial(rest_kernel, count, segments, far),
+            functools.partial(rest_kernel, count, segments, pending, far, far is odds),
             [shifted_shape, exp_shape, stats_shape],
             [],
             work * len(far),

time: 29.3 us -> 29 us (0.990)
  starting transfers between devices: 9.84 us -> 10.4 us
  Pallas kernels: 12.5 us -> 12 us
    pallas_call x9, Pallas kernels: 12.5 us -> 12 us  [call(): pl.pallas_call(kernel, out_shape=[pltpu.VMEM(s.shape, s.dtype) if pinned...]
    ppermute x8, starting transfers between devices: 9.84 us -> 10.4 us  [exchange(): lax.ppermute(array, axis, [(i, i ^ distance) for i in range(lax.axis_size...]
  transfers between devices with their start and end apart: 8 -> 8, of which waited for: 5 -> 5; matrix products, arithmetic and copies ran while one was open for 0% -> 0% of each run, Pallas kernels for 25% -> 23%
where the time goes in v14:
time: 29 us; the launch traced here: 28.8 us
  Pallas kernels  12 us (41%)
  starting transfers between devices  10.4 us (36%)
  waiting for transfers between devices  5.74 us (20%)
  between operations  0.69 us (2%)
    pallas_call x9, Pallas kernels, call(): pl.pallas_call(kernel, out_shape=[pltpu.VMEM(s.shape, s.dtype) if pinned...  12 us
    ppermute x8, starting transfers between devices, exchange(): lax.ppermute(array, axis, [(i, i ^ distance) for i in range(lax.axis_size...  10.4 us
    ppermute x8, waiting for transfers between devices, exchange(): lax.ppermute(array, axis, [(i, i ^ distance) for i in range(lax.axis_size...  5.74 us
  transfers between devices with their start and end apart: 8, of which 5 were waited for; matrix products, arithmetic and copies ran while one was open for 0% of the time, Pallas kernels for 23%

profile of v14, /device:TPU:0, one launch (start us, length us, event | category | flops | bytes accessed | tf_op | source)
XLA Modules:
  0.0 28.8 jit_solution(4092385337984338817)
XLA Ops:
  0.6 1.3 %shard_map.86 = (bf16[16,2432]{1,0:T(8,128)(2,1)S(1)}, bf16[64,2304]{1,0:T(8,128)(2,1)S(1)}, f32[1,64]{1,0:T(1,128)S(1)}, f32[48,2304]{1,0:T(8,128)S(1)}) custom-call(bf16[16,2304]{1,0:T(8,128)(2,1)} %particle_hbm.1, s32[16,16]{1,0:T(8,128)} %index_hbm.1, s32[1,16]{1,0:T(1,128)} %bitcast.4, s32[1,16]{1,0:T(1,128)} %bitcast.5, bf16[64,2304]{1,0:T(8,128)(2,1)} %class_hbm.1, ...), custom_call_target="tpu_custom_call" | custom-call | flops 36864 | bytes 147456 | tf_op jit(solution)/shard_map/pallas_call | solution.py:508
  1.9 0.5 %collective-permute-start.1 = (bf16[16,2432]{1,0:T(8,128)(2,1)S(1)}, bf16[16,2432]{1,0:T(8,128)(2,1)S(1)}, u32[]{:S(2)}, u32[]{:S(2)}) collective-permute-start(bf16[16,2432]{1,0:T(8,128)(2,1)S(1)} %get-tuple-element.29.refs_0_), channel_id=1, source_target_pairs={{0,1},{1,0},{2,3},{3,2},{4,5},{5,4},{6,7},{7,6},{8,9},{9,8},{10,11... | collective-permute-start | bytes 233480 | tf_op jit(solution)/shard_map/ppermute | solution.py:107
  2.4 2.6 %collective-permute-start = (bf16[16,2432]{1,0:T(8,128)(2,1)S(1)}, bf16[16,2432]{1,0:T(8,128)(2,1)S(1)}, u32[]{:S(2)}, u32[]{:S(2)}) collective-permute-start(bf16[16,2432]{1,0:T(8,128)(2,1)S(1)} %get-tuple-element.29.refs_0_), channel_id=1, source_target_pairs={{0,2},{1,3},{2,0},{3,1},{4,6},{5,7},{6,4},{7,5},{8,10},{9,11},{10,... | collective-permute-start | bytes 233480 | tf_op jit(solution)/shard_map/ppermute | solution.py:107
  5.0 0.0 collective-permute-done.1.refs_1_
  5.0 3.0 %shard_map.87 = (bf16[1024,2304]{1,0:T(8,128)(2,1)S(1)}, f32[512,1024]{1,0:T(8,128)S(1)}, f32[16,128]{1,0:T(8,128)S(1)}, bf16[512,2304]{1,0:T(8,128)(2,1)S(1)}, ...) custom-call(bf16[16,2432]{1,0:T(8,128)(2,1)S(1)} %get-tuple-element.29.refs_0_, ...), custom_call_target="tpu_custom_call" | custom-call | flops 1811939328 | bytes 4718592 | tf_op jit(solution)/shard_map/pallas_call | solution.py:508
  8.0 0.0 collective-permute-done.refs_0_
  8.0 0.2 collective-permute-start.2
  8.2 1.4 %shard_map.88 = (bf16[1024,2304]{1,0:T(8,128)(2,1)S(1)}, f32[512,1024]{1,0:T(8,128)S(1)}, f32[16,128]{1,0:T(8,128)S(1)}) custom-call(bf16[16,2432]{1,0:T(8,128)(2,1)S(1)} %collective-permute-done.refs_0_, bf16[256,2304]{1,0:T(8,128)(2,1)S(1)} %get-tuple-element.35.refs_1_, ...), custom_call_target="tpu_custom_call", output_to_operand_aliasing={{0}: (6, {}), {1}: (7, {})} | custom-call | flops 905969664 | bytes 2359296 | tf_op jit(solution)/shard_map/pallas_call | solution.py:508
  9.6 0.0 collective-permute-done.2.refs_0_
  9.6 1.9 %shard_map.89 = (bf16[1024,2304]{1,0:T(8,128)(2,1)S(1)}, f32[512,1024]{1,0:T(8,128)S(1)}, f32[16,128]{1,0:T(8,128)S(1)}) custom-call(bf16[16,2432]{1,0:T(8,128)(2,1)S(1)} %collective-permute-done.2.refs_0_, bf16[256,2304]{1,0:T(8,128)(2,1)S(1)} %get-tuple-element.35.refs_1_, ...), custom_call_target="tpu_custom_call", output_to_operand_aliasing={{0}: (6, {}), {1}: (7, {})} | custom-call | flops 905969664 | bytes 2359296 | tf_op jit(solution)/shard_map/pallas_call | solution.py:508
  11.5 0.4 %collective-permute-start.3 = (f32[16,128]{1,0:T(8,128)S(1)}, f32[16,128]{1,0:T(8,128)S(1)}, u32[]{:S(2)}, u32[]{:S(2)}) collective-permute-start(f32[16,128]{1,0:T(8,128)S(1)} %get-tuple-element.44.mine.refs_0_), channel_id=1, source_target_pairs={{0,1},{1,0},{2,3},{3,2},{4,5},{5,4},{6,7},{7,6},{8,9},{9,8},{10,11... | collective-permute-start | bytes 24584 | tf_op jit(solution)/shard_map/ppermute | solution.py:107
  11.8 0.8 %collective-permute-done.3.other = f32[16,128]{1,0:T(8,128)S(1)} collective-permute-done((f32[16,128]{1,0:T(8,128)S(1)}, f32[16,128]{1,0:T(8,128)S(1)}, u32[]{:S(2)}, u32[]{:S(2)}) %collective-permute-start.3) | collective-permute-done | bytes 8224 | tf_op jit(solution)/shard_map/ppermute | solution.py:107
  12.7 1.8 %collective-permute-start.4 = (f32[8,128]{1,0:T(8,128)S(1)}, f32[8,128]{1,0:T(8,128)S(1)}, u32[]{:S(2)}, u32[]{:S(2)}) collective-permute-start(f32[8,128]{1,0:T(8,128)S(1)} %shard_map.90.refs_1_), channel_id=1, source_target_pairs={{0,2},{1,3},{2,0},{3,1},{4,6},{5,7},{6,4},{7,5},{8,10},{9,11},{10,... | collective-permute-start | bytes 12296 | tf_op jit(solution)/shard_map/ppermute | solution.py:107
  14.4 1.9 %collective-permute-done.4.refs_2_ = f32[8,128]{1,0:T(8,128)S(1)} collective-permute-done((f32[8,128]{1,0:T(8,128)S(1)}, f32[8,128]{1,0:T(8,128)S(1)}, u32[]{:S(2)}, u32[]{:S(2)}) %collective-permute-start.4) | collective-permute-done | bytes 4128 | tf_op jit(solution)/shard_map/ppermute | solution.py:107
  16.3 1.5 %shard_map.91 = (bf16[512,1024]{1,0:T(8,128)(2,1)S(1)}, f32[64,128]{1,0:T(8,128)S(1)}, f32[64,256]{1,0:T(8,128)S(1)}, bf16[64,639]{1,0:T(8,128)(2,1)S(1)}) custom-call(f32[16,128]{1,0:T(8,128)S(1)} %get-tuple-element.44.mine.refs_0_, f32[8,128]{1,0:T(8,128)S(1)} %shard_map.90.refs_1_, f32[8,128]{1,0:T(8,128)S(1)} %collective-permute-done.4.refs_2_, ...), custom_call_target="tpu_custom_call" | custom-call | flops 603979776 | bytes 2359296 | tf_op jit(solution)/shard_map/pallas_call | solution.py:508
  17.8 1.8 %collective-permute-start.6 = (bf16[64,639]{1,0:T(8,128)(2,1)S(1)}, bf16[64,639]{1,0:T(8,128)(2,1)S(1)}, u32[]{:S(2)}, u32[]{:S(2)}) collective-permute-start(bf16[64,639]{1,0:T(8,128)(2,1)S(1)} %get-tuple-element.50.refs_0_), channel_id=1, source_target_pairs={{0,4},{4,0},{8,12},{12,8},{1,5},{5,1},{9,13},{13,9},{2,6},{6,2},{1... | collective-permute-start | bytes 245384 | tf_op jit(solution)/shard_map/ppermute | solution.py:107
  19.7 2.2 %shard_map.92 = (bf16[64,619]{1,0:T(8,128)(2,1)S(1)}, f32[64,579]{1,0:T(8,128)S(1)}, f32[64,599]{1,0:T(8,128)S(1)}) custom-call(bf16[512,1024]{1,0:T(8,128)(2,1)S(1)} %get-tuple-element.47.weight_ref, bf16[1024,2304]{1,0:T(8,128)(2,1)S(1)} %get-tuple-element.46.refs_4_.shifted_ref, f32[64,128]{1,0:T(8,128)S(1)} %get-tuple-element.48.mass_ref, ...), custom_call_target="tpu_custom_call" | custom-call | flops 1024 | bytes 1024 | tf_op jit(solution)/shard_map/pallas_call | solution.py:508
  21.8 0.3 collective-permute-start.5
  22.1 0.2 collective-permute-done.6.refs_1_
  22.3 0.1 shard_map.93
  22.4 2.8 %collective-permute-start.7 = (bf16[64,599]{1,0:T(8,128)(2,1)S(1)}, bf16[64,599]{1,0:T(8,128)(2,1)S(1)}, u32[]{:S(2)}, u32[]{:S(2)}) collective-permute-start(bf16[64,599]{1,0:T(8,128)(2,1)S(1)} %shard_map.93), channel_id=1, source_target_pairs={{0,8},{4,12},{8,0},{12,4},{1,9},{5,13},{9,1},{13,5},{2,10},{6,14},... | collective-permute-start | bytes 230024 | tf_op jit(solution)/shard_map/ppermute | solution.py:107
  25.3 1.0 %collective-permute-done.5.refs_0_ = bf16[64,619]{1,0:T(8,128)(2,1)S(1)} collective-permute-done((bf16[64,619]{1,0:T(8,128)(2,1)S(1)}, bf16[64,619]{1,0:T(8,128)(2,1)S(1)}, u32[]{:S(2)}, u32[]{:S(2)}) %collective-permute-start.5) | collective-permute-done | bytes 79264 | tf_op jit(solution)/shard_map/ppermute | solution.py:107
  26.3 1.7 %collective-permute-done.7.refs_1_ = bf16[64,599]{1,0:T(8,128)(2,1)S(1)} collective-permute-done((bf16[64,599]{1,0:T(8,128)(2,1)S(1)}, bf16[64,599]{1,0:T(8,128)(2,1)S(1)}, u32[]{:S(2)}, u32[]{:S(2)}) %collective-permute-start.7) | collective-permute-done | bytes 76704 | tf_op jit(solution)/shard_map/ppermute | solution.py:107
  28.0 0.7 %shard_map.94 = (f32[64,576]{1,0:T(8,128)}, f32[1,64]{1,0:T(1,128)}) custom-call(f32[64,579]{1,0:T(8,128)S(1)} %get-tuple-element.51.own_ref, bf16[64,619]{1,0:T(8,128)(2,1)S(1)} %collective-permute-done.5.refs_0_, bf16[64,599]{1,0:T(8,128)(2,1)S(1)} %collective-permute-done.7.refs_1_), custom_call_target="tpu_custom_call" | custom-call | flops 163840 | bytes 655360 | tf_op jit(solution)/shard_map/pallas_call | solution.py:508
  (1 shorter events, 0.0 us)
Async XLA Ops:
  1.9 3.1 %collective-permute-start.1 = (bf16[16,2432]{1,0:T(8,128)(2,1)S(1)}, bf16[16,2432]{1,0:T(8,128)(2,1)S(1)}, u32[]{:S(2)}, u32[]{:S(2)}) collective-permute-start(bf16[16,2432]{1,0:T(8,128)(2,1)S(1)} %get-tuple-element.29.refs_0_), channel_id=1, source_target_pairs={{0,1},{1,0},{2,3},{3,2},{4,5},{5,4},{6,7},{7,6},{8,9},{9,8},{10,11... | collective-permute-start | bytes 233480 | tf_op jit(solution)/shard_map/ppermute | solution.py:107
  2.4 5.5 %collective-permute-start = (bf16[16,2432]{1,0:T(8,128)(2,1)S(1)}, bf16[16,2432]{1,0:T(8,128)(2,1)S(1)}, u32[]{:S(2)}, u32[]{:S(2)}) collective-permute-start(bf16[16,2432]{1,0:T(8,128)(2,1)S(1)} %get-tuple-element.29.refs_0_), channel_id=1, source_target_pairs={{0,2},{1,3},{2,0},{3,1},{4,6},{5,7},{6,4},{7,5},{8,10},{9,11},{10,... | collective-permute-start | bytes 233480 | tf_op jit(solution)/shard_map/ppermute | solution.py:107
  8.0 1.6 %collective-permute-start.2 = (bf16[16,2432]{1,0:T(8,128)(2,1)S(1)}, bf16[16,2432]{1,0:T(8,128)(2,1)S(1)}, u32[]{:S(2)}, u32[]{:S(2)}) collective-permute-start(bf16[16,2432]{1,0:T(8,128)(2,1)S(1)} %collective-permute-done.refs_0_), channel_id=1, source_target_pairs={{0,1},{1,0},{2,3},{3,2},{4,5},{5,4},{6,7},{7,6},{8,9},{9,8},{10,11... | collective-permute-start | bytes 233480 | tf_op jit(solution)/shard_map/ppermute | solution.py:107
  11.5 1.2 %collective-permute-start.3 = (f32[16,128]{1,0:T(8,128)S(1)}, f32[16,128]{1,0:T(8,128)S(1)}, u32[]{:S(2)}, u32[]{:S(2)}) collective-permute-start(f32[16,128]{1,0:T(8,128)S(1)} %get-tuple-element.44.mine.refs_0_), channel_id=1, source_target_pairs={{0,1},{1,0},{2,3},{3,2},{4,5},{5,4},{6,7},{7,6},{8,9},{9,8},{10,11... | collective-permute-start | bytes 24584 | tf_op jit(solution)/shard_map/ppermute | solution.py:107
  12.7 3.7 %collective-permute-start.4 = (f32[8,128]{1,0:T(8,128)S(1)}, f32[8,128]{1,0:T(8,128)S(1)}, u32[]{:S(2)}, u32[]{:S(2)}) collective-permute-start(f32[8,128]{1,0:T(8,128)S(1)} %shard_map.90.refs_1_), channel_id=1, source_target_pairs={{0,2},{1,3},{2,0},{3,1},{4,6},{5,7},{6,4},{7,5},{8,10},{9,11},{10,... | collective-permute-start | bytes 12296 | tf_op jit(solution)/shard_map/ppermute | solution.py:107
  17.8 4.5 %collective-permute-start.6 = (bf16[64,639]{1,0:T(8,128)(2,1)S(1)}, bf16[64,639]{1,0:T(8,128)(2,1)S(1)}, u32[]{:S(2)}, u32[]{:S(2)}) collective-permute-start(bf16[64,639]{1,0:T(8,128)(2,1)S(1)} %get-tuple-element.50.refs_0_), channel_id=1, source_target_pairs={{0,4},{4,0},{8,12},{12,8},{1,5},{5,1},{9,13},{13,9},{2,6},{6,2},{1... | collective-permute-start | bytes 245384 | tf_op jit(solution)/shard_map/ppermute | solution.py:107
  21.8 4.5 %collective-permute-start.5 = (bf16[64,619]{1,0:T(8,128)(2,1)S(1)}, bf16[64,619]{1,0:T(8,128)(2,1)S(1)}, u32[]{:S(2)}, u32[]{:S(2)}) collective-permute-start(bf16[64,619]{1,0:T(8,128)(2,1)S(1)} %get-tuple-element.52), channel_id=1, source_target_pairs={{0,4},{4,0},{8,12},{12,8},{1,5},{5,1},{9,13},{13,9},{2,6},{6,2},{1... | collective-permute-start | bytes 237704 | tf_op jit(solution)/shard_map/ppermute | solution.py:107
  22.4 5.6 %collective-permute-start.7 = (bf16[64,599]{1,0:T(8,128)(2,1)S(1)}, bf16[64,599]{1,0:T(8,128)(2,1)S(1)}, u32[]{:S(2)}, u32[]{:S(2)}) collective-permute-start(bf16[64,599]{1,0:T(8,128)(2,1)S(1)} %shard_map.93), channel_id=1, source_target_pairs={{0,8},{4,12},{8,0},{12,4},{1,9},{5,13},{9,1},{13,5},{2,10},{6,14},... | collective-permute-start | bytes 230024 | tf_op jit(solution)/shard_map/ppermute | solution.py:107

commit v15 on v14

--- a/solution.py
+++ b/solution.py
@@ -608,7 +608,7 @@
     early = list(range(doms - 1, 1, -2))
     order = early + [1] + sorted(range(2, doms, 2), key=lambda b: (low_bit(b), -b))
     extents = {b: width + 3 + (doms - 1 - place) * growth for place, b in enumerate(order)}
-    late = [1] + list(range(0, doms, 2))
+    late = [1] + list(range(2, doms, 2))
     weights, mass, tails, *made = call(
         functools.partial(first_sums_kernel, count, doms, width, main, early),
         [
@@ -649,7 +649,16 @@
             blocks[b], *incoming[b],
         )
         incoming[b ^ low_bit(b)].append(exchange(block, "dom", low_bit(b)))
-    own, received = blocks[0], incoming[0]
+    (own,) = call(
+        functools.partial(rest_sums_kernel, doms, width, main, [0]),
+        [shape((classes, width + 3), f32)],
+        [],
+        1024,
+        1024,
+        weights, shifted, mass, tails, block,
+        chip=(1,),
+    )
+    received = incoming[0]
     class_sums, class_weights = call(
         functools.partial(final_kernel, width),
         [shape((classes, width), f32), shape((1, classes), f32)],

time: 29 us -> 28.8 us (level)
  waiting for transfers between devices: 5.74 us -> 5.22 us
  Pallas kernels: 12 us -> 12.4 us
    ppermute x8, waiting for transfers between devices: 5.74 us -> 5.22 us  [exchange(): lax.ppermute(array, axis, [(i, i ^ distance) for i in range(lax.axis_size...]
    pallas_call x9 -> x10, Pallas kernels: 12 us -> 12.4 us  [call(): pl.pallas_call(kernel, out_shape=[pltpu.VMEM(s.shape, s.dtype) if pinned...]
  transfers between devices with their start and end apart: 8 -> 8, of which waited for: 5 -> 4; matrix products, arithmetic and copies ran while one was open for 0% -> 0% of each run, Pallas kernels for 23% -> 25%
where the time goes in v15:
time: 28.8 us; the launch traced here: 28.6 us
  Pallas kernels  12.4 us (43%)
  starting transfers between devices  10.3 us (36%)
  waiting for transfers between devices  5.22 us (18%)
  between operations  0.7 us (2%)
    pallas_call x10, Pallas kernels, call(): pl.pallas_call(kernel, out_shape=[pltpu.VMEM(s.shape, s.dtype) if pinned...  12.4 us
    ppermute x8, starting transfers between devices, exchange(): lax.ppermute(array, axis, [(i, i ^ distance) for i in range(lax.axis_size...  10.3 us
    ppermute x8, waiting for transfers between devices, exchange(): lax.ppermute(array, axis, [(i, i ^ distance) for i in range(lax.axis_size...  5.22 us
  transfers between devices with their start and end apart: 8, of which 4 were waited for; matrix products, arithmetic and copies ran while one was open for 0% of the time, Pallas kernels for 25%

profile of v15, /device:TPU:0, one launch (start us, length us, event | category | flops | bytes accessed | tf_op | source)
XLA Modules:
  0.0 28.6 jit_solution(6622686602205167082)
XLA Ops:
  0.6 1.3 %shard_map.86 = (bf16[16,2432]{1,0:T(8,128)(2,1)S(1)}, bf16[64,2304]{1,0:T(8,128)(2,1)S(1)}, f32[1,64]{1,0:T(1,128)S(1)}, f32[48,2304]{1,0:T(8,128)S(1)}) custom-call(bf16[16,2304]{1,0:T(8,128)(2,1)} %particle_hbm.1, s32[16,16]{1,0:T(8,128)} %index_hbm.1, s32[1,16]{1,0:T(1,128)} %bitcast.4, s32[1,16]{1,0:T(1,128)} %bitcast.5, bf16[64,2304]{1,0:T(8,128)(2,1)} %class_hbm.1, ...), custom_call_target="tpu_custom_call" | custom-call | flops 36864 | bytes 147456 | tf_op jit(solution)/shard_map/pallas_call | solution.py:508
  1.9 0.5 %collective-permute-start.1 = (bf16[16,2432]{1,0:T(8,128)(2,1)S(1)}, bf16[16,2432]{1,0:T(8,128)(2,1)S(1)}, u32[]{:S(2)}, u32[]{:S(2)}) collective-permute-start(bf16[16,2432]{1,0:T(8,128)(2,1)S(1)} %get-tuple-element.28.refs_0_), channel_id=1, source_target_pairs={{0,1},{1,0},{2,3},{3,2},{4,5},{5,4},{6,7},{7,6},{8,9},{9,8},{10,11... | collective-permute-start | bytes 233480 | tf_op jit(solution)/shard_map/ppermute | solution.py:107
  2.4 2.6 %collective-permute-start = (bf16[16,2432]{1,0:T(8,128)(2,1)S(1)}, bf16[16,2432]{1,0:T(8,128)(2,1)S(1)}, u32[]{:S(2)}, u32[]{:S(2)}) collective-permute-start(bf16[16,2432]{1,0:T(8,128)(2,1)S(1)} %get-tuple-element.28.refs_0_), channel_id=1, source_target_pairs={{0,2},{1,3},{2,0},{3,1},{4,6},{5,7},{6,4},{7,5},{8,10},{9,11},{10,... | collective-permute-start | bytes 233480 | tf_op jit(solution)/shard_map/ppermute | solution.py:107
  5.0 0.0 collective-permute-done.1.refs_1_
  5.0 3.0 %shard_map.87 = (bf16[1024,2304]{1,0:T(8,128)(2,1)S(1)}, f32[512,1024]{1,0:T(8,128)S(1)}, f32[16,128]{1,0:T(8,128)S(1)}, bf16[512,2304]{1,0:T(8,128)(2,1)S(1)}, ...) custom-call(bf16[16,2432]{1,0:T(8,128)(2,1)S(1)} %get-tuple-element.28.refs_0_, ...), custom_call_target="tpu_custom_call" | custom-call | flops 1811939328 | bytes 4718592 | tf_op jit(solution)/shard_map/pallas_call | solution.py:508
  8.0 0.0 collective-permute-done.refs_0_
  8.0 0.2 collective-permute-start.2
  8.2 1.4 %shard_map.88 = (bf16[1024,2304]{1,0:T(8,128)(2,1)S(1)}, f32[512,1024]{1,0:T(8,128)S(1)}, f32[16,128]{1,0:T(8,128)S(1)}) custom-call(bf16[16,2432]{1,0:T(8,128)(2,1)S(1)} %collective-permute-done.refs_0_, bf16[256,2304]{1,0:T(8,128)(2,1)S(1)} %get-tuple-element.34.refs_1_, ...), custom_call_target="tpu_custom_call", output_to_operand_aliasing={{0}: (6, {}), {1}: (7, {})} | custom-call | flops 905969664 | bytes 2359296 | tf_op jit(solution)/shard_map/pallas_call | solution.py:508
  9.6 0.0 collective-permute-done.2.refs_0_
  9.6 1.9 %shard_map.89 = (bf16[1024,2304]{1,0:T(8,128)(2,1)S(1)}, f32[512,1024]{1,0:T(8,128)S(1)}, f32[16,128]{1,0:T(8,128)S(1)}) custom-call(bf16[16,2432]{1,0:T(8,128)(2,1)S(1)} %collective-permute-done.2.refs_0_, bf16[256,2304]{1,0:T(8,128)(2,1)S(1)} %get-tuple-element.34.refs_1_, ...), custom_call_target="tpu_custom_call", output_to_operand_aliasing={{0}: (6, {}), {1}: (7, {})} | custom-call | flops 905969664 | bytes 2359296 | tf_op jit(solution)/shard_map/pallas_call | solution.py:508
  11.5 0.4 %collective-permute-start.3 = (f32[16,128]{1,0:T(8,128)S(1)}, f32[16,128]{1,0:T(8,128)S(1)}, u32[]{:S(2)}, u32[]{:S(2)}) collective-permute-start(f32[16,128]{1,0:T(8,128)S(1)} %get-tuple-element.43.mine.refs_0_), channel_id=1, source_target_pairs={{0,1},{1,0},{2,3},{3,2},{4,5},{5,4},{6,7},{7,6},{8,9},{9,8},{10,11... | collective-permute-start | bytes 24584 | tf_op jit(solution)/shard_map/ppermute | solution.py:107
  11.8 0.8 %collective-permute-done.3.other = f32[16,128]{1,0:T(8,128)S(1)} collective-permute-done((f32[16,128]{1,0:T(8,128)S(1)}, f32[16,128]{1,0:T(8,128)S(1)}, u32[]{:S(2)}, u32[]{:S(2)}) %collective-permute-start.3) | collective-permute-done | bytes 8224 | tf_op jit(solution)/shard_map/ppermute | solution.py:107
  12.7 1.8 %collective-permute-start.4 = (f32[8,128]{1,0:T(8,128)S(1)}, f32[8,128]{1,0:T(8,128)S(1)}, u32[]{:S(2)}, u32[]{:S(2)}) collective-permute-start(f32[8,128]{1,0:T(8,128)S(1)} %shard_map.90.refs_1_), channel_id=1, source_target_pairs={{0,2},{1,3},{2,0},{3,1},{4,6},{5,7},{6,4},{7,5},{8,10},{9,11},{10,... | collective-permute-start | bytes 12296 | tf_op jit(solution)/shard_map/ppermute | solution.py:107
  14.4 1.9 %collective-permute-done.4.refs_2_ = f32[8,128]{1,0:T(8,128)S(1)} collective-permute-done((f32[8,128]{1,0:T(8,128)S(1)}, f32[8,128]{1,0:T(8,128)S(1)}, u32[]{:S(2)}, u32[]{:S(2)}) %collective-permute-start.4) | collective-permute-done | bytes 4128 | tf_op jit(solution)/shard_map/ppermute | solution.py:107
  16.3 1.5 %shard_map.91 = (bf16[512,1024]{1,0:T(8,128)(2,1)S(1)}, f32[64,128]{1,0:T(8,128)S(1)}, f32[64,256]{1,0:T(8,128)S(1)}, bf16[64,639]{1,0:T(8,128)(2,1)S(1)}) custom-call(f32[16,128]{1,0:T(8,128)S(1)} %get-tuple-element.43.mine.refs_0_, f32[8,128]{1,0:T(8,128)S(1)} %shard_map.90.refs_1_, f32[8,128]{1,0:T(8,128)S(1)} %collective-permute-done.4.refs_2_, ...), custom_call_target="tpu_custom_call" | custom-call | flops 603979776 | bytes 2359296 | tf_op jit(solution)/shard_map/pallas_call | solution.py:508
  17.8 1.8 %collective-permute-start.5 = (bf16[64,639]{1,0:T(8,128)(2,1)S(1)}, bf16[64,639]{1,0:T(8,128)(2,1)S(1)}, u32[]{:S(2)}, u32[]{:S(2)}) collective-permute-start(bf16[64,639]{1,0:T(8,128)(2,1)S(1)} %get-tuple-element.49.refs_0_), channel_id=1, source_target_pairs={{0,4},{4,0},{8,12},{12,8},{1,5},{5,1},{9,13},{13,9},{2,6},{6,2},{1... | collective-permute-start | bytes 245384 | tf_op jit(solution)/shard_map/ppermute | solution.py:107
  19.7 1.6 %shard_map.92 = (bf16[64,619]{1,0:T(8,128)(2,1)S(1)}, f32[64,599]{1,0:T(8,128)S(1)}) custom-call(bf16[512,1024]{1,0:T(8,128)(2,1)S(1)} %get-tuple-element.46.weight_ref, bf16[1024,2304]{1,0:T(8,128)(2,1)S(1)} %get-tuple-element.45.refs_4_.shifted_ref, f32[64,128]{1,0:T(8,128)S(1)} %get-tuple-element.47.mass_ref, f32[64,256]{1,0:T(8,128)S(1)} %get-tuple-element.48.tails_ref, ...), custom_call_target="tpu_custom_call" | custom-call | flops 1024 | bytes 1024 | tf_op jit(solution)/shard_map/pallas_call | solution.py:508
  21.2 0.3 %collective-permute-start.6 = (bf16[64,619]{1,0:T(8,128)(2,1)S(1)}, bf16[64,619]{1,0:T(8,128)(2,1)S(1)}, u32[]{:S(2)}, u32[]{:S(2)}) collective-permute-start(bf16[64,619]{1,0:T(8,128)(2,1)S(1)} %get-tuple-element.51), channel_id=1, source_target_pairs={{0,4},{4,0},{8,12},{12,8},{1,5},{5,1},{9,13},{13,9},{2,6},{6,2},{1... | collective-permute-start | bytes 237704 | tf_op jit(solution)/shard_map/ppermute | solution.py:107
  21.5 0.8 %collective-permute-done.5.refs_1_ = bf16[64,639]{1,0:T(8,128)(2,1)S(1)} collective-permute-done((bf16[64,639]{1,0:T(8,128)(2,1)S(1)}, bf16[64,639]{1,0:T(8,128)(2,1)S(1)}, u32[]{:S(2)}, u32[]{:S(2)}) %collective-permute-start.5) | collective-permute-done | bytes 81824 | tf_op jit(solution)/shard_map/ppermute | solution.py:107
  22.4 0.1 shard_map.93.refs_0_
  22.5 2.8 %collective-permute-start.7 = (bf16[64,599]{1,0:T(8,128)(2,1)S(1)}, bf16[64,599]{1,0:T(8,128)(2,1)S(1)}, u32[]{:S(2)}, u32[]{:S(2)}) collective-permute-start(bf16[64,599]{1,0:T(8,128)(2,1)S(1)} %shard_map.93.refs_0_), channel_id=1, source_target_pairs={{0,8},{4,12},{8,0},{12,4},{1,9},{5,13},{9,1},{13,5},{2,10},{6,14},... | collective-permute-start | bytes 230024 | tf_op jit(solution)/shard_map/ppermute | solution.py:107
  25.3 1.0 %shard_map.94.own_ref = f32[64,579]{1,0:T(8,128)S(1)} custom-call(bf16[512,1024]{1,0:T(8,128)(2,1)S(1)} %get-tuple-element.46.weight_ref, bf16[1024,2304]{1,0:T(8,128)(2,1)S(1)} %get-tuple-element.45.refs_4_.shifted_ref, f32[64,128]{1,0:T(8,128)S(1)} %get-tuple-element.47.mass_ref, f32[64,256]{1,0:T(8,128)S(1)} %get-tuple-element.48.tails_ref, ...), custom_call_target="tpu_custom_call" | custom-call | flops 1024 | bytes 1024 | tf_op jit(solution)/shard_map/pallas_call | solution.py:508
  26.3 0.0 collective-permute-done.6.refs_0_
  26.3 1.6 %collective-permute-done.7.refs_1_ = bf16[64,599]{1,0:T(8,128)(2,1)S(1)} collective-permute-done((bf16[64,599]{1,0:T(8,128)(2,1)S(1)}, bf16[64,599]{1,0:T(8,128)(2,1)S(1)}, u32[]{:S(2)}, u32[]{:S(2)}) %collective-permute-start.7) | collective-permute-done | bytes 76704 | tf_op jit(solution)/shard_map/ppermute | solution.py:107
  27.9 0.7 %shard_map.95 = (f32[64,576]{1,0:T(8,128)}, f32[1,64]{1,0:T(1,128)}) custom-call(f32[64,579]{1,0:T(8,128)S(1)} %shard_map.94.own_ref, bf16[64,619]{1,0:T(8,128)(2,1)S(1)} %collective-permute-done.6.refs_0_, bf16[64,599]{1,0:T(8,128)(2,1)S(1)} %collective-permute-done.7.refs_1_), custom_call_target="tpu_custom_call" | custom-call | flops 163840 | bytes 655360 | tf_op jit(solution)/shard_map/pallas_call | solution.py:508
  (1 shorter events, 0.0 us)
Async XLA Ops:
  1.9 3.1 %collective-permute-start.1 = (bf16[16,2432]{1,0:T(8,128)(2,1)S(1)}, bf16[16,2432]{1,0:T(8,128)(2,1)S(1)}, u32[]{:S(2)}, u32[]{:S(2)}) collective-permute-start(bf16[16,2432]{1,0:T(8,128)(2,1)S(1)} %get-tuple-element.28.refs_0_), channel_id=1, source_target_pairs={{0,1},{1,0},{2,3},{3,2},{4,5},{5,4},{6,7},{7,6},{8,9},{9,8},{10,11... | collective-permute-start | bytes 233480 | tf_op jit(solution)/shard_map/ppermute | solution.py:107
  2.4 5.5 %collective-permute-start = (bf16[16,2432]{1,0:T(8,128)(2,1)S(1)}, bf16[16,2432]{1,0:T(8,128)(2,1)S(1)}, u32[]{:S(2)}, u32[]{:S(2)}) collective-permute-start(bf16[16,2432]{1,0:T(8,128)(2,1)S(1)} %get-tuple-element.28.refs_0_), channel_id=1, source_target_pairs={{0,2},{1,3},{2,0},{3,1},{4,6},{5,7},{6,4},{7,5},{8,10},{9,11},{10,... | collective-permute-start | bytes 233480 | tf_op jit(solution)/shard_map/ppermute | solution.py:107
  8.0 1.6 %collective-permute-start.2 = (bf16[16,2432]{1,0:T(8,128)(2,1)S(1)}, bf16[16,2432]{1,0:T(8,128)(2,1)S(1)}, u32[]{:S(2)}, u32[]{:S(2)}) collective-permute-start(bf16[16,2432]{1,0:T(8,128)(2,1)S(1)} %collective-permute-done.refs_0_), channel_id=1, source_target_pairs={{0,1},{1,0},{2,3},{3,2},{4,5},{5,4},{6,7},{7,6},{8,9},{9,8},{10,11... | collective-permute-start | bytes 233480 | tf_op jit(solution)/shard_map/ppermute | solution.py:107
  11.5 1.2 %collective-permute-start.3 = (f32[16,128]{1,0:T(8,128)S(1)}, f32[16,128]{1,0:T(8,128)S(1)}, u32[]{:S(2)}, u32[]{:S(2)}) collective-permute-start(f32[16,128]{1,0:T(8,128)S(1)} %get-tuple-element.43.mine.refs_0_), channel_id=1, source_target_pairs={{0,1},{1,0},{2,3},{3,2},{4,5},{5,4},{6,7},{7,6},{8,9},{9,8},{10,11... | collective-permute-start | bytes 24584 | tf_op jit(solution)/shard_map/ppermute | solution.py:107
  12.7 3.7 %collective-permute-start.4 = (f32[8,128]{1,0:T(8,128)S(1)}, f32[8,128]{1,0:T(8,128)S(1)}, u32[]{:S(2)}, u32[]{:S(2)}) collective-permute-start(f32[8,128]{1,0:T(8,128)S(1)} %shard_map.90.refs_1_), channel_id=1, source_target_pairs={{0,2},{1,3},{2,0},{3,1},{4,6},{5,7},{6,4},{7,5},{8,10},{9,11},{10,... | collective-permute-start | bytes 12296 | tf_op jit(solution)/shard_map/ppermute | solution.py:107
  17.8 4.6 %collective-permute-start.5 = (bf16[64,639]{1,0:T(8,128)(2,1)S(1)}, bf16[64,639]{1,0:T(8,128)(2,1)S(1)}, u32[]{:S(2)}, u32[]{:S(2)}) collective-permute-start(bf16[64,639]{1,0:T(8,128)(2,1)S(1)} %get-tuple-element.49.refs_0_), channel_id=1, source_target_pairs={{0,4},{4,0},{8,12},{12,8},{1,5},{5,1},{9,13},{13,9},{2,6},{6,2},{1... | collective-permute-start | bytes 245384 | tf_op jit(solution)/shard_map/ppermute | solution.py:107
  21.2 5.0 %collective-permute-start.6 = (bf16[64,619]{1,0:T(8,128)(2,1)S(1)}, bf16[64,619]{1,0:T(8,128)(2,1)S(1)}, u32[]{:S(2)}, u32[]{:S(2)}) collective-permute-start(bf16[64,619]{1,0:T(8,128)(2,1)S(1)} %get-tuple-element.51), channel_id=1, source_target_pairs={{0,4},{4,0},{8,12},{12,8},{1,5},{5,1},{9,13},{13,9},{2,6},{6,2},{1... | collective-permute-start | bytes 237704 | tf_op jit(solution)/shard_map/ppermute | solution.py:107
  22.5 5.4 %collective-permute-start.7 = (bf16[64,599]{1,0:T(8,128)(2,1)S(1)}, bf16[64,599]{1,0:T(8,128)(2,1)S(1)}, u32[]{:S(2)}, u32[]{:S(2)}) collective-permute-start(bf16[64,599]{1,0:T(8,128)(2,1)S(1)} %shard_map.93.refs_0_), channel_id=1, source_target_pairs={{0,8},{4,12},{8,0},{12,4},{1,9},{5,13},{9,1},{13,5},{2,10},{6,14},... | collective-permute-start | bytes 230024 | tf_op jit(solution)/shard_map/ppermute | solution.py:107

commit v16 on v15

--- a/solution.py
+++ b/solution.py
@@ -638,7 +638,9 @@
         chip=(1,),
     )
     blocks = dict(zip(late, rest))
-    incoming[0].append(exchange(blocks[1], "dom", 1))
+    forwarded = [array for b in range(doms) for array in incoming[b]]
+    direct, *_ = lax.optimization_barrier((blocks[1], *forwarded))
+    incoming[0].append(exchange(direct, "dom", 1))
     for b in order[len(early) + 1 :]:
         (block,) = call(
             functools.partial(add_kernel, width),

time: 28.8 us -> 31.4 us (1.090)
  starting transfers between devices: 10.3 us -> 11.7 us
  waiting for transfers between devices: 5.22 us -> 6.48 us
    ppermute x8, starting transfers between devices: 10.3 us -> 11.7 us  [exchange(): lax.ppermute(array, axis, [(i, i ^ distance) for i in range(lax.axis_size...]
    ppermute x8, waiting for transfers between devices: 5.22 us -> 6.48 us  [exchange(): lax.ppermute(array, axis, [(i, i ^ distance) for i in range(lax.axis_size...]
  transfers between devices with their start and end apart: 8 -> 8, of which waited for: 4 -> 4; matrix products, arithmetic and copies ran while one was open for 0% -> 0% of each run, Pallas kernels for 25% -> 23%
where the time goes in v16:
time: 31.4 us; the launch traced here: 31.2 us
  Pallas kernels  12.4 us (39%)
  starting transfers between devices  11.7 us (37%)
  waiting for transfers between devices  6.48 us (21%)
  between operations  0.7 us (2%)
    pallas_call x10, Pallas kernels, call(): pl.pallas_call(kernel, out_shape=[pltpu.VMEM(s.shape, s.dtype) if pinned...  12.4 us
    ppermute x8, starting transfers between devices, exchange(): lax.ppermute(array, axis, [(i, i ^ distance) for i in range(lax.axis_size...  11.7 us
    ppermute x8, waiting for transfers between devices, exchange(): lax.ppermute(array, axis, [(i, i ^ distance) for i in range(lax.axis_size...  6.48 us
  transfers between devices with their start and end apart: 8, of which 4 were waited for; matrix products, arithmetic and copies ran while one was open for 0% of the time, Pallas kernels for 23%

profile of v16, /device:TPU:0, one launch (start us, length us, event | category | flops | bytes accessed | tf_op | source)
XLA Modules:
  0.0 31.2 jit_solution(6460533250330347546)
XLA Ops:
  0.6 1.3 %shard_map.86 = (bf16[16,2432]{1,0:T(8,128)(2,1)S(1)}, bf16[64,2304]{1,0:T(8,128)(2,1)S(1)}, f32[1,64]{1,0:T(1,128)S(1)}, f32[48,2304]{1,0:T(8,128)S(1)}) custom-call(bf16[16,2304]{1,0:T(8,128)(2,1)} %particle_hbm.1, s32[16,16]{1,0:T(8,128)} %index_hbm.1, s32[1,16]{1,0:T(1,128)} %bitcast.4, s32[1,16]{1,0:T(1,128)} %bitcast.5, bf16[64,2304]{1,0:T(8,128)(2,1)} %class_hbm.1, ...), custom_call_target="tpu_custom_call" | custom-call | flops 36864 | bytes 147456 | tf_op jit(solution)/shard_map/pallas_call | solution.py:508
  1.9 0.5 %collective-permute-start.1 = (bf16[16,2432]{1,0:T(8,128)(2,1)S(1)}, bf16[16,2432]{1,0:T(8,128)(2,1)S(1)}, u32[]{:S(2)}, u32[]{:S(2)}) collective-permute-start(bf16[16,2432]{1,0:T(8,128)(2,1)S(1)} %get-tuple-element.29.refs_0_), channel_id=1, source_target_pairs={{0,1},{1,0},{2,3},{3,2},{4,5},{5,4},{6,7},{7,6},{8,9},{9,8},{10,11... | collective-permute-start | bytes 233480 | tf_op jit(solution)/shard_map/ppermute | solution.py:107
  2.4 2.6 %collective-permute-start = (bf16[16,2432]{1,0:T(8,128)(2,1)S(1)}, bf16[16,2432]{1,0:T(8,128)(2,1)S(1)}, u32[]{:S(2)}, u32[]{:S(2)}) collective-permute-start(bf16[16,2432]{1,0:T(8,128)(2,1)S(1)} %get-tuple-element.29.refs_0_), channel_id=1, source_target_pairs={{0,2},{1,3},{2,0},{3,1},{4,6},{5,7},{6,4},{7,5},{8,10},{9,11},{10,... | collective-permute-start | bytes 233480 | tf_op jit(solution)/shard_map/ppermute | solution.py:107
  5.0 0.0 collective-permute-done.1.refs_1_
  5.0 3.0 %shard_map.87 = (bf16[1024,2304]{1,0:T(8,128)(2,1)S(1)}, f32[512,1024]{1,0:T(8,128)S(1)}, f32[16,128]{1,0:T(8,128)S(1)}, bf16[512,2304]{1,0:T(8,128)(2,1)S(1)}, ...) custom-call(bf16[16,2432]{1,0:T(8,128)(2,1)S(1)} %get-tuple-element.29.refs_0_, ...), custom_call_target="tpu_custom_call" | custom-call | flops 1811939328 | bytes 4718592 | tf_op jit(solution)/shard_map/pallas_call | solution.py:508
  8.0 0.0 collective-permute-done.refs_0_
  8.0 0.2 collective-permute-start.2
  8.2 1.4 %shard_map.88 = (bf16[1024,2304]{1,0:T(8,128)(2,1)S(1)}, f32[512,1024]{1,0:T(8,128)S(1)}, f32[16,128]{1,0:T(8,128)S(1)}) custom-call(bf16[16,2432]{1,0:T(8,128)(2,1)S(1)} %collective-permute-done.refs_0_, bf16[256,2304]{1,0:T(8,128)(2,1)S(1)} %get-tuple-element.35.refs_1_, ...), custom_call_target="tpu_custom_call", output_to_operand_aliasing={{0}: (6, {}), {1}: (7, {})} | custom-call | flops 905969664 | bytes 2359296 | tf_op jit(solution)/shard_map/pallas_call | solution.py:508
  9.6 0.0 collective-permute-done.2.refs_0_
  9.6 1.9 %shard_map.89 = (bf16[1024,2304]{1,0:T(8,128)(2,1)S(1)}, f32[512,1024]{1,0:T(8,128)S(1)}, f32[16,128]{1,0:T(8,128)S(1)}) custom-call(bf16[16,2432]{1,0:T(8,128)(2,1)S(1)} %collective-permute-done.2.refs_0_, bf16[256,2304]{1,0:T(8,128)(2,1)S(1)} %get-tuple-element.35.refs_1_, ...), custom_call_target="tpu_custom_call", output_to_operand_aliasing={{0}: (6, {}), {1}: (7, {})} | custom-call | flops 905969664 | bytes 2359296 | tf_op jit(solution)/shard_map/pallas_call | solution.py:508
  11.5 0.4 %collective-permute-start.3 = (f32[16,128]{1,0:T(8,128)S(1)}, f32[16,128]{1,0:T(8,128)S(1)}, u32[]{:S(2)}, u32[]{:S(2)}) collective-permute-start(f32[16,128]{1,0:T(8,128)S(1)} %get-tuple-element.44.mine.refs_0_), channel_id=1, source_target_pairs={{0,1},{1,0},{2,3},{3,2},{4,5},{5,4},{6,7},{7,6},{8,9},{9,8},{10,11... | collective-permute-start | bytes 24584 | tf_op jit(solution)/shard_map/ppermute | solution.py:107
  11.8 0.8 %collective-permute-done.3.other = f32[16,128]{1,0:T(8,128)S(1)} collective-permute-done((f32[16,128]{1,0:T(8,128)S(1)}, f32[16,128]{1,0:T(8,128)S(1)}, u32[]{:S(2)}, u32[]{:S(2)}) %collective-permute-start.3) | collective-permute-done | bytes 8224 | tf_op jit(solution)/shard_map/ppermute | solution.py:107
  12.7 1.8 %collective-permute-start.4 = (f32[8,128]{1,0:T(8,128)S(1)}, f32[8,128]{1,0:T(8,128)S(1)}, u32[]{:S(2)}, u32[]{:S(2)}) collective-permute-start(f32[8,128]{1,0:T(8,128)S(1)} %shard_map.90.refs_1_), channel_id=1, source_target_pairs={{0,2},{1,3},{2,0},{3,1},{4,6},{5,7},{6,4},{7,5},{8,10},{9,11},{10,... | collective-permute-start | bytes 12296 | tf_op jit(solution)/shard_map/ppermute | solution.py:107
  14.4 1.9 %collective-permute-done.4.refs_2_ = f32[8,128]{1,0:T(8,128)S(1)} collective-permute-done((f32[8,128]{1,0:T(8,128)S(1)}, f32[8,128]{1,0:T(8,128)S(1)}, u32[]{:S(2)}, u32[]{:S(2)}) %collective-permute-start.4) | collective-permute-done | bytes 4128 | tf_op jit(solution)/shard_map/ppermute | solution.py:107
  16.3 1.5 %shard_map.91 = (bf16[512,1024]{1,0:T(8,128)(2,1)S(1)}, f32[64,128]{1,0:T(8,128)S(1)}, f32[64,256]{1,0:T(8,128)S(1)}, bf16[64,639]{1,0:T(8,128)(2,1)S(1)}) custom-call(f32[16,128]{1,0:T(8,128)S(1)} %get-tuple-element.44.mine.refs_0_, f32[8,128]{1,0:T(8,128)S(1)} %shard_map.90.refs_1_, f32[8,128]{1,0:T(8,128)S(1)} %collective-permute-done.4.refs_2_, ...), custom_call_target="tpu_custom_call" | custom-call | flops 603979776 | bytes 2359296 | tf_op jit(solution)/shard_map/pallas_call | solution.py:508
  17.8 1.8 %collective-permute-start.5 = (bf16[64,639]{1,0:T(8,128)(2,1)S(1)}, bf16[64,639]{1,0:T(8,128)(2,1)S(1)}, u32[]{:S(2)}, u32[]{:S(2)}) collective-permute-start(bf16[64,639]{1,0:T(8,128)(2,1)S(1)} %get-tuple-element.50.refs_0_), channel_id=1, source_target_pairs={{0,4},{4,0},{8,12},{12,8},{1,5},{5,1},{9,13},{13,9},{2,6},{6,2},{1... | collective-permute-start | bytes 245384 | tf_op jit(solution)/shard_map/ppermute | solution.py:107
  19.7 1.6 %shard_map.92 = (bf16[64,619]{1,0:T(8,128)(2,1)S(1)}, f32[64,599]{1,0:T(8,128)S(1)}) custom-call(bf16[512,1024]{1,0:T(8,128)(2,1)S(1)} %get-tuple-element.47.weight_ref, bf16[1024,2304]{1,0:T(8,128)(2,1)S(1)} %get-tuple-element.46.refs_4_.shifted_ref, f32[64,128]{1,0:T(8,128)S(1)} %get-tuple-element.48.mass_ref, f32[64,256]{1,0:T(8,128)S(1)} %get-tuple-element.49.tails_ref, ...), custom_call_target="tpu_custom_call" | custom-call | flops 1024 | bytes 1024 | tf_op jit(solution)/shard_map/pallas_call | solution.py:508
  21.2 1.1 %collective-permute-done.5.refs_1_ = bf16[64,639]{1,0:T(8,128)(2,1)S(1)} collective-permute-done((bf16[64,639]{1,0:T(8,128)(2,1)S(1)}, bf16[64,639]{1,0:T(8,128)(2,1)S(1)}, u32[]{:S(2)}, u32[]{:S(2)}) %collective-permute-start.5) | collective-permute-done | bytes 81824 | tf_op jit(solution)/shard_map/ppermute | solution.py:107
  22.3 1.8 %collective-permute-start.6 = (bf16[64,619]{1,0:T(8,128)(2,1)S(1)}, bf16[64,619]{1,0:T(8,128)(2,1)S(1)}, u32[]{:S(2)}, u32[]{:S(2)}) collective-permute-start(bf16[64,619]{1,0:T(8,128)(2,1)S(1)} %get-tuple-element.53), channel_id=1, source_target_pairs={{0,4},{4,0},{8,12},{12,8},{1,5},{5,1},{9,13},{13,9},{2,6},{6,2},{1... | collective-permute-start | bytes 237704 | tf_op jit(solution)/shard_map/ppermute | solution.py:107
  24.1 0.1 shard_map.93.refs_0_
  24.2 2.6 %collective-permute-start.7 = (bf16[64,599]{1,0:T(8,128)(2,1)S(1)}, bf16[64,599]{1,0:T(8,128)(2,1)S(1)}, u32[]{:S(2)}, u32[]{:S(2)}) collective-permute-start(bf16[64,599]{1,0:T(8,128)(2,1)S(1)} %shard_map.93.refs_0_), channel_id=1, source_target_pairs={{0,8},{4,12},{8,0},{12,4},{1,9},{5,13},{9,1},{13,5},{2,10},{6,14},... | collective-permute-start | bytes 230024 | tf_op jit(solution)/shard_map/ppermute | solution.py:107
  26.9 1.0 %shard_map.94.own_ref = f32[64,579]{1,0:T(8,128)S(1)} custom-call(bf16[512,1024]{1,0:T(8,128)(2,1)S(1)} %get-tuple-element.47.weight_ref, bf16[1024,2304]{1,0:T(8,128)(2,1)S(1)} %get-tuple-element.46.refs_4_.shifted_ref, f32[64,128]{1,0:T(8,128)S(1)} %get-tuple-element.48.mass_ref, f32[64,256]{1,0:T(8,128)S(1)} %get-tuple-element.49.tails_ref, ...), custom_call_target="tpu_custom_call" | custom-call | flops 1024 | bytes 1024 | tf_op jit(solution)/shard_map/pallas_call | solution.py:508
  27.9 2.6 %collective-permute-done.7.refs_1_ = bf16[64,599]{1,0:T(8,128)(2,1)S(1)} collective-permute-done((bf16[64,599]{1,0:T(8,128)(2,1)S(1)}, bf16[64,599]{1,0:T(8,128)(2,1)S(1)}, u32[]{:S(2)}, u32[]{:S(2)}) %collective-permute-start.7) | collective-permute-done | bytes 76704 | tf_op jit(solution)/shard_map/ppermute | solution.py:107
  30.5 0.0 collective-permute-done.6.refs_0_
  30.5 0.7 %shard_map.95 = (f32[64,576]{1,0:T(8,128)}, f32[1,64]{1,0:T(1,128)}) custom-call(f32[64,579]{1,0:T(8,128)S(1)} %shard_map.94.own_ref, bf16[64,619]{1,0:T(8,128)(2,1)S(1)} %collective-permute-done.6.refs_0_, bf16[64,599]{1,0:T(8,128)(2,1)S(1)} %collective-permute-done.7.refs_1_), custom_call_target="tpu_custom_call" | custom-call | flops 163840 | bytes 655360 | tf_op jit(solution)/shard_map/pallas_call | solution.py:508
  (1 shorter events, 0.0 us)
Async XLA Ops:
  1.9 3.1 %collective-permute-start.1 = (bf16[16,2432]{1,0:T(8,128)(2,1)S(1)}, bf16[16,2432]{1,0:T(8,128)(2,1)S(1)}, u32[]{:S(2)}, u32[]{:S(2)}) collective-permute-start(bf16[16,2432]{1,0:T(8,128)(2,1)S(1)} %get-tuple-element.29.refs_0_), channel_id=1, source_target_pairs={{0,1},{1,0},{2,3},{3,2},{4,5},{5,4},{6,7},{7,6},{8,9},{9,8},{10,11... | collective-permute-start | bytes 233480 | tf_op jit(solution)/shard_map/ppermute | solution.py:107
  2.4 5.5 %collective-permute-start = (bf16[16,2432]{1,0:T(8,128)(2,1)S(1)}, bf16[16,2432]{1,0:T(8,128)(2,1)S(1)}, u32[]{:S(2)}, u32[]{:S(2)}) collective-permute-start(bf16[16,2432]{1,0:T(8,128)(2,1)S(1)} %get-tuple-element.29.refs_0_), channel_id=1, source_target_pairs={{0,2},{1,3},{2,0},{3,1},{4,6},{5,7},{6,4},{7,5},{8,10},{9,11},{10,... | collective-permute-start | bytes 233480 | tf_op jit(solution)/shard_map/ppermute | solution.py:107
  8.0 1.6 %collective-permute-start.2 = (bf16[16,2432]{1,0:T(8,128)(2,1)S(1)}, bf16[16,2432]{1,0:T(8,128)(2,1)S(1)}, u32[]{:S(2)}, u32[]{:S(2)}) collective-permute-start(bf16[16,2432]{1,0:T(8,128)(2,1)S(1)} %collective-permute-done.refs_0_), channel_id=1, source_target_pairs={{0,1},{1,0},{2,3},{3,2},{4,5},{5,4},{6,7},{7,6},{8,9},{9,8},{10,11... | collective-permute-start | bytes 233480 | tf_op jit(solution)/shard_map/ppermute | solution.py:107
  11.5 1.2 %collective-permute-start.3 = (f32[16,128]{1,0:T(8,128)S(1)}, f32[16,128]{1,0:T(8,128)S(1)}, u32[]{:S(2)}, u32[]{:S(2)}) collective-permute-start(f32[16,128]{1,0:T(8,128)S(1)} %get-tuple-element.44.mine.refs_0_), channel_id=1, source_target_pairs={{0,1},{1,0},{2,3},{3,2},{4,5},{5,4},{6,7},{7,6},{8,9},{9,8},{10,11... | collective-permute-start | bytes 24584 | tf_op jit(solution)/shard_map/ppermute | solution.py:107
  12.7 3.7 %collective-permute-start.4 = (f32[8,128]{1,0:T(8,128)S(1)}, f32[8,128]{1,0:T(8,128)S(1)}, u32[]{:S(2)}, u32[]{:S(2)}) collective-permute-start(f32[8,128]{1,0:T(8,128)S(1)} %shard_map.90.refs_1_), channel_id=1, source_target_pairs={{0,2},{1,3},{2,0},{3,1},{4,6},{5,7},{6,4},{7,5},{8,10},{9,11},{10,... | collective-permute-start | bytes 12296 | tf_op jit(solution)/shard_map/ppermute | solution.py:107
  17.8 4.5 %collective-permute-start.5 = (bf16[64,639]{1,0:T(8,128)(2,1)S(1)}, bf16[64,639]{1,0:T(8,128)(2,1)S(1)}, u32[]{:S(2)}, u32[]{:S(2)}) collective-permute-start(bf16[64,639]{1,0:T(8,128)(2,1)S(1)} %get-tuple-element.50.refs_0_), channel_id=1, source_target_pairs={{0,4},{4,0},{8,12},{12,8},{1,5},{5,1},{9,13},{13,9},{2,6},{6,2},{1... | collective-permute-start | bytes 245384 | tf_op jit(solution)/shard_map/ppermute | solution.py:107
  22.3 8.2 %collective-permute-start.6 = (bf16[64,619]{1,0:T(8,128)(2,1)S(1)}, bf16[64,619]{1,0:T(8,128)(2,1)S(1)}, u32[]{:S(2)}, u32[]{:S(2)}) collective-permute-start(bf16[64,619]{1,0:T(8,128)(2,1)S(1)} %get-tuple-element.53), channel_id=1, source_target_pairs={{0,4},{4,0},{8,12},{12,8},{1,5},{5,1},{9,13},{13,9},{2,6},{6,2},{1... | collective-permute-start | bytes 237704 | tf_op jit(solution)/shard_map/ppermute | solution.py:107
  24.2 6.3 %collective-permute-start.7 = (bf16[64,599]{1,0:T(8,128)(2,1)S(1)}, bf16[64,599]{1,0:T(8,128)(2,1)S(1)}, u32[]{:S(2)}, u32[]{:S(2)}) collective-permute-start(bf16[64,599]{1,0:T(8,128)(2,1)S(1)} %shard_map.93.refs_0_), channel_id=1, source_target_pairs={{0,8},{4,12},{8,0},{12,4},{1,9},{5,13},{9,1},{13,5},{2,10},{6,14},... | collective-permute-start | bytes 230024 | tf_op jit(solution)/shard_map/ppermute | solution.py:107

commit v17 on v15

--- a/solution.py
+++ b/solution.py
@@ -357,14 +357,16 @@
         top, total = merged(mine, other, block, count // 2)
         factor = jnp.exp(stats_ref[2 * block : 2 * block + 1, :] - top) / total
         scale = stats_ref[2 * count + block : 2 * count + block + 1, :]
-        factor = jnp.concatenate([factor] * repeat, axis=1)
+        factor = jnp.concatenate([factor * scale] * repeat, axis=1)
         scale = jnp.concatenate([scale] * repeat, axis=1)
         part = slice(block * rows, (block + 1) * rows)
+        turned = None
         for rotation in range(ROTS):
             rotated = slice(rotation * classes, (rotation + 1) * classes)
-            weight = exp_ref[rotated, part] * factor * scale
-            mass = mass + weight * scale
+            weight = exp_ref[rotated, part] * factor
+            turned = weight if turned is None else turned + weight
             weight_ref[rotated, part] = weight.astype(jnp.bfloat16)
+        mass = mass + turned * scale
     return jnp.broadcast_to(jnp.sum(mass, axis=1, keepdims=True), (classes, LANES))
 
 

time: 28.8 us -> 28.7 us (level)
  no operation moved by 1% of the time
where the time goes in v17:
time: 28.7 us; the launch traced here: 28.5 us
  Pallas kernels  12.3 us (43%)
  starting transfers between devices  10.3 us (36%)
  waiting for transfers between devices  5.24 us (18%)
  between operations  0.7 us (2%)
    pallas_call x10, Pallas kernels, call(): pl.pallas_call(kernel, out_shape=[pltpu.VMEM(s.shape, s.dtype) if pinned...  12.3 us
    ppermute x8, starting transfers between devices, exchange(): lax.ppermute(array, axis, [(i, i ^ distance) for i in range(lax.axis_size...  10.3 us
    ppermute x8, waiting for transfers between devices, exchange(): lax.ppermute(array, axis, [(i, i ^ distance) for i in range(lax.axis_size...  5.24 us
  transfers between devices with their start and end apart: 8, of which 4 were waited for; matrix products, arithmetic and copies ran while one was open for 0% of the time, Pallas kernels for 25%

profile of v17, /device:TPU:0, one launch (start us, length us, event | category | flops | bytes accessed | tf_op | source)
XLA Modules:
  0.0 28.5 jit_solution(16819439016695921561)
XLA Ops:
  0.6 1.3 %shard_map.86 = (bf16[16,2432]{1,0:T(8,128)(2,1)S(1)}, bf16[64,2304]{1,0:T(8,128)(2,1)S(1)}, f32[1,64]{1,0:T(1,128)S(1)}, f32[48,2304]{1,0:T(8,128)S(1)}) custom-call(bf16[16,2304]{1,0:T(8,128)(2,1)} %particle_hbm.1, s32[16,16]{1,0:T(8,128)} %index_hbm.1, s32[1,16]{1,0:T(1,128)} %bitcast.4, s32[1,16]{1,0:T(1,128)} %bitcast.5, bf16[64,2304]{1,0:T(8,128)(2,1)} %class_hbm.1, ...), custom_call_target="tpu_custom_call" | custom-call | flops 36864 | bytes 147456 | tf_op jit(solution)/shard_map/pallas_call | solution.py:510
  1.9 0.5 %collective-permute-start.1 = (bf16[16,2432]{1,0:T(8,128)(2,1)S(1)}, bf16[16,2432]{1,0:T(8,128)(2,1)S(1)}, u32[]{:S(2)}, u32[]{:S(2)}) collective-permute-start(bf16[16,2432]{1,0:T(8,128)(2,1)S(1)} %get-tuple-element.28.refs_0_), channel_id=1, source_target_pairs={{0,1},{1,0},{2,3},{3,2},{4,5},{5,4},{6,7},{7,6},{8,9},{9,8},{10,11... | collective-permute-start | bytes 233480 | tf_op jit(solution)/shard_map/ppermute | solution.py:107
  2.4 2.6 %collective-permute-start = (bf16[16,2432]{1,0:T(8,128)(2,1)S(1)}, bf16[16,2432]{1,0:T(8,128)(2,1)S(1)}, u32[]{:S(2)}, u32[]{:S(2)}) collective-permute-start(bf16[16,2432]{1,0:T(8,128)(2,1)S(1)} %get-tuple-element.28.refs_0_), channel_id=1, source_target_pairs={{0,2},{1,3},{2,0},{3,1},{4,6},{5,7},{6,4},{7,5},{8,10},{9,11},{10,... | collective-permute-start | bytes 233480 | tf_op jit(solution)/shard_map/ppermute | solution.py:107
  5.0 0.0 collective-permute-done.1.refs_1_
  5.0 3.0 %shard_map.87 = (bf16[1024,2304]{1,0:T(8,128)(2,1)S(1)}, f32[512,1024]{1,0:T(8,128)S(1)}, f32[16,128]{1,0:T(8,128)S(1)}, bf16[512,2304]{1,0:T(8,128)(2,1)S(1)}, ...) custom-call(bf16[16,2432]{1,0:T(8,128)(2,1)S(1)} %get-tuple-element.28.refs_0_, ...), custom_call_target="tpu_custom_call" | custom-call | flops 1811939328 | bytes 4718592 | tf_op jit(solution)/shard_map/pallas_call | solution.py:510
  8.0 0.0 collective-permute-done.refs_0_
  8.0 0.2 collective-permute-start.2
  8.2 1.4 %shard_map.88 = (bf16[1024,2304]{1,0:T(8,128)(2,1)S(1)}, f32[512,1024]{1,0:T(8,128)S(1)}, f32[16,128]{1,0:T(8,128)S(1)}) custom-call(bf16[16,2432]{1,0:T(8,128)(2,1)S(1)} %collective-permute-done.refs_0_, bf16[256,2304]{1,0:T(8,128)(2,1)S(1)} %get-tuple-element.34.refs_1_, ...), custom_call_target="tpu_custom_call", output_to_operand_aliasing={{0}: (6, {}), {1}: (7, {})} | custom-call | flops 905969664 | bytes 2359296 | tf_op jit(solution)/shard_map/pallas_call | solution.py:510
  9.6 0.0 collective-permute-done.2.refs_0_
  9.6 1.9 %shard_map.89 = (bf16[1024,2304]{1,0:T(8,128)(2,1)S(1)}, f32[512,1024]{1,0:T(8,128)S(1)}, f32[16,128]{1,0:T(8,128)S(1)}) custom-call(bf16[16,2432]{1,0:T(8,128)(2,1)S(1)} %collective-permute-done.2.refs_0_, bf16[256,2304]{1,0:T(8,128)(2,1)S(1)} %get-tuple-element.34.refs_1_, ...), custom_call_target="tpu_custom_call", output_to_operand_aliasing={{0}: (6, {}), {1}: (7, {})} | custom-call | flops 905969664 | bytes 2359296 | tf_op jit(solution)/shard_map/pallas_call | solution.py:510
  11.5 0.4 %collective-permute-start.3 = (f32[16,128]{1,0:T(8,128)S(1)}, f32[16,128]{1,0:T(8,128)S(1)}, u32[]{:S(2)}, u32[]{:S(2)}) collective-permute-start(f32[16,128]{1,0:T(8,128)S(1)} %get-tuple-element.43.mine.refs_0_), channel_id=1, source_target_pairs={{0,1},{1,0},{2,3},{3,2},{4,5},{5,4},{6,7},{7,6},{8,9},{9,8},{10,11... | collective-permute-start | bytes 24584 | tf_op jit(solution)/shard_map/ppermute | solution.py:107
  11.8 0.8 %collective-permute-done.3.other = f32[16,128]{1,0:T(8,128)S(1)} collective-permute-done((f32[16,128]{1,0:T(8,128)S(1)}, f32[16,128]{1,0:T(8,128)S(1)}, u32[]{:S(2)}, u32[]{:S(2)}) %collective-permute-start.3) | collective-permute-done | bytes 8224 | tf_op jit(solution)/shard_map/ppermute | solution.py:107
  12.7 1.8 %collective-permute-start.4 = (f32[8,128]{1,0:T(8,128)S(1)}, f32[8,128]{1,0:T(8,128)S(1)}, u32[]{:S(2)}, u32[]{:S(2)}) collective-permute-start(f32[8,128]{1,0:T(8,128)S(1)} %shard_map.90.refs_1_), channel_id=1, source_target_pairs={{0,2},{1,3},{2,0},{3,1},{4,6},{5,7},{6,4},{7,5},{8,10},{9,11},{10,... | collective-permute-start | bytes 12296 | tf_op jit(solution)/shard_map/ppermute | solution.py:107
  14.4 1.9 %collective-permute-done.4.refs_2_ = f32[8,128]{1,0:T(8,128)S(1)} collective-permute-done((f32[8,128]{1,0:T(8,128)S(1)}, f32[8,128]{1,0:T(8,128)S(1)}, u32[]{:S(2)}, u32[]{:S(2)}) %collective-permute-start.4) | collective-permute-done | bytes 4128 | tf_op jit(solution)/shard_map/ppermute | solution.py:107
  16.3 1.4 %shard_map.91 = (bf16[512,1024]{1,0:T(8,128)(2,1)S(1)}, f32[64,128]{1,0:T(8,128)S(1)}, f32[64,256]{1,0:T(8,128)S(1)}, bf16[64,639]{1,0:T(8,128)(2,1)S(1)}) custom-call(f32[16,128]{1,0:T(8,128)S(1)} %get-tuple-element.43.mine.refs_0_, f32[8,128]{1,0:T(8,128)S(1)} %shard_map.90.refs_1_, f32[8,128]{1,0:T(8,128)S(1)} %collective-permute-done.4.refs_2_, ...), custom_call_target="tpu_custom_call" | custom-call | flops 603979776 | bytes 2359296 | tf_op jit(solution)/shard_map/pallas_call | solution.py:510
  17.7 1.9 %collective-permute-start.5 = (bf16[64,639]{1,0:T(8,128)(2,1)S(1)}, bf16[64,639]{1,0:T(8,128)(2,1)S(1)}, u32[]{:S(2)}, u32[]{:S(2)}) collective-permute-start(bf16[64,639]{1,0:T(8,128)(2,1)S(1)} %get-tuple-element.49.refs_0_), channel_id=1, source_target_pairs={{0,4},{4,0},{8,12},{12,8},{1,5},{5,1},{9,13},{13,9},{2,6},{6,2},{1... | collective-permute-start | bytes 245384 | tf_op jit(solution)/shard_map/ppermute | solution.py:107
  19.6 1.6 %shard_map.92 = (bf16[64,619]{1,0:T(8,128)(2,1)S(1)}, f32[64,599]{1,0:T(8,128)S(1)}) custom-call(bf16[512,1024]{1,0:T(8,128)(2,1)S(1)} %get-tuple-element.46.weight_ref, bf16[1024,2304]{1,0:T(8,128)(2,1)S(1)} %get-tuple-element.45.refs_4_.shifted_ref, f32[64,128]{1,0:T(8,128)S(1)} %get-tuple-element.47.mass_ref, f32[64,256]{1,0:T(8,128)S(1)} %get-tuple-element.48.tails_ref, ...), custom_call_target="tpu_custom_call" | custom-call | flops 1024 | bytes 1024 | tf_op jit(solution)/shard_map/pallas_call | solution.py:510
  21.1 0.3 %collective-permute-start.6 = (bf16[64,619]{1,0:T(8,128)(2,1)S(1)}, bf16[64,619]{1,0:T(8,128)(2,1)S(1)}, u32[]{:S(2)}, u32[]{:S(2)}) collective-permute-start(bf16[64,619]{1,0:T(8,128)(2,1)S(1)} %get-tuple-element.51), channel_id=1, source_target_pairs={{0,4},{4,0},{8,12},{12,8},{1,5},{5,1},{9,13},{13,9},{2,6},{6,2},{1... | collective-permute-start | bytes 237704 | tf_op jit(solution)/shard_map/ppermute | solution.py:107
  21.4 0.9 %collective-permute-done.5.refs_1_ = bf16[64,639]{1,0:T(8,128)(2,1)S(1)} collective-permute-done((bf16[64,639]{1,0:T(8,128)(2,1)S(1)}, bf16[64,639]{1,0:T(8,128)(2,1)S(1)}, u32[]{:S(2)}, u32[]{:S(2)}) %collective-permute-start.5) | collective-permute-done | bytes 81824 | tf_op jit(solution)/shard_map/ppermute | solution.py:107
  22.3 0.1 shard_map.93.refs_0_
  22.4 2.8 %collective-permute-start.7 = (bf16[64,599]{1,0:T(8,128)(2,1)S(1)}, bf16[64,599]{1,0:T(8,128)(2,1)S(1)}, u32[]{:S(2)}, u32[]{:S(2)}) collective-permute-start(bf16[64,599]{1,0:T(8,128)(2,1)S(1)} %shard_map.93.refs_0_), channel_id=1, source_target_pairs={{0,8},{4,12},{8,0},{12,4},{1,9},{5,13},{9,1},{13,5},{2,10},{6,14},... | collective-permute-start | bytes 230024 | tf_op jit(solution)/shard_map/ppermute | solution.py:107
  25.2 1.0 %shard_map.94.own_ref = f32[64,579]{1,0:T(8,128)S(1)} custom-call(bf16[512,1024]{1,0:T(8,128)(2,1)S(1)} %get-tuple-element.46.weight_ref, bf16[1024,2304]{1,0:T(8,128)(2,1)S(1)} %get-tuple-element.45.refs_4_.shifted_ref, f32[64,128]{1,0:T(8,128)S(1)} %get-tuple-element.47.mass_ref, f32[64,256]{1,0:T(8,128)S(1)} %get-tuple-element.48.tails_ref, ...), custom_call_target="tpu_custom_call" | custom-call | flops 1024 | bytes 1024 | tf_op jit(solution)/shard_map/pallas_call | solution.py:510
  26.2 0.0 collective-permute-done.6.refs_0_
  26.2 1.6 %collective-permute-done.7.refs_1_ = bf16[64,599]{1,0:T(8,128)(2,1)S(1)} collective-permute-done((bf16[64,599]{1,0:T(8,128)(2,1)S(1)}, bf16[64,599]{1,0:T(8,128)(2,1)S(1)}, u32[]{:S(2)}, u32[]{:S(2)}) %collective-permute-start.7) | collective-permute-done | bytes 76704 | tf_op jit(solution)/shard_map/ppermute | solution.py:107
  27.8 0.7 %shard_map.95 = (f32[64,576]{1,0:T(8,128)}, f32[1,64]{1,0:T(1,128)}) custom-call(f32[64,579]{1,0:T(8,128)S(1)} %shard_map.94.own_ref, bf16[64,619]{1,0:T(8,128)(2,1)S(1)} %collective-permute-done.6.refs_0_, bf16[64,599]{1,0:T(8,128)(2,1)S(1)} %collective-permute-done.7.refs_1_), custom_call_target="tpu_custom_call" | custom-call | flops 163840 | bytes 655360 | tf_op jit(solution)/shard_map/pallas_call | solution.py:510
  (1 shorter events, 0.0 us)
Async XLA Ops:
  1.9 3.1 %collective-permute-start.1 = (bf16[16,2432]{1,0:T(8,128)(2,1)S(1)}, bf16[16,2432]{1,0:T(8,128)(2,1)S(1)}, u32[]{:S(2)}, u32[]{:S(2)}) collective-permute-start(bf16[16,2432]{1,0:T(8,128)(2,1)S(1)} %get-tuple-element.28.refs_0_), channel_id=1, source_target_pairs={{0,1},{1,0},{2,3},{3,2},{4,5},{5,4},{6,7},{7,6},{8,9},{9,8},{10,11... | collective-permute-start | bytes 233480 | tf_op jit(solution)/shard_map/ppermute | solution.py:107
  2.4 5.5 %collective-permute-start = (bf16[16,2432]{1,0:T(8,128)(2,1)S(1)}, bf16[16,2432]{1,0:T(8,128)(2,1)S(1)}, u32[]{:S(2)}, u32[]{:S(2)}) collective-permute-start(bf16[16,2432]{1,0:T(8,128)(2,1)S(1)} %get-tuple-element.28.refs_0_), channel_id=1, source_target_pairs={{0,2},{1,3},{2,0},{3,1},{4,6},{5,7},{6,4},{7,5},{8,10},{9,11},{10,... | collective-permute-start | bytes 233480 | tf_op jit(solution)/shard_map/ppermute | solution.py:107
  8.0 1.6 %collective-permute-start.2 = (bf16[16,2432]{1,0:T(8,128)(2,1)S(1)}, bf16[16,2432]{1,0:T(8,128)(2,1)S(1)}, u32[]{:S(2)}, u32[]{:S(2)}) collective-permute-start(bf16[16,2432]{1,0:T(8,128)(2,1)S(1)} %collective-permute-done.refs_0_), channel_id=1, source_target_pairs={{0,1},{1,0},{2,3},{3,2},{4,5},{5,4},{6,7},{7,6},{8,9},{9,8},{10,11... | collective-permute-start | bytes 233480 | tf_op jit(solution)/shard_map/ppermute | solution.py:107
  11.5 1.2 %collective-permute-start.3 = (f32[16,128]{1,0:T(8,128)S(1)}, f32[16,128]{1,0:T(8,128)S(1)}, u32[]{:S(2)}, u32[]{:S(2)}) collective-permute-start(f32[16,128]{1,0:T(8,128)S(1)} %get-tuple-element.43.mine.refs_0_), channel_id=1, source_target_pairs={{0,1},{1,0},{2,3},{3,2},{4,5},{5,4},{6,7},{7,6},{8,9},{9,8},{10,11... | collective-permute-start | bytes 24584 | tf_op jit(solution)/shard_map/ppermute | solution.py:107
  12.7 3.7 %collective-permute-start.4 = (f32[8,128]{1,0:T(8,128)S(1)}, f32[8,128]{1,0:T(8,128)S(1)}, u32[]{:S(2)}, u32[]{:S(2)}) collective-permute-start(f32[8,128]{1,0:T(8,128)S(1)} %shard_map.90.refs_1_), channel_id=1, source_target_pairs={{0,2},{1,3},{2,0},{3,1},{4,6},{5,7},{6,4},{7,5},{8,10},{9,11},{10,... | collective-permute-start | bytes 12296 | tf_op jit(solution)/shard_map/ppermute | solution.py:107
  17.7 4.6 %collective-permute-start.5 = (bf16[64,639]{1,0:T(8,128)(2,1)S(1)}, bf16[64,639]{1,0:T(8,128)(2,1)S(1)}, u32[]{:S(2)}, u32[]{:S(2)}) collective-permute-start(bf16[64,639]{1,0:T(8,128)(2,1)S(1)} %get-tuple-element.49.refs_0_), channel_id=1, source_target_pairs={{0,4},{4,0},{8,12},{12,8},{1,5},{5,1},{9,13},{13,9},{2,6},{6,2},{1... | collective-permute-start | bytes 245384 | tf_op jit(solution)/shard_map/ppermute | solution.py:107
  21.1 5.0 %collective-permute-start.6 = (bf16[64,619]{1,0:T(8,128)(2,1)S(1)}, bf16[64,619]{1,0:T(8,128)(2,1)S(1)}, u32[]{:S(2)}, u32[]{:S(2)}) collective-permute-start(bf16[64,619]{1,0:T(8,128)(2,1)S(1)} %get-tuple-element.51), channel_id=1, source_target_pairs={{0,4},{4,0},{8,12},{12,8},{1,5},{5,1},{9,13},{13,9},{2,6},{6,2},{1... | collective-permute-start | bytes 237704 | tf_op jit(solution)/shard_map/ppermute | solution.py:107
  22.4 5.4 %collective-permute-start.7 = (bf16[64,599]{1,0:T(8,128)(2,1)S(1)}, bf16[64,599]{1,0:T(8,128)(2,1)S(1)}, u32[]{:S(2)}, u32[]{:S(2)}) collective-permute-start(bf16[64,599]{1,0:T(8,128)(2,1)S(1)} %shard_map.93.refs_0_), channel_id=1, source_target_pairs={{0,8},{4,12},{8,0},{12,4},{1,9},{5,13},{9,1},{13,5},{2,10},{6,14},... | collective-permute-start | bytes 230024 | tf_op jit(solution)/shard_map/ppermute | solution.py:107

commit v18 on v17

--- a/solution.py
+++ b/solution.py
@@ -395,7 +395,7 @@
     return tiles
 
 
-def block_sums(doms, width, main, distance, weight_ref, shifted_ref, tails_ref):
+def block_sums(doms, width, main, distance, weight_ref, shifted_ref):
     classes = weight_ref.shape[0] // ROTS
     padded = -(-(width + 3) // LANES) * LANES
     place = lax.axis_index("dom") ^ distance
@@ -412,13 +412,9 @@
             min(2 * LANES, span - start),
         )
     if main:
-        tail = None
-        for dom in range(doms):
-            part = dom * ANG // LANES * LANES
-            piece = tails_ref[:, part : part + LANES]
-            piece = pltpu.roll(piece, ANG, 1) if dom % 2 else piece
-            tail = piece if tail is None else jnp.where(place == dom, piece, tail)
-        tiles.append(tail)
+        start = pl.multiple_of(doms * main + place * ANG // LANES * LANES, LANES)
+        (tail,) = window_sums(weight_ref, shifted_ref, start, LANES)
+        tiles.append(jnp.where(place % 2 == 1, pltpu.roll(tail, ANG, 1), tail))
     total = jnp.concatenate(tiles, axis=1)
     aligned = total
     for shift in shifts:
@@ -455,21 +451,17 @@
 
 
 def first_sums_kernel(count, doms, width, main, blocks, *refs):
-    stats_ref, mine, other, exp_ref, shifted_ref, weight_ref, mass_ref, tails_ref = refs[:8]
+    stats_ref, mine, other, exp_ref, shifted_ref, weight_ref, mass_ref = refs[:7]
     mass = weigh(count, stats_ref, mine, other, exp_ref, weight_ref)
     mass_ref[...] = mass
-    tails_ref[...] = jnp.zeros_like(tails_ref)
-    for start in range(0, doms * ANG if main else 0, 2 * LANES):
-        tiles = window_sums(weight_ref, shifted_ref, doms * main + start, 2 * LANES)
-        tails_ref[:, start : start + 2 * LANES] = jnp.concatenate(tiles, axis=1)
-    for block, out_ref in zip(blocks, refs[8:]):
-        value = block_sums(doms, width, main, block, weight_ref, shifted_ref, tails_ref)
+    for block, out_ref in zip(blocks, refs[7:]):
+        value = block_sums(doms, width, main, block, weight_ref, shifted_ref)
         store_block(width, value, mass[:, :1], out_ref)
 
 
-def rest_sums_kernel(doms, width, main, blocks, weight_ref, shifted_ref, mass_ref, tails_ref, *refs):
+def rest_sums_kernel(doms, width, main, blocks, weight_ref, shifted_ref, mass_ref, *refs):
     for block, out_ref in zip(blocks, refs[-len(blocks) :]):
-        value = block_sums(doms, width, main, block, weight_ref, shifted_ref, tails_ref)
+        value = block_sums(doms, width, main, block, weight_ref, shifted_ref)
         store_block(width, value, mass_ref[:, :1], out_ref)
 
 
@@ -611,12 +603,11 @@
     order = early + [1] + sorted(range(2, doms, 2), key=lambda b: (low_bit(b), -b))
     extents = {b: width + 3 + (doms - 1 - place) * growth for place, b in enumerate(order)}
     late = [1] + list(range(2, doms, 2))
-    weights, mass, tails, *made = call(
+    weights, mass, *made = call(
         functools.partial(first_sums_kernel, count, doms, width, main, early),
         [
             shape((ROTS * classes, count * rows), bf16),
             shape((classes, LANES), f32),
-            shape((classes, doms * ANG if main else LANES), f32),
         ]
         + [shape((classes, extents[b]), bf16) for b in early],
         [],
@@ -636,7 +627,7 @@
         [],
         1024,
         1024,
-        weights, shifted, mass, tails, *made,
+        weights, shifted, mass, *made,
         chip=(1,),
     )
     blocks = dict(zip(late, rest))
@@ -657,7 +648,7 @@
         [],
         1024,
         1024,
-        weights, shifted, mass, tails, block,
+        weights, shifted, mass, block,
         chip=(1,),
     )
     received = incoming[0]

time: 28.7 us -> 28.9 us (level)
  Pallas kernels: 12.3 us -> 13.1 us
  waiting for transfers between devices: 5.24 us -> 4.46 us
    pallas_call x10, Pallas kernels: 12.3 us -> 13.1 us  [call(): pl.pallas_call(kernel, out_shape=[pltpu.VMEM(s.shape, s.dtype) if pinned...]
    ppermute x8, waiting for transfers between devices: 5.24 us -> 4.46 us  [exchange(): lax.ppermute(array, axis, [(i, i ^ distance) for i in range(lax.axis_size...]
  transfers between devices with their start and end apart: 8 -> 8, of which waited for: 4 -> 4; matrix products, arithmetic and copies ran while one was open for 0% -> 0% of each run, Pallas kernels for 25% -> 27%
where the time goes in v18:
time: 28.9 us; the launch traced here: 28.7 us
  Pallas kernels  13.1 us (45%)
  starting transfers between devices  10.4 us (36%)
  waiting for transfers between devices  4.46 us (15%)
  between operations  0.69 us (2%)
    pallas_call x10, Pallas kernels, call(): pl.pallas_call(kernel, out_shape=[pltpu.VMEM(s.shape, s.dtype) if pinned...  13.1 us
    ppermute x8, starting transfers between devices, exchange(): lax.ppermute(array, axis, [(i, i ^ distance) for i in range(lax.axis_size...  10.4 us
    ppermute x8, waiting for transfers between devices, exchange(): lax.ppermute(array, axis, [(i, i ^ distance) for i in range(lax.axis_size...  4.46 us
  transfers between devices with their start and end apart: 8, of which 4 were waited for; matrix products, arithmetic and copies ran while one was open for 0% of the time, Pallas kernels for 27%

profile of v18, /device:TPU:0, one launch (start us, length us, event | category | flops | bytes accessed | tf_op | source)
XLA Modules:
  0.0 28.7 jit_solution(14069224136279388193)
XLA Ops:
  0.6 1.3 %shard_map.86 = (bf16[16,2432]{1,0:T(8,128)(2,1)S(1)}, bf16[64,2304]{1,0:T(8,128)(2,1)S(1)}, f32[1,64]{1,0:T(1,128)S(1)}, f32[48,2304]{1,0:T(8,128)S(1)}) custom-call(bf16[16,2304]{1,0:T(8,128)(2,1)} %particle_hbm.1, s32[16,16]{1,0:T(8,128)} %index_hbm.1, s32[1,16]{1,0:T(1,128)} %bitcast.4, s32[1,16]{1,0:T(1,128)} %bitcast.5, bf16[64,2304]{1,0:T(8,128)(2,1)} %class_hbm.1, ...), custom_call_target="tpu_custom_call" | custom-call | flops 36864 | bytes 147456 | tf_op jit(solution)/shard_map/pallas_call | solution.py:502
  1.9 0.5 %collective-permute-start.1 = (bf16[16,2432]{1,0:T(8,128)(2,1)S(1)}, bf16[16,2432]{1,0:T(8,128)(2,1)S(1)}, u32[]{:S(2)}, u32[]{:S(2)}) collective-permute-start(bf16[16,2432]{1,0:T(8,128)(2,1)S(1)} %get-tuple-element.27.refs_0_), channel_id=1, source_target_pairs={{0,1},{1,0},{2,3},{3,2},{4,5},{5,4},{6,7},{7,6},{8,9},{9,8},{10,11... | collective-permute-start | bytes 233480 | tf_op jit(solution)/shard_map/ppermute | solution.py:107
  2.4 2.6 %collective-permute-start = (bf16[16,2432]{1,0:T(8,128)(2,1)S(1)}, bf16[16,2432]{1,0:T(8,128)(2,1)S(1)}, u32[]{:S(2)}, u32[]{:S(2)}) collective-permute-start(bf16[16,2432]{1,0:T(8,128)(2,1)S(1)} %get-tuple-element.27.refs_0_), channel_id=1, source_target_pairs={{0,2},{1,3},{2,0},{3,1},{4,6},{5,7},{6,4},{7,5},{8,10},{9,11},{10,... | collective-permute-start | bytes 233480 | tf_op jit(solution)/shard_map/ppermute | solution.py:107
  5.0 0.0 collective-permute-done.1.refs_1_
  5.0 3.0 %shard_map.87 = (bf16[1024,2304]{1,0:T(8,128)(2,1)S(1)}, f32[512,1024]{1,0:T(8,128)S(1)}, f32[16,128]{1,0:T(8,128)S(1)}, bf16[512,2304]{1,0:T(8,128)(2,1)S(1)}, ...) custom-call(bf16[16,2432]{1,0:T(8,128)(2,1)S(1)} %get-tuple-element.27.refs_0_, ...), custom_call_target="tpu_custom_call" | custom-call | flops 1811939328 | bytes 4718592 | tf_op jit(solution)/shard_map/pallas_call | solution.py:502
  8.0 0.0 collective-permute-done.refs_0_
  8.0 0.2 collective-permute-start.2
  8.2 1.4 %shard_map.88 = (bf16[1024,2304]{1,0:T(8,128)(2,1)S(1)}, f32[512,1024]{1,0:T(8,128)S(1)}, f32[16,128]{1,0:T(8,128)S(1)}) custom-call(bf16[16,2432]{1,0:T(8,128)(2,1)S(1)} %collective-permute-done.refs_0_, bf16[256,2304]{1,0:T(8,128)(2,1)S(1)} %get-tuple-element.33.refs_1_, ...), custom_call_target="tpu_custom_call", output_to_operand_aliasing={{0}: (6, {}), {1}: (7, {})} | custom-call | flops 905969664 | bytes 2359296 | tf_op jit(solution)/shard_map/pallas_call | solution.py:502
  9.6 0.0 collective-permute-done.2.refs_0_
  9.6 1.9 %shard_map.89 = (bf16[1024,2304]{1,0:T(8,128)(2,1)S(1)}, f32[512,1024]{1,0:T(8,128)S(1)}, f32[16,128]{1,0:T(8,128)S(1)}) custom-call(bf16[16,2432]{1,0:T(8,128)(2,1)S(1)} %collective-permute-done.2.refs_0_, bf16[256,2304]{1,0:T(8,128)(2,1)S(1)} %get-tuple-element.33.refs_1_, ...), custom_call_target="tpu_custom_call", output_to_operand_aliasing={{0}: (6, {}), {1}: (7, {})} | custom-call | flops 905969664 | bytes 2359296 | tf_op jit(solution)/shard_map/pallas_call | solution.py:502
  11.5 0.4 %collective-permute-start.3 = (f32[16,128]{1,0:T(8,128)S(1)}, f32[16,128]{1,0:T(8,128)S(1)}, u32[]{:S(2)}, u32[]{:S(2)}) collective-permute-start(f32[16,128]{1,0:T(8,128)S(1)} %get-tuple-element.42.mine.refs_0_), channel_id=1, source_target_pairs={{0,1},{1,0},{2,3},{3,2},{4,5},{5,4},{6,7},{7,6},{8,9},{9,8},{10,11... | collective-permute-start | bytes 24584 | tf_op jit(solution)/shard_map/ppermute | solution.py:107
  11.8 0.8 %collective-permute-done.3.other = f32[16,128]{1,0:T(8,128)S(1)} collective-permute-done((f32[16,128]{1,0:T(8,128)S(1)}, f32[16,128]{1,0:T(8,128)S(1)}, u32[]{:S(2)}, u32[]{:S(2)}) %collective-permute-start.3) | collective-permute-done | bytes 8224 | tf_op jit(solution)/shard_map/ppermute | solution.py:107
  12.7 1.8 %collective-permute-start.4 = (f32[8,128]{1,0:T(8,128)S(1)}, f32[8,128]{1,0:T(8,128)S(1)}, u32[]{:S(2)}, u32[]{:S(2)}) collective-permute-start(f32[8,128]{1,0:T(8,128)S(1)} %shard_map.90.refs_1_), channel_id=1, source_target_pairs={{0,2},{1,3},{2,0},{3,1},{4,6},{5,7},{6,4},{7,5},{8,10},{9,11},{10,... | collective-permute-start | bytes 12296 | tf_op jit(solution)/shard_map/ppermute | solution.py:107
  14.4 1.9 %collective-permute-done.4.refs_2_ = f32[8,128]{1,0:T(8,128)S(1)} collective-permute-done((f32[8,128]{1,0:T(8,128)S(1)}, f32[8,128]{1,0:T(8,128)S(1)}, u32[]{:S(2)}, u32[]{:S(2)}) %collective-permute-start.4) | collective-permute-done | bytes 4128 | tf_op jit(solution)/shard_map/ppermute | solution.py:107
  16.3 1.4 %shard_map.91 = (bf16[512,1024]{1,0:T(8,128)(2,1)S(1)}, f32[64,128]{1,0:T(8,128)S(1)}, bf16[64,639]{1,0:T(8,128)(2,1)S(1)}) custom-call(f32[16,128]{1,0:T(8,128)S(1)} %get-tuple-element.42.mine.refs_0_, f32[8,128]{1,0:T(8,128)S(1)} %shard_map.90.refs_1_, f32[8,128]{1,0:T(8,128)S(1)} %collective-permute-done.4.refs_2_, ...), custom_call_target="tpu_custom_call" | custom-call | flops 603979776 | bytes 2359296 | tf_op jit(solution)/shard_map/pallas_call | solution.py:502
  17.7 1.9 %collective-permute-start.5 = (bf16[64,639]{1,0:T(8,128)(2,1)S(1)}, bf16[64,639]{1,0:T(8,128)(2,1)S(1)}, u32[]{:S(2)}, u32[]{:S(2)}) collective-permute-start(bf16[64,639]{1,0:T(8,128)(2,1)S(1)} %get-tuple-element.47.refs_0_), channel_id=1, source_target_pairs={{0,4},{4,0},{8,12},{12,8},{1,5},{5,1},{9,13},{13,9},{2,6},{6,2},{1... | collective-permute-start | bytes 245384 | tf_op jit(solution)/shard_map/ppermute | solution.py:107
  19.6 2.1 %shard_map.92 = (bf16[64,619]{1,0:T(8,128)(2,1)S(1)}, f32[64,599]{1,0:T(8,128)S(1)}) custom-call(bf16[512,1024]{1,0:T(8,128)(2,1)S(1)} %get-tuple-element.45.weight_ref, bf16[1024,2304]{1,0:T(8,128)(2,1)S(1)} %get-tuple-element.44.refs_4_.shifted_ref, f32[64,128]{1,0:T(8,128)S(1)} %get-tuple-element.46.mass_ref, bf16[64,639]{1,0:T(8,128)(2,1)S(1)} %get-tuple-element.47.refs_0_), custom_call_target="tpu_custom_call" | custom-call | flops 1024 | bytes 1024 | tf_op jit(solution)/shard_map/pallas_call | solution.py:502
  21.7 0.3 collective-permute-start.6
  22.0 0.2 collective-permute-done.5.refs_1_
  22.2 0.1 shard_map.93.refs_0_
  22.4 2.8 %collective-permute-start.7 = (bf16[64,599]{1,0:T(8,128)(2,1)S(1)}, bf16[64,599]{1,0:T(8,128)(2,1)S(1)}, u32[]{:S(2)}, u32[]{:S(2)}) collective-permute-start(bf16[64,599]{1,0:T(8,128)(2,1)S(1)} %shard_map.93.refs_0_), channel_id=1, source_target_pairs={{0,8},{4,12},{8,0},{12,4},{1,9},{5,13},{9,1},{13,5},{2,10},{6,14},... | collective-permute-start | bytes 230024 | tf_op jit(solution)/shard_map/ppermute | solution.py:107
  25.2 1.3 %shard_map.94.own_ref = f32[64,579]{1,0:T(8,128)S(1)} custom-call(bf16[512,1024]{1,0:T(8,128)(2,1)S(1)} %get-tuple-element.45.weight_ref, bf16[1024,2304]{1,0:T(8,128)(2,1)S(1)} %get-tuple-element.44.refs_4_.shifted_ref, f32[64,128]{1,0:T(8,128)S(1)} %get-tuple-element.46.mass_ref, bf16[64,599]{1,0:T(8,128)(2,1)S(1)} %shard_map.93.refs_0_), custom_call_target="tpu_custom_call" | custom-call | flops 1024 | bytes 1024 | tf_op jit(solution)/shard_map/pallas_call | solution.py:502
  26.5 0.0 collective-permute-done.6.refs_0_
  26.5 1.5 %collective-permute-done.7.refs_1_ = bf16[64,599]{1,0:T(8,128)(2,1)S(1)} collective-permute-done((bf16[64,599]{1,0:T(8,128)(2,1)S(1)}, bf16[64,599]{1,0:T(8,128)(2,1)S(1)}, u32[]{:S(2)}, u32[]{:S(2)}) %collective-permute-start.7) | collective-permute-done | bytes 76704 | tf_op jit(solution)/shard_map/ppermute | solution.py:107
  27.9 0.7 %shard_map.95 = (f32[64,576]{1,0:T(8,128)}, f32[1,64]{1,0:T(1,128)}) custom-call(f32[64,579]{1,0:T(8,128)S(1)} %shard_map.94.own_ref, bf16[64,619]{1,0:T(8,128)(2,1)S(1)} %collective-permute-done.6.refs_0_, bf16[64,599]{1,0:T(8,128)(2,1)S(1)} %collective-permute-done.7.refs_1_), custom_call_target="tpu_custom_call" | custom-call | flops 163840 | bytes 655360 | tf_op jit(solution)/shard_map/pallas_call | solution.py:502
  (1 shorter events, 0.0 us)
Async XLA Ops:
  1.9 3.1 %collective-permute-start.1 = (bf16[16,2432]{1,0:T(8,128)(2,1)S(1)}, bf16[16,2432]{1,0:T(8,128)(2,1)S(1)}, u32[]{:S(2)}, u32[]{:S(2)}) collective-permute-start(bf16[16,2432]{1,0:T(8,128)(2,1)S(1)} %get-tuple-element.27.refs_0_), channel_id=1, source_target_pairs={{0,1},{1,0},{2,3},{3,2},{4,5},{5,4},{6,7},{7,6},{8,9},{9,8},{10,11... | collective-permute-start | bytes 233480 | tf_op jit(solution)/shard_map/ppermute | solution.py:107
  2.4 5.5 %collective-permute-start = (bf16[16,2432]{1,0:T(8,128)(2,1)S(1)}, bf16[16,2432]{1,0:T(8,128)(2,1)S(1)}, u32[]{:S(2)}, u32[]{:S(2)}) collective-permute-start(bf16[16,2432]{1,0:T(8,128)(2,1)S(1)} %get-tuple-element.27.refs_0_), channel_id=1, source_target_pairs={{0,2},{1,3},{2,0},{3,1},{4,6},{5,7},{6,4},{7,5},{8,10},{9,11},{10,... | collective-permute-start | bytes 233480 | tf_op jit(solution)/shard_map/ppermute | solution.py:107
  8.0 1.6 %collective-permute-start.2 = (bf16[16,2432]{1,0:T(8,128)(2,1)S(1)}, bf16[16,2432]{1,0:T(8,128)(2,1)S(1)}, u32[]{:S(2)}, u32[]{:S(2)}) collective-permute-start(bf16[16,2432]{1,0:T(8,128)(2,1)S(1)} %collective-permute-done.refs_0_), channel_id=1, source_target_pairs={{0,1},{1,0},{2,3},{3,2},{4,5},{5,4},{6,7},{7,6},{8,9},{9,8},{10,11... | collective-permute-start | bytes 233480 | tf_op jit(solution)/shard_map/ppermute | solution.py:107
  11.5 1.2 %collective-permute-start.3 = (f32[16,128]{1,0:T(8,128)S(1)}, f32[16,128]{1,0:T(8,128)S(1)}, u32[]{:S(2)}, u32[]{:S(2)}) collective-permute-start(f32[16,128]{1,0:T(8,128)S(1)} %get-tuple-element.42.mine.refs_0_), channel_id=1, source_target_pairs={{0,1},{1,0},{2,3},{3,2},{4,5},{5,4},{6,7},{7,6},{8,9},{9,8},{10,11... | collective-permute-start | bytes 24584 | tf_op jit(solution)/shard_map/ppermute | solution.py:107
  12.7 3.7 %collective-permute-start.4 = (f32[8,128]{1,0:T(8,128)S(1)}, f32[8,128]{1,0:T(8,128)S(1)}, u32[]{:S(2)}, u32[]{:S(2)}) collective-permute-start(f32[8,128]{1,0:T(8,128)S(1)} %shard_map.90.refs_1_), channel_id=1, source_target_pairs={{0,2},{1,3},{2,0},{3,1},{4,6},{5,7},{6,4},{7,5},{8,10},{9,11},{10,... | collective-permute-start | bytes 12296 | tf_op jit(solution)/shard_map/ppermute | solution.py:107
  17.7 4.5 %collective-permute-start.5 = (bf16[64,639]{1,0:T(8,128)(2,1)S(1)}, bf16[64,639]{1,0:T(8,128)(2,1)S(1)}, u32[]{:S(2)}, u32[]{:S(2)}) collective-permute-start(bf16[64,639]{1,0:T(8,128)(2,1)S(1)} %get-tuple-element.47.refs_0_), channel_id=1, source_target_pairs={{0,4},{4,0},{8,12},{12,8},{1,5},{5,1},{9,13},{13,9},{2,6},{6,2},{1... | collective-permute-start | bytes 245384 | tf_op jit(solution)/shard_map/ppermute | solution.py:107
  21.7 4.7 %collective-permute-start.6 = (bf16[64,619]{1,0:T(8,128)(2,1)S(1)}, bf16[64,619]{1,0:T(8,128)(2,1)S(1)}, u32[]{:S(2)}, u32[]{:S(2)}) collective-permute-start(bf16[64,619]{1,0:T(8,128)(2,1)S(1)} %get-tuple-element.49), channel_id=1, source_target_pairs={{0,4},{4,0},{8,12},{12,8},{1,5},{5,1},{9,13},{13,9},{2,6},{6,2},{1... | collective-permute-start | bytes 237704 | tf_op jit(solution)/shard_map/ppermute | solution.py:107
  22.4 5.6 %collective-permute-start.7 = (bf16[64,599]{1,0:T(8,128)(2,1)S(1)}, bf16[64,599]{1,0:T(8,128)(2,1)S(1)}, u32[]{:S(2)}, u32[]{:S(2)}) collective-permute-start(bf16[64,599]{1,0:T(8,128)(2,1)S(1)} %shard_map.93.refs_0_), channel_id=1, source_target_pairs={{0,8},{4,12},{8,0},{12,4},{1,9},{5,13},{9,1},{13,5},{2,10},{6,14},... | collective-permute-start | bytes 230024 | tf_op jit(solution)/shard_map/ppermute | solution.py:107

commit v19 on v17

--- a/solution.py
+++ b/solution.py
@@ -61,8 +61,8 @@
     along_x = unit * offsets[:, None] * fx[None, :]
     along_y = unit * offsets[:, None] * fy[None, :]
     both = (along_x[SUB:, None, :] + along_y[None, SUB:, :]).reshape(-1, HALF)
-    values = np.zeros((48, COLS), np.float32)
-    for start, phase in ((0, along_x), (16, along_y), (32, both)):
+    values = np.zeros((40, COLS), np.float32)
+    for start, phase in ((0, along_x), (11, along_y), (22, both)):
         values[start : start + len(phase)] = np.concatenate([np.cos(phase), np.sin(phase)], axis=1)
     columns = np.concatenate([np.arange(ANG) + ANG * group for group in groups])
     return values[:, columns]
@@ -78,11 +78,11 @@
             d, t = rows_ref[row : row + 1, real], rows_ref[row : row + 1, imag]
             return c * d - s * t, s * d + c * t
 
-        blocks = [product(0, 16 + y) for y in range(SHIFTW)]
-        blocks += [product(16, x) for x in range(SUB, SHIFTW)]
+        blocks = [product(0, 11 + y) for y in range(SHIFTW)]
+        blocks += [product(11, x) for x in range(SUB, SHIFTW)]
         blocks += [
             (rows_ref[row : row + SUB, real], rows_ref[row : row + SUB, imag])
-            for row in (32, 32 + SUB)
+            for row in (22, 22 + SUB)
         ]
         for pair in range(0, len(blocks), 2):
             for part, columns in ((0, real), (1, imag)):

time: 28.7 us -> 28.7 us (level)
  no operation moved by 1% of the time
where the time goes in v19:
time: 28.7 us; the launch traced here: 28.5 us
  Pallas kernels  12.3 us (43%)
  starting transfers between devices  10.3 us (36%)
  waiting for transfers between devices  5.19 us (18%)
  between operations  0.7 us (2%)
    pallas_call x10, Pallas kernels, call(): pl.pallas_call(kernel, out_shape=[pltpu.VMEM(s.shape, s.dtype) if pinned...  12.3 us
    ppermute x8, starting transfers between devices, exchange(): lax.ppermute(array, axis, [(i, i ^ distance) for i in range(lax.axis_size...  10.3 us
    ppermute x8, waiting for transfers between devices, exchange(): lax.ppermute(array, axis, [(i, i ^ distance) for i in range(lax.axis_size...  5.19 us
  transfers between devices with their start and end apart: 8, of which 4 were waited for; matrix products, arithmetic and copies ran while one was open for 0% of the time, Pallas kernels for 25%

profile of v19, /device:TPU:0, one launch (start us, length us, event | category | flops | bytes accessed | tf_op | source)
XLA Modules:
  0.0 28.5 jit_solution(4925546787755950879)
XLA Ops:
  0.6 1.2 %shard_map.86 = (bf16[16,2432]{1,0:T(8,128)(2,1)S(1)}, bf16[64,2304]{1,0:T(8,128)(2,1)S(1)}, f32[1,64]{1,0:T(1,128)S(1)}, f32[40,2304]{1,0:T(8,128)S(1)}) custom-call(bf16[16,2304]{1,0:T(8,128)(2,1)} %particle_hbm.1, s32[16,16]{1,0:T(8,128)} %index_hbm.1, s32[1,16]{1,0:T(1,128)} %bitcast.4, s32[1,16]{1,0:T(1,128)} %bitcast.5, bf16[64,2304]{1,0:T(8,128)(2,1)} %class_hbm.1, ...), custom_call_target="tpu_custom_call" | custom-call | flops 36864 | bytes 147456 | tf_op jit(solution)/shard_map/pallas_call | solution.py:510
  1.9 0.5 %collective-permute-start.1 = (bf16[16,2432]{1,0:T(8,128)(2,1)S(1)}, bf16[16,2432]{1,0:T(8,128)(2,1)S(1)}, u32[]{:S(2)}, u32[]{:S(2)}) collective-permute-start(bf16[16,2432]{1,0:T(8,128)(2,1)S(1)} %get-tuple-element.28.refs_0_), channel_id=1, source_target_pairs={{0,1},{1,0},{2,3},{3,2},{4,5},{5,4},{6,7},{7,6},{8,9},{9,8},{10,11... | collective-permute-start | bytes 233480 | tf_op jit(solution)/shard_map/ppermute | solution.py:107
  2.4 2.6 %collective-permute-start = (bf16[16,2432]{1,0:T(8,128)(2,1)S(1)}, bf16[16,2432]{1,0:T(8,128)(2,1)S(1)}, u32[]{:S(2)}, u32[]{:S(2)}) collective-permute-start(bf16[16,2432]{1,0:T(8,128)(2,1)S(1)} %get-tuple-element.28.refs_0_), channel_id=1, source_target_pairs={{0,2},{1,3},{2,0},{3,1},{4,6},{5,7},{6,4},{7,5},{8,10},{9,11},{10,... | collective-permute-start | bytes 233480 | tf_op jit(solution)/shard_map/ppermute | solution.py:107
  5.0 0.0 collective-permute-done.1.refs_1_
  5.0 3.0 %shard_map.87 = (bf16[1024,2304]{1,0:T(8,128)(2,1)S(1)}, f32[512,1024]{1,0:T(8,128)S(1)}, f32[16,128]{1,0:T(8,128)S(1)}, bf16[512,2304]{1,0:T(8,128)(2,1)S(1)}, ...) custom-call(bf16[16,2432]{1,0:T(8,128)(2,1)S(1)} %get-tuple-element.28.refs_0_, ...), custom_call_target="tpu_custom_call" | custom-call | flops 1811939328 | bytes 4718592 | tf_op jit(solution)/shard_map/pallas_call | solution.py:510
  8.0 0.0 collective-permute-done.refs_0_
  8.0 0.2 collective-permute-start.2
  8.2 1.4 %shard_map.88 = (bf16[1024,2304]{1,0:T(8,128)(2,1)S(1)}, f32[512,1024]{1,0:T(8,128)S(1)}, f32[16,128]{1,0:T(8,128)S(1)}) custom-call(bf16[16,2432]{1,0:T(8,128)(2,1)S(1)} %collective-permute-done.refs_0_, bf16[256,2304]{1,0:T(8,128)(2,1)S(1)} %get-tuple-element.34.refs_1_, ...), custom_call_target="tpu_custom_call", output_to_operand_aliasing={{0}: (6, {}), {1}: (7, {})} | custom-call | flops 905969664 | bytes 2359296 | tf_op jit(solution)/shard_map/pallas_call | solution.py:510
  9.6 0.0 collective-permute-done.2.refs_0_
  9.6 1.9 %shard_map.89 = (bf16[1024,2304]{1,0:T(8,128)(2,1)S(1)}, f32[512,1024]{1,0:T(8,128)S(1)}, f32[16,128]{1,0:T(8,128)S(1)}) custom-call(bf16[16,2432]{1,0:T(8,128)(2,1)S(1)} %collective-permute-done.2.refs_0_, bf16[256,2304]{1,0:T(8,128)(2,1)S(1)} %get-tuple-element.34.refs_1_, ...), custom_call_target="tpu_custom_call", output_to_operand_aliasing={{0}: (6, {}), {1}: (7, {})} | custom-call | flops 905969664 | bytes 2359296 | tf_op jit(solution)/shard_map/pallas_call | solution.py:510
  11.5 0.3 %collective-permute-start.3 = (f32[16,128]{1,0:T(8,128)S(1)}, f32[16,128]{1,0:T(8,128)S(1)}, u32[]{:S(2)}, u32[]{:S(2)}) collective-permute-start(f32[16,128]{1,0:T(8,128)S(1)} %get-tuple-element.43.mine.refs_0_), channel_id=1, source_target_pairs={{0,1},{1,0},{2,3},{3,2},{4,5},{5,4},{6,7},{7,6},{8,9},{9,8},{10,11... | collective-permute-start | bytes 24584 | tf_op jit(solution)/shard_map/ppermute | solution.py:107
  11.8 0.8 %collective-permute-done.3.other = f32[16,128]{1,0:T(8,128)S(1)} collective-permute-done((f32[16,128]{1,0:T(8,128)S(1)}, f32[16,128]{1,0:T(8,128)S(1)}, u32[]{:S(2)}, u32[]{:S(2)}) %collective-permute-start.3) | collective-permute-done | bytes 8224 | tf_op jit(solution)/shard_map/ppermute | solution.py:107
  12.7 1.7 %collective-permute-start.4 = (f32[8,128]{1,0:T(8,128)S(1)}, f32[8,128]{1,0:T(8,128)S(1)}, u32[]{:S(2)}, u32[]{:S(2)}) collective-permute-start(f32[8,128]{1,0:T(8,128)S(1)} %shard_map.90.refs_1_), channel_id=1, source_target_pairs={{0,2},{1,3},{2,0},{3,1},{4,6},{5,7},{6,4},{7,5},{8,10},{9,11},{10,... | collective-permute-start | bytes 12296 | tf_op jit(solution)/shard_map/ppermute | solution.py:107
  14.4 2.0 %collective-permute-done.4.refs_2_ = f32[8,128]{1,0:T(8,128)S(1)} collective-permute-done((f32[8,128]{1,0:T(8,128)S(1)}, f32[8,128]{1,0:T(8,128)S(1)}, u32[]{:S(2)}, u32[]{:S(2)}) %collective-permute-start.4) | collective-permute-done | bytes 4128 | tf_op jit(solution)/shard_map/ppermute | solution.py:107
  16.3 1.4 %shard_map.91 = (bf16[512,1024]{1,0:T(8,128)(2,1)S(1)}, f32[64,128]{1,0:T(8,128)S(1)}, f32[64,256]{1,0:T(8,128)S(1)}, bf16[64,639]{1,0:T(8,128)(2,1)S(1)}) custom-call(f32[16,128]{1,0:T(8,128)S(1)} %get-tuple-element.43.mine.refs_0_, f32[8,128]{1,0:T(8,128)S(1)} %shard_map.90.refs_1_, f32[8,128]{1,0:T(8,128)S(1)} %collective-permute-done.4.refs_2_, ...), custom_call_target="tpu_custom_call" | custom-call | flops 603979776 | bytes 2359296 | tf_op jit(solution)/shard_map/pallas_call | solution.py:510
  17.7 1.8 %collective-permute-start.5 = (bf16[64,639]{1,0:T(8,128)(2,1)S(1)}, bf16[64,639]{1,0:T(8,128)(2,1)S(1)}, u32[]{:S(2)}, u32[]{:S(2)}) collective-permute-start(bf16[64,639]{1,0:T(8,128)(2,1)S(1)} %get-tuple-element.49.refs_0_), channel_id=1, source_target_pairs={{0,4},{4,0},{8,12},{12,8},{1,5},{5,1},{9,13},{13,9},{2,6},{6,2},{1... | collective-permute-start | bytes 245384 | tf_op jit(solution)/shard_map/ppermute | solution.py:107
  19.5 1.6 %shard_map.92 = (bf16[64,619]{1,0:T(8,128)(2,1)S(1)}, f32[64,599]{1,0:T(8,128)S(1)}) custom-call(bf16[512,1024]{1,0:T(8,128)(2,1)S(1)} %get-tuple-element.46.weight_ref, bf16[1024,2304]{1,0:T(8,128)(2,1)S(1)} %get-tuple-element.45.refs_4_.shifted_ref, f32[64,128]{1,0:T(8,128)S(1)} %get-tuple-element.47.mass_ref, f32[64,256]{1,0:T(8,128)S(1)} %get-tuple-element.48.tails_ref, ...), custom_call_target="tpu_custom_call" | custom-call | flops 1024 | bytes 1024 | tf_op jit(solution)/shard_map/pallas_call | solution.py:510
  21.1 0.4 %collective-permute-start.6 = (bf16[64,619]{1,0:T(8,128)(2,1)S(1)}, bf16[64,619]{1,0:T(8,128)(2,1)S(1)}, u32[]{:S(2)}, u32[]{:S(2)}) collective-permute-start(bf16[64,619]{1,0:T(8,128)(2,1)S(1)} %get-tuple-element.51), channel_id=1, source_target_pairs={{0,4},{4,0},{8,12},{12,8},{1,5},{5,1},{9,13},{13,9},{2,6},{6,2},{1... | collective-permute-start | bytes 237704 | tf_op jit(solution)/shard_map/ppermute | solution.py:107
  21.5 0.8 %collective-permute-done.5.refs_1_ = bf16[64,639]{1,0:T(8,128)(2,1)S(1)} collective-permute-done((bf16[64,639]{1,0:T(8,128)(2,1)S(1)}, bf16[64,639]{1,0:T(8,128)(2,1)S(1)}, u32[]{:S(2)}, u32[]{:S(2)}) %collective-permute-start.5) | collective-permute-done | bytes 81824 | tf_op jit(solution)/shard_map/ppermute | solution.py:107
  22.2 0.1 shard_map.93.refs_0_
  22.4 2.8 %collective-permute-start.7 = (bf16[64,599]{1,0:T(8,128)(2,1)S(1)}, bf16[64,599]{1,0:T(8,128)(2,1)S(1)}, u32[]{:S(2)}, u32[]{:S(2)}) collective-permute-start(bf16[64,599]{1,0:T(8,128)(2,1)S(1)} %shard_map.93.refs_0_), channel_id=1, source_target_pairs={{0,8},{4,12},{8,0},{12,4},{1,9},{5,13},{9,1},{13,5},{2,10},{6,14},... | collective-permute-start | bytes 230024 | tf_op jit(solution)/shard_map/ppermute | solution.py:107
  25.2 1.0 %shard_map.94.own_ref = f32[64,579]{1,0:T(8,128)S(1)} custom-call(bf16[512,1024]{1,0:T(8,128)(2,1)S(1)} %get-tuple-element.46.weight_ref, bf16[1024,2304]{1,0:T(8,128)(2,1)S(1)} %get-tuple-element.45.refs_4_.shifted_ref, f32[64,128]{1,0:T(8,128)S(1)} %get-tuple-element.47.mass_ref, f32[64,256]{1,0:T(8,128)S(1)} %get-tuple-element.48.tails_ref, ...), custom_call_target="tpu_custom_call" | custom-call | flops 1024 | bytes 1024 | tf_op jit(solution)/shard_map/pallas_call | solution.py:510
  26.2 0.0 collective-permute-done.6.refs_0_
  26.2 1.6 %collective-permute-done.7.refs_1_ = bf16[64,599]{1,0:T(8,128)(2,1)S(1)} collective-permute-done((bf16[64,599]{1,0:T(8,128)(2,1)S(1)}, bf16[64,599]{1,0:T(8,128)(2,1)S(1)}, u32[]{:S(2)}, u32[]{:S(2)}) %collective-permute-start.7) | collective-permute-done | bytes 76704 | tf_op jit(solution)/shard_map/ppermute | solution.py:107
  27.8 0.7 %shard_map.95 = (f32[64,576]{1,0:T(8,128)}, f32[1,64]{1,0:T(1,128)}) custom-call(f32[64,579]{1,0:T(8,128)S(1)} %shard_map.94.own_ref, bf16[64,619]{1,0:T(8,128)(2,1)S(1)} %collective-permute-done.6.refs_0_, bf16[64,599]{1,0:T(8,128)(2,1)S(1)} %collective-permute-done.7.refs_1_), custom_call_target="tpu_custom_call" | custom-call | flops 163840 | bytes 655360 | tf_op jit(solution)/shard_map/pallas_call | solution.py:510
  (1 shorter events, 0.0 us)
Async XLA Ops:
  1.9 3.1 %collective-permute-start.1 = (bf16[16,2432]{1,0:T(8,128)(2,1)S(1)}, bf16[16,2432]{1,0:T(8,128)(2,1)S(1)}, u32[]{:S(2)}, u32[]{:S(2)}) collective-permute-start(bf16[16,2432]{1,0:T(8,128)(2,1)S(1)} %get-tuple-element.28.refs_0_), channel_id=1, source_target_pairs={{0,1},{1,0},{2,3},{3,2},{4,5},{5,4},{6,7},{7,6},{8,9},{9,8},{10,11... | collective-permute-start | bytes 233480 | tf_op jit(solution)/shard_map/ppermute | solution.py:107
  2.4 5.6 %collective-permute-start = (bf16[16,2432]{1,0:T(8,128)(2,1)S(1)}, bf16[16,2432]{1,0:T(8,128)(2,1)S(1)}, u32[]{:S(2)}, u32[]{:S(2)}) collective-permute-start(bf16[16,2432]{1,0:T(8,128)(2,1)S(1)} %get-tuple-element.28.refs_0_), channel_id=1, source_target_pairs={{0,2},{1,3},{2,0},{3,1},{4,6},{5,7},{6,4},{7,5},{8,10},{9,11},{10,... | collective-permute-start | bytes 233480 | tf_op jit(solution)/shard_map/ppermute | solution.py:107
  8.0 1.6 %collective-permute-start.2 = (bf16[16,2432]{1,0:T(8,128)(2,1)S(1)}, bf16[16,2432]{1,0:T(8,128)(2,1)S(1)}, u32[]{:S(2)}, u32[]{:S(2)}) collective-permute-start(bf16[16,2432]{1,0:T(8,128)(2,1)S(1)} %collective-permute-done.refs_0_), channel_id=1, source_target_pairs={{0,1},{1,0},{2,3},{3,2},{4,5},{5,4},{6,7},{7,6},{8,9},{9,8},{10,11... | collective-permute-start | bytes 233480 | tf_op jit(solution)/shard_map/ppermute | solution.py:107
  11.5 1.2 %collective-permute-start.3 = (f32[16,128]{1,0:T(8,128)S(1)}, f32[16,128]{1,0:T(8,128)S(1)}, u32[]{:S(2)}, u32[]{:S(2)}) collective-permute-start(f32[16,128]{1,0:T(8,128)S(1)} %get-tuple-element.43.mine.refs_0_), channel_id=1, source_target_pairs={{0,1},{1,0},{2,3},{3,2},{4,5},{5,4},{6,7},{7,6},{8,9},{9,8},{10,11... | collective-permute-start | bytes 24584 | tf_op jit(solution)/shard_map/ppermute | solution.py:107
  12.7 3.7 %collective-permute-start.4 = (f32[8,128]{1,0:T(8,128)S(1)}, f32[8,128]{1,0:T(8,128)S(1)}, u32[]{:S(2)}, u32[]{:S(2)}) collective-permute-start(f32[8,128]{1,0:T(8,128)S(1)} %shard_map.90.refs_1_), channel_id=1, source_target_pairs={{0,2},{1,3},{2,0},{3,1},{4,6},{5,7},{6,4},{7,5},{8,10},{9,11},{10,... | collective-permute-start | bytes 12296 | tf_op jit(solution)/shard_map/ppermute | solution.py:107
  17.7 4.5 %collective-permute-start.5 = (bf16[64,639]{1,0:T(8,128)(2,1)S(1)}, bf16[64,639]{1,0:T(8,128)(2,1)S(1)}, u32[]{:S(2)}, u32[]{:S(2)}) collective-permute-start(bf16[64,639]{1,0:T(8,128)(2,1)S(1)} %get-tuple-element.49.refs_0_), channel_id=1, source_target_pairs={{0,4},{4,0},{8,12},{12,8},{1,5},{5,1},{9,13},{13,9},{2,6},{6,2},{1... | collective-permute-start | bytes 245384 | tf_op jit(solution)/shard_map/ppermute | solution.py:107
  21.1 5.1 %collective-permute-start.6 = (bf16[64,619]{1,0:T(8,128)(2,1)S(1)}, bf16[64,619]{1,0:T(8,128)(2,1)S(1)}, u32[]{:S(2)}, u32[]{:S(2)}) collective-permute-start(bf16[64,619]{1,0:T(8,128)(2,1)S(1)} %get-tuple-element.51), channel_id=1, source_target_pairs={{0,4},{4,0},{8,12},{12,8},{1,5},{5,1},{9,13},{13,9},{2,6},{6,2},{1... | collective-permute-start | bytes 237704 | tf_op jit(solution)/shard_map/ppermute | solution.py:107
  22.4 5.4 %collective-permute-start.7 = (bf16[64,599]{1,0:T(8,128)(2,1)S(1)}, bf16[64,599]{1,0:T(8,128)(2,1)S(1)}, u32[]{:S(2)}, u32[]{:S(2)}) collective-permute-start(bf16[64,599]{1,0:T(8,128)(2,1)S(1)} %shard_map.93.refs_0_), channel_id=1, source_target_pairs={{0,8},{4,12},{8,0},{12,4},{1,9},{5,13},{9,1},{13,5},{2,10},{6,14},... | collective-permute-start | bytes 230024 | tf_op jit(solution)/shard_map/ppermute | solution.py:107
